TPU v7x, 32 devices: a whole 2x2x4 slice. The times are simulated.
32 devices in a mesh: groups: 2 (over x), dp: 8 (over z, y), expert: 2 (over core).
Axes of the slice: x: 2, y: 2, z: 4, core: 2. Of those that a mesh axis runs over, the one named last changes fastest.
Arguments:
- expert_ids: int32 [12288, 2], P(('groups', 'dp')), parts along dimension 0, may hold values from 0 to 7, all different within a row; in each aligned block of 768 rows (0 to 767, 768 to 1535, ...) at most 384 rows name the same one
- gates: float32 [12288, 2], P(('groups', 'dp')), parts along dimension 0, may hold values from 0.2 to 1
- expert_out: bfloat16 [49152, 3072], P(('groups', 'dp', 'expert')), parts along dimension 0, may hold values from -6 to 6
Outputs:
- moment: float32 [6144, 3072], P(('groups', 'dp'), 'expert'), parts along dimension 0
There are 2 independent parts, one for each index of `groups`. A program takes and returns all parts, laid end to end along the dimension named above; each array names one. Nothing has to cross between parts.
Inputs may be any that keep to these rules, and one draw needn't show every extreme that they name: `expert_ids`: the two experts of a token differ; of the 768 tokens of one index of dp at most 384 name one expert, a bound that some block reaches.
All inputs are finite; a program needn't handle non-finite values.
Results may differ from a plain program's by a relative error of at most 0.0026.
Values may be sent and summed in bfloat16 or wider, within the bound.
No kernel may reach another device: no remote copies, remote signals or barrier semaphores. Data moves between devices by JAX's collectives and lax.ppermute only.
A program may use at most 128 MiB of HBM per device.

v0:
```python
import jax
import jax.numpy as jnp
from jax import lax
from jax.sharding import PartitionSpec as P

EXPERTS = 8
CAP = 384


def slot_rows(shard_ids):
    labels = jnp.arange(EXPERTS, dtype=jnp.int32)
    matches = (shard_ids[:, :, None] == labels[None, None, :]).astype(jnp.int32)
    named = jnp.sum(matches, axis=1)
    before = jnp.cumsum(named, axis=0) - named
    counts = jnp.sum(matches * before[:, None, :], axis=2)
    return shard_ids * CAP + counts


def gated_rows(source, row_index, weights):
    tokens_here = row_index.shape[0]
    channels = source.shape[1]
    picked = jnp.take(source, row_index.reshape(-1), axis=0).reshape(tokens_here, 2, channels)
    return weights[:, 0:1] * picked[:, 0].astype(jnp.float32) + weights[:, 1:2] * picked[
        :, 1
    ].astype(jnp.float32)


def per_device(expert_ids, gates, expert_out):
    row_index = slot_rows(expert_ids)
    member = lax.axis_index("expert")
    members = lax.axis_size("expert")
    token_count = row_index.shape[0]
    channels = expert_out.shape[1]
    gathered = lax.all_gather(expert_out, "expert", axis=0, tiled=True)
    combined = gated_rows(gathered, row_index, gates).astype(jnp.bfloat16)
    dp_size = lax.axis_size("dp")
    total_tokens = token_count * dp_size
    halfwidth = channels // members
    columns = lax.dynamic_slice_in_dim(combined, member * halfwidth, halfwidth, 1)
    moment_slab = lax.psum_scatter(
        lax.dot_general(
            combined, columns, (((0,), (0,)), ((), ())), preferred_element_type=jnp.float32
        ),
        "dp",
        scatter_dimension=0,
        tiled=True,
    )
    return moment_slab / total_tokens


def solution(mesh):
    in_specs = (
        P(("groups", "dp"), None),
        P(("groups", "dp"), None),
        P(("groups", "dp", "expert"), None),
    )
    out_specs = P(("groups", "dp"), "expert")
    return jax.shard_map(
        per_device, mesh=mesh, in_specs=in_specs, out_specs=out_specs, check_vma=False
    )
```

profile of v0, /device:TPU:1, one launch (start us, length us, event | category | flops | bytes accessed | tf_op | source)
XLA Modules:
  0.0 461.9 jit_solution(7475522562778077054)
XLA Ops:
  6.5 0.0 copy-start
  6.5 0.0 copy-start.1
  6.5 0.0 all-gather.2.cloned.1.call-start
  6.5 0.7 all-gather.2.cloned.1.call-update
  7.3 0.0 reduce-scatter.2.cloned.1.call-start
  7.3 0.0 copy-done
  7.3 1.7 reduce-window.6
  9.0 0.1 slice.26
  9.1 0.1 copy.16
  9.3 0.2 reduce-window.9
  9.4 0.1 copy.17
  9.5 0.1 bitcast_subtract_fusion
  9.6 0.2 copy.19
  9.8 0.3 reshape.61
  10.1 0.2 copy.18
  10.4 0.0 copy-done.1
  10.4 34.8 %all-gather.2.cloned.1.call-done = bf16[3072,3072]{1,0:T(8,128)(2,1)} async-done(((bf16[1536,3072]{1,0:T(8,128)(2,1)}), bf16[3072,3072]{1,0:T(8,128)(2,1)}) %all-gather.2.cloned.1.call-update) | async-done | bytes 18874384 | tf_op jit(solution)/shard_map/all_gather | solution.py:34
  45.2 26.5 %gather_fusion = bf16[1536,3072]{1,0:T(8,128)(2,1)} fusion(bf16[3072,3072]{1,0:T(8,128)(2,1)} %all-gather.2.cloned.1.call-done, s32[2048]{0:T(1024)S(1)} %pad_clamp_fusion), kind=kCustom, calls=%fused_computation | custom fusion | bytes 18880512 | tf_op jit(solution)/shard_map/jit(_take)/gather | solution.py:22
  71.8 19.0 %gather.7 = bf16[768,2,3072]{2,1,0:T(2,128)(2,1)} reshape(bf16[1536,3072]{1,0:T(8,128)(2,1)} %gather_fusion) | data formatting | bytes 18874368 | tf_op jit(solution)/shard_map/jit(_take)/gather | solution.py:22
  90.8 12.3 %broadcast_select_fusion = bf16[768,2,3072]{2,1,0:T(2,128)(2,1)S(1)} fusion(bf16[768,2,3072]{2,1,0:T(2,128)(2,1)} %gather.7, pred[768,2]{1,0:T(8,128)(4,1)S(1)} %copy.18), kind=kLoop, calls=%fused_computation.1 | loop fusion | flops 4718592 | bytes 18875904 | tf_op jit(solution)/shard_map/jit(_take)/select_n | solution.py:22
  103.2 14.4 %fusion.6 = (bf16[768,1,3072]{2,1,0:T(2,128)(2,1)S(1)}, f32[768,1,3072]{2,1,0:T(1,128)}) fusion(bf16[768,2,3072]{2,1,0:T(2,128)(2,1)S(1)} %broadcast_select_fusion), kind=kLoop, calls=%fused_computation.24 | loop fusion | flops 2359296 | bytes 23592960 | tf_op jit(solution)/shard_map/slice | solution.py:23
  117.5 8.9 %fusion.1 = bf16[768,3072]{1,0:T(8,128)(2,1)S(1)} fusion(f32[768,1,3072]{2,1,0:T(1,128)} %get-tuple-element.10, bf16[768,1,3072]{2,1,0:T(2,128)(2,1)S(1)} %get-tuple-element.9, f32[768]{0:T(1024)S(1)} %get-tuple-element.6, f32[768]{0:T(1024)S(1)} %get-tuple-element.5), kind=kLoop, calls=%fused_computation.5 | loop fusion | flops 11796480 | bytes 18880512 | tf_op jit(solution)/shard_map/convert_element_type | solution.py:35
  126.4 11.1 %fusion.2 = f32[3072,1536]{1,0:T(8,128)} fusion(bf16[768,3072]{1,0:T(8,128)(2,1)S(1)} %fusion.1, s32[]{:T(128)S(6)} %select_n.28), kind=kOutput, calls=%fused_computation.8 | convolution fusion | flops 7247757312 | bytes 25952260 | tf_op jit(solution)/shard_map/dot_general | solution.py:41
  137.5 0.0 reduce-scatter.2.cloned.1.call-update
  137.5 314.3 %reduce-scatter.2.cloned.1.call-done = f32[384,1536]{1,0:T(8,128)} async-done(((f32[3072,1536]{1,0:T(8,128)}), f32[384,1536]{1,0:T(8,128)}) %reduce-scatter.2.cloned.1.call-update) | async-done | bytes 2359312 | tf_op jit(solution)/shard_map/reduce_scatter | solution.py:40
  451.8 3.3 broadcast_multiply_fusion
  (6 shorter events, 0.1 us)
Async XLA Ops:
  6.5 0.8 copy-start
  6.5 3.9 copy-start.1
  6.5 38.7 %all-gather.2.cloned.1.call-start = ((), (), s32[]{:S(2)}) async-start(), calls=%async_computation.1 | async-start | bytes 28311552 | tf_op jit(solution)/shard_map/all_gather | solution.py:34
  7.3 444.5 %reduce-scatter.2.cloned.1.call-start = ((), (), s32[]{:S(2)}) async-start(), calls=%async_computation.2 | async-start | bytes 21233664 | tf_op jit(solution)/shard_map/reduce_scatter | solution.py:40
Sparse Core Ops, SparseCore 0:
  8.9 36.2 all-gather.1
  137.6 314.1 reduce-scatter.1
where the time goes:
time: 463 us; the launch traced here: 462 us
  waiting for transfers between devices  350 us (76%)
  local copies, waits for them, and re-layouts  46.6 us (10%)
  other arithmetic  40.9 us (9%)
  between operations  13.5 us (3%)
  matrix products  11.1 us (2%)
    reduce_scatter x1, waiting for transfers between devices, per_device(): lax.psum_scatter(lax.dot_general(combined, columns, (((0,), (0,)), ((), (...  314 us
    gather x2, local copies, waits for them, and re-layouts, gated_rows(): jnp.take(source, row_index.reshape(-1), axis=0)  45.6 us
    all_gather x1, waiting for transfers between devices, per_device(): gathered = lax.all_gather(expert_out, 'expert', axis=0, tiled=True)  34.8 us
    slice x1, other arithmetic, gated_rows(): picked[:, 0].astype(jnp.float32)  14.4 us
    select_n x2, other arithmetic, gated_rows(): jnp.take(source, row_index.reshape(-1), axis=0)  12.4 us
    dot_general x1, matrix products, per_device(): lax.dot_general(combined, columns, (((0,), (0,)), ((), ())), preferred_el...  11.1 us
  transfers between devices with their start and end apart: 2, of which 2 were waited for; matrix products, arithmetic and copies ran while one was open for 1% of the time, Pallas kernels for 0%

commit v1 on v0

v1 whole, which is shorter than its diff:
```python
import functools

import jax
import jax.numpy as jnp
import numpy as np
from jax import lax
from jax.experimental import pallas as pl
from jax.experimental.pallas import tpu as pltpu
from jax.sharding import PartitionSpec as P

EXPERTS = 8
CAP = 384
SNAKE = (0, 2, 4, 6, 7, 5, 3, 1)
F32, BF16 = jnp.float32, jnp.bfloat16


def dot_tn(a, b):
    return lax.dot_general(a, b, (((0,), (0,)), ((), ())), preferred_element_type=F32)


def select_kernel(final, scalars, ids_ref, gates_ref, rows_ref, *refs):
    if final:
        acc_ref, out_ref, sel_ref = refs
    else:
        out_ref, sel_ref = refs
    tokens = ids_ref.shape[0]
    depth = rows_ref.shape[0]

    @pl.when(pl.program_id(0) == 0)
    def _():
        lanes = lax.broadcasted_iota(jnp.int32, (tokens, 128), 1)
        hits = [ids_ref[:, k : k + 1] == lanes for k in range(2)]
        named = (hits[0] | hits[1]).astype(F32).astype(BF16)
        earlier = (
            lax.broadcasted_iota(jnp.int32, (tokens, tokens), 1)
            < lax.broadcasted_iota(jnp.int32, (tokens, tokens), 0)
        ).astype(F32).astype(BF16)
        before = jnp.dot(earlier, named, preferred_element_type=F32)
        for k in range(2):
            count = jnp.sum(jnp.where(hits[k], before, 0.0), axis=1, keepdims=True)
            row = ids_ref[:, k : k + 1] * CAP + count.astype(jnp.int32) - scalars[1]
            here = lax.broadcasted_iota(jnp.int32, (tokens, depth), 1) == row
            sel_ref[k * tokens : (k + 1) * tokens, :] = here.astype(F32).astype(BF16)

    picked = jnp.dot(sel_ref[...], rows_ref[...], preferred_element_type=F32)
    total = gates_ref[:, 0:1] * picked[:tokens] + gates_ref[:, 1:2] * picked[tokens:]
    if final:
        total = total + acc_ref[...]
    out_ref[...] = total.astype(out_ref.dtype)


def gated_half(ids, gates, rows, column_block, first_row, width, acc=None, tile=512):
    tokens, depth = ids.shape[0], rows.shape[0]
    steps = width // tile
    scalars = jnp.stack([column_block * steps, first_row]).astype(jnp.int32)
    whole = lambda j, s: (0, 0)
    in_specs = [
        pl.BlockSpec((tokens, 2), whole),
        pl.BlockSpec((tokens, 2), whole),
        pl.BlockSpec((depth, tile), lambda j, s: (0, s[0] + j)),
    ]
    args = [ids, gates, rows]
    if acc is not None:
        in_specs.append(pl.BlockSpec((tokens, tile), lambda j, s: (0, j)))
        args.append(acc)
    return pl.pallas_call(
        functools.partial(select_kernel, acc is not None),
        out_shape=jax.ShapeDtypeStruct((tokens, width), F32 if acc is None else BF16),
        grid_spec=pltpu.PrefetchScalarGridSpec(
            num_scalar_prefetch=1,
            grid=(steps,),
            in_specs=in_specs,
            out_specs=pl.BlockSpec((tokens, tile), lambda j, s: (0, j)),
            scratch_shapes=[pltpu.VMEM((2 * tokens, depth), BF16)],
        ),
        cost_estimate=pl.CostEstimate(
            flops=4 * tokens * depth * width, bytes_accessed=depth * width * 2 + tokens * width * 6, transcendentals=0
        ),
        compiler_params=pltpu.CompilerParams(vmem_limit_bytes=48 << 20),
        name="gated_first" if acc is None else "gated_second",
    )(scalars, *args)


def blocks_kernel(jobs, mine_ref, other_ref, out_ref, turned_ref):
    n = pl.program_id(0)
    width = out_ref.shape[1]

    @pl.when(jobs[n, 3] == 1)
    def _():
        at = pl.ds(pl.multiple_of(jobs[n, 1] * width, 128), width)

        @pl.when(jobs[n, 0] == 1)
        def _():
            turned_ref[...] = mine_ref[:, at].T

        @pl.when(jobs[n, 0] == 0)
        def _():
            turned_ref[...] = other_ref[:, at].T

    at = pl.ds(pl.multiple_of(jobs[n, 2] * width, 128), width)
    out_ref[0] = jnp.dot(turned_ref[...], mine_ref[:, at], preferred_element_type=F32).astype(out_ref.dtype)


def moment_blocks(jobs, mine, other, width, dtype):
    tokens = mine.shape[0]
    count = jobs.shape[0]
    whole = pl.BlockSpec(mine.shape, lambda n, s: (0, 0))
    return pl.pallas_call(
        blocks_kernel,
        out_shape=jax.ShapeDtypeStruct((count, width, width), dtype),
        grid_spec=pltpu.PrefetchScalarGridSpec(
            num_scalar_prefetch=1,
            grid=(count,),
            in_specs=[whole, whole],
            out_specs=pl.BlockSpec((1, width, width), lambda n, s: (n, 0, 0)),
            scratch_shapes=[pltpu.VMEM((width, tokens), BF16)],
        ),
        cost_estimate=pl.CostEstimate(
            flops=2 * count * tokens * width * width,
            bytes_accessed=4 * mine.size + count * width * width * 4,
            transcendentals=0,
        ),
        compiler_params=pltpu.CompilerParams(vmem_limit_bytes=40 << 20),
        name="blocks_first" if dtype == BF16 else "blocks_rest",
    )(jobs, mine, other)


def is_diagonal(b, e):
    return b // 4 == e


def owns_extra(b, e):
    return (b, e) in ((0, 0), (3, 0), (4, 1), (7, 1))


def owned_columns(b, e):
    shift = 0 if is_diagonal(b, e) or e == 1 else 1
    return [(b + shift) % 4, (b + shift + 1) % 4, (b + 2) % 4]


FIRST = ((1, 3), (0, 4), (1, 4), (2, 4), (0, 5), (2, 5))
REST = tuple((x, t) for t in (3, 2, 6, 5, 1, 7, 0) for x in range(3) if (x, t) not in FIRST)


def job_table(which):
    table = np.zeros((8, 2, len(which), 4), np.int32)
    for p, b in enumerate(SNAKE):
        for e in range(2):
            last = None
            for n, (x, t) in enumerate(which):
                q = SNAKE[(p + t) % 8]
                table[b, e, n] = (q // 4 == e, q % 4, owned_columns(q, e)[x], q != last)
                last = q
    return table


def ring_perm(x, distance, direction):
    pairs = []
    for q, b in enumerate(SNAKE):
        for e in range(2):
            if x == 2 and not owns_extra(b, e):
                continue
            source = SNAKE[(q - direction * distance) % 8]
            target = SNAKE[(q - direction * (distance - 1)) % 8]
            pairs.append((source * 2 + e, target * 2 + e))
    return pairs


def mirror_perms():
    perms = [[], [], []]
    for b in range(8):
        for e in range(2):
            here = b * 2 + e
            if is_diagonal(b, e):
                perms[1].append((here, (b // 4 * 4 + (b + 1) % 4) * 2 + e))
                if owns_extra(b, e):
                    perms[2].append((here, (b // 4 * 4 + (b + 2) % 4) * 2 + e))
            elif e == 1:
                perms[0].append((here, (4 + b) * 2))
                perms[1].append((here, (4 + (b + 1) % 4) * 2))
            else:
                perms[0].append((here, (b + 1) % 4 * 2 + 1))
                perms[1].append((here, (b + 2) % 4 * 2 + 1))
    return perms


def place_table():
    table = np.zeros((8, 2, 5), np.int32)
    for b in range(8):
        for e in range(2):
            own = owned_columns(b, e)
            if is_diagonal(b, e):
                table[b, e] = (own[0], own[1], (b + 3) % 4, (b + 2) % 4, 1 if owns_extra(b, e) else 2)
            elif e == 1:
                table[b, e] = (own[0], own[1], (b + 2) % 4, (b + 3) % 4, 0)
            else:
                table[b, e] = (own[0], own[1], (b + 3) % 4, b % 4, 0)
    return table


def finish_kernel(scale, place, parts_ref, right0, left0, right1, left1, right2, left2, w0, w1, w2, out_ref):
    width = w0.shape[0]

    def put(n, value):
        out_ref[:, pl.ds(pl.multiple_of(place[n] * width, 128), width)] = value

    def owned(n, right, left):
        return (parts_ref[n] + right[...].astype(F32) + left[...].astype(F32)) * scale

    put(0, owned(0, right0, left0))
    put(1, owned(1, right1, left1))
    put(2, w1[...].astype(F32).T)

    @pl.when(place[4] == 0)
    def _():
        put(3, w0[...].astype(F32).T)

    @pl.when(place[4] == 1)
    def _():
        put(3, owned(2, right2, left2))

    @pl.when(place[4] == 2)
    def _():
        put(3, w2[...].astype(F32).T)


def symmetric_moment(mine, other, total_tokens):
    width = mine.shape[1] // 4
    both = ("dp", "expert")
    dp, e = lax.axis_index("dp"), lax.axis_index("expert")
    first = moment_blocks(jnp.asarray(job_table(FIRST))[dp, e], mine, other, width, BF16)
    rest = moment_blocks(jnp.asarray(job_table(REST))[dp, e], mine, other, width, F32)
    scale = 1.0 / total_tokens

    arrived = {}
    chains = []
    for x in range(3):
        right_steps = 3 if x == 1 else 4
        chains.append((x, 1, right_steps))
        chains.append((x, -1, 7 - right_steps))
    for x, direction, steps in chains:
        at = lambda d: (x, d if direction == 1 else 8 - d)
        value = first[FIRST.index(at(steps))]
        for distance in range(steps, 0, -1):
            value = lax.ppermute(value, both, ring_perm(x, distance, direction))
            if distance > 1:
                value = (value.astype(F32) + rest[REST.index(at(distance - 1))]).astype(BF16)
        arrived[x, direction] = value

    own = [REST.index((x, 0)) for x in range(3)]
    mirrored = []
    for x, perm in enumerate(mirror_perms()):
        done = rest[own[x]] + arrived[x, 1].astype(F32) + arrived[x, -1].astype(F32)
        mirrored.append(lax.ppermute((done * scale).astype(BF16), both, perm))

    assert own == [own[0], own[0] + 1, own[0] + 2] and own[0] % 3 == 0
    block = pl.BlockSpec((width, width), lambda i, s: (0, 0))
    return pl.pallas_call(
        functools.partial(finish_kernel, scale),
        out_shape=jax.ShapeDtypeStruct((width, 4 * width), F32),
        grid_spec=pltpu.PrefetchScalarGridSpec(
            num_scalar_prefetch=1,
            grid=(1,),
            in_specs=[pl.BlockSpec((3, width, width), lambda i, s: (own[0] // 3, 0, 0))] + [block] * 9,
            out_specs=pl.BlockSpec((width, 4 * width), lambda i, s: (0, 0)),
        ),
        compiler_params=pltpu.CompilerParams(vmem_limit_bytes=32 << 20),
        name="finish",
    )(
        jnp.asarray(place_table())[dp, e],
        rest,
        *[arrived[x, direction] for x in range(3) for direction in (1, -1)],
        *mirrored,
    )


def per_device(expert_ids, gates, expert_out):
    tokens = expert_ids.shape[0]
    channels = expert_out.shape[1]
    depth = expert_out.shape[0]
    members = lax.axis_size("expert")
    dp_size = lax.axis_size("dp")
    member = lax.axis_index("expert")
    half = channels // members
    swap = [(0, 1), (1, 0)]

    peer_rows = lax.ppermute(
        lax.dynamic_slice_in_dim(expert_out, (1 - member) * half, half, 1), "expert", swap
    )
    part = gated_half(expert_ids, gates, expert_out, member, member * depth, half)
    mine = gated_half(
        expert_ids, gates, peer_rows, jnp.zeros_like(member), (1 - member) * depth, half, acc=part
    )
    other = lax.ppermute(mine, "expert", swap)

    total_tokens = tokens * dp_size
    if dp_size == 8 and channels == 8 * 384:
        return symmetric_moment(mine, other, total_tokens)
    low = jnp.where(member == 0, mine, other)
    high = jnp.where(member == 0, other, mine)
    slab = dot_tn(jnp.concatenate([low, high], axis=1), mine)
    return lax.psum_scatter(slab, "dp", scatter_dimension=0, tiled=True) / total_tokens


def solution(mesh):
    assert mesh.shape["expert"] == 2
    in_specs = (
        P(("groups", "dp"), None),
        P(("groups", "dp"), None),
        P(("groups", "dp", "expert"), None),
    )
    out_specs = P(("groups", "dp"), "expert")
    return jax.shard_map(
        per_device, mesh=mesh, in_specs=in_specs, out_specs=out_specs, check_vma=False
    )
```

time: 463 us -> 145 us (0.31)
  the two profiles are of different devices: /device:TPU:1 before, /device:TPU:6 now
where the time goes in v1:
time: 145 us
  Pallas kernels  49.5 us (34%)
  waiting for transfers between devices  49.4 us (34%)
  starting transfers between devices  31 us (21%)
  local copies, waits for them, and re-layouts  9.82 us (7%)
  other arithmetic  5.07 us (3%)
    ppermute x21, waiting for transfers between devices, symmetric_moment(): value = lax.ppermute(value, both, ring_perm(x, distance, direction))  32 us
    ppermute x21, starting transfers between devices, symmetric_moment(): value = lax.ppermute(value, both, ring_perm(x, distance, direction))  26.6 us
    pallas_call x2, Pallas kernels, gated_half(): pl.pallas_call(functools.partial(select_kernel, acc is not None), out_sha...  25.4 us
    pallas_call x2, Pallas kernels, moment_blocks(): pl.pallas_call(blocks_kernel, out_shape=jax.ShapeDtypeStruct((count, widt...  21.5 us
    ppermute x3, waiting for transfers between devices, symmetric_moment(): mirrored.append(lax.ppermute((done * scale).astype(BF16), both, perm))  14.7 us
    dynamic_slice x1, local copies, waits for them, and re-layouts, per_device(): lax.dynamic_slice_in_dim(expert_out, (1 - member) * half, half, 1)  4.8 us
    convert_element_type x3, other arithmetic, symmetric_moment(): (value.astype(F32) + rest[REST.index(at(distance - 1))]).astype(BF16)  4.66 us
    ppermute x3, starting transfers between devices, symmetric_moment(): mirrored.append(lax.ppermute((done * scale).astype(BF16), both, perm))  3.77 us
  transfers between devices with their start and end apart: 26, of which 16 were waited for; matrix products, arithmetic and copies ran while one was open for 3% of the time, Pallas kernels for 19%

profile of v1, /device:TPU:6, one launch (start us, length us, event | category | flops | bytes accessed | tf_op | source)
XLA Modules:
  0.0 145.0 jit_solution(8730575895558195768)
XLA Ops:
  0.0 4.8 %constant_dynamic-slice_fusion = bf16[1536,1536]{1,0:T(8,128)(2,1)} fusion(bf16[1536,3072]{1,0:T(8,128)(2,1)} %rows_ref.1, s32[]{:T(128)S(6)} %select_n.15), kind=kLoop, calls=%fused_computation.68 | loop fusion | bytes 9437188 | tf_op jit(solution)/shard_map/dynamic_slice | solution.py:288
  4.8 0.0 collective-permute-start
  4.8 0.2 copy.9.ids_ref
  5.0 0.2 copy.10.gates_ref
  5.2 0.1 pad_add_fusion
  5.3 12.4 %gated_first.1.refs_0_ = f32[768,1536]{1,0:T(8,128)S(1)} custom-call(s32[2]{0:T(128)S(1)} %get-tuple-element.30.scalars, s32[768,2]{1,0:T(8,128)S(1)} %copy.9.ids_ref, f32[768,2]{1,0:T(8,128)S(1)} %copy.10.gates_ref, bf16[1536,3072]{1,0:T(8,128)(2,1)} %rows_ref.1), custom_call_target="tpu_custom_call" | custom-call | flops 7247757312 | bytes 11796480 | tf_op jit(solution)/shard_map/gated_first/pallas_call | solution.py:66
  17.7 2.2 %copy-done.1 = f32[768,1536]{1,0:T(8,128)} copy-done((f32[768,1536]{1,0:T(8,128)}, f32[768,1536]{1,0:T(8,128)S(1)}, u32[]{:S(2)}) %copy-start.1) | copy-done | bytes 4718616
  19.9 13.0 %gated_second.1.mine_ref = bf16[768,1536]{1,0:T(8,128)(2,1)S(1)} custom-call(s32[2]{0:T(128)S(1)} %get-tuple-element.29.scalars, s32[768,2]{1,0:T(8,128)S(1)} %copy.9.ids_ref, f32[768,2]{1,0:T(8,128)S(1)} %copy.10.gates_ref, bf16[1536,1536]{1,0:T(8,128)(2,1)} %collective-permute-done.rows_ref, f32[768,1536]{1,0:T(8,128)} %copy-done.1), custom_call_target="tpu_custom_call" | custom-call | flops 7247757312 | bytes 11796480 | tf_op jit(solution)/shard_map/gated_second/pallas_call | solution.py:66
  32.9 0.6 collective-permute-start.1
  33.5 0.7 dynamic-slice_bitcast_fusion.1
  34.1 0.1 copy.11.jobs
  34.2 0.7 dynamic-slice_bitcast_fusion
  34.9 0.1 copy.12.jobs
  35.0 2.7 %collective-permute-done.1.other_ref = bf16[768,1536]{1,0:T(8,128)(2,1)} collective-permute-done((bf16[768,1536]{1,0:T(8,128)(2,1)S(1)}, bf16[768,1536]{1,0:T(8,128)(2,1)}, u32[]{:S(2)}, u32[]{:S(2)}) %collective-permute-start.1) | collective-permute-done | bytes 2359328 | tf_op jit(solution)/shard_map/ppermute | solution.py:294
  37.7 5.9 %blocks_first.1 = bf16[6,384,384]{2,1,0:T(8,128)(2,1)S(1)} custom-call(s32[6,4]{1,0:T(8,128)S(1)} %copy.12.jobs, bf16[768,1536]{1,0:T(8,128)(2,1)S(1)} %gated_second.1.mine_ref, bf16[768,1536]{1,0:T(8,128)(2,1)} %collective-permute-done.1.other_ref), custom_call_target="tpu_custom_call" | custom-call | flops 1358954496 | bytes 8257536 | tf_op jit(solution)/shard_map/blocks_first/pallas_call | solution.py:108
  43.6 0.2 slice_bitcast_fusion.18
  43.8 0.7 collective-permute-start.20
  44.5 0.7 collective-permute-start.16
  45.2 1.7 %collective-permute-start.12 = (bf16[384,384]{1,0:T(8,128)(2,1)S(1)}, bf16[384,384]{1,0:T(8,128)(2,1)S(1)}, u32[]{:S(2)}, u32[]{:S(2)}) collective-permute-start(bf16[384,384]{1,0:T(8,128)(2,1)S(1)} %get-tuple-element.25), channel_id=1, source_target_pairs={{14,12},{15,13},{10,14},{11,15},{6,10},{7,11},{2,6},{3,7},{0,2},{1... | collective-permute-start | bytes 884744 | tf_op jit(solution)/shard_map/ppermute | solution.py:245
  46.8 0.4 collective-permute-start.2
  47.3 1.8 %collective-permute-start.9 = (bf16[384,384]{1,0:T(8,128)(2,1)S(1)}, bf16[384,384]{1,0:T(8,128)(2,1)S(1)}, u32[]{:S(2)}, u32[]{:S(2)}) collective-permute-start(bf16[384,384]{1,0:T(8,128)(2,1)S(1)} %get-tuple-element.26), channel_id=1, source_target_pairs={{10,6},{11,7},{6,2},{7,3},{2,0},{3,1},{0,4},{1,5},{4,8},{5,9},{8,1... | collective-permute-start | bytes 884744 | tf_op jit(solution)/shard_map/ppermute | solution.py:245
  49.1 15.7 %blocks_rest.1.parts_ref = f32[18,384,384]{2,1,0:T(8,128)} custom-call(s32[18,4]{1,0:T(8,128)S(1)} %copy.11.jobs, bf16[768,1536]{1,0:T(8,128)(2,1)S(1)} %gated_second.1.mine_ref, bf16[768,1536]{1,0:T(8,128)(2,1)} %collective-permute-done.1.other_ref), custom_call_target="tpu_custom_call" | custom-call | flops 4076863488 | bytes 15335424 | tf_op jit(solution)/shard_map/blocks_rest/pallas_call | solution.py:108
  64.8 0.2 collective-permute-start.6
  65.0 0.0 collective-permute-done.12
  65.0 1.7 %fusion.21 = (bf16[384,384]{1,0:T(8,128)(2,1)S(1)}, bf16[384,384]{1,0:T(8,128)(2,1)S(1)}, bf16[384,384]{1,0:T(8,128)(2,1)S(1)}) fusion(f32[18,384,384]{2,1,0:T(8,128)} %blocks_rest.1.parts_ref, bf16[384,384]{1,0:T(8,128)(2,1)S(1)} %collective-permute-done.16, bf16[384,384]{1,0:T(8,128)(2,1)S(1)} %collective-permute-done.12, ...), kind=kLoop, calls=%fused_computation.29 | loop fusion | flops 1327104 | bytes 3538944 | tf_op jit(solution)/shard_map/convert_element_type | solution.py:247
  66.7 0.8 collective-permute-start.17
  67.5 3.4 %collective-permute-start.13 = (bf16[384,384]{1,0:T(8,128)(2,1)S(1)}, bf16[384,384]{1,0:T(8,128)(2,1)S(1)}, u32[]{:S(2)}, u32[]{:S(2)}) collective-permute-start(bf16[384,384]{1,0:T(8,128)(2,1)S(1)} %get-tuple-element.21), channel_id=1, source_target_pairs={{12,8},{13,9},{14,12},{15,13},{10,14},{11,15},{6,10},{7,11},{2,6},... | collective-permute-start | bytes 884744 | tf_op jit(solution)/shard_map/ppermute | solution.py:245
  70.9 0.0 collective-permute-done.20
  70.9 0.9 collective-permute-start.3
  71.9 0.0 collective-permute-done.9
  71.9 4.0 %collective-permute-done.6 = bf16[384,384]{1,0:T(8,128)(2,1)S(1)} collective-permute-done((bf16[384,384]{1,0:T(8,128)(2,1)S(1)}, bf16[384,384]{1,0:T(8,128)(2,1)S(1)}, u32[]{:S(2)}, u32[]{:S(2)}) %collective-permute-start.6) | collective-permute-done | bytes 294944 | tf_op jit(solution)/shard_map/ppermute | solution.py:245
  75.9 5.9 %collective-permute-done.13 = bf16[384,384]{1,0:T(8,128)(2,1)S(1)} collective-permute-done((bf16[384,384]{1,0:T(8,128)(2,1)S(1)}, bf16[384,384]{1,0:T(8,128)(2,1)S(1)}, u32[]{:S(2)}, u32[]{:S(2)}) %collective-permute-start.13) | collective-permute-done | bytes 294944 | tf_op jit(solution)/shard_map/ppermute | solution.py:245
  81.8 2.4 %fusion.15 = (bf16[384,384]{1,0:T(8,128)(2,1)S(1)}, bf16[384,384]{1,0:T(8,128)(2,1)S(1)}, bf16[384,384]{1,0:T(8,128)(2,1)S(1)}, bf16[384,384]{1,0:T(8,128)(2,1)S...) fusion(f32[18,384,384]{2,1,0:T(8,128)} %blocks_rest.1.parts_ref, ...), kind=kLoop, calls=%fused_computation.20 | loop fusion | flops 2654208 | bytes 7077888 | tf_op jit(solution)/shard_map/convert_element_type | solution.py:247
  84.2 1.3 collective-permute-start.21
  85.5 1.3 collective-permute-start.18
  86.8 2.7 %collective-permute-start.14 = (bf16[384,384]{1,0:T(8,128)(2,1)S(1)}, bf16[384,384]{1,0:T(8,128)(2,1)S(1)}, u32[]{:S(2)}, u32[]{:S(2)}) collective-permute-start(bf16[384,384]{1,0:T(8,128)(2,1)S(1)} %get-tuple-element.16), channel_id=1, source_target_pairs={{8,4},{9,5},{12,8},{13,9},{14,12},{15,13},{10,14},{11,15},{6,10},{... | collective-permute-start | bytes 884744 | tf_op jit(solution)/shard_map/ppermute | solution.py:245
  89.5 2.0 %collective-permute-start.7 = (bf16[384,384]{1,0:T(8,128)(2,1)S(1)}, bf16[384,384]{1,0:T(8,128)(2,1)S(1)}, u32[]{:S(2)}, u32[]{:S(2)}) collective-permute-start(bf16[384,384]{1,0:T(8,128)(2,1)S(1)} %get-tuple-element.18), channel_id=1, source_target_pairs={{8,4},{9,5},{12,8},{13,9},{14,12},{15,13},{10,14},{11,15},{6,10},{... | collective-permute-start | bytes 884744 | tf_op jit(solution)/shard_map/ppermute | solution.py:245
  91.5 4.3 %collective-permute-done.21 = bf16[384,384]{1,0:T(8,128)(2,1)S(1)} collective-permute-done((bf16[384,384]{1,0:T(8,128)(2,1)S(1)}, bf16[384,384]{1,0:T(8,128)(2,1)S(1)}, u32[]{:S(2)}, u32[]{:S(2)}) %collective-permute-start.21) | collective-permute-done | bytes 294944 | tf_op jit(solution)/shard_map/ppermute | solution.py:245
  95.9 0.0 collective-permute-start.4
  95.9 1.4 collective-permute-done.18
  97.3 4.9 %collective-permute-done.14 = bf16[384,384]{1,0:T(8,128)(2,1)S(1)} collective-permute-done((bf16[384,384]{1,0:T(8,128)(2,1)S(1)}, bf16[384,384]{1,0:T(8,128)(2,1)S(1)}, u32[]{:S(2)}, u32[]{:S(2)}) %collective-permute-start.14) | collective-permute-done | bytes 294944 | tf_op jit(solution)/shard_map/ppermute | solution.py:245
  102.2 1.2 collective-permute-done.10
  103.4 2.0 %collective-permute-done.7 = bf16[384,384]{1,0:T(8,128)(2,1)S(1)} collective-permute-done((bf16[384,384]{1,0:T(8,128)(2,1)S(1)}, bf16[384,384]{1,0:T(8,128)(2,1)S(1)}, u32[]{:S(2)}, u32[]{:S(2)}) %collective-permute-start.7) | collective-permute-done | bytes 294944 | tf_op jit(solution)/shard_map/ppermute | solution.py:245
  105.5 1.1 collective-permute-done.4
  106.6 0.5 fusion.13
  107.1 0.1 collective-permute-start.5
  107.2 2.0 %collective-permute-start.8 = (bf16[384,384]{1,0:T(8,128)(2,1)S(1)}, bf16[384,384]{1,0:T(8,128)(2,1)S(1)}, u32[]{:S(2)}, u32[]{:S(2)}) collective-permute-start(bf16[384,384]{1,0:T(8,128)(2,1)S(1)} %get-tuple-element.12), channel_id=1, source_target_pairs={{4,0},{5,1},{8,4},{9,5},{12,8},{13,9},{14,12},{15,13},{10,14},{11,... | collective-permute-start | bytes 884744 | tf_op jit(solution)/shard_map/ppermute | solution.py:245
  109.2 0.1 collective-permute-start.11
  109.2 2.0 %collective-permute-start.15 = (bf16[384,384]{1,0:T(8,128)(2,1)S(1)}, bf16[384,384]{1,0:T(8,128)(2,1)S(1)}, u32[]{:S(2)}, u32[]{:S(2)}) collective-permute-start(bf16[384,384]{1,0:T(8,128)(2,1)S(1)} %get-tuple-element.10), channel_id=1, source_target_pairs={{4,0},{5,1},{8,4},{9,5},{12,8},{13,9},{14,12},{15,13},{10,14},{11,... | collective-permute-start | bytes 884744 | tf_op jit(solution)/shard_map/ppermute | solution.py:245
  111.2 2.0 %collective-permute-start.19 = (bf16[384,384]{1,0:T(8,128)(2,1)S(1)}, bf16[384,384]{1,0:T(8,128)(2,1)S(1)}, u32[]{:S(2)}, u32[]{:S(2)}) collective-permute-start(bf16[384,384]{1,0:T(8,128)(2,1)S(1)} %get-tuple-element.9), channel_id=1, source_target_pairs={{2,0},{5,9},{13,15},{10,6},{18,16},{21,25},{29,31},{26,22}} | collective-permute-start | bytes 884744 | tf_op jit(solution)/shard_map/ppermute | solution.py:245
  113.2 2.9 %collective-permute-done.5.right0 = bf16[384,384]{1,0:T(8,128)(2,1)S(1)} collective-permute-done((bf16[384,384]{1,0:T(8,128)(2,1)S(1)}, bf16[384,384]{1,0:T(8,128)(2,1)S(1)}, u32[]{:S(2)}, u32[]{:S(2)}) %collective-permute-start.5) | collective-permute-done | bytes 294944 | tf_op jit(solution)/shard_map/ppermute | solution.py:245
  116.0 2.6 %collective-permute-start.22 = (bf16[384,384]{1,0:T(8,128)(2,1)S(1)}, bf16[384,384]{1,0:T(8,128)(2,1)S(1)}, u32[]{:S(2)}, u32[]{:S(2)}) collective-permute-start(bf16[384,384]{1,0:T(8,128)(2,1)S(1)} %get-tuple-element.8), channel_id=1, source_target_pairs={{4,0},{13,9},{11,15},{2,6},{20,16},{29,25},{27,31},{18,22}} | collective-permute-start | bytes 884744 | tf_op jit(solution)/shard_map/ppermute | solution.py:245
  118.7 0.5 collective-permute-done.11.right1
  119.2 1.5 %collective-permute-done.15.left1 = bf16[384,384]{1,0:T(8,128)(2,1)S(1)} collective-permute-done((bf16[384,384]{1,0:T(8,128)(2,1)S(1)}, bf16[384,384]{1,0:T(8,128)(2,1)S(1)}, u32[]{:S(2)}, u32[]{:S(2)}) %collective-permute-start.15) | collective-permute-done | bytes 294944 | tf_op jit(solution)/shard_map/ppermute | solution.py:245
  120.7 0.2 collective-permute-done.19.right2
  120.9 2.0 %collective-permute-done.22.left2 = bf16[384,384]{1,0:T(8,128)(2,1)S(1)} collective-permute-done((bf16[384,384]{1,0:T(8,128)(2,1)S(1)}, bf16[384,384]{1,0:T(8,128)(2,1)S(1)}, u32[]{:S(2)}, u32[]{:S(2)}) %collective-permute-start.22) | collective-permute-done | bytes 294944 | tf_op jit(solution)/shard_map/ppermute | solution.py:245
  122.9 0.3 fusion.3
  123.2 0.7 collective-permute-start.23
  123.9 1.8 %collective-permute-start.24 = (bf16[384,384]{1,0:T(8,128)(2,1)S(1)}, bf16[384,384]{1,0:T(8,128)(2,1)S(1)}, u32[]{:S(2)}, u32[]{:S(2)}) collective-permute-start(bf16[384,384]{1,0:T(8,128)(2,1)S(1)} %get-tuple-element.6), channel_id=1, source_target_pairs={{0,2},{1,10},{2,4},{3,12},{4,6},{5,14},{6,0},{7,8},{8,5},{9,11},{1... | collective-permute-start | bytes 884744 | tf_op jit(solution)/shard_map/ppermute | solution.py:254
  125.7 1.3 collective-permute-start.25
  127.0 0.7 fusion.42.place
  127.7 5.4 %collective-permute-done.24.w1 = bf16[384,384]{1,0:T(8,128)(2,1)S(1)} collective-permute-done((bf16[384,384]{1,0:T(8,128)(2,1)S(1)}, bf16[384,384]{1,0:T(8,128)(2,1)S(1)}, u32[]{:S(2)}, u32[]{:S(2)}) %collective-permute-start.24) | collective-permute-done | bytes 294944 | tf_op jit(solution)/shard_map/ppermute | solution.py:254
  133.1 9.3 %collective-permute-done.25.w2 = bf16[384,384]{1,0:T(8,128)(2,1)S(1)} collective-permute-done((bf16[384,384]{1,0:T(8,128)(2,1)S(1)}, bf16[384,384]{1,0:T(8,128)(2,1)S(1)}, u32[]{:S(2)}, u32[]{:S(2)}) %collective-permute-start.25) | collective-permute-done | bytes 294944 | tf_op jit(solution)/shard_map/ppermute | solution.py:254
  142.4 2.6 %finish.1 = f32[384,1536]{1,0:T(8,128)} custom-call(s32[5]{0:T(128)S(1)} %fusion.42.place, f32[18,384,384]{2,1,0:T(8,128)S(1)} %copy-done, bf16[384,384]{1,0:T(8,128)(2,1)S(1)} %collective-permute-done.5.right0, bf16[384,384]{1,0:T(8,128)(2,1)S(1)} %collective-permute-done.8.left0, bf16[384,384]{1,0:T(8,128)(2,1)S(1)} %collective-permute-done.11.right1, ...), custom_call_target="tpu_custom_call" | custom-call | tf_op jit(solution)/shard_map/finish/pallas_call | solution.py:258
  (15 shorter events, 0.0 us)
Async XLA Ops:
  0.0 4.8 %copy-start.2 = (s32[768,2]{0,1:T(2,128)S(1)}, s32[768,2]{0,1:T(2,128)}, u32[]{:S(2)}) copy-start(s32[768,2]{0,1:T(2,128)} %param.6) | copy-start | bytes 18436
  0.0 5.0 %copy-start.3 = (f32[768,2]{0,1:T(2,128)S(1)}, f32[768,2]{0,1:T(2,128)}, u32[]{:S(2)}) copy-start(f32[768,2]{0,1:T(2,128)} %param.7) | copy-start | bytes 18436
  4.8 15.1 %collective-permute-start = (bf16[1536,1536]{1,0:T(8,128)(2,1)}, bf16[1536,1536]{1,0:T(8,128)(2,1)}, u32[]{:S(2)}, u32[]{:S(2)}) collective-permute-start(bf16[1536,1536]{1,0:T(8,128)(2,1)} %constant_dynamic-slice_fusion), channel_id=1, source_target_pairs={{0,1},{1,0},{2,3},{3,2},{4,5},{5,4},{6,7},{7,6},{8,9},{9,8},{10,11... | collective-permute-start | bytes 14155784 | tf_op jit(solution)/shard_map/ppermute | solution.py:287
  17.6 2.2 %copy-start.1 = (f32[768,1536]{1,0:T(8,128)}, f32[768,1536]{1,0:T(8,128)S(1)}, u32[]{:S(2)}) copy-start(f32[768,1536]{1,0:T(8,128)S(1)} %gated_first.1.refs_0_) | copy-start | bytes 14155780
  32.9 4.9 %collective-permute-start.1 = (bf16[768,1536]{1,0:T(8,128)(2,1)S(1)}, bf16[768,1536]{1,0:T(8,128)(2,1)}, u32[]{:S(2)}, u32[]{:S(2)}) collective-permute-start(bf16[768,1536]{1,0:T(8,128)(2,1)S(1)} %gated_second.1.mine_ref), channel_id=1, source_target_pairs={{0,1},{1,0},{2,3},{3,2},{4,5},{5,4},{6,7},{7,6},{8,9},{9,8},{10,11... | collective-permute-start | bytes 7077896 | tf_op jit(solution)/shard_map/ppermute | solution.py:294
  43.8 27.1 %collective-permute-start.20 = (bf16[384,384]{1,0:T(8,128)(2,1)S(1)}, bf16[384,384]{1,0:T(8,128)(2,1)S(1)}, u32[]{:S(2)}, u32[]{:S(2)}) collective-permute-start(bf16[384,384]{1,0:T(8,128)(2,1)S(1)} %get-tuple-element.23), channel_id=1, source_target_pairs={{12,8},{11,15},{3,7},{4,0},{28,24},{27,31},{19,23},{20,16}} | collective-permute-start | bytes 884744 | tf_op jit(solution)/shard_map/ppermute | solution.py:245
  44.5 20.3 %collective-permute-start.16 = (bf16[384,384]{1,0:T(8,128)(2,1)S(1)}, bf16[384,384]{1,0:T(8,128)(2,1)S(1)}, u32[]{:S(2)}, u32[]{:S(2)}) collective-permute-start(bf16[384,384]{1,0:T(8,128)(2,1)S(1)} %get-tuple-element.24), channel_id=1, source_target_pairs={{14,10},{7,3},{1,5},{8,12},{30,26},{23,19},{17,21},{24,28}} | collective-permute-start | bytes 884744 | tf_op jit(solution)/shard_map/ppermute | solution.py:245
  45.2 19.8 %collective-permute-start.12 = (bf16[384,384]{1,0:T(8,128)(2,1)S(1)}, bf16[384,384]{1,0:T(8,128)(2,1)S(1)}, u32[]{:S(2)}, u32[]{:S(2)}) collective-permute-start(bf16[384,384]{1,0:T(8,128)(2,1)S(1)} %get-tuple-element.25), channel_id=1, source_target_pairs={{14,12},{15,13},{10,14},{11,15},{6,10},{7,11},{2,6},{3,7},{0,2},{1... | collective-permute-start | bytes 884744 | tf_op jit(solution)/shard_map/ppermute | solution.py:245
  46.8 18.1 %collective-permute-start.2 = (bf16[384,384]{1,0:T(8,128)(2,1)S(1)}, bf16[384,384]{1,0:T(8,128)(2,1)S(1)}, u32[]{:S(2)}, u32[]{:S(2)}) collective-permute-start(bf16[384,384]{1,0:T(8,128)(2,1)S(1)} %get-tuple-element.28), channel_id=1, source_target_pairs={{14,10},{15,11},{10,6},{11,7},{6,2},{7,3},{2,0},{3,1},{0,4},{1,5},... | collective-permute-start | bytes 884744 | tf_op jit(solution)/shard_map/ppermute | solution.py:245
  47.3 24.6 %collective-permute-start.9 = (bf16[384,384]{1,0:T(8,128)(2,1)S(1)}, bf16[384,384]{1,0:T(8,128)(2,1)S(1)}, u32[]{:S(2)}, u32[]{:S(2)}) collective-permute-start(bf16[384,384]{1,0:T(8,128)(2,1)S(1)} %get-tuple-element.26), channel_id=1, source_target_pairs={{10,6},{11,7},{6,2},{7,3},{2,0},{3,1},{0,4},{1,5},{4,8},{5,9},{8,1... | collective-permute-start | bytes 884744 | tf_op jit(solution)/shard_map/ppermute | solution.py:245
  64.8 41.8 %copy-start = (f32[18,384,384]{2,1,0:T(8,128)S(1)}, f32[18,384,384]{2,1,0:T(8,128)}, u32[]{:S(2)}) copy-start(f32[18,384,384]{2,1,0:T(8,128)} %blocks_rest.1.parts_ref) | copy-start | bytes 31850500
  64.8 11.1 %collective-permute-start.6 = (bf16[384,384]{1,0:T(8,128)(2,1)S(1)}, bf16[384,384]{1,0:T(8,128)(2,1)S(1)}, u32[]{:S(2)}, u32[]{:S(2)}) collective-permute-start(bf16[384,384]{1,0:T(8,128)(2,1)S(1)} %get-tuple-element.27), channel_id=1, source_target_pairs={{12,8},{13,9},{14,12},{15,13},{10,14},{11,15},{6,10},{7,11},{2,6},... | collective-permute-start | bytes 884744 | tf_op jit(solution)/shard_map/ppermute | solution.py:245
  66.7 9.2 %collective-permute-start.17 = (bf16[384,384]{1,0:T(8,128)(2,1)S(1)}, bf16[384,384]{1,0:T(8,128)(2,1)S(1)}, u32[]{:S(2)}, u32[]{:S(2)}) collective-permute-start(bf16[384,384]{1,0:T(8,128)(2,1)S(1)} %get-tuple-element.20), channel_id=1, source_target_pairs={{10,6},{3,1},{5,9},{12,14},{26,22},{19,17},{21,25},{28,30}} | collective-permute-start | bytes 884744 | tf_op jit(solution)/shard_map/ppermute | solution.py:245
  67.5 14.2 %collective-permute-start.13 = (bf16[384,384]{1,0:T(8,128)(2,1)S(1)}, bf16[384,384]{1,0:T(8,128)(2,1)S(1)}, u32[]{:S(2)}, u32[]{:S(2)}) collective-permute-start(bf16[384,384]{1,0:T(8,128)(2,1)S(1)} %get-tuple-element.21), channel_id=1, source_target_pairs={{12,8},{13,9},{14,12},{15,13},{10,14},{11,15},{6,10},{7,11},{2,6},... | collective-permute-start | bytes 884744 | tf_op jit(solution)/shard_map/ppermute | solution.py:245
  70.9 10.9 %collective-permute-start.3 = (bf16[384,384]{1,0:T(8,128)(2,1)S(1)}, bf16[384,384]{1,0:T(8,128)(2,1)S(1)}, u32[]{:S(2)}, u32[]{:S(2)}) collective-permute-start(bf16[384,384]{1,0:T(8,128)(2,1)S(1)} %get-tuple-element.22), channel_id=1, source_target_pairs={{10,6},{11,7},{6,2},{7,3},{2,0},{3,1},{0,4},{1,5},{4,8},{5,9},{8,1... | collective-permute-start | bytes 884744 | tf_op jit(solution)/shard_map/ppermute | solution.py:245
  84.2 11.7 %collective-permute-start.21 = (bf16[384,384]{1,0:T(8,128)(2,1)S(1)}, bf16[384,384]{1,0:T(8,128)(2,1)S(1)}, u32[]{:S(2)}, u32[]{:S(2)}) collective-permute-start(bf16[384,384]{1,0:T(8,128)(2,1)S(1)} %get-tuple-element.14), channel_id=1, source_target_pairs={{8,4},{15,13},{7,11},{0,2},{24,20},{31,29},{23,27},{16,18}} | collective-permute-start | bytes 884744 | tf_op jit(solution)/shard_map/ppermute | solution.py:245
  85.5 11.8 %collective-permute-start.18 = (bf16[384,384]{1,0:T(8,128)(2,1)S(1)}, bf16[384,384]{1,0:T(8,128)(2,1)S(1)}, u32[]{:S(2)}, u32[]{:S(2)}) collective-permute-start(bf16[384,384]{1,0:T(8,128)(2,1)S(1)} %get-tuple-element.15), channel_id=1, source_target_pairs={{6,2},{1,5},{9,13},{14,10},{22,18},{17,21},{25,29},{30,26}} | collective-permute-start | bytes 884744 | tf_op jit(solution)/shard_map/ppermute | solution.py:245
  86.8 15.4 %collective-permute-start.14 = (bf16[384,384]{1,0:T(8,128)(2,1)S(1)}, bf16[384,384]{1,0:T(8,128)(2,1)S(1)}, u32[]{:S(2)}, u32[]{:S(2)}) collective-permute-start(bf16[384,384]{1,0:T(8,128)(2,1)S(1)} %get-tuple-element.16), channel_id=1, source_target_pairs={{8,4},{9,5},{12,8},{13,9},{14,12},{15,13},{10,14},{11,15},{6,10},{... | collective-permute-start | bytes 884744 | tf_op jit(solution)/shard_map/ppermute | solution.py:245
  89.5 13.9 %collective-permute-start.10 = (bf16[384,384]{1,0:T(8,128)(2,1)S(1)}, bf16[384,384]{1,0:T(8,128)(2,1)S(1)}, u32[]{:S(2)}, u32[]{:S(2)}) collective-permute-start(bf16[384,384]{1,0:T(8,128)(2,1)S(1)} %get-tuple-element.17), channel_id=1, source_target_pairs={{6,2},{7,3},{2,0},{3,1},{0,4},{1,5},{4,8},{5,9},{8,12},{9,13},{12,... | collective-permute-start | bytes 884744 | tf_op jit(solution)/shard_map/ppermute | solution.py:245
  89.5 15.9 %collective-permute-start.7 = (bf16[384,384]{1,0:T(8,128)(2,1)S(1)}, bf16[384,384]{1,0:T(8,128)(2,1)S(1)}, u32[]{:S(2)}, u32[]{:S(2)}) collective-permute-start(bf16[384,384]{1,0:T(8,128)(2,1)S(1)} %get-tuple-element.18), channel_id=1, source_target_pairs={{8,4},{9,5},{12,8},{13,9},{14,12},{15,13},{10,14},{11,15},{6,10},{... | collective-permute-start | bytes 884744 | tf_op jit(solution)/shard_map/ppermute | solution.py:245
  95.9 10.7 %collective-permute-start.4 = (bf16[384,384]{1,0:T(8,128)(2,1)S(1)}, bf16[384,384]{1,0:T(8,128)(2,1)S(1)}, u32[]{:S(2)}, u32[]{:S(2)}) collective-permute-start(bf16[384,384]{1,0:T(8,128)(2,1)S(1)} %get-tuple-element.19), channel_id=1, source_target_pairs={{6,2},{7,3},{2,0},{3,1},{0,4},{1,5},{4,8},{5,9},{8,12},{9,13},{12,... | collective-permute-start | bytes 884744 | tf_op jit(solution)/shard_map/ppermute | solution.py:245
  107.1 9.0 %collective-permute-start.5 = (bf16[384,384]{1,0:T(8,128)(2,1)S(1)}, bf16[384,384]{1,0:T(8,128)(2,1)S(1)}, u32[]{:S(2)}, u32[]{:S(2)}) collective-permute-start(bf16[384,384]{1,0:T(8,128)(2,1)S(1)} %get-tuple-element.13), channel_id=1, source_target_pairs={{2,0},{3,1},{0,4},{1,5},{4,8},{5,9},{8,12},{9,13},{12,14},{13,15},... | collective-permute-start | bytes 884744 | tf_op jit(solution)/shard_map/ppermute | solution.py:245
  107.2 11.5 %collective-permute-start.8 = (bf16[384,384]{1,0:T(8,128)(2,1)S(1)}, bf16[384,384]{1,0:T(8,128)(2,1)S(1)}, u32[]{:S(2)}, u32[]{:S(2)}) collective-permute-start(bf16[384,384]{1,0:T(8,128)(2,1)S(1)} %get-tuple-element.12), channel_id=1, source_target_pairs={{4,0},{5,1},{8,4},{9,5},{12,8},{13,9},{14,12},{15,13},{10,14},{11,... | collective-permute-start | bytes 884744 | tf_op jit(solution)/shard_map/ppermute | solution.py:245
  109.2 10.0 %collective-permute-start.11 = (bf16[384,384]{1,0:T(8,128)(2,1)S(1)}, bf16[384,384]{1,0:T(8,128)(2,1)S(1)}, u32[]{:S(2)}, u32[]{:S(2)}) collective-permute-start(bf16[384,384]{1,0:T(8,128)(2,1)S(1)} %get-tuple-element.11), channel_id=1, source_target_pairs={{2,0},{3,1},{0,4},{1,5},{4,8},{5,9},{8,12},{9,13},{12,14},{13,15},... | collective-permute-start | bytes 884744 | tf_op jit(solution)/shard_map/ppermute | solution.py:245
  109.2 11.5 %collective-permute-start.15 = (bf16[384,384]{1,0:T(8,128)(2,1)S(1)}, bf16[384,384]{1,0:T(8,128)(2,1)S(1)}, u32[]{:S(2)}, u32[]{:S(2)}) collective-permute-start(bf16[384,384]{1,0:T(8,128)(2,1)S(1)} %get-tuple-element.10), channel_id=1, source_target_pairs={{4,0},{5,1},{8,4},{9,5},{12,8},{13,9},{14,12},{15,13},{10,14},{11,... | collective-permute-start | bytes 884744 | tf_op jit(solution)/shard_map/ppermute | solution.py:245
  111.2 9.7 %collective-permute-start.19 = (bf16[384,384]{1,0:T(8,128)(2,1)S(1)}, bf16[384,384]{1,0:T(8,128)(2,1)S(1)}, u32[]{:S(2)}, u32[]{:S(2)}) collective-permute-start(bf16[384,384]{1,0:T(8,128)(2,1)S(1)} %get-tuple-element.9), channel_id=1, source_target_pairs={{2,0},{5,9},{13,15},{10,6},{18,16},{21,25},{29,31},{26,22}} | collective-permute-start | bytes 884744 | tf_op jit(solution)/shard_map/ppermute | solution.py:245
  116.0 6.9 %collective-permute-start.22 = (bf16[384,384]{1,0:T(8,128)(2,1)S(1)}, bf16[384,384]{1,0:T(8,128)(2,1)S(1)}, u32[]{:S(2)}, u32[]{:S(2)}) collective-permute-start(bf16[384,384]{1,0:T(8,128)(2,1)S(1)} %get-tuple-element.8), channel_id=1, source_target_pairs={{4,0},{13,9},{11,15},{2,6},{20,16},{29,25},{27,31},{18,22}} | collective-permute-start | bytes 884744 | tf_op jit(solution)/shard_map/ppermute | solution.py:245
  123.2 4.5 %collective-permute-start.23 = (bf16[384,384]{1,0:T(8,128)(2,1)S(1)}, bf16[384,384]{1,0:T(8,128)(2,1)S(1)}, u32[]{:S(2)}, u32[]{:S(2)}) collective-permute-start(bf16[384,384]{1,0:T(8,128)(2,1)S(1)} %get-tuple-element.7), channel_id=1, source_target_pairs={{1,8},{3,10},{5,12},{7,14},{8,3},{10,5},{12,7},{14,1},{17,24},{19,... | collective-permute-start | bytes 884744 | tf_op jit(solution)/shard_map/ppermute | solution.py:254
  123.9 9.2 %collective-permute-start.24 = (bf16[384,384]{1,0:T(8,128)(2,1)S(1)}, bf16[384,384]{1,0:T(8,128)(2,1)S(1)}, u32[]{:S(2)}, u32[]{:S(2)}) collective-permute-start(bf16[384,384]{1,0:T(8,128)(2,1)S(1)} %get-tuple-element.6), channel_id=1, source_target_pairs={{0,2},{1,10},{2,4},{3,12},{4,6},{5,14},{6,0},{7,8},{8,5},{9,11},{1... | collective-permute-start | bytes 884744 | tf_op jit(solution)/shard_map/ppermute | solution.py:254
  125.7 16.7 %collective-permute-start.25 = (bf16[384,384]{1,0:T(8,128)(2,1)S(1)}, bf16[384,384]{1,0:T(8,128)(2,1)S(1)}, u32[]{:S(2)}, u32[]{:S(2)}) collective-permute-start(bf16[384,384]{1,0:T(8,128)(2,1)S(1)} %get-tuple-element.5), channel_id=1, source_target_pairs={{0,4},{6,2},{9,13},{15,11},{16,20},{22,18},{25,29},{31,27}} | collective-permute-start | bytes 884744 | tf_op jit(solution)/shard_map/ppermute | solution.py:254

commit v2 on v0

v2 whole, which is shorter than its diff:
```python
import functools

import jax
import jax.numpy as jnp
import numpy as np
from jax import lax
from jax.experimental import pallas as pl
from jax.experimental.pallas import tpu as pltpu
from jax.sharding import PartitionSpec as P

EXPERTS = 8
CAP = 384
BATCH = 96
WINDOW = 128
SNAKE = (0, 2, 4, 6, 7, 5, 3, 1)
F32, BF16, I32 = jnp.float32, jnp.bfloat16, jnp.int32


def plan_kernel(member, ids_ref, gates_ref, pick_ref, starts_ref, coef_ref):
    tokens = ids_ref.shape[0]
    local = EXPERTS // 2
    lanes = lax.broadcasted_iota(I32, (tokens, 128), 1)
    ids = [ids_ref[:, k : k + 1] for k in range(2)]
    hits = [ids[k] == lanes for k in range(2)]
    named = jnp.where(hits[0] | hits[1], 1.0, 0.0).astype(BF16)
    earlier = jnp.where(
        lax.broadcasted_iota(I32, (tokens, tokens), 1) < lax.broadcasted_iota(I32, (tokens, tokens), 0), 1.0, 0.0
    ).astype(BF16)
    before = jnp.dot(earlier, named, preferred_element_type=F32)

    slots = [ids[k] - member[0] * local for k in range(2)]
    here = [jnp.where((slots[k] >= 0) & (slots[k] < local), 1.0, 0.0) for k in range(2)]
    gates = [gates_ref[:, k : k + 1] for k in range(2)]
    both = here[0] * here[1]
    neither = (1.0 - here[0]) * (1.0 - here[1])
    mixed = 1.0 - both - neither
    weights = [here[k] * jnp.where(both > 0.5, gates[k], 1.0) for k in range(2)]
    ours = here[0] * gates[0] + here[1] * gates[1]
    theirs = (1.0 - here[0]) * gates[0] + (1.0 - here[1]) * gates[1]
    ours = jnp.where(mixed > 0.5, ours, both)
    theirs = jnp.where(mixed > 0.5, theirs, neither)
    coef_ref[...] = jnp.where(
        lanes == 0, weights[0], jnp.where(lanes == 1, weights[1], jnp.where(lanes == 2, ours, theirs))
    )

    columns = lax.broadcasted_iota(I32, (BATCH, local * WINDOW), 1)
    for b in range(tokens // BATCH):
        rows = slice(b * BATCH, (b + 1) * BATCH)
        start = before[b * BATCH : b * BATCH + 1, :].astype(I32)
        start = jnp.minimum((start >> 4) << 4, CAP - WINDOW)
        starts_ref[b : b + 1, :] = start
        ahead = before[rows] - start.astype(F32)
        for k in range(2):
            offset = jnp.sum(jnp.where(hits[k][rows], ahead, 0.0), axis=1, keepdims=True).astype(I32)
            at = jnp.where(here[k][rows] > 0.5, slots[k][rows] * WINDOW + offset, -1)
            pick_ref[(2 * b + k) * BATCH : (2 * b + k + 1) * BATCH, :] = jnp.where(columns == at, 1.0, 0.0).astype(BF16)


def plan(ids, gates, member):
    tokens = ids.shape[0]
    whole = lambda shape: pl.BlockSpec(shape, lambda i, s: (0, 0))
    shapes = [((2 * tokens, EXPERTS // 2 * WINDOW), BF16), ((tokens // BATCH, 128), I32), ((tokens, 128), F32)]
    return pl.pallas_call(
        plan_kernel,
        out_shape=[jax.ShapeDtypeStruct(*s) for s in shapes],
        grid_spec=pltpu.PrefetchScalarGridSpec(
            num_scalar_prefetch=1,
            grid=(1,),
            in_specs=[whole(ids.shape), whole(gates.shape)],
            out_specs=[whole(s[0]) for s in shapes],
        ),
        compiler_params=pltpu.CompilerParams(vmem_limit_bytes=32 << 20),
        name="plan",
    )(member.reshape(1).astype(I32), ids, gates)


def pick_kernel(where_, starts, pick_ref, coef_ref, rows_ref, out_ref):
    local = EXPERTS // 2
    for b in range(out_ref.shape[0] // BATCH):
        windows = []
        for k in range(local):
            first = k * CAP + starts[b, where_[1] * local + k]
            windows.append(rows_ref[pl.ds(pl.multiple_of(first, 16), WINDOW), :])
        picked = jnp.dot(
            pick_ref[2 * b * BATCH : 2 * (b + 1) * BATCH, :],
            jnp.concatenate(windows, axis=0),
            preferred_element_type=F32,
        )
        rows = slice(b * BATCH, (b + 1) * BATCH)
        total = coef_ref[rows, 0:1] * picked[:BATCH] + coef_ref[rows, 1:2] * picked[BATCH:]
        out_ref[rows, :] = total.astype(BF16)


def pick_half(where_, starts, pick, coef, rows, width, tile=512):
    tokens = coef.shape[0]
    steps = width // tile
    whole = lambda shape: pl.BlockSpec(shape, lambda j, w, s: (0, 0))
    return pl.pallas_call(
        pick_kernel,
        out_shape=jax.ShapeDtypeStruct((tokens, width), BF16),
        grid_spec=pltpu.PrefetchScalarGridSpec(
            num_scalar_prefetch=2,
            grid=(steps,),
            in_specs=[
                whole(pick.shape),
                whole(coef.shape),
                pl.BlockSpec((rows.shape[0], tile), lambda j, w, s: (0, w[0] * steps + j)),
            ],
            out_specs=pl.BlockSpec((tokens, tile), lambda j, w, s: (0, j)),
        ),
        cost_estimate=pl.CostEstimate(
            flops=2 * pick.size * width, bytes_accessed=2 * (rows.shape[0] + tokens) * width, transcendentals=0
        ),
        compiler_params=pltpu.CompilerParams(vmem_limit_bytes=60 << 20),
        name="pick",
    )(where_, starts, pick, coef, rows)


def merge_kernel(first, coef_ref, ours_ref, theirs_ref, *refs):
    total = coef_ref[:, 2:3] * ours_ref[...].astype(F32) + coef_ref[:, 3:4] * theirs_ref[...].astype(F32)
    total = total.astype(BF16)
    if first:
        refs[0][...] = total
    refs[-1][...] = total.T


def merge(coef, ours, theirs, turned=None, tile=384):
    tokens, width = ours.shape
    first = turned is None
    steps = width // tile
    tall = pl.BlockSpec((tokens, tile), lambda j: (0, j))
    flat = pl.BlockSpec((tile, tokens), lambda j: (j if first else j + steps, 0))
    in_specs = [pl.BlockSpec(coef.shape, lambda j: (0, 0)), tall, tall]
    args = [coef, ours, theirs]
    out_shape = [jax.ShapeDtypeStruct((2 * width, tokens), BF16)]
    out_specs = [flat]
    if first:
        out_shape.insert(0, jax.ShapeDtypeStruct((tokens, width), BF16))
        out_specs.insert(0, tall)
    else:
        in_specs.append(pl.BlockSpec(memory_space=pl.ANY))
        args.append(turned)
    return pl.pallas_call(
        functools.partial(merge_kernel, first),
        out_shape=out_shape,
        grid=(steps,),
        in_specs=in_specs,
        out_specs=out_specs,
        input_output_aliases={} if first else {3: 0},
        compiler_params=pltpu.CompilerParams(vmem_limit_bytes=32 << 20),
        cost_estimate=pl.CostEstimate(flops=4 * ours.size, bytes_accessed=6 * ours.size, transcendentals=0),
        name="merge_first" if first else "merge_second",
    )(*args)


def blocks_kernel(jobs, turned_ref, mine_ref, *refs):
    width = refs[-1].shape[0]
    for n, out_ref in enumerate(refs[-jobs.shape[0] :]):

        @pl.when(jobs[n, 0] >= 0)
        def _(n=n, out_ref=out_ref):
            down = pl.ds(pl.multiple_of(jobs[n, 0] * width, 128), width)
            along = pl.ds(pl.multiple_of(jobs[n, 1] * width, 128), width)
            block = jnp.dot(turned_ref[down, :], mine_ref[:, along], preferred_element_type=F32)
            out_ref[...] = block.astype(out_ref.dtype)


def moment_blocks(jobs, turned, mine, width, dtype, name, after=()):
    count = jobs.shape[0]
    whole = lambda shape: pl.BlockSpec(shape, lambda i, s: (0, 0))
    return pl.pallas_call(
        blocks_kernel,
        out_shape=[jax.ShapeDtypeStruct((width, width), dtype)] * count,
        grid_spec=pltpu.PrefetchScalarGridSpec(
            num_scalar_prefetch=1,
            grid=(1,),
            in_specs=[whole(turned.shape), whole(mine.shape)] + [pl.BlockSpec(memory_space=pl.ANY)] * len(after),
            out_specs=[whole((width, width))] * count,
        ),
        cost_estimate=pl.CostEstimate(
            flops=2 * count * mine.shape[0] * width * width,
            bytes_accessed=2 * turned.size + 2 * mine.size + count * width * width * 4,
            transcendentals=0,
        ),
        compiler_params=pltpu.CompilerParams(vmem_limit_bytes=40 << 20),
        name=name,
    )(jobs, turned, mine, *after)


def is_diagonal(b, e):
    return b // 4 == e


EXTRA = ((0, 0), (3, 0), (4, 1), (7, 1))


def owned_columns(b, e):
    shift = 0 if is_diagonal(b, e) or e == 1 else 1
    return [(b + shift) % 4, (b + shift + 1) % 4, (b + 2) % 4]


def extra_role(p, e, d):
    for b, core in EXTRA:
        q = SNAKE.index(b)
        if core == e and (q - p) % 8 == d:
            return b, 1
        if core == e and d >= 2 and (p - q) % 8 == d - 1:
            return b, -1
    return None


FIRST = ((0, 4), (0, 5), (1, 4), (1, 3), (2, 4))
SECOND = ((0, 3), (0, 6), (1, 5), (1, 2), (2, 3))
REST = ((0, 2), (0, 7), (1, 6), (1, 1), (2, 2), (0, 1), (1, 7), (2, 1), (0, 0), (1, 0), (2, 0))


def job_table(which):
    table = np.full((8, 2, len(which), 2), -1, np.int32)
    for p, b in enumerate(SNAKE):
        for e in range(2):
            for n, (x, t) in enumerate(which):
                if x < 2:
                    q = SNAKE[(p + t) % 8]
                else:
                    role = extra_role(p, e, t)
                    if role is None:
                        continue
                    q = role[0]
                table[b, e, n] = (q % 4 + (0 if q // 4 == e else 4), owned_columns(q, e)[x])
    return table


def ring_perm(distance, direction):
    pairs = [(SNAKE[p], SNAKE[(p + direction) % 8]) for p in range(8)]
    return [(a * 2 + e, b * 2 + e) for a, b in pairs for e in range(2)]


def extra_perm(d):
    pairs = []
    for p in range(8):
        for e in range(2):
            role = extra_role(p, e, d)
            if role is not None:
                pairs.append((SNAKE[p] * 2 + e, SNAKE[(p + role[1]) % 8] * 2 + e))
    return pairs


def mirror_perms():
    one, other = [], []
    for b in range(8):
        for e in range(2):
            here = b * 2 + e
            if is_diagonal(b, e):
                one.append((here, (b // 4 * 4 + (b + 1) % 4) * 2 + e))
                if (b, e) in EXTRA:
                    other.append((here, (b // 4 * 4 + (b + 2) % 4) * 2 + e))
            elif e == 1:
                other.append((here, (4 + b) * 2))
                one.append((here, (4 + (b + 1) % 4) * 2))
            else:
                other.append((here, (b + 1) % 4 * 2 + 1))
                one.append((here, (b + 2) % 4 * 2 + 1))
    return one, other


def place_table():
    table = np.zeros((8, 2, 6), np.int32)
    for b in range(8):
        for e in range(2):
            own = owned_columns(b, e)
            if is_diagonal(b, e):
                table[b, e] = (own[0], own[1], (b + 3) % 4, (b + 2) % 4, (b, e) in EXTRA, 1)
            elif e == 1:
                table[b, e] = (own[0], own[1], (b + 2) % 4, (b + 3) % 4, 0, 0)
            else:
                table[b, e] = (own[0], own[1], (b + 3) % 4, b % 4, 0, 0)
    return table


def finish_kernel(scale, place, own0, own1, own2, right0, left0, right1, left1, right2, left2, one, other, out_ref):
    width = one.shape[0]

    def put(n, value):
        out_ref[:, pl.ds(pl.multiple_of(place[n] * width, 128), width)] = value

    def owned(own, right, left):
        return (own[...] + right[...].astype(F32) + left[...].astype(F32)) * scale

    put(0, owned(own0, right0, left0))
    put(1, owned(own1, right1, left1))
    put(2, one[...].astype(F32).T)

    @pl.when(place[4] == 1)
    def _():
        put(3, owned(own2, right2, left2))

    @pl.when(place[4] == 0)
    def _():
        put(3, other[...].astype(F32).T)


def symmetric_moment(mine, turned, total_tokens):
    width = mine.shape[1] // 4
    both = ("dp", "expert")
    dp, e = lax.axis_index("dp"), lax.axis_index("expert")
    blocks = {}

    def compute(which, dtype, name, after=()):
        jobs = jnp.asarray(job_table(which))[dp, e]
        blocks.update(zip(which, moment_blocks(jobs, turned, mine, width, dtype, name, after)))

    def send(value, perm):
        return lax.ppermute(value, both, perm)

    def join(value, key):
        return (value.astype(F32) + blocks[key]).astype(BF16)

    compute(FIRST, BF16, "blocks_first")
    right = [send(blocks[0, 4], ring_perm(4, 1)), send(blocks[1, 3], ring_perm(3, 1))]
    left = [send(blocks[0, 5], ring_perm(3, -1)), send(blocks[1, 4], ring_perm(4, -1))]
    extra = send(blocks[2, 4], extra_perm(4))

    compute(SECOND, F32, "blocks_second")
    right = [send(join(right[0], (0, 3)), ring_perm(3, 1)), send(join(right[1], (1, 2)), ring_perm(2, 1))]
    left = [send(join(left[0], (0, 6)), ring_perm(2, -1)), send(join(left[1], (1, 5)), ring_perm(3, -1))]
    extra = send(join(extra, (2, 3)), extra_perm(3))

    compute(REST, F32, "blocks_rest")
    right = [send(join(right[0], (0, 2)), ring_perm(2, 1)), send(join(right[1], (1, 1)), ring_perm(1, 1))]
    left = [send(join(left[0], (0, 7)), ring_perm(1, -1)), send(join(left[1], (1, 6)), ring_perm(2, -1))]
    left2 = send(join(extra, (2, 2)), extra_perm(2))

    right[0] = send(join(right[0], (0, 1)), ring_perm(1, 1))
    left[1] = send(join(left[1], (1, 7)), ring_perm(1, -1))
    right2 = send(join(left2, (2, 1)), extra_perm(1))

    scale = 1.0 / total_tokens
    place = jnp.asarray(place_table())[dp, e]

    def done(x, r, l):
        return blocks[x, 0] + r.astype(F32) + l.astype(F32)

    perm_one, perm_other = mirror_perms()
    other = jnp.where(place[5] == 1, done(2, right2, left2), done(0, right[0], left[0]))
    other = send((other * scale).astype(BF16), perm_other)
    one = send((done(1, right[1], left[1]) * scale).astype(BF16), perm_one)

    block = pl.BlockSpec((width, width), lambda i, s: (0, 0))
    return pl.pallas_call(
        functools.partial(finish_kernel, scale),
        out_shape=jax.ShapeDtypeStruct((width, 4 * width), F32),
        grid_spec=pltpu.PrefetchScalarGridSpec(
            num_scalar_prefetch=1,
            grid=(1,),
            in_specs=[block] * 11,
            out_specs=pl.BlockSpec((width, 4 * width), lambda i, s: (0, 0)),
        ),
        compiler_params=pltpu.CompilerParams(vmem_limit_bytes=32 << 20),
        name="finish",
    )(
        place,
        *[blocks[x, 0] for x in range(3)],
        right[0],
        left[0],
        right[1],
        left[1],
        right2,
        left2,
        one,
        other,
    )


def per_device(expert_ids, gates, expert_out):
    tokens, channels = expert_ids.shape[0], expert_out.shape[1]
    dp_size = lax.axis_size("dp")
    member = lax.axis_index("expert")
    half = channels // 2
    swap = [(0, 1), (1, 0)]

    pick, starts, coef = plan(expert_ids, gates, member)
    mine, theirs = [], []
    for column_half in (1 - member, member):
        where_ = jnp.stack([column_half, member]).astype(I32)
        mine.append(pick_half(where_, starts, pick, coef, expert_out, half))
        theirs.append(lax.ppermute(mine[-1], "expert", swap))
    rows, turned = merge(coef, mine[1], theirs[0])
    (turned,) = merge(coef, mine[0], theirs[1], turned)

    total_tokens = tokens * dp_size
    if dp_size == 8 and channels == 8 * 384:
        return symmetric_moment(rows, turned, total_tokens)
    slab = jnp.dot(turned, rows, preferred_element_type=F32)
    slab = jnp.where(member == 0, slab, jnp.roll(slab, half, axis=0))
    return lax.psum_scatter(slab, "dp", scatter_dimension=0, tiled=True) / total_tokens


def solution(mesh):
    assert mesh.shape["expert"] == 2
    in_specs = (
        P(("groups", "dp"), None),
        P(("groups", "dp"), None),
        P(("groups", "dp", "expert"), None),
    )
    out_specs = P(("groups", "dp"), "expert")
    return jax.shard_map(
        per_device, mesh=mesh, in_specs=in_specs, out_specs=out_specs, check_vma=False
    )
```

time: 463 us -> 124 us (0.27)
  the two profiles are of different devices: /device:TPU:1 before, /device:TPU:0 now
where the time goes in v2:
time: 124 us; the launch traced here: 123 us
  waiting for transfers between devices  37.4 us (30%)
  Pallas kernels  36.6 us (30%)
  starting transfers between devices  36.1 us (29%)
  local copies, waits for them, and re-layouts  9.72 us (8%)
  other arithmetic  2.55 us (2%)
    ppermute x20, waiting for transfers between devices, send(): return lax.ppermute(value, both, perm)  37.4 us
    ppermute x20, starting transfers between devices, send(): return lax.ppermute(value, both, perm)  35.5 us
    pallas_call x2, Pallas kernels, pick_half(): pl.pallas_call(pick_kernel, out_shape=jax.ShapeDtypeStruct((tokens, width...  14.9 us
    pallas_call x3, Pallas kernels, moment_blocks(): pl.pallas_call(blocks_kernel, out_shape=[jax.ShapeDtypeStruct((width, wid...  10.5 us
    pallas_call x2, Pallas kernels, merge(): pl.pallas_call(functools.partial(merge_kernel, first), out_shape=out_shap...  6.88 us
    unnamed x14, local copies, waits for them, and re-layouts  6.11 us
    pallas_call x1, Pallas kernels, symmetric_moment(): pl.pallas_call(functools.partial(finish_kernel, scale), out_shape=jax.Sha...  2.53 us
  transfers between devices with their start and end apart: 22, of which 10 were waited for; matrix products, arithmetic and copies ran while one was open for 4% of the time, Pallas kernels for 16%

profile of v2, /device:TPU:0, one launch (start us, length us, event | category | flops | bytes accessed | tf_op | source)
XLA Modules:
  0.0 123.3 jit_solution(7875016738951602537)
XLA Ops:
  0.0 0.9 copy.10.gates_ref
  0.9 0.9 copy.9.ids_ref
  1.8 0.7 pad_add_fusion.where_
  2.4 1.8 %plan.1 = (bf16[1536,512]{1,0:T(8,128)(2,1)S(1)}, s32[8,128]{1,0:T(8,128)S(1)}, f32[768,128]{1,0:T(8,128)S(1)}) custom-call(s32[1]{0:T(128)} %bitcast.2.member, s32[768,2]{1,0:T(8,128)S(1)} %copy.9.ids_ref, f32[768,2]{1,0:T(8,128)S(1)} %copy.10.gates_ref), custom_call_target="tpu_custom_call" | custom-call | tf_op jit(solution)/shard_map/plan/pallas_call | solution.py:63
  4.3 0.8 copy-done.2
  5.0 1.2 copy-done.4
  6.2 0.6 copy-done.5
  6.8 7.4 %pick.2.ours_ref = bf16[768,1536]{1,0:T(8,128)(2,1)} custom-call(s32[2]{0:T(128)} %pad_add_fusion.where_, s32[8,128]{1,0:T(8,128)} %copy-done.5, bf16[1536,512]{1,0:T(8,128)(2,1)} %copy-done.4, f32[768,128]{1,0:T(8,128)} %copy-done.2, bf16[1536,3072]{1,0:T(8,128)(2,1)} %rows_ref.3), custom_call_target="tpu_custom_call" | custom-call | flops 2415919104 | bytes 7077888 | tf_op jit(solution)/shard_map/pick/pallas_call | solution.py:98
  14.2 0.4 collective-permute-start.1
  14.5 0.6 pad_add_fusion.1.where_
  15.2 7.5 %pick.3.ours_ref = bf16[768,1536]{1,0:T(8,128)(2,1)} custom-call(s32[2]{0:T(128)} %pad_add_fusion.1.where_, s32[8,128]{1,0:T(8,128)} %copy-done.5, bf16[1536,512]{1,0:T(8,128)(2,1)} %copy-done.4, f32[768,128]{1,0:T(8,128)} %copy-done.2, bf16[1536,3072]{1,0:T(8,128)(2,1)} %rows_ref.3), custom_call_target="tpu_custom_call" | custom-call | flops 2415919104 | bytes 7077888 | tf_op jit(solution)/shard_map/pick/pallas_call | solution.py:98
  22.7 0.2 collective-permute-start
  22.9 0.7 dynamic-slice_bitcast_fusion
  23.6 0.1 copy.12.jobs
  23.7 0.1 copy.13.jobs
  23.8 0.7 dynamic-slice_bitcast_fusion.2
  24.5 0.1 copy.11.jobs
  24.6 1.8 %copy-done.1 = bf16[768,1536]{1,0:T(8,128)(2,1)S(1)} copy-done((bf16[768,1536]{1,0:T(8,128)(2,1)S(1)}, bf16[768,1536]{1,0:T(8,128)(2,1)}, u32[]{:S(2)}) %copy-start.1) | copy-done | bytes 2359320
  26.4 4.2 %merge_first.1 = (bf16[768,1536]{1,0:T(8,128)(2,1)S(1)}, bf16[3072,768]{1,0:T(8,128)(2,1)S(1)}) custom-call(f32[768,128]{1,0:T(8,128)S(1)} %copy-done.3, bf16[768,1536]{1,0:T(8,128)(2,1)S(1)} %copy-done.1, bf16[768,1536]{1,0:T(8,128)(2,1)} %collective-permute-done.1.theirs_ref), custom_call_target="tpu_custom_call" | custom-call | flops 4718592 | bytes 7077888 | tf_op jit(solution)/shard_map/merge_first/pallas_call | solution.py:143
  30.6 2.7 %merge_second.1.turned_ref = bf16[3072,768]{1,0:T(8,128)(2,1)S(1)} custom-call(f32[768,128]{1,0:T(8,128)S(1)} %copy-done.3, bf16[768,1536]{1,0:T(8,128)(2,1)S(1)} %copy-done, bf16[768,1536]{1,0:T(8,128)(2,1)S(1)} %collective-permute-done.theirs_ref, bf16[3072,768]{1,0:T(8,128)(2,1)S(1)} %get-tuple-element.34.refs_0_), custom_call_target="tpu_custom_call", output_to_operand_aliasing={{}: (3, {})} | custom-call | flops 4718592 | bytes 7077888 | tf_op jit(solution)/shard_map/merge_second/pallas_call | solution.py:143
  33.3 2.5 %blocks_first.1 = (bf16[384,384]{1,0:T(8,128)(2,1)S(1)}, bf16[384,384]{1,0:T(8,128)(2,1)S(1)}, bf16[384,384]{1,0:T(8,128)(2,1)S(1)}, bf16[384,384]{1,0:T(8,128)(2,1)S(1)}, bf16[384,384]{1,0:T(8,128)(2,1)S(1)}) custom-call(s32[5,2]{1,0:T(8,128)S(1)} %copy.12.jobs, bf16[3072,768]{1,0:T(8,128)(2,1)S(1)} %merge_second.1.turned_ref, ...), custom_call_target="tpu_custom_call" | custom-call | flops 1132462080 | bytes 10027008 | tf_op jit(solution)/shard_map/blocks_first/pallas_call | solution.py:171
  35.8 1.3 %collective-permute-start.16 = (bf16[384,384]{1,0:T(8,128)(2,1)S(1)}, bf16[384,384]{1,0:T(8,128)(2,1)S(1)}, u32[]{:S(2)}, u32[]{:S(2)}) collective-permute-start(bf16[384,384]{1,0:T(8,128)(2,1)S(1)} %get-tuple-element.53), channel_id=1, source_target_pairs={{1,5},{4,0},{8,12},{12,8},{14,10},{11,15},{7,3},{3,7},{17,21},{20,... | collective-permute-start | bytes 884744 | tf_op jit(solution)/shard_map/ppermute | solution.py:313
  37.1 2.4 %collective-permute-start.6 = (bf16[384,384]{1,0:T(8,128)(2,1)S(1)}, bf16[384,384]{1,0:T(8,128)(2,1)S(1)}, u32[]{:S(2)}, u32[]{:S(2)}) collective-permute-start(bf16[384,384]{1,0:T(8,128)(2,1)S(1)} %get-tuple-element.43), channel_id=1, source_target_pairs={{0,2},{1,3},{4,0},{5,1},{8,4},{9,5},{12,8},{13,9},{14,12},{15,13},... | collective-permute-start | bytes 884744 | tf_op jit(solution)/shard_map/ppermute | solution.py:313
  39.5 5.0 %blocks_rest.1 = (f32[384,384]{1,0:T(8,128)S(1)}, f32[384,384]{1,0:T(8,128)S(1)}, f32[384,384]{1,0:T(8,128)S(1)}, f32[384,384]{1,0:T(8,128)S(1)}, f32[384,384]{1...) custom-call(s32[11,2]{1,0:T(8,128)S(1)} %copy.11.jobs, ...), custom_call_target="tpu_custom_call" | custom-call | flops 2491416576 | bytes 13565952 | tf_op jit(solution)/shard_map/blocks_rest/pallas_call | solution.py:171
  44.5 3.0 %blocks_second.1 = (f32[384,384]{1,0:T(8,128)S(1)}, f32[384,384]{1,0:T(8,128)S(1)}, f32[384,384]{1,0:T(8,128)S(1)}, f32[384,384]{1,0:T(8,128)S(1)}, f32[384,384]{1,0:T(8,128)S(1)}) custom-call(s32[5,2]{1,0:T(8,128)S(1)} %copy.13.jobs, bf16[3072,768]{1,0:T(8,128)(2,1)S(1)} %merge_second.1.turned_ref, bf16[768,1536]{1,0:T(8,128)(2,1)S(1)} %get-tuple-element.35.mine_ref), custom_call_target="tpu_custom_call" | custom-call | flops 1132462080 | bytes 10027008 | tf_op jit(solution)/shard_map/blocks_second/pallas_call | solution.py:171
  47.5 0.7 collective-permute-start.2
  48.3 1.3 %collective-permute-start.12 = (bf16[384,384]{1,0:T(8,128)(2,1)S(1)}, bf16[384,384]{1,0:T(8,128)(2,1)S(1)}, u32[]{:S(2)}, u32[]{:S(2)}) collective-permute-start(bf16[384,384]{1,0:T(8,128)(2,1)S(1)} %get-tuple-element.49), channel_id=1, source_target_pairs={{0,2},{1,3},{4,0},{5,1},{8,4},{9,5},{12,8},{13,9},{14,12},{15,13},... | collective-permute-start | bytes 884744 | tf_op jit(solution)/shard_map/ppermute | solution.py:313
  49.6 2.4 %collective-permute-start.9 = (bf16[384,384]{1,0:T(8,128)(2,1)S(1)}, bf16[384,384]{1,0:T(8,128)(2,1)S(1)}, u32[]{:S(2)}, u32[]{:S(2)}) collective-permute-start(bf16[384,384]{1,0:T(8,128)(2,1)S(1)} %get-tuple-element.46), channel_id=1, source_target_pairs={{0,4},{1,5},{4,8},{5,9},{8,12},{9,13},{12,14},{13,15},{14,10},{15,... | collective-permute-start | bytes 884744 | tf_op jit(solution)/shard_map/ppermute | solution.py:313
  52.0 0.1 add_convert_fusion.1
  52.1 1.5 %collective-permute-start.17 = (bf16[384,384]{1,0:T(8,128)(2,1)S(1)}, bf16[384,384]{1,0:T(8,128)(2,1)S(1)}, u32[]{:S(2)}, u32[]{:S(2)}) collective-permute-start(bf16[384,384]{1,0:T(8,128)(2,1)S(1)} %add_convert_fusion.1), channel_id=1, source_target_pairs={{0,2},{5,9},{8,4},{12,14},{15,13},{10,6},{7,11},{3,1},{16,18},{21,... | collective-permute-start | bytes 884744 | tf_op jit(solution)/shard_map/ppermute | solution.py:313
  53.6 0.1 add_convert_fusion.8
  53.8 2.4 %collective-permute-done.2 = bf16[384,384]{1,0:T(8,128)(2,1)S(1)} collective-permute-done((bf16[384,384]{1,0:T(8,128)(2,1)S(1)}, bf16[384,384]{1,0:T(8,128)(2,1)S(1)}, u32[]{:S(2)}, u32[]{:S(2)}) %collective-permute-start.2) | collective-permute-done | bytes 294944 | tf_op jit(solution)/shard_map/ppermute | solution.py:313
  56.2 3.4 %collective-permute-start.3 = (bf16[384,384]{1,0:T(8,128)(2,1)S(1)}, bf16[384,384]{1,0:T(8,128)(2,1)S(1)}, u32[]{:S(2)}, u32[]{:S(2)}) collective-permute-start(bf16[384,384]{1,0:T(8,128)(2,1)S(1)} %add_convert_fusion.11), channel_id=1, source_target_pairs={{0,4},{1,5},{4,8},{5,9},{8,12},{9,13},{12,14},{13,15},{14,10},{15,... | collective-permute-start | bytes 884744 | tf_op jit(solution)/shard_map/ppermute | solution.py:313
  59.6 0.3 collective-permute-done.12
  60.0 2.5 %collective-permute-done.9 = bf16[384,384]{1,0:T(8,128)(2,1)S(1)} collective-permute-done((bf16[384,384]{1,0:T(8,128)(2,1)S(1)}, bf16[384,384]{1,0:T(8,128)(2,1)S(1)}, u32[]{:S(2)}, u32[]{:S(2)}) %collective-permute-start.9) | collective-permute-done | bytes 294944 | tf_op jit(solution)/shard_map/ppermute | solution.py:313
  62.5 0.1 add_convert_fusion.6
  62.5 3.4 %collective-permute-start.10 = (bf16[384,384]{1,0:T(8,128)(2,1)S(1)}, bf16[384,384]{1,0:T(8,128)(2,1)S(1)}, u32[]{:S(2)}, u32[]{:S(2)}) collective-permute-start(bf16[384,384]{1,0:T(8,128)(2,1)S(1)} %add_convert_fusion.6), channel_id=1, source_target_pairs={{0,4},{1,5},{4,8},{5,9},{8,12},{9,13},{12,14},{13,15},{14,10},{15,... | collective-permute-start | bytes 884744 | tf_op jit(solution)/shard_map/ppermute | solution.py:313
  65.9 0.1 add_convert_fusion
  66.0 1.3 %collective-permute-start.18 = (bf16[384,384]{1,0:T(8,128)(2,1)S(1)}, bf16[384,384]{1,0:T(8,128)(2,1)S(1)}, u32[]{:S(2)}, u32[]{:S(2)}) collective-permute-start(bf16[384,384]{1,0:T(8,128)(2,1)S(1)} %add_convert_fusion), channel_id=1, source_target_pairs={{1,5},{4,0},{9,13},{13,9},{14,10},{11,15},{6,2},{2,6},{17,21},{20,... | collective-permute-start | bytes 884744 | tf_op jit(solution)/shard_map/ppermute | solution.py:313
  67.3 1.3 %collective-permute-done.7 = bf16[384,384]{1,0:T(8,128)(2,1)S(1)} collective-permute-done((bf16[384,384]{1,0:T(8,128)(2,1)S(1)}, bf16[384,384]{1,0:T(8,128)(2,1)S(1)}, u32[]{:S(2)}, u32[]{:S(2)}) %collective-permute-start.7) | collective-permute-done | bytes 294944 | tf_op jit(solution)/shard_map/ppermute | solution.py:313
  68.6 0.1 add_convert_fusion.7
  68.7 7.8 %collective-permute-start.8 = (bf16[384,384]{1,0:T(8,128)(2,1)S(1)}, bf16[384,384]{1,0:T(8,128)(2,1)S(1)}, u32[]{:S(2)}, u32[]{:S(2)}) collective-permute-start(bf16[384,384]{1,0:T(8,128)(2,1)S(1)} %add_convert_fusion.7), channel_id=1, source_target_pairs={{0,2},{1,3},{4,0},{5,1},{8,4},{9,5},{12,8},{13,9},{14,12},{15,13},... | collective-permute-start | bytes 884744 | tf_op jit(solution)/shard_map/ppermute | solution.py:313
  76.7 0.1 add_convert_fusion.3
  76.7 2.1 %collective-permute-start.14 = (bf16[384,384]{1,0:T(8,128)(2,1)S(1)}, bf16[384,384]{1,0:T(8,128)(2,1)S(1)}, u32[]{:S(2)}, u32[]{:S(2)}) collective-permute-start(bf16[384,384]{1,0:T(8,128)(2,1)S(1)} %add_convert_fusion.3), channel_id=1, source_target_pairs={{0,2},{1,3},{4,0},{5,1},{8,4},{9,5},{12,8},{13,9},{14,12},{15,13},... | collective-permute-start | bytes 884744 | tf_op jit(solution)/shard_map/ppermute | solution.py:313
  78.8 0.1 add_convert_fusion.5
  78.9 0.1 collective-permute-start.11
  79.0 0.1 fusion
  79.0 1.3 %collective-permute-start.19 = (bf16[384,384]{1,0:T(8,128)(2,1)S(1)}, bf16[384,384]{1,0:T(8,128)(2,1)S(1)}, u32[]{:S(2)}, u32[]{:S(2)}) collective-permute-start(bf16[384,384]{1,0:T(8,128)(2,1)S(1)} %fusion), channel_id=1, source_target_pairs={{5,9},{13,15},{10,6},{2,0},{21,25},{29,31},{26,22},{18,16}} | collective-permute-start | bytes 884744 | tf_op jit(solution)/shard_map/ppermute | solution.py:313
  80.3 6.3 %collective-permute-done.4 = bf16[384,384]{1,0:T(8,128)(2,1)S(1)} collective-permute-done((bf16[384,384]{1,0:T(8,128)(2,1)S(1)}, bf16[384,384]{1,0:T(8,128)(2,1)S(1)}, u32[]{:S(2)}, u32[]{:S(2)}) %collective-permute-start.4) | collective-permute-done | bytes 294944 | tf_op jit(solution)/shard_map/ppermute | solution.py:313
  86.6 0.1 add_convert_fusion.9
  86.7 0.3 collective-permute-done.14
  87.1 0.1 add_convert_fusion.2
  87.2 4.9 %collective-permute-start.15 = (bf16[384,384]{1,0:T(8,128)(2,1)S(1)}, bf16[384,384]{1,0:T(8,128)(2,1)S(1)}, u32[]{:S(2)}, u32[]{:S(2)}) collective-permute-start(bf16[384,384]{1,0:T(8,128)(2,1)S(1)} %add_convert_fusion.2), channel_id=1, source_target_pairs={{0,2},{1,3},{4,0},{5,1},{8,4},{9,5},{12,8},{13,9},{14,12},{15,13},... | collective-permute-start | bytes 884744 | tf_op jit(solution)/shard_map/ppermute | solution.py:313
  92.1 0.7 constant_dynamic-slice_fusion
  92.8 0.6 slice.4
  94.0 4.5 %collective-permute-done.19.right2 = bf16[384,384]{1,0:T(8,128)(2,1)S(1)} collective-permute-done((bf16[384,384]{1,0:T(8,128)(2,1)S(1)}, bf16[384,384]{1,0:T(8,128)(2,1)S(1)}, u32[]{:S(2)}, u32[]{:S(2)}) %collective-permute-start.19) | collective-permute-done | bytes 294944 | tf_op jit(solution)/shard_map/ppermute | solution.py:313
  98.5 3.2 %collective-permute-done.5.right0 = bf16[384,384]{1,0:T(8,128)(2,1)S(1)} collective-permute-done((bf16[384,384]{1,0:T(8,128)(2,1)S(1)}, bf16[384,384]{1,0:T(8,128)(2,1)S(1)}, u32[]{:S(2)}, u32[]{:S(2)}) %collective-permute-start.5) | collective-permute-done | bytes 294944 | tf_op jit(solution)/shard_map/ppermute | solution.py:313
  101.7 0.2 fusion.3
  101.9 1.3 %collective-permute-start.21 = (bf16[384,384]{1,0:T(8,128)(2,1)S(1)}, bf16[384,384]{1,0:T(8,128)(2,1)S(1)}, u32[]{:S(2)}, u32[]{:S(2)}) collective-permute-start(bf16[384,384]{1,0:T(8,128)(2,1)S(1)} %fusion.3), channel_id=1, source_target_pairs={{0,4},{1,8},{3,10},{5,12},{6,2},{7,14},{8,3},{9,13},{10,5},{12,7},... | collective-permute-start | bytes 884744 | tf_op jit(solution)/shard_map/ppermute | solution.py:313
  103.3 0.1 multiply_convert_fusion
  103.4 0.7 fusion.4.place
  104.1 5.4 %collective-permute-done.21.other = bf16[384,384]{1,0:T(8,128)(2,1)S(1)} collective-permute-done((bf16[384,384]{1,0:T(8,128)(2,1)S(1)}, bf16[384,384]{1,0:T(8,128)(2,1)S(1)}, u32[]{:S(2)}, u32[]{:S(2)}) %collective-permute-start.21) | collective-permute-done | bytes 294944 | tf_op jit(solution)/shard_map/ppermute | solution.py:313
  109.5 11.2 %collective-permute-done.20.one = bf16[384,384]{1,0:T(8,128)(2,1)S(1)} collective-permute-done((bf16[384,384]{1,0:T(8,128)(2,1)S(1)}, bf16[384,384]{1,0:T(8,128)(2,1)S(1)}, u32[]{:S(2)}, u32[]{:S(2)}) %collective-permute-start.20) | collective-permute-done | bytes 294944 | tf_op jit(solution)/shard_map/ppermute | solution.py:313
  120.8 2.5 %finish.1 = f32[384,1536]{1,0:T(8,128)} custom-call(s32[6]{0:T(128)S(1)} %fusion.4.place, f32[384,384]{1,0:T(8,128)S(1)} %get-tuple-element.36.own0, f32[384,384]{1,0:T(8,128)S(1)} %get-tuple-element.37.own1, f32[384,384]{1,0:T(8,128)S(1)} %get-tuple-element.38.own2, bf16[384,384]{1,0:T(8,128)(2,1)S(1)} %collective-permute-done.5.right0, ...), custom_call_target="tpu_custom_call" | custom-call | tf_op jit(solution)/shard_map/finish/pallas_call | solution.py:349
  (28 shorter events, 0.5 us)
Async XLA Ops:
  4.2 0.8 copy-start.2
  5.0 1.2 copy-start.4
  6.2 0.6 copy-start.5
  14.2 10.4 %collective-permute-start.1 = (bf16[768,1536]{1,0:T(8,128)(2,1)}, bf16[768,1536]{1,0:T(8,128)(2,1)}, u32[]{:S(2)}, u32[]{:S(2)}) collective-permute-start(bf16[768,1536]{1,0:T(8,128)(2,1)} %pick.2.ours_ref), channel_id=1, source_target_pairs={{0,1},{1,0},{2,3},{3,2},{4,5},{5,4},{6,7},{7,6},{8,9},{9,8},{10,11... | collective-permute-start | bytes 7077896 | tf_op jit(solution)/shard_map/ppermute | solution.py:386
  15.2 9.4 %copy-start.3 = (f32[768,128]{1,0:T(8,128)S(1)}, f32[768,128]{1,0:T(8,128)}, u32[]{:S(2)}) copy-start(f32[768,128]{1,0:T(8,128)} %copy-done.2) | copy-start | bytes 1179652
  22.7 7.9 %collective-permute-start = (bf16[768,1536]{1,0:T(8,128)(2,1)}, bf16[768,1536]{1,0:T(8,128)(2,1)S(1)}, u32[]{:S(2)}, u32[]{:S(2)}) collective-permute-start(bf16[768,1536]{1,0:T(8,128)(2,1)} %pick.3.ours_ref), channel_id=1, source_target_pairs={{0,1},{1,0},{2,3},{3,2},{4,5},{5,4},{6,7},{7,6},{8,9},{9,8},{10,11... | collective-permute-start | bytes 7077896 | tf_op jit(solution)/shard_map/ppermute | solution.py:386
  24.6 6.0 %copy-start = (bf16[768,1536]{1,0:T(8,128)(2,1)S(1)}, bf16[768,1536]{1,0:T(8,128)(2,1)}, u32[]{:S(2)}) copy-start(bf16[768,1536]{1,0:T(8,128)(2,1)} %pick.2.ours_ref) | copy-start | bytes 7077892
  24.6 1.8 %copy-start.1 = (bf16[768,1536]{1,0:T(8,128)(2,1)S(1)}, bf16[768,1536]{1,0:T(8,128)(2,1)}, u32[]{:S(2)}) copy-start(bf16[768,1536]{1,0:T(8,128)(2,1)} %pick.3.ours_ref) | copy-start | bytes 7077892
  35.8 16.2 %collective-permute-start.16 = (bf16[384,384]{1,0:T(8,128)(2,1)S(1)}, bf16[384,384]{1,0:T(8,128)(2,1)S(1)}, u32[]{:S(2)}, u32[]{:S(2)}) collective-permute-start(bf16[384,384]{1,0:T(8,128)(2,1)S(1)} %get-tuple-element.53), channel_id=1, source_target_pairs={{1,5},{4,0},{8,12},{12,8},{14,10},{11,15},{7,3},{3,7},{17,21},{20,... | collective-permute-start | bytes 884744 | tf_op jit(solution)/shard_map/ppermute | solution.py:313
  37.1 16.5 %collective-permute-start.6 = (bf16[384,384]{1,0:T(8,128)(2,1)S(1)}, bf16[384,384]{1,0:T(8,128)(2,1)S(1)}, u32[]{:S(2)}, u32[]{:S(2)}) collective-permute-start(bf16[384,384]{1,0:T(8,128)(2,1)S(1)} %get-tuple-element.43), channel_id=1, source_target_pairs={{0,2},{1,3},{4,0},{5,1},{8,4},{9,5},{12,8},{13,9},{14,12},{15,13},... | collective-permute-start | bytes 884744 | tf_op jit(solution)/shard_map/ppermute | solution.py:313
  47.5 8.6 %collective-permute-start.2 = (bf16[384,384]{1,0:T(8,128)(2,1)S(1)}, bf16[384,384]{1,0:T(8,128)(2,1)S(1)}, u32[]{:S(2)}, u32[]{:S(2)}) collective-permute-start(bf16[384,384]{1,0:T(8,128)(2,1)S(1)} %get-tuple-element.39), channel_id=1, source_target_pairs={{0,4},{1,5},{4,8},{5,9},{8,12},{9,13},{12,14},{13,15},{14,10},{15,... | collective-permute-start | bytes 884744 | tf_op jit(solution)/shard_map/ppermute | solution.py:313
  48.3 11.6 %collective-permute-start.12 = (bf16[384,384]{1,0:T(8,128)(2,1)S(1)}, bf16[384,384]{1,0:T(8,128)(2,1)S(1)}, u32[]{:S(2)}, u32[]{:S(2)}) collective-permute-start(bf16[384,384]{1,0:T(8,128)(2,1)S(1)} %get-tuple-element.49), channel_id=1, source_target_pairs={{0,2},{1,3},{4,0},{5,1},{8,4},{9,5},{12,8},{13,9},{14,12},{15,13},... | collective-permute-start | bytes 884744 | tf_op jit(solution)/shard_map/ppermute | solution.py:313
  49.6 12.9 %collective-permute-start.9 = (bf16[384,384]{1,0:T(8,128)(2,1)S(1)}, bf16[384,384]{1,0:T(8,128)(2,1)S(1)}, u32[]{:S(2)}, u32[]{:S(2)}) collective-permute-start(bf16[384,384]{1,0:T(8,128)(2,1)S(1)} %get-tuple-element.46), channel_id=1, source_target_pairs={{0,4},{1,5},{4,8},{5,9},{8,12},{9,13},{12,14},{13,15},{14,10},{15,... | collective-permute-start | bytes 884744 | tf_op jit(solution)/shard_map/ppermute | solution.py:313
  52.1 13.8 %collective-permute-start.17 = (bf16[384,384]{1,0:T(8,128)(2,1)S(1)}, bf16[384,384]{1,0:T(8,128)(2,1)S(1)}, u32[]{:S(2)}, u32[]{:S(2)}) collective-permute-start(bf16[384,384]{1,0:T(8,128)(2,1)S(1)} %add_convert_fusion.1), channel_id=1, source_target_pairs={{0,2},{5,9},{8,4},{12,14},{15,13},{10,6},{7,11},{3,1},{16,18},{21,... | collective-permute-start | bytes 884744 | tf_op jit(solution)/shard_map/ppermute | solution.py:313
  53.7 14.9 %collective-permute-start.7 = (bf16[384,384]{1,0:T(8,128)(2,1)S(1)}, bf16[384,384]{1,0:T(8,128)(2,1)S(1)}, u32[]{:S(2)}, u32[]{:S(2)}) collective-permute-start(bf16[384,384]{1,0:T(8,128)(2,1)S(1)} %add_convert_fusion.8), channel_id=1, source_target_pairs={{0,2},{1,3},{4,0},{5,1},{8,4},{9,5},{12,8},{13,9},{14,12},{15,13},... | collective-permute-start | bytes 884744 | tf_op jit(solution)/shard_map/ppermute | solution.py:313
  56.2 20.3 %collective-permute-start.3 = (bf16[384,384]{1,0:T(8,128)(2,1)S(1)}, bf16[384,384]{1,0:T(8,128)(2,1)S(1)}, u32[]{:S(2)}, u32[]{:S(2)}) collective-permute-start(bf16[384,384]{1,0:T(8,128)(2,1)S(1)} %add_convert_fusion.11), channel_id=1, source_target_pairs={{0,4},{1,5},{4,8},{5,9},{8,12},{9,13},{12,14},{13,15},{14,10},{15,... | collective-permute-start | bytes 884744 | tf_op jit(solution)/shard_map/ppermute | solution.py:313
  59.9 16.7 %collective-permute-start.13 = (bf16[384,384]{1,0:T(8,128)(2,1)S(1)}, bf16[384,384]{1,0:T(8,128)(2,1)S(1)}, u32[]{:S(2)}, u32[]{:S(2)}) collective-permute-start(bf16[384,384]{1,0:T(8,128)(2,1)S(1)} %add_convert_fusion.4), channel_id=1, source_target_pairs={{0,2},{1,3},{4,0},{5,1},{8,4},{9,5},{12,8},{13,9},{14,12},{15,13},... | collective-permute-start | bytes 884744 | tf_op jit(solution)/shard_map/ppermute | solution.py:313
  62.5 16.3 %collective-permute-start.10 = (bf16[384,384]{1,0:T(8,128)(2,1)S(1)}, bf16[384,384]{1,0:T(8,128)(2,1)S(1)}, u32[]{:S(2)}, u32[]{:S(2)}) collective-permute-start(bf16[384,384]{1,0:T(8,128)(2,1)S(1)} %add_convert_fusion.6), channel_id=1, source_target_pairs={{0,4},{1,5},{4,8},{5,9},{8,12},{9,13},{12,14},{13,15},{14,10},{15,... | collective-permute-start | bytes 884744 | tf_op jit(solution)/shard_map/ppermute | solution.py:313
  66.0 12.9 %collective-permute-start.18 = (bf16[384,384]{1,0:T(8,128)(2,1)S(1)}, bf16[384,384]{1,0:T(8,128)(2,1)S(1)}, u32[]{:S(2)}, u32[]{:S(2)}) collective-permute-start(bf16[384,384]{1,0:T(8,128)(2,1)S(1)} %add_convert_fusion), channel_id=1, source_target_pairs={{1,5},{4,0},{9,13},{13,9},{14,10},{11,15},{6,2},{2,6},{17,21},{20,... | collective-permute-start | bytes 884744 | tf_op jit(solution)/shard_map/ppermute | solution.py:313
  68.7 25.3 %collective-permute-start.8 = (bf16[384,384]{1,0:T(8,128)(2,1)S(1)}, bf16[384,384]{1,0:T(8,128)(2,1)S(1)}, u32[]{:S(2)}, u32[]{:S(2)}) collective-permute-start(bf16[384,384]{1,0:T(8,128)(2,1)S(1)} %add_convert_fusion.7), channel_id=1, source_target_pairs={{0,2},{1,3},{4,0},{5,1},{8,4},{9,5},{12,8},{13,9},{14,12},{15,13},... | collective-permute-start | bytes 884744 | tf_op jit(solution)/shard_map/ppermute | solution.py:313
  76.6 10.0 %collective-permute-start.4 = (bf16[384,384]{1,0:T(8,128)(2,1)S(1)}, bf16[384,384]{1,0:T(8,128)(2,1)S(1)}, u32[]{:S(2)}, u32[]{:S(2)}) collective-permute-start(bf16[384,384]{1,0:T(8,128)(2,1)S(1)} %add_convert_fusion.10), channel_id=1, source_target_pairs={{0,4},{1,5},{4,8},{5,9},{8,12},{9,13},{12,14},{13,15},{14,10},{15,... | collective-permute-start | bytes 884744 | tf_op jit(solution)/shard_map/ppermute | solution.py:313
  76.7 10.3 %collective-permute-start.14 = (bf16[384,384]{1,0:T(8,128)(2,1)S(1)}, bf16[384,384]{1,0:T(8,128)(2,1)S(1)}, u32[]{:S(2)}, u32[]{:S(2)}) collective-permute-start(bf16[384,384]{1,0:T(8,128)(2,1)S(1)} %add_convert_fusion.3), channel_id=1, source_target_pairs={{0,2},{1,3},{4,0},{5,1},{8,4},{9,5},{12,8},{13,9},{14,12},{15,13},... | collective-permute-start | bytes 884744 | tf_op jit(solution)/shard_map/ppermute | solution.py:313
  78.9 24.4 %collective-permute-start.11 = (bf16[384,384]{1,0:T(8,128)(2,1)S(1)}, bf16[384,384]{1,0:T(8,128)(2,1)S(1)}, u32[]{:S(2)}, u32[]{:S(2)}) collective-permute-start(bf16[384,384]{1,0:T(8,128)(2,1)S(1)} %add_convert_fusion.5), channel_id=1, source_target_pairs={{0,4},{1,5},{4,8},{5,9},{8,12},{9,13},{12,14},{13,15},{14,10},{15,... | collective-permute-start | bytes 884744 | tf_op jit(solution)/shard_map/ppermute | solution.py:313
  79.0 19.5 %collective-permute-start.19 = (bf16[384,384]{1,0:T(8,128)(2,1)S(1)}, bf16[384,384]{1,0:T(8,128)(2,1)S(1)}, u32[]{:S(2)}, u32[]{:S(2)}) collective-permute-start(bf16[384,384]{1,0:T(8,128)(2,1)S(1)} %fusion), channel_id=1, source_target_pairs={{5,9},{13,15},{10,6},{2,0},{21,25},{29,31},{26,22},{18,16}} | collective-permute-start | bytes 884744 | tf_op jit(solution)/shard_map/ppermute | solution.py:313
  86.7 15.0 %collective-permute-start.5 = (bf16[384,384]{1,0:T(8,128)(2,1)S(1)}, bf16[384,384]{1,0:T(8,128)(2,1)S(1)}, u32[]{:S(2)}, u32[]{:S(2)}) collective-permute-start(bf16[384,384]{1,0:T(8,128)(2,1)S(1)} %add_convert_fusion.9), channel_id=1, source_target_pairs={{0,4},{1,5},{4,8},{5,9},{8,12},{9,13},{12,14},{13,15},{14,10},{15,... | collective-permute-start | bytes 884744 | tf_op jit(solution)/shard_map/ppermute | solution.py:313
  87.2 16.1 %collective-permute-start.15 = (bf16[384,384]{1,0:T(8,128)(2,1)S(1)}, bf16[384,384]{1,0:T(8,128)(2,1)S(1)}, u32[]{:S(2)}, u32[]{:S(2)}) collective-permute-start(bf16[384,384]{1,0:T(8,128)(2,1)S(1)} %add_convert_fusion.2), channel_id=1, source_target_pairs={{0,2},{1,3},{4,0},{5,1},{8,4},{9,5},{12,8},{13,9},{14,12},{15,13},... | collective-permute-start | bytes 884744 | tf_op jit(solution)/shard_map/ppermute | solution.py:313
  101.9 7.6 %collective-permute-start.21 = (bf16[384,384]{1,0:T(8,128)(2,1)S(1)}, bf16[384,384]{1,0:T(8,128)(2,1)S(1)}, u32[]{:S(2)}, u32[]{:S(2)}) collective-permute-start(bf16[384,384]{1,0:T(8,128)(2,1)S(1)} %fusion.3), channel_id=1, source_target_pairs={{0,4},{1,8},{3,10},{5,12},{6,2},{7,14},{8,3},{9,13},{10,5},{12,7},... | collective-permute-start | bytes 884744 | tf_op jit(solution)/shard_map/ppermute | solution.py:313
  103.4 17.4 %collective-permute-start.20 = (bf16[384,384]{1,0:T(8,128)(2,1)S(1)}, bf16[384,384]{1,0:T(8,128)(2,1)S(1)}, u32[]{:S(2)}, u32[]{:S(2)}) collective-permute-start(bf16[384,384]{1,0:T(8,128)(2,1)S(1)} %multiply_convert_fusion), channel_id=1, source_target_pairs={{0,2},{1,10},{2,4},{3,12},{4,6},{5,14},{6,0},{7,8},{8,5},{9,11},{1... | collective-permute-start | bytes 884744 | tf_op jit(solution)/shard_map/ppermute | solution.py:313

commit v3 on v2

--- a/solution.py
+++ b/solution.py
@@ -154,28 +154,36 @@
 
 
 def blocks_kernel(jobs, turned_ref, mine_ref, *refs):
-    width = refs[-1].shape[0]
+    tall, width = refs[-1].shape
+    strip = tall - width
     for n, out_ref in enumerate(refs[-jobs.shape[0] :]):
-
-        @pl.when(jobs[n, 0] >= 0)
-        def _(n=n, out_ref=out_ref):
-            down = pl.ds(pl.multiple_of(jobs[n, 0] * width, 128), width)
-            along = pl.ds(pl.multiple_of(jobs[n, 1] * width, 128), width)
-            block = jnp.dot(turned_ref[down, :], mine_ref[:, along], preferred_element_type=F32)
-            out_ref[...] = block.astype(out_ref.dtype)
-
-
-def moment_blocks(jobs, turned, mine, width, dtype, name, after=()):
+        parts = ((0, width, width), (width, strip, strip))
+        for k, (at, rows, unit) in enumerate(parts):
+
+            @pl.when(jobs[n, 2 * k] >= 0)
+            def _(n=n, k=k, out_ref=out_ref, at=at, rows=rows, unit=unit):
+                down = pl.ds(pl.multiple_of(jobs[n, 2 * k] * unit, 32), rows)
+                along = pl.ds(pl.multiple_of(jobs[n, 2 * k + 1] * width, 128), width)
+                block = jnp.dot(turned_ref[down, :], mine_ref[:, along], preferred_element_type=F32)
+                out_ref[at : at + rows, :] = block.astype(out_ref.dtype)
+
+        @pl.when(jobs[n, 2] < 0)
+        def _(out_ref=out_ref):
+            out_ref[width:, :] = jnp.zeros((strip, width), out_ref.dtype)
+
+
+def moment_blocks(jobs, turned, mine, width, strip, dtype, name, after=()):
     count = jobs.shape[0]
     whole = lambda shape: pl.BlockSpec(shape, lambda i, s: (0, 0))
+    piece = (width + strip, width)
     return pl.pallas_call(
         blocks_kernel,
-        out_shape=[jax.ShapeDtypeStruct((width, width), dtype)] * count,
+        out_shape=[jax.ShapeDtypeStruct(piece, dtype)] * count,
         grid_spec=pltpu.PrefetchScalarGridSpec(
             num_scalar_prefetch=1,
             grid=(1,),
             in_specs=[whole(turned.shape), whole(mine.shape)] + [pl.BlockSpec(memory_space=pl.ANY)] * len(after),
-            out_specs=[whole((width, width))] * count,
+            out_specs=[whole(piece)] * count,
         ),
         cost_estimate=pl.CostEstimate(
             flops=2 * count * mine.shape[0] * width * width,
@@ -187,62 +195,47 @@
     )(jobs, turned, mine, *after)
 
 
+STRIP = 96
+
+
 def is_diagonal(b, e):
     return b // 4 == e
 
 
-EXTRA = ((0, 0), (3, 0), (4, 1), (7, 1))
-
-
 def owned_columns(b, e):
     shift = 0 if is_diagonal(b, e) or e == 1 else 1
-    return [(b + shift) % 4, (b + shift + 1) % 4, (b + 2) % 4]
-
-
-def extra_role(p, e, d):
-    for b, core in EXTRA:
-        q = SNAKE.index(b)
-        if core == e and (q - p) % 8 == d:
-            return b, 1
-        if core == e and d >= 2 and (p - q) % 8 == d - 1:
-            return b, -1
-    return None
-
-
-FIRST = ((0, 4), (0, 5), (1, 4), (1, 3), (2, 4))
-SECOND = ((0, 3), (0, 6), (1, 5), (1, 2), (2, 3))
-REST = ((0, 2), (0, 7), (1, 6), (1, 1), (2, 2), (0, 1), (1, 7), (2, 1), (0, 0), (1, 0), (2, 0))
-
-
-def job_table(which):
-    table = np.full((8, 2, len(which), 2), -1, np.int32)
+    return [(b + shift) % 4, (b + shift + 1) % 4]
+
+
+def leads(b):
+    return b % 4 < 2
+
+
+ROUNDS = (
+    ((0, 4), (1, 4), (1, 3), (0, 5)),
+    ((0, 3), (1, 5), (1, 2), (0, 6)),
+    ((0, 2), (1, 6), (1, 1), (0, 7)),
+    ((0, 1), (1, 7), (0, 0), (1, 0)),
+)
+
+
+def job_table(which, width):
+    table = np.full((8, 2, len(which), 4), -1, np.int32)
     for p, b in enumerate(SNAKE):
         for e in range(2):
             for n, (x, t) in enumerate(which):
-                if x < 2:
-                    q = SNAKE[(p + t) % 8]
-                else:
-                    role = extra_role(p, e, t)
-                    if role is None:
-                        continue
-                    q = role[0]
-                table[b, e, n] = (q % 4 + (0 if q // 4 == e else 4), owned_columns(q, e)[x])
+                q = SNAKE[(p + t) % 8]
+                table[b, e, n, :2] = (q % 4 + (0 if q // 4 == e else 4), owned_columns(q, e)[x])
+                if is_diagonal(q, e):
+                    lead, other = (q % 4, (q + 2) % 4) if leads(q) else ((q + 2) % 4, q % 4)
+                    first = lead * width + (0 if leads(q) else width // 2) + x * STRIP
+                    table[b, e, n, 2:] = (first // STRIP, other)
     return table
 
 
-def ring_perm(distance, direction):
+def ring_perm(direction):
     pairs = [(SNAKE[p], SNAKE[(p + direction) % 8]) for p in range(8)]
     return [(a * 2 + e, b * 2 + e) for a, b in pairs for e in range(2)]
-
-
-def extra_perm(d):
-    pairs = []
-    for p in range(8):
-        for e in range(2):
-            role = extra_role(p, e, d)
-            if role is not None:
-                pairs.append((SNAKE[p] * 2 + e, SNAKE[(p + role[1]) % 8] * 2 + e))
-    return pairs
 
 
 def mirror_perms():
@@ -252,8 +245,7 @@
             here = b * 2 + e
             if is_diagonal(b, e):
                 one.append((here, (b // 4 * 4 + (b + 1) % 4) * 2 + e))
-                if (b, e) in EXTRA:
-                    other.append((here, (b // 4 * 4 + (b + 2) % 4) * 2 + e))
+                other.append((here, (b // 4 * 4 + (b + 2) % 4) * 2 + e))
             elif e == 1:
                 other.append((here, (4 + b) * 2))
                 one.append((here, (4 + (b + 1) % 4) * 2))
@@ -264,39 +256,47 @@
 
 
 def place_table():
-    table = np.zeros((8, 2, 6), np.int32)
+    table = np.zeros((8, 2, 5), np.int32)
     for b in range(8):
         for e in range(2):
             own = owned_columns(b, e)
             if is_diagonal(b, e):
-                table[b, e] = (own[0], own[1], (b + 3) % 4, (b + 2) % 4, (b, e) in EXTRA, 1)
+                table[b, e] = (own[0], own[1], (b + 3) % 4, (b + 2) % 4, 1 if leads(b) else 2)
             elif e == 1:
-                table[b, e] = (own[0], own[1], (b + 2) % 4, (b + 3) % 4, 0, 0)
+                table[b, e] = (own[0], own[1], (b + 2) % 4, (b + 3) % 4, 0)
             else:
-                table[b, e] = (own[0], own[1], (b + 3) % 4, b % 4, 0, 0)
+                table[b, e] = (own[0], own[1], (b + 3) % 4, b % 4, 0)
     return table
 
 
-def finish_kernel(scale, place, own0, own1, own2, right0, left0, right1, left1, right2, left2, one, other, out_ref):
+def finish_kernel(scale, place, own0, own1, right0, left0, right1, left1, one, other, out_ref):
     width = one.shape[0]
 
     def put(n, value):
         out_ref[:, pl.ds(pl.multiple_of(place[n] * width, 128), width)] = value
 
-    def owned(own, right, left):
-        return (own[...] + right[...].astype(F32) + left[...].astype(F32)) * scale
-
-    put(0, owned(own0, right0, left0))
-    put(1, owned(own1, right1, left1))
+    def owned(own, right, left, rows):
+        return (own[rows, :] + right[rows, :].astype(F32) + left[rows, :].astype(F32)) * scale
+
+    put(0, owned(own0, right0, left0, slice(0, width)))
+    put(1, owned(own1, right1, left1, slice(0, width)))
     put(2, one[...].astype(F32).T)
 
-    @pl.when(place[4] == 1)
-    def _():
-        put(3, owned(own2, right2, left2))
+    def share():
+        rows = slice(width, width + STRIP)
+        return [owned(own0, right0, left0, rows), owned(own1, right1, left1, rows)]
 
     @pl.when(place[4] == 0)
     def _():
         put(3, other[...].astype(F32).T)
+
+    @pl.when(place[4] == 1)
+    def _():
+        put(3, jnp.concatenate(share() + [other[: width // 2, :].astype(F32)], axis=0))
+
+    @pl.when(place[4] == 2)
+    def _():
+        put(3, jnp.concatenate([other[: width // 2, :].astype(F32)] + share(), axis=0).T)
 
 
 def symmetric_moment(mine, turned, total_tokens):
@@ -305,46 +305,48 @@
     dp, e = lax.axis_index("dp"), lax.axis_index("expert")
     blocks = {}
 
-    def compute(which, dtype, name, after=()):
-        jobs = jnp.asarray(job_table(which))[dp, e]
-        blocks.update(zip(which, moment_blocks(jobs, turned, mine, width, dtype, name, after)))
-
-    def send(value, perm):
-        return lax.ppermute(value, both, perm)
-
-    def join(value, key):
-        return (value.astype(F32) + blocks[key]).astype(BF16)
-
-    compute(FIRST, BF16, "blocks_first")
-    right = [send(blocks[0, 4], ring_perm(4, 1)), send(blocks[1, 3], ring_perm(3, 1))]
-    left = [send(blocks[0, 5], ring_perm(3, -1)), send(blocks[1, 4], ring_perm(4, -1))]
-    extra = send(blocks[2, 4], extra_perm(4))
-
-    compute(SECOND, F32, "blocks_second")
-    right = [send(join(right[0], (0, 3)), ring_perm(3, 1)), send(join(right[1], (1, 2)), ring_perm(2, 1))]
-    left = [send(join(left[0], (0, 6)), ring_perm(2, -1)), send(join(left[1], (1, 5)), ring_perm(3, -1))]
-    extra = send(join(extra, (2, 3)), extra_perm(3))
-
-    compute(REST, F32, "blocks_rest")
-    right = [send(join(right[0], (0, 2)), ring_perm(2, 1)), send(join(right[1], (1, 1)), ring_perm(1, 1))]
-    left = [send(join(left[0], (0, 7)), ring_perm(1, -1)), send(join(left[1], (1, 6)), ring_perm(2, -1))]
-    left2 = send(join(extra, (2, 2)), extra_perm(2))
-
-    right[0] = send(join(right[0], (0, 1)), ring_perm(1, 1))
-    left[1] = send(join(left[1], (1, 7)), ring_perm(1, -1))
-    right2 = send(join(left2, (2, 1)), extra_perm(1))
+    def compute(n, dtype, after=()):
+        which = ROUNDS[n]
+        jobs = jnp.asarray(job_table(which, width))[dp, e]
+        blocks.update(zip(which, moment_blocks(jobs, turned, mine, width, STRIP, dtype, f"blocks{n}", after)))
+
+    def hop(value, key):
+        return lax.ppermute(value, both, ring_perm(1 if key[1] <= (4 if key[0] == 0 else 3) else -1))
+
+    compute(0, BF16)
+    moving = {key: blocks[key] for key in ROUNDS[0]}
+    arrived = {}
+    for n in range(4):
+        landed = {}
+        for key in ROUNDS[n]:
+            if key in moving:
+                landed[key] = hop(moving[key], key)
+        if n < 3:
+            compute(n + 1, F32, after=(landed[ROUNDS[n][0]],))
+        moving = {}
+        for (x, t), value in landed.items():
+            rightwards = t <= (4 if x == 0 else 3)
+            t = t - 1 if rightwards else (t + 1) % 8
+            if t == 0:
+                arrived[x, rightwards] = value
+            else:
+                moving[x, t] = (value.astype(F32) + blocks[x, t]).astype(BF16)
 
     scale = 1.0 / total_tokens
     place = jnp.asarray(place_table())[dp, e]
 
-    def done(x, r, l):
-        return blocks[x, 0] + r.astype(F32) + l.astype(F32)
+    def done(x, rows):
+        pieces = (blocks[x, 0], arrived[x, True], arrived[x, False])
+        return sum(piece[rows].astype(F32) for piece in pieces) * scale
 
     perm_one, perm_other = mirror_perms()
-    other = jnp.where(place[5] == 1, done(2, right2, left2), done(0, right[0], left[0]))
-    other = send((other * scale).astype(BF16), perm_other)
-    one = send((done(1, right[1], left[1]) * scale).astype(BF16), perm_one)
-
+    own, share = slice(0, width), slice(width, width + STRIP)
+    third = jnp.concatenate([done(0, share), done(1, share), jnp.zeros((width // 2, width), F32)], axis=0)
+    other = jnp.where(place[4] > 0, third, done(0, own))
+    one = lax.ppermute(done(1, own).astype(BF16), both, perm_one)
+    other = lax.ppermute(other.astype(BF16), both, perm_other)
+
+    piece = pl.BlockSpec((width + STRIP, width), lambda i, s: (0, 0))
     block = pl.BlockSpec((width, width), lambda i, s: (0, 0))
     return pl.pallas_call(
         functools.partial(finish_kernel, scale),
@@ -352,20 +354,19 @@
         grid_spec=pltpu.PrefetchScalarGridSpec(
             num_scalar_prefetch=1,
             grid=(1,),
-            in_specs=[block] * 11,
+            in_specs=[piece] * 6 + [block] * 2,
             out_specs=pl.BlockSpec((width, 4 * width), lambda i, s: (0, 0)),
         ),
         compiler_params=pltpu.CompilerParams(vmem_limit_bytes=32 << 20),
         name="finish",
     )(
         place,
-        *[blocks[x, 0] for x in range(3)],
-        right[0],
-        left[0],
-        right[1],
-        left[1],
-        right2,
-        left2,
+        blocks[0, 0],
+        blocks[1, 0],
+        arrived[0, True],
+        arrived[0, False],
+        arrived[1, True],
+        arrived[1, False],
         one,
         other,
     )

time: 124 us -> 118 us (0.952)
  starting transfers between devices: 36.1 us -> 19 us
  waiting for transfers between devices: 37.4 us -> 46.1 us
  Pallas kernels: 36.6 us -> 38.4 us
    ppermute x20 -> x16, starting transfers between devices: 35.5 us -> 18.4 us  [the longest x14 15.8 us: hop(): lax.ppermute(value, both, ring_perm(1 if key[1] <= (4 if key[0] == 0 else...]
    ppermute x20 -> x16, waiting for transfers between devices: 37.4 us -> 46.1 us  [the longest x14 32.9 us: hop(): lax.ppermute(value, both, ring_perm(1 if key[1] <= (4 if key[0] == 0 else...]
    pallas_call x3 -> x4, Pallas kernels: 10.5 us -> 12.4 us  [moment_blocks(): pl.pallas_call(blocks_kernel, out_shape=[jax.ShapeDtypeStruct(piece, dtyp...]
    squeeze x5 -> x4, local copies, waits for them, and re-layouts: 1.66 us -> 2.73 us  [compute(): jobs = jnp.asarray(job_table(which, width))[dp, e]]
  transfers between devices with their start and end apart: 22 -> 18, of which waited for: 10 -> 10; matrix products, arithmetic and copies ran while one was open for 4% -> 5% of each run, Pallas kernels for 16% -> 18%
where the time goes in v3:
time: 118 us
  waiting for transfers between devices  46.1 us (39%)
  Pallas kernels  38.4 us (33%)
  starting transfers between devices  19 us (16%)
  local copies, waits for them, and re-layouts  10.8 us (9%)
  other arithmetic  2.34 us (2%)
    ppermute x14, waiting for transfers between devices, hop(): lax.ppermute(value, both, ring_perm(1 if key[1] <= (4 if key[0] == 0 else...  32.9 us
    ppermute x14, starting transfers between devices, hop(): lax.ppermute(value, both, ring_perm(1 if key[1] <= (4 if key[0] == 0 else...  15.8 us
    pallas_call x2, Pallas kernels, pick_half(): pl.pallas_call(pick_kernel, out_shape=jax.ShapeDtypeStruct((tokens, width...  14.8 us
    pallas_call x4, Pallas kernels, moment_blocks(): pl.pallas_call(blocks_kernel, out_shape=[jax.ShapeDtypeStruct(piece, dtyp...  12.4 us
    ppermute x1, waiting for transfers between devices, symmetric_moment(): one = lax.ppermute(done(1, own).astype(BF16), both, perm_one)  9.06 us
    pallas_call x2, Pallas kernels, merge(): pl.pallas_call(functools.partial(merge_kernel, first), out_shape=out_shap...  6.88 us
    unnamed x14, local copies, waits for them, and re-layouts  6.08 us
    ppermute x1, waiting for transfers between devices, symmetric_moment(): other = lax.ppermute(other.astype(BF16), both, perm_other)  4.18 us
  transfers between devices with their start and end apart: 18, of which 10 were waited for; matrix products, arithmetic and copies ran while one was open for 5% of the time, Pallas kernels for 18%

profile of v3, /device:TPU:0, one launch (start us, length us, event | category | flops | bytes accessed | tf_op | source)
XLA Modules:
  0.0 117.6 jit_solution(142318834397236007)
XLA Ops:
  0.0 0.9 copy.10.ids_ref
  0.9 0.9 copy.11.gates_ref
  1.8 0.6 pad_add_fusion.where_
  2.4 1.8 %plan.1 = (bf16[1536,512]{1,0:T(8,128)(2,1)S(1)}, s32[8,128]{1,0:T(8,128)S(1)}, f32[768,128]{1,0:T(8,128)S(1)}) custom-call(s32[1]{0:T(128)} %bitcast.2.member, s32[768,2]{1,0:T(8,128)S(1)} %copy.10.ids_ref, f32[768,2]{1,0:T(8,128)S(1)} %copy.11.gates_ref), custom_call_target="tpu_custom_call" | custom-call | tf_op jit(solution)/shard_map/plan/pallas_call | solution.py:63
  4.2 0.7 copy-done.2
  4.9 1.2 %copy-done.4 = bf16[1536,512]{1,0:T(8,128)(2,1)} copy-done((bf16[1536,512]{1,0:T(8,128)(2,1)}, bf16[1536,512]{1,0:T(8,128)(2,1)S(1)}, u32[]{:S(2)}) %copy-start.4) | copy-done | bytes 1572888
  6.2 0.6 copy-done.5
  6.7 7.3 %pick.2.ours_ref = bf16[768,1536]{1,0:T(8,128)(2,1)} custom-call(s32[2]{0:T(128)} %pad_add_fusion.where_, s32[8,128]{1,0:T(8,128)} %copy-done.5, bf16[1536,512]{1,0:T(8,128)(2,1)} %copy-done.4, f32[768,128]{1,0:T(8,128)} %copy-done.2, bf16[1536,3072]{1,0:T(8,128)(2,1)} %rows_ref.3), custom_call_target="tpu_custom_call" | custom-call | flops 2415919104 | bytes 7077888 | tf_op jit(solution)/shard_map/pick/pallas_call | solution.py:98
  14.1 0.4 collective-permute-start.1
  14.5 0.6 pad_add_fusion.1.where_
  15.0 7.5 %pick.3.ours_ref = bf16[768,1536]{1,0:T(8,128)(2,1)} custom-call(s32[2]{0:T(128)} %pad_add_fusion.1.where_, s32[8,128]{1,0:T(8,128)} %copy-done.5, bf16[1536,512]{1,0:T(8,128)(2,1)} %copy-done.4, f32[768,128]{1,0:T(8,128)} %copy-done.2, bf16[1536,3072]{1,0:T(8,128)(2,1)} %rows_ref.3), custom_call_target="tpu_custom_call" | custom-call | flops 2415919104 | bytes 7077888 | tf_op jit(solution)/shard_map/pick/pallas_call | solution.py:98
  22.5 0.2 collective-permute-start
  22.7 0.7 dynamic-slice_bitcast_fusion.2.jobs
  23.4 1.8 %copy-done.1 = bf16[768,1536]{1,0:T(8,128)(2,1)S(1)} copy-done((bf16[768,1536]{1,0:T(8,128)(2,1)S(1)}, bf16[768,1536]{1,0:T(8,128)(2,1)}, u32[]{:S(2)}) %copy-start.1) | copy-done | bytes 2359320
  25.2 4.2 %merge_first.1 = (bf16[768,1536]{1,0:T(8,128)(2,1)S(1)}, bf16[3072,768]{1,0:T(8,128)(2,1)S(1)}) custom-call(f32[768,128]{1,0:T(8,128)S(1)} %copy-done.3, bf16[768,1536]{1,0:T(8,128)(2,1)S(1)} %copy-done.1, bf16[768,1536]{1,0:T(8,128)(2,1)} %collective-permute-done.1.theirs_ref), custom_call_target="tpu_custom_call" | custom-call | flops 4718592 | bytes 7077888 | tf_op jit(solution)/shard_map/merge_first/pallas_call | solution.py:143
  29.4 2.7 %merge_second.1.turned_ref = bf16[3072,768]{1,0:T(8,128)(2,1)S(1)} custom-call(f32[768,128]{1,0:T(8,128)S(1)} %copy-done.3, bf16[768,1536]{1,0:T(8,128)(2,1)S(1)} %copy-done, bf16[768,1536]{1,0:T(8,128)(2,1)S(1)} %collective-permute-done.theirs_ref, bf16[3072,768]{1,0:T(8,128)(2,1)S(1)} %get-tuple-element.29.refs_0_), custom_call_target="tpu_custom_call", output_to_operand_aliasing={{}: (3, {})} | custom-call | flops 4718592 | bytes 7077888 | tf_op jit(solution)/shard_map/merge_second/pallas_call | solution.py:143
  32.1 2.6 %blocks0.1 = (bf16[480,384]{1,0:T(8,128)(2,1)S(1)}, bf16[480,384]{1,0:T(8,128)(2,1)S(1)}, bf16[480,384]{1,0:T(8,128)(2,1)S(1)}, bf16[480,384]{1,0:T(8,128)(2,1)S(1)}) custom-call(s32[4,4]{1,0:T(4,128)S(1)} %dynamic-slice_bitcast_fusion.2.jobs, bf16[3072,768]{1,0:T(8,128)(2,1)S(1)} %merge_second.1.turned_ref, bf16[768,1536]{1,0:T(8,128)(2,1)S(1)} %get-tuple-element.30.mine_ref), custom_call_target="tpu_custom_call" | custom-call | flops 905969664 | bytes 9437184 | tf_op jit(solution)/shard_map/blocks0/pallas_call | solution.py:179
  34.6 3.3 %collective-permute-start.2 = (bf16[480,384]{1,0:T(8,128)(2,1)S(1)}, bf16[480,384]{1,0:T(8,128)(2,1)S(1)}, u32[]{:S(2)}, u32[]{:S(2)}) collective-permute-start(bf16[480,384]{1,0:T(8,128)(2,1)S(1)} %get-tuple-element.31), channel_id=1, source_target_pairs={{0,4},{1,5},{4,8},{5,9},{8,12},{9,13},{12,14},{13,15},{14,10},{15,... | collective-permute-start | bytes 1105928 | tf_op jit(solution)/shard_map/ppermute | solution.py:314
  38.0 0.7 dynamic-slice_bitcast_fusion.1.jobs
  38.7 0.7 dynamic-slice_bitcast_fusion.jobs
  39.4 0.7 dynamic-slice_bitcast_fusion.3.jobs
  40.0 1.7 %collective-permute-start.12 = (bf16[480,384]{1,0:T(8,128)(2,1)S(1)}, bf16[480,384]{1,0:T(8,128)(2,1)S(1)}, u32[]{:S(2)}, u32[]{:S(2)}) collective-permute-start(bf16[480,384]{1,0:T(8,128)(2,1)S(1)} %get-tuple-element.43), channel_id=1, source_target_pairs={{0,2},{1,3},{4,0},{5,1},{8,4},{9,5},{12,8},{13,9},{14,12},{15,13},... | collective-permute-start | bytes 1105928 | tf_op jit(solution)/shard_map/ppermute | solution.py:314
  41.7 0.4 collective-permute-start.9
  42.1 4.8 %collective-permute-done.2.refs_0_ = bf16[480,384]{1,0:T(8,128)(2,1)S(1)} collective-permute-done((bf16[480,384]{1,0:T(8,128)(2,1)S(1)}, bf16[480,384]{1,0:T(8,128)(2,1)S(1)}, u32[]{:S(2)}, u32[]{:S(2)}) %collective-permute-start.2) | collective-permute-done | bytes 368672 | tf_op jit(solution)/shard_map/ppermute | solution.py:314
  46.9 2.8 %blocks1.1 = (f32[480,384]{1,0:T(8,128)S(1)}, f32[480,384]{1,0:T(8,128)S(1)}, f32[480,384]{1,0:T(8,128)S(1)}, f32[480,384]{1,0:T(8,128)S(1)}) custom-call(s32[4,4]{1,0:T(4,128)S(1)} %dynamic-slice_bitcast_fusion.1.jobs, bf16[3072,768]{1,0:T(8,128)(2,1)S(1)} %merge_second.1.turned_ref, bf16[768,1536]{1,0:T(8,128)(2,1)S(1)} %get-tuple-element.30.mine_ref, ...), custom_call_target="tpu_custom_call" | custom-call | flops 905969664 | bytes 9437184 | tf_op jit(solution)/shard_map/blocks1/pallas_call | solution.py:179
  49.7 0.1 add_convert_fusion.6
  49.8 2.2 %collective-permute-start.7 = (bf16[480,384]{1,0:T(8,128)(2,1)S(1)}, bf16[480,384]{1,0:T(8,128)(2,1)S(1)}, u32[]{:S(2)}, u32[]{:S(2)}) collective-permute-start(bf16[480,384]{1,0:T(8,128)(2,1)S(1)} %add_convert_fusion.6), channel_id=1, source_target_pairs={{0,2},{1,3},{4,0},{5,1},{8,4},{9,5},{12,8},{13,9},{14,12},{15,13},... | collective-permute-start | bytes 1105928 | tf_op jit(solution)/shard_map/ppermute | solution.py:314
  52.0 0.1 add_convert_fusion.9
  52.1 0.6 collective-permute-start.3
  52.7 4.6 %collective-permute-done.12 = bf16[480,384]{1,0:T(8,128)(2,1)S(1)} collective-permute-done((bf16[480,384]{1,0:T(8,128)(2,1)S(1)}, bf16[480,384]{1,0:T(8,128)(2,1)S(1)}, u32[]{:S(2)}, u32[]{:S(2)}) %collective-permute-start.12) | collective-permute-done | bytes 368672 | tf_op jit(solution)/shard_map/ppermute | solution.py:314
  57.4 0.1 add_convert_fusion.2
  57.5 0.1 add_convert_fusion.4
  57.6 2.2 %collective-permute-start.10 = (bf16[480,384]{1,0:T(8,128)(2,1)S(1)}, bf16[480,384]{1,0:T(8,128)(2,1)S(1)}, u32[]{:S(2)}, u32[]{:S(2)}) collective-permute-start(bf16[480,384]{1,0:T(8,128)(2,1)S(1)} %add_convert_fusion.4), channel_id=1, source_target_pairs={{0,4},{1,5},{4,8},{5,9},{8,12},{9,13},{12,14},{13,15},{14,10},{15,... | collective-permute-start | bytes 1105928 | tf_op jit(solution)/shard_map/ppermute | solution.py:314
  59.8 3.9 %collective-permute-done.3.refs_0_ = bf16[480,384]{1,0:T(8,128)(2,1)S(1)} collective-permute-done((bf16[480,384]{1,0:T(8,128)(2,1)S(1)}, bf16[480,384]{1,0:T(8,128)(2,1)S(1)}, u32[]{:S(2)}, u32[]{:S(2)}) %collective-permute-start.3) | collective-permute-done | bytes 368672 | tf_op jit(solution)/shard_map/ppermute | solution.py:314
  63.7 3.5 %blocks2.1 = (f32[480,384]{1,0:T(8,128)S(1)}, f32[480,384]{1,0:T(8,128)S(1)}, f32[480,384]{1,0:T(8,128)S(1)}, f32[480,384]{1,0:T(8,128)S(1)}) custom-call(s32[4,4]{1,0:T(4,128)S(1)} %dynamic-slice_bitcast_fusion.jobs, bf16[3072,768]{1,0:T(8,128)(2,1)S(1)} %merge_second.1.turned_ref, bf16[768,1536]{1,0:T(8,128)(2,1)S(1)} %get-tuple-element.30.mine_ref, ...), custom_call_target="tpu_custom_call" | custom-call | flops 905969664 | bytes 9437184 | tf_op jit(solution)/shard_map/blocks2/pallas_call | solution.py:179
  67.2 0.1 add_convert_fusion.5
  67.3 2.3 %collective-permute-start.8 = (bf16[480,384]{1,0:T(8,128)(2,1)S(1)}, bf16[480,384]{1,0:T(8,128)(2,1)S(1)}, u32[]{:S(2)}, u32[]{:S(2)}) collective-permute-start(bf16[480,384]{1,0:T(8,128)(2,1)S(1)} %add_convert_fusion.5), channel_id=1, source_target_pairs={{0,2},{1,3},{4,0},{5,1},{8,4},{9,5},{12,8},{13,9},{14,12},{15,13},... | collective-permute-start | bytes 1105928 | tf_op jit(solution)/shard_map/ppermute | solution.py:314
  69.6 0.1 add_convert_fusion.8
  69.7 0.1 collective-permute-start.4
  69.8 3.4 %collective-permute-done.13 = bf16[480,384]{1,0:T(8,128)(2,1)S(1)} collective-permute-done((bf16[480,384]{1,0:T(8,128)(2,1)S(1)}, bf16[480,384]{1,0:T(8,128)(2,1)S(1)}, u32[]{:S(2)}, u32[]{:S(2)}) %collective-permute-start.13) | collective-permute-done | bytes 368672 | tf_op jit(solution)/shard_map/ppermute | solution.py:314
  73.2 0.1 add_convert_fusion.1
  73.2 0.1 collective-permute-start.14
  73.3 0.1 add_convert_fusion.3
  73.4 2.2 %collective-permute-start.11 = (bf16[480,384]{1,0:T(8,128)(2,1)S(1)}, bf16[480,384]{1,0:T(8,128)(2,1)S(1)}, u32[]{:S(2)}, u32[]{:S(2)}) collective-permute-start(bf16[480,384]{1,0:T(8,128)(2,1)S(1)} %add_convert_fusion.3), channel_id=1, source_target_pairs={{0,4},{1,5},{4,8},{5,9},{8,12},{9,13},{12,14},{13,15},{14,10},{15,... | collective-permute-start | bytes 1105928 | tf_op jit(solution)/shard_map/ppermute | solution.py:314
  75.6 5.7 %collective-permute-done.4.refs_0_ = bf16[480,384]{1,0:T(8,128)(2,1)S(1)} collective-permute-done((bf16[480,384]{1,0:T(8,128)(2,1)S(1)}, bf16[480,384]{1,0:T(8,128)(2,1)S(1)}, u32[]{:S(2)}, u32[]{:S(2)}) %collective-permute-start.4) | collective-permute-done | bytes 368672 | tf_op jit(solution)/shard_map/ppermute | solution.py:314
  81.3 3.5 %blocks3.1 = (f32[480,384]{1,0:T(8,128)S(1)}, f32[480,384]{1,0:T(8,128)S(1)}, f32[480,384]{1,0:T(8,128)S(1)}, f32[480,384]{1,0:T(8,128)S(1)}) custom-call(s32[4,4]{1,0:T(4,128)S(1)} %dynamic-slice_bitcast_fusion.3.jobs, bf16[3072,768]{1,0:T(8,128)(2,1)S(1)} %merge_second.1.turned_ref, bf16[768,1536]{1,0:T(8,128)(2,1)S(1)} %get-tuple-element.30.mine_ref, ...), custom_call_target="tpu_custom_call" | custom-call | flops 905969664 | bytes 9437184 | tf_op jit(solution)/shard_map/blocks3/pallas_call | solution.py:179
  84.8 0.1 add_convert_fusion.7
  84.9 0.1 collective-permute-start.5
  85.0 3.2 %collective-permute-done.14 = bf16[480,384]{1,0:T(8,128)(2,1)S(1)} collective-permute-done((bf16[480,384]{1,0:T(8,128)(2,1)S(1)}, bf16[480,384]{1,0:T(8,128)(2,1)S(1)}, u32[]{:S(2)}, u32[]{:S(2)}) %collective-permute-start.14) | collective-permute-done | bytes 368672 | tf_op jit(solution)/shard_map/ppermute | solution.py:314
  88.2 0.1 add_convert_fusion
  88.3 0.6 collective-permute-start.15
  88.9 0.7 constant_dynamic-slice_fusion
  89.6 0.6 slice.43
  90.8 0.1 pad.2.clone
  90.9 3.8 %collective-permute-done.5.right0 = bf16[480,384]{1,0:T(8,128)(2,1)S(1)} collective-permute-done((bf16[480,384]{1,0:T(8,128)(2,1)S(1)}, bf16[480,384]{1,0:T(8,128)(2,1)S(1)}, u32[]{:S(2)}, u32[]{:S(2)}) %collective-permute-start.5) | collective-permute-done | bytes 368672 | tf_op jit(solution)/shard_map/ppermute | solution.py:314
  94.8 3.4 %collective-permute-done.15.left1 = bf16[480,384]{1,0:T(8,128)(2,1)S(1)} collective-permute-done((bf16[480,384]{1,0:T(8,128)(2,1)S(1)}, bf16[480,384]{1,0:T(8,128)(2,1)S(1)}, u32[]{:S(2)}, u32[]{:S(2)}) %collective-permute-start.15) | collective-permute-done | bytes 368672 | tf_op jit(solution)/shard_map/ppermute | solution.py:314
  98.2 0.2 fusion
  98.4 0.1 collective-permute-start.17
  98.5 0.1 multiply_convert_fusion
  98.6 2.6 %collective-permute-start.16 = (bf16[384,384]{1,0:T(8,128)(2,1)S(1)}, bf16[384,384]{1,0:T(8,128)(2,1)S(1)}, u32[]{:S(2)}, u32[]{:S(2)}) collective-permute-start(bf16[384,384]{1,0:T(8,128)(2,1)S(1)} %multiply_convert_fusion), channel_id=1, source_target_pairs={{0,2},{1,10},{2,4},{3,12},{4,6},{5,14},{6,0},{7,8},{8,5},{9,11},{1... | collective-permute-start | bytes 884744 | tf_op jit(solution)/shard_map/ppermute | solution.py:346
  101.2 0.7 fusion.1.place
  101.9 4.2 %collective-permute-done.17.other = bf16[384,384]{1,0:T(8,128)(2,1)S(1)} collective-permute-done((bf16[384,384]{1,0:T(8,128)(2,1)S(1)}, bf16[384,384]{1,0:T(8,128)(2,1)S(1)}, u32[]{:S(2)}, u32[]{:S(2)}) %collective-permute-start.17) | collective-permute-done | bytes 294944 | tf_op jit(solution)/shard_map/ppermute | solution.py:347
  106.1 9.1 %collective-permute-done.16.one = bf16[384,384]{1,0:T(8,128)(2,1)S(1)} collective-permute-done((bf16[384,384]{1,0:T(8,128)(2,1)S(1)}, bf16[384,384]{1,0:T(8,128)(2,1)S(1)}, u32[]{:S(2)}, u32[]{:S(2)}) %collective-permute-start.16) | collective-permute-done | bytes 294944 | tf_op jit(solution)/shard_map/ppermute | solution.py:346
  115.1 2.5 %finish.1 = f32[384,1536]{1,0:T(8,128)} custom-call(s32[5]{0:T(128)S(1)} %fusion.1.place, f32[480,384]{1,0:T(8,128)S(1)} %get-tuple-element.34.own0, f32[480,384]{1,0:T(8,128)S(1)} %get-tuple-element.35.own1, bf16[480,384]{1,0:T(8,128)(2,1)S(1)} %collective-permute-done.5.right0, bf16[480,384]{1,0:T(8,128)(2,1)S(1)} %collective-permute-done.8.left0, ...), custom_call_target="tpu_custom_call" | custom-call | tf_op jit(solution)/shard_map/finish/pallas_call | solution.py:351
  (21 shorter events, 0.2 us)
Async XLA Ops:
  4.2 0.7 copy-start.2
  4.9 1.2 %copy-start.4 = (bf16[1536,512]{1,0:T(8,128)(2,1)}, bf16[1536,512]{1,0:T(8,128)(2,1)S(1)}, u32[]{:S(2)}) copy-start(bf16[1536,512]{1,0:T(8,128)(2,1)S(1)} %get-tuple-element.28.pick_ref) | copy-start | bytes 4718596
  6.1 0.6 copy-start.5
  14.1 9.3 %collective-permute-start.1 = (bf16[768,1536]{1,0:T(8,128)(2,1)}, bf16[768,1536]{1,0:T(8,128)(2,1)}, u32[]{:S(2)}, u32[]{:S(2)}) collective-permute-start(bf16[768,1536]{1,0:T(8,128)(2,1)} %pick.2.ours_ref), channel_id=1, source_target_pairs={{0,1},{1,0},{2,3},{3,2},{4,5},{5,4},{6,7},{7,6},{8,9},{9,8},{10,11... | collective-permute-start | bytes 7077896 | tf_op jit(solution)/shard_map/ppermute | solution.py:387
  15.0 8.3 %copy-start.3 = (f32[768,128]{1,0:T(8,128)S(1)}, f32[768,128]{1,0:T(8,128)}, u32[]{:S(2)}) copy-start(f32[768,128]{1,0:T(8,128)} %copy-done.2) | copy-start | bytes 1179652
  22.5 6.9 %collective-permute-start = (bf16[768,1536]{1,0:T(8,128)(2,1)}, bf16[768,1536]{1,0:T(8,128)(2,1)S(1)}, u32[]{:S(2)}, u32[]{:S(2)}) collective-permute-start(bf16[768,1536]{1,0:T(8,128)(2,1)} %pick.3.ours_ref), channel_id=1, source_target_pairs={{0,1},{1,0},{2,3},{3,2},{4,5},{5,4},{6,7},{7,6},{8,9},{9,8},{10,11... | collective-permute-start | bytes 7077896 | tf_op jit(solution)/shard_map/ppermute | solution.py:387
  23.3 6.0 %copy-start = (bf16[768,1536]{1,0:T(8,128)(2,1)S(1)}, bf16[768,1536]{1,0:T(8,128)(2,1)}, u32[]{:S(2)}) copy-start(bf16[768,1536]{1,0:T(8,128)(2,1)} %pick.2.ours_ref) | copy-start | bytes 7077892
  23.4 1.8 %copy-start.1 = (bf16[768,1536]{1,0:T(8,128)(2,1)S(1)}, bf16[768,1536]{1,0:T(8,128)(2,1)}, u32[]{:S(2)}) copy-start(bf16[768,1536]{1,0:T(8,128)(2,1)} %pick.3.ours_ref) | copy-start | bytes 7077892
  34.6 12.2 %collective-permute-start.2 = (bf16[480,384]{1,0:T(8,128)(2,1)S(1)}, bf16[480,384]{1,0:T(8,128)(2,1)S(1)}, u32[]{:S(2)}, u32[]{:S(2)}) collective-permute-start(bf16[480,384]{1,0:T(8,128)(2,1)S(1)} %get-tuple-element.31), channel_id=1, source_target_pairs={{0,4},{1,5},{4,8},{5,9},{8,12},{9,13},{12,14},{13,15},{14,10},{15,... | collective-permute-start | bytes 1105928 | tf_op jit(solution)/shard_map/ppermute | solution.py:314
  38.0 11.7 %collective-permute-start.6 = (bf16[480,384]{1,0:T(8,128)(2,1)S(1)}, bf16[480,384]{1,0:T(8,128)(2,1)S(1)}, u32[]{:S(2)}, u32[]{:S(2)}) collective-permute-start(bf16[480,384]{1,0:T(8,128)(2,1)S(1)} %get-tuple-element.37), channel_id=1, source_target_pairs={{0,2},{1,3},{4,0},{5,1},{8,4},{9,5},{12,8},{13,9},{14,12},{15,13},... | collective-permute-start | bytes 1105928 | tf_op jit(solution)/shard_map/ppermute | solution.py:314
  40.0 17.3 %collective-permute-start.12 = (bf16[480,384]{1,0:T(8,128)(2,1)S(1)}, bf16[480,384]{1,0:T(8,128)(2,1)S(1)}, u32[]{:S(2)}, u32[]{:S(2)}) collective-permute-start(bf16[480,384]{1,0:T(8,128)(2,1)S(1)} %get-tuple-element.43), channel_id=1, source_target_pairs={{0,2},{1,3},{4,0},{5,1},{8,4},{9,5},{12,8},{13,9},{14,12},{15,13},... | collective-permute-start | bytes 1105928 | tf_op jit(solution)/shard_map/ppermute | solution.py:314
  41.7 15.8 %collective-permute-start.9 = (bf16[480,384]{1,0:T(8,128)(2,1)S(1)}, bf16[480,384]{1,0:T(8,128)(2,1)S(1)}, u32[]{:S(2)}, u32[]{:S(2)}) collective-permute-start(bf16[480,384]{1,0:T(8,128)(2,1)S(1)} %get-tuple-element.40), channel_id=1, source_target_pairs={{0,4},{1,5},{4,8},{5,9},{8,12},{9,13},{12,14},{13,15},{14,10},{15,... | collective-permute-start | bytes 1105928 | tf_op jit(solution)/shard_map/ppermute | solution.py:314
  49.8 17.4 %collective-permute-start.7 = (bf16[480,384]{1,0:T(8,128)(2,1)S(1)}, bf16[480,384]{1,0:T(8,128)(2,1)S(1)}, u32[]{:S(2)}, u32[]{:S(2)}) collective-permute-start(bf16[480,384]{1,0:T(8,128)(2,1)S(1)} %add_convert_fusion.6), channel_id=1, source_target_pairs={{0,2},{1,3},{4,0},{5,1},{8,4},{9,5},{12,8},{13,9},{14,12},{15,13},... | collective-permute-start | bytes 1105928 | tf_op jit(solution)/shard_map/ppermute | solution.py:314
  52.1 11.5 %collective-permute-start.3 = (bf16[480,384]{1,0:T(8,128)(2,1)S(1)}, bf16[480,384]{1,0:T(8,128)(2,1)S(1)}, u32[]{:S(2)}, u32[]{:S(2)}) collective-permute-start(bf16[480,384]{1,0:T(8,128)(2,1)S(1)} %add_convert_fusion.9), channel_id=1, source_target_pairs={{0,4},{1,5},{4,8},{5,9},{8,12},{9,13},{12,14},{13,15},{14,10},{15,... | collective-permute-start | bytes 1105928 | tf_op jit(solution)/shard_map/ppermute | solution.py:314
  57.4 15.7 %collective-permute-start.13 = (bf16[480,384]{1,0:T(8,128)(2,1)S(1)}, bf16[480,384]{1,0:T(8,128)(2,1)S(1)}, u32[]{:S(2)}, u32[]{:S(2)}) collective-permute-start(bf16[480,384]{1,0:T(8,128)(2,1)S(1)} %add_convert_fusion.2), channel_id=1, source_target_pairs={{0,2},{1,3},{4,0},{5,1},{8,4},{9,5},{12,8},{13,9},{14,12},{15,13},... | collective-permute-start | bytes 1105928 | tf_op jit(solution)/shard_map/ppermute | solution.py:314
  57.6 15.7 %collective-permute-start.10 = (bf16[480,384]{1,0:T(8,128)(2,1)S(1)}, bf16[480,384]{1,0:T(8,128)(2,1)S(1)}, u32[]{:S(2)}, u32[]{:S(2)}) collective-permute-start(bf16[480,384]{1,0:T(8,128)(2,1)S(1)} %add_convert_fusion.4), channel_id=1, source_target_pairs={{0,4},{1,5},{4,8},{5,9},{8,12},{9,13},{12,14},{13,15},{14,10},{15,... | collective-permute-start | bytes 1105928 | tf_op jit(solution)/shard_map/ppermute | solution.py:314
  67.3 23.6 %collective-permute-start.8 = (bf16[480,384]{1,0:T(8,128)(2,1)S(1)}, bf16[480,384]{1,0:T(8,128)(2,1)S(1)}, u32[]{:S(2)}, u32[]{:S(2)}) collective-permute-start(bf16[480,384]{1,0:T(8,128)(2,1)S(1)} %add_convert_fusion.5), channel_id=1, source_target_pairs={{0,2},{1,3},{4,0},{5,1},{8,4},{9,5},{12,8},{13,9},{14,12},{15,13},... | collective-permute-start | bytes 1105928 | tf_op jit(solution)/shard_map/ppermute | solution.py:314
  69.7 11.6 %collective-permute-start.4 = (bf16[480,384]{1,0:T(8,128)(2,1)S(1)}, bf16[480,384]{1,0:T(8,128)(2,1)S(1)}, u32[]{:S(2)}, u32[]{:S(2)}) collective-permute-start(bf16[480,384]{1,0:T(8,128)(2,1)S(1)} %add_convert_fusion.8), channel_id=1, source_target_pairs={{0,4},{1,5},{4,8},{5,9},{8,12},{9,13},{12,14},{13,15},{14,10},{15,... | collective-permute-start | bytes 1105928 | tf_op jit(solution)/shard_map/ppermute | solution.py:314
  73.2 15.0 %collective-permute-start.14 = (bf16[480,384]{1,0:T(8,128)(2,1)S(1)}, bf16[480,384]{1,0:T(8,128)(2,1)S(1)}, u32[]{:S(2)}, u32[]{:S(2)}) collective-permute-start(bf16[480,384]{1,0:T(8,128)(2,1)S(1)} %add_convert_fusion.1), channel_id=1, source_target_pairs={{0,2},{1,3},{4,0},{5,1},{8,4},{9,5},{12,8},{13,9},{14,12},{15,13},... | collective-permute-start | bytes 1105928 | tf_op jit(solution)/shard_map/ppermute | solution.py:314
  73.4 21.4 %collective-permute-start.11 = (bf16[480,384]{1,0:T(8,128)(2,1)S(1)}, bf16[480,384]{1,0:T(8,128)(2,1)S(1)}, u32[]{:S(2)}, u32[]{:S(2)}) collective-permute-start(bf16[480,384]{1,0:T(8,128)(2,1)S(1)} %add_convert_fusion.3), channel_id=1, source_target_pairs={{0,4},{1,5},{4,8},{5,9},{8,12},{9,13},{12,14},{13,15},{14,10},{15,... | collective-permute-start | bytes 1105928 | tf_op jit(solution)/shard_map/ppermute | solution.py:314
  84.9 9.8 %collective-permute-start.5 = (bf16[480,384]{1,0:T(8,128)(2,1)S(1)}, bf16[480,384]{1,0:T(8,128)(2,1)S(1)}, u32[]{:S(2)}, u32[]{:S(2)}) collective-permute-start(bf16[480,384]{1,0:T(8,128)(2,1)S(1)} %add_convert_fusion.7), channel_id=1, source_target_pairs={{0,4},{1,5},{4,8},{5,9},{8,12},{9,13},{12,14},{13,15},{14,10},{15,... | collective-permute-start | bytes 1105928 | tf_op jit(solution)/shard_map/ppermute | solution.py:314
  88.3 9.9 %collective-permute-start.15 = (bf16[480,384]{1,0:T(8,128)(2,1)S(1)}, bf16[480,384]{1,0:T(8,128)(2,1)S(1)}, u32[]{:S(2)}, u32[]{:S(2)}) collective-permute-start(bf16[480,384]{1,0:T(8,128)(2,1)S(1)} %add_convert_fusion), channel_id=1, source_target_pairs={{0,2},{1,3},{4,0},{5,1},{8,4},{9,5},{12,8},{13,9},{14,12},{15,13},... | collective-permute-start | bytes 1105928 | tf_op jit(solution)/shard_map/ppermute | solution.py:314
  98.4 7.7 %collective-permute-start.17 = (bf16[384,384]{1,0:T(8,128)(2,1)S(1)}, bf16[384,384]{1,0:T(8,128)(2,1)S(1)}, u32[]{:S(2)}, u32[]{:S(2)}) collective-permute-start(bf16[384,384]{1,0:T(8,128)(2,1)S(1)} %fusion), channel_id=1, source_target_pairs={{0,4},{1,8},{2,6},{3,10},{4,0},{5,12},{6,2},{7,14},{8,3},{9,13},{1... | collective-permute-start | bytes 884744 | tf_op jit(solution)/shard_map/ppermute | solution.py:347
  98.6 16.5 %collective-permute-start.16 = (bf16[384,384]{1,0:T(8,128)(2,1)S(1)}, bf16[384,384]{1,0:T(8,128)(2,1)S(1)}, u32[]{:S(2)}, u32[]{:S(2)}) collective-permute-start(bf16[384,384]{1,0:T(8,128)(2,1)S(1)} %multiply_convert_fusion), channel_id=1, source_target_pairs={{0,2},{1,10},{2,4},{3,12},{4,6},{5,14},{6,0},{7,8},{8,5},{9,11},{1... | collective-permute-start | bytes 884744 | tf_op jit(solution)/shard_map/ppermute | solution.py:346

commit v4 on v3

v4 whole, which is shorter than its diff:
```python
import functools

import jax
import jax.numpy as jnp
import numpy as np
from jax import lax
from jax.experimental import pallas as pl
from jax.experimental.pallas import tpu as pltpu
from jax.sharding import PartitionSpec as P

EXPERTS = 8
CAP = 384
BATCH = 96
WINDOW = 128
SNAKE = (0, 2, 4, 6, 7, 5, 3, 1)
F32, BF16, I32 = jnp.float32, jnp.bfloat16, jnp.int32


def plan_tokens(ids_ref, gates_ref, pick_ref, starts_ref, coef_ref):
    tokens = ids_ref.shape[1]
    local = EXPERTS // 2
    lanes = lax.broadcasted_iota(I32, (tokens, 128), 1)
    rows = jnp.concatenate([ids_ref[...].astype(F32), gates_ref[...], jnp.zeros((4, tokens), F32)], axis=0).T
    ids = [rows[:, k : k + 1].astype(I32) for k in range(2)]
    gates = [rows[:, k : k + 1] for k in (2, 3)]
    hits = [ids[k] == lanes for k in range(2)]
    named = jnp.where(hits[0] | hits[1], 1.0, 0.0).astype(BF16)
    earlier = jnp.where(
        lax.broadcasted_iota(I32, (tokens, tokens), 1) < lax.broadcasted_iota(I32, (tokens, tokens), 0), 1.0, 0.0
    ).astype(BF16)
    before = jnp.dot(earlier, named, preferred_element_type=F32)

    slots = [ids[k] - lax.axis_index("expert") * local for k in range(2)]
    here = [jnp.where((slots[k] >= 0) & (slots[k] < local), 1.0, 0.0) for k in range(2)]
    both = here[0] * here[1]
    neither = (1.0 - here[0]) * (1.0 - here[1])
    mixed = 1.0 - both - neither
    weights = [here[k] * jnp.where(both > 0.5, gates[k], 1.0) for k in range(2)]
    ours = here[0] * gates[0] + here[1] * gates[1]
    theirs = (1.0 - here[0]) * gates[0] + (1.0 - here[1]) * gates[1]
    ours = jnp.where(mixed > 0.5, ours, both)
    theirs = jnp.where(mixed > 0.5, theirs, neither)
    coef_ref[...] = jnp.where(
        lanes == 0, weights[0], jnp.where(lanes == 1, weights[1], jnp.where(lanes == 2, ours, theirs))
    )

    columns = lax.broadcasted_iota(I32, (BATCH, local * WINDOW), 1)
    for b in range(tokens // BATCH):
        rows = slice(b * BATCH, (b + 1) * BATCH)
        start = before[b * BATCH : b * BATCH + 1, :].astype(I32)
        start = jnp.minimum((start >> 4) << 4, CAP - WINDOW)
        starts_ref[b : b + 1, :] = start
        ahead = before[rows] - start.astype(F32)
        for k in range(2):
            offset = jnp.sum(jnp.where(hits[k][rows], ahead, 0.0), axis=1, keepdims=True).astype(I32)
            at = jnp.where(here[k][rows] > 0.5, slots[k][rows] * WINDOW + offset, -1)
            pick_ref[(2 * b + k) * BATCH : (2 * b + k + 1) * BATCH, :] = jnp.where(columns == at, 1.0, 0.0).astype(BF16)


def pick_kernel(first, *refs):
    if first:
        ids_ref, gates_ref, rows_ref, out_ref, pick_ref, starts_ref, coef_ref = refs[:7]
        held, made, in_sems, out_sems, starts, starts_sem = refs[7:]
    else:
        starts, pick_ref, coef_ref, rows_ref, out_ref, held, made, in_sems, out_sems = refs
    tokens, width = out_ref.shape
    tiles, _, tile = held.shape
    local = EXPERTS // 2
    member = lax.axis_index("expert")
    base = (1 - member if first else member) * width

    loads = []
    for j in range(tiles):
        at = pl.ds(pl.multiple_of(base + j * tile, 128), tile)
        loads.append(pltpu.make_async_copy(rows_ref.at[:, at], held.at[j], in_sems.at[j]))
        loads[-1].start()
    if first:
        plan_tokens(ids_ref, gates_ref, pick_ref, starts_ref, coef_ref)
        copy = pltpu.make_async_copy(starts_ref, starts, starts_sem)
        copy.start()
        copy.wait()
    stores = []
    for j in range(tiles):
        loads[j].wait()
        for b in range(tokens // BATCH):
            windows = []
            for k in range(local):
                at = k * CAP + starts[b, member * local + k]
                windows.append(held[j, pl.ds(pl.multiple_of(at, 16), WINDOW), :])
            picked = jnp.dot(
                pick_ref[2 * b * BATCH : 2 * (b + 1) * BATCH, :],
                jnp.concatenate(windows, axis=0),
                preferred_element_type=F32,
            )
            rows = slice(b * BATCH, (b + 1) * BATCH)
            total = coef_ref[rows, 0:1] * picked[:BATCH] + coef_ref[rows, 1:2] * picked[BATCH:]
            made[j, rows, :] = total.astype(BF16)
        stores.append(
            pltpu.make_async_copy(made.at[j], out_ref.at[:, j * tile : (j + 1) * tile], out_sems.at[j])
        )
        stores[-1].start()
    for store in stores:
        store.wait()


def pick_half(args, rows, tokens, width, first, tile=512):
    tiles = width // tile
    depth = EXPERTS // 2 * WINDOW
    any_, vmem = pl.BlockSpec(memory_space=pl.ANY), pl.BlockSpec(memory_space=pltpu.VMEM)
    out_shape = [jax.ShapeDtypeStruct((tokens, width), BF16)]
    scratch = [
        pltpu.VMEM((tiles, rows.shape[0], tile), BF16),
        pltpu.VMEM((tiles, tokens, tile), BF16),
        pltpu.SemaphoreType.DMA((tiles,)),
        pltpu.SemaphoreType.DMA((tiles,)),
    ]
    if first:
        out_shape += [
            jax.ShapeDtypeStruct((2 * tokens, depth), BF16),
            jax.ShapeDtypeStruct((tokens // BATCH, 128), I32),
            jax.ShapeDtypeStruct((tokens, 128), F32),
        ]
        in_specs = [vmem, vmem, any_]
        scratch += [pltpu.SMEM((tokens // BATCH, 128), I32), pltpu.SemaphoreType.DMA]
    else:
        in_specs = [pl.BlockSpec(memory_space=pltpu.SMEM), vmem, vmem, any_]
    return pl.pallas_call(
        functools.partial(pick_kernel, first),
        out_shape=out_shape,
        in_specs=in_specs,
        out_specs=[any_] + [vmem] * (len(out_shape) - 1),
        scratch_shapes=scratch,
        cost_estimate=pl.CostEstimate(
            flops=4 * tokens * depth * width, bytes_accessed=2 * (rows.shape[0] + tokens) * width, transcendentals=0
        ),
        compiler_params=pltpu.CompilerParams(vmem_limit_bytes=56 << 20),
        name="pick_first" if first else "pick_second",
    )(*args, rows)


def merge_kernel(first, coef_ref, ours_ref, theirs_ref, *refs):
    total = coef_ref[:, 2:3] * ours_ref[...].astype(F32) + coef_ref[:, 3:4] * theirs_ref[...].astype(F32)
    total = total.astype(BF16)
    if first:
        refs[0][...] = total
    refs[-1][...] = total.T


def merge(coef, ours, theirs, turned=None, tile=384):
    tokens, width = ours.shape
    first = turned is None
    steps = width // tile
    tall = pl.BlockSpec((tokens, tile), lambda j: (0, j))
    flat = pl.BlockSpec((tile, tokens), lambda j: (j if first else j + steps, 0))
    in_specs = [pl.BlockSpec(coef.shape, lambda j: (0, 0)), tall, tall]
    args = [coef, ours, theirs]
    out_shape = [jax.ShapeDtypeStruct((2 * width, tokens), BF16)]
    out_specs = [flat]
    if first:
        out_shape.insert(0, jax.ShapeDtypeStruct((tokens, width), BF16))
        out_specs.insert(0, tall)
    else:
        in_specs.append(pl.BlockSpec(memory_space=pl.ANY))
        args.append(turned)
    return pl.pallas_call(
        functools.partial(merge_kernel, first),
        out_shape=out_shape,
        grid=(steps,),
        in_specs=in_specs,
        out_specs=out_specs,
        input_output_aliases={} if first else {3: 0},
        compiler_params=pltpu.CompilerParams(vmem_limit_bytes=32 << 20),
        cost_estimate=pl.CostEstimate(flops=4 * ours.size, bytes_accessed=6 * ours.size, transcendentals=0),
        name="merge_first" if first else "merge_second",
    )(*args)


def my_row():
    return lax.axis_index("dp") * 2 + lax.axis_index("expert")


def blocks_kernel(count, table, turned_ref, mine_ref, *refs):
    tall, width = refs[-1].shape
    strip = tall - width
    me = my_row()
    for n, out_ref in enumerate(refs[-count:]):
        jobs = [table[me, 4 * n + k] for k in range(4)]
        parts = ((0, width, width), (width, strip, strip))
        for k, (at, rows, unit) in enumerate(parts):

            @pl.when(jobs[2 * k] >= 0)
            def _(jobs=jobs, k=k, out_ref=out_ref, at=at, rows=rows, unit=unit):
                down = pl.ds(pl.multiple_of(jobs[2 * k] * unit, 32), rows)
                along = pl.ds(pl.multiple_of(jobs[2 * k + 1] * width, 128), width)
                block = jnp.dot(turned_ref[down, :], mine_ref[:, along], preferred_element_type=F32)
                out_ref[at : at + rows, :] = block.astype(out_ref.dtype)

        @pl.when(jobs[2] < 0)
        def _(out_ref=out_ref):
            out_ref[width:, :] = jnp.zeros((strip, width), out_ref.dtype)


def moment_blocks(table, turned, mine, width, strip, dtype, name, after=()):
    count = table.shape[1] // 4
    whole = lambda shape: pl.BlockSpec(shape, lambda i, s: (0, 0))
    piece = (width + strip, width)
    return pl.pallas_call(
        functools.partial(blocks_kernel, count),
        out_shape=[jax.ShapeDtypeStruct(piece, dtype)] * count,
        grid_spec=pltpu.PrefetchScalarGridSpec(
            num_scalar_prefetch=1,
            grid=(1,),
            in_specs=[whole(turned.shape), whole(mine.shape)] + [pl.BlockSpec(memory_space=pl.ANY)] * len(after),
            out_specs=[whole(piece)] * count,
        ),
        cost_estimate=pl.CostEstimate(
            flops=2 * count * mine.shape[0] * width * width,
            bytes_accessed=2 * turned.size + 2 * mine.size + count * width * width * 4,
            transcendentals=0,
        ),
        compiler_params=pltpu.CompilerParams(vmem_limit_bytes=40 << 20),
        name=name,
    )(table, turned, mine, *after)


STRIP = 96


def is_diagonal(b, e):
    return b // 4 == e


def owned_columns(b, e):
    shift = 0 if is_diagonal(b, e) or e == 1 else 1
    return [(b + shift) % 4, (b + shift + 1) % 4]


def leads(b):
    return b % 4 < 2


ROUNDS = (
    ((0, 4), (1, 4), (1, 3), (0, 5)),
    ((0, 3), (1, 5), (1, 2), (0, 6)),
    ((0, 2), (1, 6), (1, 1), (0, 7)),
    ((0, 1), (1, 7), (0, 0), (1, 0)),
)


def job_table(which, width):
    table = np.full((8, 2, len(which), 4), -1, np.int32)
    for p, b in enumerate(SNAKE):
        for e in range(2):
            for n, (x, t) in enumerate(which):
                q = SNAKE[(p + t) % 8]
                table[b, e, n, :2] = (q % 4 + (0 if q // 4 == e else 4), owned_columns(q, e)[x])
                if is_diagonal(q, e):
                    lead, other = (q % 4, (q + 2) % 4) if leads(q) else ((q + 2) % 4, q % 4)
                    first = lead * width + (0 if leads(q) else width // 2) + x * STRIP
                    table[b, e, n, 2:] = (first // STRIP, other)
    return table.reshape(16, -1)


def ring_perm(direction):
    pairs = [(SNAKE[p], SNAKE[(p + direction) % 8]) for p in range(8)]
    return [(a * 2 + e, b * 2 + e) for a, b in pairs for e in range(2)]


def mirror_perms():
    one, other = [], []
    for b in range(8):
        for e in range(2):
            here = b * 2 + e
            if is_diagonal(b, e):
                one.append((here, (b // 4 * 4 + (b + 1) % 4) * 2 + e))
                other.append((here, (b // 4 * 4 + (b + 2) % 4) * 2 + e))
            elif e == 1:
                other.append((here, (4 + b) * 2))
                one.append((here, (4 + (b + 1) % 4) * 2))
            else:
                other.append((here, (b + 1) % 4 * 2 + 1))
                one.append((here, (b + 2) % 4 * 2 + 1))
    return one, other


def place_table():
    table = np.zeros((8, 2, 5), np.int32)
    for b in range(8):
        for e in range(2):
            own = owned_columns(b, e)
            if is_diagonal(b, e):
                table[b, e] = (own[0], own[1], (b + 3) % 4, (b + 2) % 4, 1 if leads(b) else 2)
            elif e == 1:
                table[b, e] = (own[0], own[1], (b + 2) % 4, (b + 3) % 4, 0)
            else:
                table[b, e] = (own[0], own[1], (b + 3) % 4, b % 4, 0)
    return table


def total_kernel(scale, place, own0, own1, right0, left0, right1, left1, out_ref, one, other, share, made, sems):
    width = one.shape[0]
    me = my_row()

    def total(own, right, left, rows):
        return (own[rows, :] + right[rows, :].astype(F32) + left[rows, :].astype(F32)) * scale

    block, strip = slice(0, width), slice(width, width + STRIP)
    made[0] = total(own0, right0, left0, block)
    made[1] = total(own1, right1, left1, block)
    copies = []
    for n in range(2):
        at = pl.ds(pl.multiple_of(place[me, n] * width, 128), width)
        copies.append(pltpu.make_async_copy(made.at[n], out_ref.at[:, at], sems.at[n]))
        copies[-1].start()
    one[...] = made[1].astype(BF16)
    share[:STRIP, :] = total(own0, right0, left0, strip)
    share[STRIP:, :] = total(own1, right1, left1, strip)

    @pl.when(place[me, 4] == 0)
    def _():
        other[...] = made[0].astype(BF16)

    @pl.when(place[me, 4] > 0)
    def _():
        other[: width // 2, :] = share[...].astype(BF16)
        other[width // 2 :, :] = jnp.zeros((width - width // 2, width), BF16)

    for copy in copies:
        copy.wait()


def mirror_kernel(place, share, one, other, result_ref, out_ref, made, sems):
    width = one.shape[0]
    me = my_row()
    made[0] = one[...].astype(F32).T
    copies = []
    for n in range(2):
        at = pl.ds(pl.multiple_of(place[me, 2 + n] * width, 128), width)
        copies.append(pltpu.make_async_copy(made.at[n], out_ref.at[:, at], sems.at[n]))
    copies[0].start()

    @pl.when(place[me, 4] == 0)
    def _():
        made[1] = other[...].astype(F32).T

    @pl.when(place[me, 4] == 1)
    def _():
        made[1, : width // 2, :] = share[...]
        made[1, width // 2 :, :] = other[: width // 2, :].astype(F32)

    @pl.when(place[me, 4] == 2)
    def _():
        made[1] = jnp.concatenate([other[: width // 2, :].astype(F32), share[...]], axis=0).T

    copies[1].start()
    for copy in copies:
        copy.wait()


def symmetric_moment(mine, turned, total_tokens):
    width = mine.shape[1] // 4
    both = ("dp", "expert")
    blocks = {}

    def compute(n, dtype, after=()):
        which = ROUNDS[n]
        table = jnp.asarray(job_table(which, width))
        blocks.update(zip(which, moment_blocks(table, turned, mine, width, STRIP, dtype, f"blocks{n}", after)))

    def hop(value, key):
        return lax.ppermute(value, both, ring_perm(1 if key[1] <= (4 if key[0] == 0 else 3) else -1))

    compute(0, BF16)
    moving = {key: blocks[key] for key in ROUNDS[0]}
    arrived = {}
    for n in range(4):
        landed = {}
        for key in ROUNDS[n]:
            if key in moving:
                landed[key] = hop(moving[key], key)
        if n < 3:
            compute(n + 1, F32, after=(landed[ROUNDS[n][0]],))
        moving = {}
        for (x, t), value in landed.items():
            rightwards = t <= (4 if x == 0 else 3)
            t = t - 1 if rightwards else (t + 1) % 8
            if t == 0:
                arrived[x, rightwards] = value
            else:
                moving[x, t] = (value.astype(F32) + blocks[x, t]).astype(BF16)

    place = jnp.asarray(place_table().reshape(16, -1))
    smem, vmem, any_ = [pl.BlockSpec(memory_space=m) for m in (pltpu.SMEM, pltpu.VMEM, pl.ANY)]
    scratch = [pltpu.VMEM((2, width, width), F32), pltpu.SemaphoreType.DMA((2,))]
    block = jax.ShapeDtypeStruct((width, width), BF16)
    result = jax.ShapeDtypeStruct((width, 4 * width), F32)
    result, one, other, share = pl.pallas_call(
        functools.partial(total_kernel, 1.0 / total_tokens),
        out_shape=[result, block, block, jax.ShapeDtypeStruct((2 * STRIP, width), F32)],
        in_specs=[smem] + [vmem] * 6,
        out_specs=[any_, vmem, vmem, vmem],
        scratch_shapes=scratch,
        compiler_params=pltpu.CompilerParams(vmem_limit_bytes=32 << 20),
        name="total",
    )(
        place,
        blocks[0, 0],
        blocks[1, 0],
        arrived[0, True],
        arrived[0, False],
        arrived[1, True],
        arrived[1, False],
    )
    perm_one, perm_other = mirror_perms()
    other = lax.ppermute(other, both, perm_other)
    one = lax.ppermute(one, both, perm_one)
    return pl.pallas_call(
        mirror_kernel,
        out_shape=jax.ShapeDtypeStruct((width, 4 * width), F32),
        in_specs=[smem, vmem, vmem, vmem, any_],
        out_specs=any_,
        scratch_shapes=scratch,
        input_output_aliases={4: 0},
        compiler_params=pltpu.CompilerParams(vmem_limit_bytes=32 << 20),
        name="mirror",
    )(place, share, one, other, result)


def per_device(expert_ids, gates, expert_out):
    tokens, channels = expert_ids.shape[0], expert_out.shape[1]
    dp_size = lax.axis_size("dp")
    member = lax.axis_index("expert")
    half = channels // 2
    swap = [(0, 1), (1, 0)]

    sent, pick, starts, coef = pick_half((expert_ids.T, gates.T), expert_out, tokens, half, True)
    from_peer = lax.ppermute(sent, "expert", swap)
    (kept,) = pick_half((starts, pick, coef), expert_out, tokens, half, False)
    from_peer_too = lax.ppermute(kept, "expert", swap)
    rows, turned = merge(coef, kept, from_peer)
    (turned,) = merge(coef, sent, from_peer_too, turned)

    total_tokens = tokens * dp_size
    if dp_size == 8 and channels == 8 * 384:
        return symmetric_moment(rows, turned, total_tokens)
    slab = jnp.dot(turned, rows, preferred_element_type=F32)
    slab = jnp.where(member == 0, slab, jnp.roll(slab, half, axis=0))
    return lax.psum_scatter(slab, "dp", scatter_dimension=0, tiled=True) / total_tokens


def solution(mesh):
    assert mesh.shape["expert"] == 2
    in_specs = (
        P(("groups", "dp"), None),
        P(("groups", "dp"), None),
        P(("groups", "dp", "expert"), None),
    )
    out_specs = P(("groups", "dp"), "expert")
    return jax.shard_map(
        per_device, mesh=mesh, in_specs=in_specs, out_specs=out_specs, check_vma=False
    )
```

time: 118 us -> 112 us (0.949)
  the two profiles are of different devices: /device:TPU:0 before, /device:TPU:6 now
where the time goes in v4:
time: 112 us; the launch traced here: 111 us
  waiting for transfers between devices  50.6 us (45%)
  Pallas kernels  37.5 us (33%)
  starting transfers between devices  17.4 us (16%)
  local copies, waits for them, and re-layouts  4.81 us (4%)
    ppermute x14, waiting for transfers between devices, hop(): lax.ppermute(value, both, ring_perm(1 if key[1] <= (4 if key[0] == 0 else...  36.4 us
    pallas_call x2, Pallas kernels, pick_half(): pl.pallas_call(functools.partial(pick_kernel, first), out_shape=out_shape...  15.3 us
    ppermute x14, starting transfers between devices, hop(): lax.ppermute(value, both, ring_perm(1 if key[1] <= (4 if key[0] == 0 else...  14.5 us
    pallas_call x4, Pallas kernels, moment_blocks(): pl.pallas_call(functools.partial(blocks_kernel, count), out_shape=[jax.Sh...  12.7 us
    ppermute x1, waiting for transfers between devices, symmetric_moment(): other = lax.ppermute(other, both, perm_other)  9.37 us
    pallas_call x2, Pallas kernels, merge(): pl.pallas_call(functools.partial(merge_kernel, first), out_shape=out_shap...  5.64 us
    unnamed x20, local copies, waits for them, and re-layouts  4.81 us
    ppermute x1, waiting for transfers between devices, symmetric_moment(): one = lax.ppermute(one, both, perm_one)  4.81 us
  transfers between devices with their start and end apart: 18, of which 11 were waited for; matrix products, arithmetic and copies ran while one was open for 1% of the time, Pallas kernels for 18%

profile of v4, /device:TPU:6, one launch (start us, length us, event | category | flops | bytes accessed | tf_op | source)
XLA Modules:
  0.0 111.5 jit_solution(9989183753173544979)
XLA Ops:
  0.0 8.4 %pick_first.1 = (bf16[768,1536]{1,0:T(8,128)(2,1)}, bf16[1536,512]{1,0:T(8,128)(2,1)}, s32[8,128]{1,0:T(8,128)}, f32[768,128]{1,0:T(8,128)}) custom-call(s32[2,768]{1,0:T(2,128)} %bitcast.2, f32[2,768]{1,0:T(2,128)} %bitcast.3, bf16[1536,3072]{1,0:T(8,128)(2,1)} %refs_3_.1), custom_call_target="tpu_custom_call" | custom-call | flops 2415919104 | bytes 7077888 | tf_op jit(solution)/shard_map/pick_first/pallas_call | solution.py:127
  8.4 0.1 collective-permute-start.1
  8.5 6.9 %pick_second.1.ours_ref = bf16[768,1536]{1,0:T(8,128)(2,1)} custom-call(s32[8,128]{1,0:T(8,128)} %get-tuple-element.33.refs_0_, bf16[1536,512]{1,0:T(8,128)(2,1)} %get-tuple-element.34.refs_1_, f32[768,128]{1,0:T(8,128)} %get-tuple-element.31.refs_2_.coef_ref, bf16[1536,3072]{1,0:T(8,128)(2,1)} %refs_3_.1), custom_call_target="tpu_custom_call" | custom-call | flops 2415919104 | bytes 7077888 | tf_op jit(solution)/shard_map/pick_second/pallas_call | solution.py:127
  15.4 0.6 collective-permute-start
  15.9 0.0 collective-permute-done.1.theirs_ref
  15.9 1.4 %copy-done.3 = bf16[768,1536]{1,0:T(8,128)(2,1)} copy-done((bf16[768,1536]{1,0:T(8,128)(2,1)}, bf16[768,1536]{1,0:T(8,128)(2,1)S(1)}, u32[]{:S(2)}) %copy-start.3) | copy-done | bytes 2359320
  17.4 1.7 %copy-done = bf16[768,1536]{1,0:T(8,128)(2,1)S(1)} copy-done((bf16[768,1536]{1,0:T(8,128)(2,1)S(1)}, bf16[768,1536]{1,0:T(8,128)(2,1)}, u32[]{:S(2)}) %copy-start) | copy-done | bytes 2359320
  19.1 1.7 %copy-done.4 = bf16[768,1536]{1,0:T(8,128)(2,1)S(1)} copy-done((bf16[768,1536]{1,0:T(8,128)(2,1)S(1)}, bf16[768,1536]{1,0:T(8,128)(2,1)}, u32[]{:S(2)}) %copy-start.4) | copy-done | bytes 2359320
  20.7 2.9 %merge_first.1 = (bf16[768,1536]{1,0:T(8,128)(2,1)S(1)}, bf16[3072,768]{1,0:T(8,128)(2,1)S(1)}) custom-call(f32[768,128]{1,0:T(8,128)S(1)} %copy-done.1, bf16[768,1536]{1,0:T(8,128)(2,1)S(1)} %copy-done, bf16[768,1536]{1,0:T(8,128)(2,1)S(1)} %copy-done.4), custom_call_target="tpu_custom_call" | custom-call | flops 4718592 | bytes 7077888 | tf_op jit(solution)/shard_map/merge_first/pallas_call | solution.py:165
  23.7 0.0 collective-permute-done.theirs_ref
  23.7 0.0 copy-start.9
  23.7 2.7 %merge_second.1.turned_ref = bf16[3072,768]{1,0:T(8,128)(2,1)S(1)} custom-call(f32[768,128]{1,0:T(8,128)S(1)} %copy-done.1, bf16[768,1536]{1,0:T(8,128)(2,1)S(1)} %copy-done.2, bf16[768,1536]{1,0:T(8,128)(2,1)S(1)} %collective-permute-done.theirs_ref, bf16[3072,768]{1,0:T(8,128)(2,1)S(1)} %get-tuple-element.35.refs_0_), custom_call_target="tpu_custom_call", output_to_operand_aliasing={{}: (3, {})} | custom-call | flops 4718592 | bytes 7077888 | tf_op jit(solution)/shard_map/merge_second/pallas_call | solution.py:165
  26.4 0.0 copy-start.8
  26.4 2.6 %blocks0.1 = (bf16[480,384]{1,0:T(8,128)(2,1)S(1)}, bf16[480,384]{1,0:T(8,128)(2,1)S(1)}, bf16[480,384]{1,0:T(8,128)(2,1)S(1)}, bf16[480,384]{1,0:T(8,128)(2,1)S(1)}) custom-call(s32[16,16]{1,0:T(8,128)S(1)} %copy-done.9, bf16[3072,768]{1,0:T(8,128)(2,1)S(1)} %merge_second.1.turned_ref, bf16[768,1536]{1,0:T(8,128)(2,1)S(1)} %get-tuple-element.36.mine_ref), custom_call_target="tpu_custom_call" | custom-call | flops 905969664 | bytes 9437184 | tf_op jit(solution)/shard_map/blocks0/pallas_call | solution.py:207
  29.1 0.5 collective-permute-start.2
  29.6 1.5 %collective-permute-start.6 = (bf16[480,384]{1,0:T(8,128)(2,1)S(1)}, bf16[480,384]{1,0:T(8,128)(2,1)S(1)}, u32[]{:S(2)}, u32[]{:S(2)}) collective-permute-start(bf16[480,384]{1,0:T(8,128)(2,1)S(1)} %get-tuple-element.43), channel_id=1, source_target_pairs={{0,2},{1,3},{4,0},{5,1},{8,4},{9,5},{12,8},{13,9},{14,12},{15,13},... | collective-permute-start | bytes 1105928 | tf_op jit(solution)/shard_map/ppermute | solution.py:371
  31.1 0.5 collective-permute-start.9
  31.6 1.5 %collective-permute-start.12 = (bf16[480,384]{1,0:T(8,128)(2,1)S(1)}, bf16[480,384]{1,0:T(8,128)(2,1)S(1)}, u32[]{:S(2)}, u32[]{:S(2)}) collective-permute-start(bf16[480,384]{1,0:T(8,128)(2,1)S(1)} %get-tuple-element.49), channel_id=1, source_target_pairs={{0,2},{1,3},{4,0},{5,1},{8,4},{9,5},{12,8},{13,9},{14,12},{15,13},... | collective-permute-start | bytes 1105928 | tf_op jit(solution)/shard_map/ppermute | solution.py:371
  33.2 7.3 %collective-permute-done.2.refs_0_ = bf16[480,384]{1,0:T(8,128)(2,1)S(1)} collective-permute-done((bf16[480,384]{1,0:T(8,128)(2,1)S(1)}, bf16[480,384]{1,0:T(8,128)(2,1)S(1)}, u32[]{:S(2)}, u32[]{:S(2)}) %collective-permute-start.2) | collective-permute-done | bytes 368672 | tf_op jit(solution)/shard_map/ppermute | solution.py:371
  40.5 3.1 %blocks1.1 = (f32[480,384]{1,0:T(8,128)S(1)}, f32[480,384]{1,0:T(8,128)S(1)}, f32[480,384]{1,0:T(8,128)S(1)}, f32[480,384]{1,0:T(8,128)S(1)}) custom-call(s32[16,16]{1,0:T(8,128)S(1)} %copy-done.8, bf16[3072,768]{1,0:T(8,128)(2,1)S(1)} %merge_second.1.turned_ref, bf16[768,1536]{1,0:T(8,128)(2,1)S(1)} %get-tuple-element.36.mine_ref, ...), custom_call_target="tpu_custom_call" | custom-call | flops 905969664 | bytes 9437184 | tf_op jit(solution)/shard_map/blocks1/pallas_call | solution.py:207
  43.6 0.0 collective-permute-done.6
  43.6 0.1 add_convert_fusion.6
  43.7 0.0 copy-start.7
  43.7 2.2 %collective-permute-start.7 = (bf16[480,384]{1,0:T(8,128)(2,1)S(1)}, bf16[480,384]{1,0:T(8,128)(2,1)S(1)}, u32[]{:S(2)}, u32[]{:S(2)}) collective-permute-start(bf16[480,384]{1,0:T(8,128)(2,1)S(1)} %add_convert_fusion.6), channel_id=1, source_target_pairs={{0,2},{1,3},{4,0},{5,1},{8,4},{9,5},{12,8},{13,9},{14,12},{15,13},... | collective-permute-start | bytes 1105928 | tf_op jit(solution)/shard_map/ppermute | solution.py:371
  45.9 0.1 add_convert_fusion.9
  45.9 0.1 collective-permute-start.3
  46.0 2.4 %collective-permute-done.9 = bf16[480,384]{1,0:T(8,128)(2,1)S(1)} collective-permute-done((bf16[480,384]{1,0:T(8,128)(2,1)S(1)}, bf16[480,384]{1,0:T(8,128)(2,1)S(1)}, u32[]{:S(2)}, u32[]{:S(2)}) %collective-permute-start.9) | collective-permute-done | bytes 368672 | tf_op jit(solution)/shard_map/ppermute | solution.py:371
  48.4 0.1 add_convert_fusion.4
  48.5 0.5 collective-permute-start.10
  49.0 0.0 collective-permute-done.12
  49.0 0.1 add_convert_fusion.2
  49.1 1.6 %collective-permute-start.13 = (bf16[480,384]{1,0:T(8,128)(2,1)S(1)}, bf16[480,384]{1,0:T(8,128)(2,1)S(1)}, u32[]{:S(2)}, u32[]{:S(2)}) collective-permute-start(bf16[480,384]{1,0:T(8,128)(2,1)S(1)} %add_convert_fusion.2), channel_id=1, source_target_pairs={{0,2},{1,3},{4,0},{5,1},{8,4},{9,5},{12,8},{13,9},{14,12},{15,13},... | collective-permute-start | bytes 1105928 | tf_op jit(solution)/shard_map/ppermute | solution.py:371
  50.7 6.9 %collective-permute-done.3.refs_0_ = bf16[480,384]{1,0:T(8,128)(2,1)S(1)} collective-permute-done((bf16[480,384]{1,0:T(8,128)(2,1)S(1)}, bf16[480,384]{1,0:T(8,128)(2,1)S(1)}, u32[]{:S(2)}, u32[]{:S(2)}) %collective-permute-start.3) | collective-permute-done | bytes 368672 | tf_op jit(solution)/shard_map/ppermute | solution.py:371
  57.6 3.4 %blocks2.1 = (f32[480,384]{1,0:T(8,128)S(1)}, f32[480,384]{1,0:T(8,128)S(1)}, f32[480,384]{1,0:T(8,128)S(1)}, f32[480,384]{1,0:T(8,128)S(1)}) custom-call(s32[16,16]{1,0:T(8,128)S(1)} %copy-done.7, bf16[3072,768]{1,0:T(8,128)(2,1)S(1)} %merge_second.1.turned_ref, bf16[768,1536]{1,0:T(8,128)(2,1)S(1)} %get-tuple-element.36.mine_ref, ...), custom_call_target="tpu_custom_call" | custom-call | flops 905969664 | bytes 9437184 | tf_op jit(solution)/shard_map/blocks2/pallas_call | solution.py:207
  61.0 0.0 collective-permute-done.7
  61.0 0.1 add_convert_fusion.5
  61.1 0.0 copy-start.6
  61.1 1.9 %collective-permute-start.8 = (bf16[480,384]{1,0:T(8,128)(2,1)S(1)}, bf16[480,384]{1,0:T(8,128)(2,1)S(1)}, u32[]{:S(2)}, u32[]{:S(2)}) collective-permute-start(bf16[480,384]{1,0:T(8,128)(2,1)S(1)} %add_convert_fusion.5), channel_id=1, source_target_pairs={{0,2},{1,3},{4,0},{5,1},{8,4},{9,5},{12,8},{13,9},{14,12},{15,13},... | collective-permute-start | bytes 1105928 | tf_op jit(solution)/shard_map/ppermute | solution.py:371
  63.0 0.1 add_convert_fusion.8
  63.1 0.2 collective-permute-start.4
  63.3 1.4 %collective-permute-done.13 = bf16[480,384]{1,0:T(8,128)(2,1)S(1)} collective-permute-done((bf16[480,384]{1,0:T(8,128)(2,1)S(1)}, bf16[480,384]{1,0:T(8,128)(2,1)S(1)}, u32[]{:S(2)}, u32[]{:S(2)}) %collective-permute-start.13) | collective-permute-done | bytes 368672 | tf_op jit(solution)/shard_map/ppermute | solution.py:371
  64.8 0.1 add_convert_fusion.1
  64.8 1.6 %collective-permute-start.14 = (bf16[480,384]{1,0:T(8,128)(2,1)S(1)}, bf16[480,384]{1,0:T(8,128)(2,1)S(1)}, u32[]{:S(2)}, u32[]{:S(2)}) collective-permute-start(bf16[480,384]{1,0:T(8,128)(2,1)S(1)} %add_convert_fusion.1), channel_id=1, source_target_pairs={{0,2},{1,3},{4,0},{5,1},{8,4},{9,5},{12,8},{13,9},{14,12},{15,13},... | collective-permute-start | bytes 1105928 | tf_op jit(solution)/shard_map/ppermute | solution.py:371
  66.4 0.0 collective-permute-done.10
  66.4 0.1 add_convert_fusion.3
  66.5 0.5 collective-permute-start.11
  67.0 7.6 %collective-permute-done.4.refs_0_ = bf16[480,384]{1,0:T(8,128)(2,1)S(1)} collective-permute-done((bf16[480,384]{1,0:T(8,128)(2,1)S(1)}, bf16[480,384]{1,0:T(8,128)(2,1)S(1)}, u32[]{:S(2)}, u32[]{:S(2)}) %collective-permute-start.4) | collective-permute-done | bytes 368672 | tf_op jit(solution)/shard_map/ppermute | solution.py:371
  74.7 3.6 %blocks3.1 = (f32[480,384]{1,0:T(8,128)S(1)}, f32[480,384]{1,0:T(8,128)S(1)}, f32[480,384]{1,0:T(8,128)S(1)}, f32[480,384]{1,0:T(8,128)S(1)}) custom-call(s32[16,16]{1,0:T(8,128)S(1)} %copy-done.6, bf16[3072,768]{1,0:T(8,128)(2,1)S(1)} %merge_second.1.turned_ref, bf16[768,1536]{1,0:T(8,128)(2,1)S(1)} %get-tuple-element.36.mine_ref, ...), custom_call_target="tpu_custom_call" | custom-call | flops 905969664 | bytes 9437184 | tf_op jit(solution)/shard_map/blocks3/pallas_call | solution.py:207
  78.3 0.0 copy-start.5
  78.3 0.1 add_convert_fusion.7
  78.4 0.2 collective-permute-start.5
  78.6 1.7 %collective-permute-done.14 = bf16[480,384]{1,0:T(8,128)(2,1)S(1)} collective-permute-done((bf16[480,384]{1,0:T(8,128)(2,1)S(1)}, bf16[480,384]{1,0:T(8,128)(2,1)S(1)}, u32[]{:S(2)}, u32[]{:S(2)}) %collective-permute-start.14) | collective-permute-done | bytes 368672 | tf_op jit(solution)/shard_map/ppermute | solution.py:371
  80.4 0.1 add_convert_fusion
  80.4 1.6 %collective-permute-start.15 = (bf16[480,384]{1,0:T(8,128)(2,1)S(1)}, bf16[480,384]{1,0:T(8,128)(2,1)S(1)}, u32[]{:S(2)}, u32[]{:S(2)}) collective-permute-start(bf16[480,384]{1,0:T(8,128)(2,1)S(1)} %add_convert_fusion), channel_id=1, source_target_pairs={{0,2},{1,3},{4,0},{5,1},{8,4},{9,5},{12,8},{13,9},{14,12},{15,13},... | collective-permute-start | bytes 1105928 | tf_op jit(solution)/shard_map/ppermute | solution.py:371
  82.0 0.0 collective-permute-done.8.left0
  82.0 0.5 collective-permute-done.11.right1
  82.6 5.4 %collective-permute-done.5.right0 = bf16[480,384]{1,0:T(8,128)(2,1)S(1)} collective-permute-done((bf16[480,384]{1,0:T(8,128)(2,1)S(1)}, bf16[480,384]{1,0:T(8,128)(2,1)S(1)}, u32[]{:S(2)}, u32[]{:S(2)}) %collective-permute-start.5) | collective-permute-done | bytes 368672 | tf_op jit(solution)/shard_map/ppermute | solution.py:371
  88.0 2.9 %collective-permute-done.15.left1 = bf16[480,384]{1,0:T(8,128)(2,1)S(1)} collective-permute-done((bf16[480,384]{1,0:T(8,128)(2,1)S(1)}, bf16[480,384]{1,0:T(8,128)(2,1)S(1)}, u32[]{:S(2)}, u32[]{:S(2)}) %collective-permute-start.15) | collective-permute-done | bytes 368672 | tf_op jit(solution)/shard_map/ppermute | solution.py:371
  90.9 2.1 %total.1 = (f32[384,1536]{1,0:T(8,128)}, bf16[384,384]{1,0:T(8,128)(2,1)S(1)}, bf16[384,384]{1,0:T(8,128)(2,1)S(1)}, f32[192,384]{1,0:T(8,128)S(1)}) custom-call(s32[16,5]{1,0:T(8,128)S(1)} %copy-done.5, f32[480,384]{1,0:T(8,128)S(1)} %get-tuple-element.40.own0, f32[480,384]{1,0:T(8,128)S(1)} %get-tuple-element.41.own1, ...), custom_call_target="tpu_custom_call" | custom-call | tf_op jit(solution)/shard_map/total/pallas_call | solution.py:397
  93.0 0.2 collective-permute-start.16
  93.2 2.0 %collective-permute-start.17 = (bf16[384,384]{1,0:T(8,128)(2,1)S(1)}, bf16[384,384]{1,0:T(8,128)(2,1)S(1)}, u32[]{:S(2)}, u32[]{:S(2)}) collective-permute-start(bf16[384,384]{1,0:T(8,128)(2,1)S(1)} %get-tuple-element.55), channel_id=1, source_target_pairs={{0,4},{1,8},{2,6},{3,10},{4,0},{5,12},{6,2},{7,14},{8,3},{9,13},{1... | collective-permute-start | bytes 884744 | tf_op jit(solution)/shard_map/ppermute | solution.py:415
  95.3 4.8 %collective-permute-done.16.one = bf16[384,384]{1,0:T(8,128)(2,1)S(1)} collective-permute-done((bf16[384,384]{1,0:T(8,128)(2,1)S(1)}, bf16[384,384]{1,0:T(8,128)(2,1)S(1)}, u32[]{:S(2)}, u32[]{:S(2)}) %collective-permute-start.16) | collective-permute-done | bytes 294944 | tf_op jit(solution)/shard_map/ppermute | solution.py:416
  100.1 9.4 %collective-permute-done.17.other = bf16[384,384]{1,0:T(8,128)(2,1)S(1)} collective-permute-done((bf16[384,384]{1,0:T(8,128)(2,1)S(1)}, bf16[384,384]{1,0:T(8,128)(2,1)S(1)}, u32[]{:S(2)}, u32[]{:S(2)}) %collective-permute-start.17) | collective-permute-done | bytes 294944 | tf_op jit(solution)/shard_map/ppermute | solution.py:415
  109.4 1.9 %mirror.1 = f32[384,1536]{1,0:T(8,128)} custom-call(s32[16,5]{1,0:T(8,128)S(1)} %copy-done.5, f32[192,384]{1,0:T(8,128)S(1)} %get-tuple-element.53.share, bf16[384,384]{1,0:T(8,128)(2,1)S(1)} %collective-permute-done.16.one, bf16[384,384]{1,0:T(8,128)(2,1)S(1)} %collective-permute-done.17.other, ...), custom_call_target="tpu_custom_call", output_to_operand_aliasing={{}: (4, {})} | custom-call | tf_op jit(solution)/shard_map/mirror/pallas_call | solution.py:417
  (12 shorter events, 0.0 us)
Async XLA Ops:
  8.4 7.6 %collective-permute-start.1 = (bf16[768,1536]{1,0:T(8,128)(2,1)}, bf16[768,1536]{1,0:T(8,128)(2,1)S(1)}, u32[]{:S(2)}, u32[]{:S(2)}) collective-permute-start(bf16[768,1536]{1,0:T(8,128)(2,1)} %get-tuple-element.32.ours_ref), channel_id=1, source_target_pairs={{0,1},{1,0},{2,3},{3,2},{4,5},{5,4},{6,7},{7,6},{8,9},{9,8},{10,11... | collective-permute-start | bytes 7077896 | tf_op jit(solution)/shard_map/ppermute | solution.py:437
  8.4 8.9 %copy-start.1 = (f32[768,128]{1,0:T(8,128)S(1)}, f32[768,128]{1,0:T(8,128)}, u32[]{:S(2)}) copy-start(f32[768,128]{1,0:T(8,128)} %get-tuple-element.31.refs_2_.coef_ref) | copy-start | bytes 1179652
  15.4 8.3 %collective-permute-start = (bf16[768,1536]{1,0:T(8,128)(2,1)}, bf16[768,1536]{1,0:T(8,128)(2,1)S(1)}, u32[]{:S(2)}, u32[]{:S(2)}) collective-permute-start(bf16[768,1536]{1,0:T(8,128)(2,1)} %pick_second.1.ours_ref), channel_id=1, source_target_pairs={{0,1},{1,0},{2,3},{3,2},{4,5},{5,4},{6,7},{7,6},{8,9},{9,8},{10,11... | collective-permute-start | bytes 7077896 | tf_op jit(solution)/shard_map/ppermute | solution.py:439
  15.9 1.4 %copy-start.3 = (bf16[768,1536]{1,0:T(8,128)(2,1)}, bf16[768,1536]{1,0:T(8,128)(2,1)S(1)}, u32[]{:S(2)}) copy-start(bf16[768,1536]{1,0:T(8,128)(2,1)S(1)} %collective-permute-done.1.theirs_ref) | copy-start | bytes 7077892
  17.4 1.7 %copy-start = (bf16[768,1536]{1,0:T(8,128)(2,1)S(1)}, bf16[768,1536]{1,0:T(8,128)(2,1)}, u32[]{:S(2)}) copy-start(bf16[768,1536]{1,0:T(8,128)(2,1)} %pick_second.1.ours_ref) | copy-start | bytes 7077892
  19.1 1.7 %copy-start.4 = (bf16[768,1536]{1,0:T(8,128)(2,1)S(1)}, bf16[768,1536]{1,0:T(8,128)(2,1)}, u32[]{:S(2)}) copy-start(bf16[768,1536]{1,0:T(8,128)(2,1)} %copy-done.3) | copy-start | bytes 7077892
  20.7 3.0 %copy-start.2 = (bf16[768,1536]{1,0:T(8,128)(2,1)S(1)}, bf16[768,1536]{1,0:T(8,128)(2,1)}, u32[]{:S(2)}) copy-start(bf16[768,1536]{1,0:T(8,128)(2,1)} %get-tuple-element.32.ours_ref) | copy-start | bytes 7077892
  23.7 2.7 %copy-start.9 = (s32[16,16]{1,0:T(8,128)S(1)}, s32[16,16]{1,0:T(8,128)}, u32[]{:S(2)}) copy-start(s32[16,16]{1,0:T(8,128)} %constant.10.clone.table) | copy-start | bytes 3076
  26.4 14.1 %copy-start.8 = (s32[16,16]{1,0:T(8,128)S(1)}, s32[16,16]{1,0:T(8,128)}, u32[]{:S(2)}) copy-start(s32[16,16]{1,0:T(8,128)} %constant.11.clone.table) | copy-start | bytes 3076
  29.1 11.4 %collective-permute-start.2 = (bf16[480,384]{1,0:T(8,128)(2,1)S(1)}, bf16[480,384]{1,0:T(8,128)(2,1)S(1)}, u32[]{:S(2)}, u32[]{:S(2)}) collective-permute-start(bf16[480,384]{1,0:T(8,128)(2,1)S(1)} %get-tuple-element.37), channel_id=1, source_target_pairs={{0,4},{1,5},{4,8},{5,9},{8,12},{9,13},{12,14},{13,15},{14,10},{15,... | collective-permute-start | bytes 1105928 | tf_op jit(solution)/shard_map/ppermute | solution.py:371
  29.6 14.0 %collective-permute-start.6 = (bf16[480,384]{1,0:T(8,128)(2,1)S(1)}, bf16[480,384]{1,0:T(8,128)(2,1)S(1)}, u32[]{:S(2)}, u32[]{:S(2)}) collective-permute-start(bf16[480,384]{1,0:T(8,128)(2,1)S(1)} %get-tuple-element.43), channel_id=1, source_target_pairs={{0,2},{1,3},{4,0},{5,1},{8,4},{9,5},{12,8},{13,9},{14,12},{15,13},... | collective-permute-start | bytes 1105928 | tf_op jit(solution)/shard_map/ppermute | solution.py:371
  31.1 17.3 %collective-permute-start.9 = (bf16[480,384]{1,0:T(8,128)(2,1)S(1)}, bf16[480,384]{1,0:T(8,128)(2,1)S(1)}, u32[]{:S(2)}, u32[]{:S(2)}) collective-permute-start(bf16[480,384]{1,0:T(8,128)(2,1)S(1)} %get-tuple-element.46), channel_id=1, source_target_pairs={{0,4},{1,5},{4,8},{5,9},{8,12},{9,13},{12,14},{13,15},{14,10},{15,... | collective-permute-start | bytes 1105928 | tf_op jit(solution)/shard_map/ppermute | solution.py:371
  31.6 17.4 %collective-permute-start.12 = (bf16[480,384]{1,0:T(8,128)(2,1)S(1)}, bf16[480,384]{1,0:T(8,128)(2,1)S(1)}, u32[]{:S(2)}, u32[]{:S(2)}) collective-permute-start(bf16[480,384]{1,0:T(8,128)(2,1)S(1)} %get-tuple-element.49), channel_id=1, source_target_pairs={{0,2},{1,3},{4,0},{5,1},{8,4},{9,5},{12,8},{13,9},{14,12},{15,13},... | collective-permute-start | bytes 1105928 | tf_op jit(solution)/shard_map/ppermute | solution.py:371
  43.7 14.0 %copy-start.7 = (s32[16,16]{1,0:T(8,128)S(1)}, s32[16,16]{1,0:T(8,128)}, u32[]{:S(2)}) copy-start(s32[16,16]{1,0:T(8,128)} %constant.12.clone.table) | copy-start | bytes 3076
  43.7 17.3 %collective-permute-start.7 = (bf16[480,384]{1,0:T(8,128)(2,1)S(1)}, bf16[480,384]{1,0:T(8,128)(2,1)S(1)}, u32[]{:S(2)}, u32[]{:S(2)}) collective-permute-start(bf16[480,384]{1,0:T(8,128)(2,1)S(1)} %add_convert_fusion.6), channel_id=1, source_target_pairs={{0,2},{1,3},{4,0},{5,1},{8,4},{9,5},{12,8},{13,9},{14,12},{15,13},... | collective-permute-start | bytes 1105928 | tf_op jit(solution)/shard_map/ppermute | solution.py:371
  45.9 11.7 %collective-permute-start.3 = (bf16[480,384]{1,0:T(8,128)(2,1)S(1)}, bf16[480,384]{1,0:T(8,128)(2,1)S(1)}, u32[]{:S(2)}, u32[]{:S(2)}) collective-permute-start(bf16[480,384]{1,0:T(8,128)(2,1)S(1)} %add_convert_fusion.9), channel_id=1, source_target_pairs={{0,4},{1,5},{4,8},{5,9},{8,12},{9,13},{12,14},{13,15},{14,10},{15,... | collective-permute-start | bytes 1105928 | tf_op jit(solution)/shard_map/ppermute | solution.py:371
  48.5 17.9 %collective-permute-start.10 = (bf16[480,384]{1,0:T(8,128)(2,1)S(1)}, bf16[480,384]{1,0:T(8,128)(2,1)S(1)}, u32[]{:S(2)}, u32[]{:S(2)}) collective-permute-start(bf16[480,384]{1,0:T(8,128)(2,1)S(1)} %add_convert_fusion.4), channel_id=1, source_target_pairs={{0,4},{1,5},{4,8},{5,9},{8,12},{9,13},{12,14},{13,15},{14,10},{15,... | collective-permute-start | bytes 1105928 | tf_op jit(solution)/shard_map/ppermute | solution.py:371
  49.1 15.7 %collective-permute-start.13 = (bf16[480,384]{1,0:T(8,128)(2,1)S(1)}, bf16[480,384]{1,0:T(8,128)(2,1)S(1)}, u32[]{:S(2)}, u32[]{:S(2)}) collective-permute-start(bf16[480,384]{1,0:T(8,128)(2,1)S(1)} %add_convert_fusion.2), channel_id=1, source_target_pairs={{0,2},{1,3},{4,0},{5,1},{8,4},{9,5},{12,8},{13,9},{14,12},{15,13},... | collective-permute-start | bytes 1105928 | tf_op jit(solution)/shard_map/ppermute | solution.py:371
  61.1 13.6 %copy-start.6 = (s32[16,16]{1,0:T(8,128)S(1)}, s32[16,16]{1,0:T(8,128)}, u32[]{:S(2)}) copy-start(s32[16,16]{1,0:T(8,128)} %constant.13.clone.table) | copy-start | bytes 3076
  61.1 20.9 %collective-permute-start.8 = (bf16[480,384]{1,0:T(8,128)(2,1)S(1)}, bf16[480,384]{1,0:T(8,128)(2,1)S(1)}, u32[]{:S(2)}, u32[]{:S(2)}) collective-permute-start(bf16[480,384]{1,0:T(8,128)(2,1)S(1)} %add_convert_fusion.5), channel_id=1, source_target_pairs={{0,2},{1,3},{4,0},{5,1},{8,4},{9,5},{12,8},{13,9},{14,12},{15,13},... | collective-permute-start | bytes 1105928 | tf_op jit(solution)/shard_map/ppermute | solution.py:371
  63.1 11.6 %collective-permute-start.4 = (bf16[480,384]{1,0:T(8,128)(2,1)S(1)}, bf16[480,384]{1,0:T(8,128)(2,1)S(1)}, u32[]{:S(2)}, u32[]{:S(2)}) collective-permute-start(bf16[480,384]{1,0:T(8,128)(2,1)S(1)} %add_convert_fusion.8), channel_id=1, source_target_pairs={{0,4},{1,5},{4,8},{5,9},{8,12},{9,13},{12,14},{13,15},{14,10},{15,... | collective-permute-start | bytes 1105928 | tf_op jit(solution)/shard_map/ppermute | solution.py:371
  64.8 15.5 %collective-permute-start.14 = (bf16[480,384]{1,0:T(8,128)(2,1)S(1)}, bf16[480,384]{1,0:T(8,128)(2,1)S(1)}, u32[]{:S(2)}, u32[]{:S(2)}) collective-permute-start(bf16[480,384]{1,0:T(8,128)(2,1)S(1)} %add_convert_fusion.1), channel_id=1, source_target_pairs={{0,2},{1,3},{4,0},{5,1},{8,4},{9,5},{12,8},{13,9},{14,12},{15,13},... | collective-permute-start | bytes 1105928 | tf_op jit(solution)/shard_map/ppermute | solution.py:371
  66.5 16.1 %collective-permute-start.11 = (bf16[480,384]{1,0:T(8,128)(2,1)S(1)}, bf16[480,384]{1,0:T(8,128)(2,1)S(1)}, u32[]{:S(2)}, u32[]{:S(2)}) collective-permute-start(bf16[480,384]{1,0:T(8,128)(2,1)S(1)} %add_convert_fusion.3), channel_id=1, source_target_pairs={{0,4},{1,5},{4,8},{5,9},{8,12},{9,13},{12,14},{13,15},{14,10},{15,... | collective-permute-start | bytes 1105928 | tf_op jit(solution)/shard_map/ppermute | solution.py:371
  78.3 12.6 %copy-start.5 = (s32[16,5]{1,0:T(8,128)S(1)}, s32[16,5]{1,0:T(8,128)}, u32[]{:S(2)}) copy-start(s32[16,5]{1,0:T(8,128)} %constant.14.clone.place) | copy-start | bytes 964
  78.4 9.6 %collective-permute-start.5 = (bf16[480,384]{1,0:T(8,128)(2,1)S(1)}, bf16[480,384]{1,0:T(8,128)(2,1)S(1)}, u32[]{:S(2)}, u32[]{:S(2)}) collective-permute-start(bf16[480,384]{1,0:T(8,128)(2,1)S(1)} %add_convert_fusion.7), channel_id=1, source_target_pairs={{0,4},{1,5},{4,8},{5,9},{8,12},{9,13},{12,14},{13,15},{14,10},{15,... | collective-permute-start | bytes 1105928 | tf_op jit(solution)/shard_map/ppermute | solution.py:371
  80.4 10.5 %collective-permute-start.15 = (bf16[480,384]{1,0:T(8,128)(2,1)S(1)}, bf16[480,384]{1,0:T(8,128)(2,1)S(1)}, u32[]{:S(2)}, u32[]{:S(2)}) collective-permute-start(bf16[480,384]{1,0:T(8,128)(2,1)S(1)} %add_convert_fusion), channel_id=1, source_target_pairs={{0,2},{1,3},{4,0},{5,1},{8,4},{9,5},{12,8},{13,9},{14,12},{15,13},... | collective-permute-start | bytes 1105928 | tf_op jit(solution)/shard_map/ppermute | solution.py:371
  93.0 7.1 %collective-permute-start.16 = (bf16[384,384]{1,0:T(8,128)(2,1)S(1)}, bf16[384,384]{1,0:T(8,128)(2,1)S(1)}, u32[]{:S(2)}, u32[]{:S(2)}) collective-permute-start(bf16[384,384]{1,0:T(8,128)(2,1)S(1)} %get-tuple-element.54), channel_id=1, source_target_pairs={{0,2},{1,10},{2,4},{3,12},{4,6},{5,14},{6,0},{7,8},{8,5},{9,11},{1... | collective-permute-start | bytes 884744 | tf_op jit(solution)/shard_map/ppermute | solution.py:416
  93.2 16.2 %collective-permute-start.17 = (bf16[384,384]{1,0:T(8,128)(2,1)S(1)}, bf16[384,384]{1,0:T(8,128)(2,1)S(1)}, u32[]{:S(2)}, u32[]{:S(2)}) collective-permute-start(bf16[384,384]{1,0:T(8,128)(2,1)S(1)} %get-tuple-element.55), channel_id=1, source_target_pairs={{0,4},{1,8},{2,6},{3,10},{4,0},{5,12},{6,2},{7,14},{8,3},{9,13},{1... | collective-permute-start | bytes 884744 | tf_op jit(solution)/shard_map/ppermute | solution.py:415

commit v5 on v4

--- a/solution.py
+++ b/solution.py
@@ -10,8 +10,8 @@
 
 EXPERTS = 8
 CAP = 384
-BATCH = 96
-WINDOW = 128
+BATCH = 48
+WINDOW = 64
 SNAKE = (0, 2, 4, 6, 7, 5, 3, 1)
 F32, BF16, I32 = jnp.float32, jnp.bfloat16, jnp.int32
 
@@ -133,9 +133,9 @@
         cost_estimate=pl.CostEstimate(
             flops=4 * tokens * depth * width, bytes_accessed=2 * (rows.shape[0] + tokens) * width, transcendentals=0
         ),
-        compiler_params=pltpu.CompilerParams(vmem_limit_bytes=56 << 20),
+        compiler_params=pltpu.CompilerParams(vmem_limit_bytes=24 << 20),
         name="pick_first" if first else "pick_second",
-    )(*args, rows)
+    )(*args, pltpu.with_memory_space_constraint(rows, pltpu.HBM))
 
 
 def merge_kernel(first, coef_ref, ours_ref, theirs_ref, *refs):
@@ -239,6 +239,12 @@
     return b % 4 < 2
 
 
+def fourth_column(b, e):
+    if is_diagonal(b, e):
+        return (b + 2) % 4
+    return (b + 3) % 4 if e == 1 else b % 4
+
+
 ROUNDS = (
     ((0, 4), (1, 4), (1, 3), (0, 5)),
     ((0, 3), (1, 5), (1, 2), (0, 6)),
@@ -256,8 +262,10 @@
                 table[b, e, n, :2] = (q % 4 + (0 if q // 4 == e else 4), owned_columns(q, e)[x])
                 if is_diagonal(q, e):
                     lead, other = (q % 4, (q + 2) % 4) if leads(q) else ((q + 2) % 4, q % 4)
-                    first = lead * width + (0 if leads(q) else width // 2) + x * STRIP
-                    table[b, e, n, 2:] = (first // STRIP, other)
+                    first = lead * width + (0 if leads(q) else width // 2)
+                else:
+                    first, other = (4 + q % 4) * width, fourth_column(q, e)
+                table[b, e, n, 2:] = (first // STRIP + x, other)
     return table.reshape(16, -1)
 
 
@@ -287,74 +295,74 @@
     table = np.zeros((8, 2, 5), np.int32)
     for b in range(8):
         for e in range(2):
-            own = owned_columns(b, e)
-            if is_diagonal(b, e):
-                table[b, e] = (own[0], own[1], (b + 3) % 4, (b + 2) % 4, 1 if leads(b) else 2)
-            elif e == 1:
-                table[b, e] = (own[0], own[1], (b + 2) % 4, (b + 3) % 4, 0)
-            else:
-                table[b, e] = (own[0], own[1], (b + 3) % 4, b % 4, 0)
+            diagonal = is_diagonal(b, e)
+            mirrored = (b + 2) % 4 if not diagonal and e == 1 else (b + 3) % 4
+            kind = (1 if leads(b) else 2) if diagonal else 0
+            table[b, e] = (*owned_columns(b, e), mirrored, fourth_column(b, e), kind)
     return table
 
 
-def total_kernel(scale, place, own0, own1, right0, left0, right1, left1, out_ref, one, other, share, made, sems):
+def total(own, right, left, rows):
+    return own[rows, :] + right[rows, :].astype(F32) + left[rows, :].astype(F32)
+
+
+def outgoing_kernel(scale, place, own0, own1, right0, left0, right1, left1, one, other, share):
     width = one.shape[0]
-    me = my_row()
-
-    def total(own, right, left, rows):
-        return (own[rows, :] + right[rows, :].astype(F32) + left[rows, :].astype(F32)) * scale
-
+    kind = place[my_row(), 4]
     block, strip = slice(0, width), slice(width, width + STRIP)
-    made[0] = total(own0, right0, left0, block)
-    made[1] = total(own1, right1, left1, block)
+    one[...] = (total(own1, right1, left1, block) * scale).astype(BF16)
+    share[:STRIP, :] = total(own0, right0, left0, strip) * scale
+    share[STRIP:, :] = total(own1, right1, left1, strip) * scale
+
+    @pl.when(kind == 0)
+    def _():
+        other[...] = ((total(own0, right0, left0, block) * scale).T[width // 2 :, :]).astype(BF16)
+
+    @pl.when(kind > 0)
+    def _():
+        other[...] = share[...].astype(BF16)
+
+
+def put(place, n, made, out_ref, sem):
+    width = made.shape[0]
+    at = pl.ds(pl.multiple_of(place[my_row(), n] * width, 128), width)
+    return pltpu.make_async_copy(made, out_ref.at[:, at], sem)
+
+
+def own_kernel(scale, place, own0, own1, right0, left0, right1, left1, out_ref, made, sems):
+    block = slice(0, made.shape[1])
     copies = []
-    for n in range(2):
-        at = pl.ds(pl.multiple_of(place[me, n] * width, 128), width)
-        copies.append(pltpu.make_async_copy(made.at[n], out_ref.at[:, at], sems.at[n]))
+    for n, parts in enumerate(((own0, right0, left0), (own1, right1, left1))):
+        made[n] = total(*parts, block) * scale
+        copies.append(put(place, n, made.at[n], out_ref, sems.at[n]))
         copies[-1].start()
-    one[...] = made[1].astype(BF16)
-    share[:STRIP, :] = total(own0, right0, left0, strip)
-    share[STRIP:, :] = total(own1, right1, left1, strip)
-
-    @pl.when(place[me, 4] == 0)
-    def _():
-        other[...] = made[0].astype(BF16)
-
-    @pl.when(place[me, 4] > 0)
-    def _():
-        other[: width // 2, :] = share[...].astype(BF16)
-        other[width // 2 :, :] = jnp.zeros((width - width // 2, width), BF16)
-
     for copy in copies:
         copy.wait()
 
 
-def mirror_kernel(place, share, one, other, result_ref, out_ref, made, sems):
-    width = one.shape[0]
-    me = my_row()
-    made[0] = one[...].astype(F32).T
-    copies = []
-    for n in range(2):
-        at = pl.ds(pl.multiple_of(place[me, 2 + n] * width, 128), width)
-        copies.append(pltpu.make_async_copy(made.at[n], out_ref.at[:, at], sems.at[n]))
-    copies[0].start()
-
-    @pl.when(place[me, 4] == 0)
+def one_kernel(place, one, result_ref, out_ref, made, sem):
+    made[...] = one[...].astype(F32).T
+    copy = put(place, 2, made, out_ref, sem)
+    copy.start()
+    copy.wait()
+
+
+def other_kernel(place, share, other, result_ref, out_ref, made, sem):
+    kind = place[my_row(), 4]
+    half = other.shape[0]
+
+    @pl.when(kind < 2)
     def _():
-        made[1] = other[...].astype(F32).T
-
-    @pl.when(place[me, 4] == 1)
+        made[:half, :] = share[...]
+        made[half:, :] = other[...].astype(F32)
+
+    @pl.when(kind == 2)
     def _():
-        made[1, : width // 2, :] = share[...]
-        made[1, width // 2 :, :] = other[: width // 2, :].astype(F32)
-
-    @pl.when(place[me, 4] == 2)
-    def _():
-        made[1] = jnp.concatenate([other[: width // 2, :].astype(F32), share[...]], axis=0).T
-
-    copies[1].start()
-    for copy in copies:
-        copy.wait()
+        made[...] = jnp.concatenate([other[...].astype(F32), share[...]], axis=0).T
+
+    copy = put(place, 3, made, out_ref, sem)
+    copy.start()
+    copy.wait()
 
 
 def symmetric_moment(mine, turned, total_tokens):
@@ -391,39 +399,46 @@
 
     place = jnp.asarray(place_table().reshape(16, -1))
     smem, vmem, any_ = [pl.BlockSpec(memory_space=m) for m in (pltpu.SMEM, pltpu.VMEM, pl.ANY)]
-    scratch = [pltpu.VMEM((2, width, width), F32), pltpu.SemaphoreType.DMA((2,))]
-    block = jax.ShapeDtypeStruct((width, width), BF16)
     result = jax.ShapeDtypeStruct((width, 4 * width), F32)
-    result, one, other, share = pl.pallas_call(
-        functools.partial(total_kernel, 1.0 / total_tokens),
-        out_shape=[result, block, block, jax.ShapeDtypeStruct((2 * STRIP, width), F32)],
+    params = pltpu.CompilerParams(vmem_limit_bytes=24 << 20)
+    sums = (blocks[0, 0], blocks[1, 0], arrived[0, True], arrived[0, False], arrived[1, True], arrived[1, False])
+    scale = 1.0 / total_tokens
+    one, other, share = pl.pallas_call(
+        functools.partial(outgoing_kernel, scale),
+        out_shape=[
+            jax.ShapeDtypeStruct((width, width), BF16),
+            jax.ShapeDtypeStruct((2 * STRIP, width), BF16),
+            jax.ShapeDtypeStruct((2 * STRIP, width), F32),
+        ],
         in_specs=[smem] + [vmem] * 6,
-        out_specs=[any_, vmem, vmem, vmem],
-        scratch_shapes=scratch,
-        compiler_params=pltpu.CompilerParams(vmem_limit_bytes=32 << 20),
-        name="total",
-    )(
-        place,
-        blocks[0, 0],
-        blocks[1, 0],
-        arrived[0, True],
-        arrived[0, False],
-        arrived[1, True],
-        arrived[1, False],
-    )
+        out_specs=[vmem] * 3,
+        compiler_params=params,
+        name="outgoing",
+    )(place, *sums)
     perm_one, perm_other = mirror_perms()
+    one = lax.ppermute(one, both, perm_one)
     other = lax.ppermute(other, both, perm_other)
-    one = lax.ppermute(one, both, perm_one)
-    return pl.pallas_call(
-        mirror_kernel,
-        out_shape=jax.ShapeDtypeStruct((width, 4 * width), F32),
-        in_specs=[smem, vmem, vmem, vmem, any_],
+    partial_result = pl.pallas_call(
+        functools.partial(own_kernel, scale),
+        out_shape=result,
+        in_specs=[smem] + [vmem] * 6,
         out_specs=any_,
-        scratch_shapes=scratch,
-        input_output_aliases={4: 0},
-        compiler_params=pltpu.CompilerParams(vmem_limit_bytes=32 << 20),
-        name="mirror",
-    )(place, share, one, other, result)
+        scratch_shapes=[pltpu.VMEM((2, width, width), F32), pltpu.SemaphoreType.DMA((2,))],
+        compiler_params=params,
+        name="own",
+    )(place, *sums)
+    for kernel, args, name in ((one_kernel, (one,), "one"), (other_kernel, (share, other), "other")):
+        partial_result = pl.pallas_call(
+            kernel,
+            out_shape=result,
+            in_specs=[smem] + [vmem] * len(args) + [any_],
+            out_specs=any_,
+            scratch_shapes=[pltpu.VMEM((width, width), F32), pltpu.SemaphoreType.DMA],
+            input_output_aliases={len(args) + 1: 0},
+            compiler_params=params,
+            name=name,
+        )(place, *args, partial_result)
+    return partial_result
 
 
 def per_device(expert_ids, gates, expert_out):

time: 112 us -> 101 us (0.902)
  the two profiles are of different devices: /device:TPU:6 before, /device:TPU:1 now
where the time goes in v5:
time: 101 us
  waiting for transfers between devices  43.2 us (43%)
  Pallas kernels  36.5 us (36%)
  starting transfers between devices  18.9 us (19%)
  local copies, waits for them, and re-layouts  1.41 us (1%)
    ppermute x14, waiting for transfers between devices, hop(): lax.ppermute(value, both, ring_perm(1 if key[1] <= (4 if key[0] == 0 else...  35.2 us
    pallas_call x4, Pallas kernels, moment_blocks(): pl.pallas_call(functools.partial(blocks_kernel, count), out_shape=[jax.Sh...  14.7 us
    ppermute x14, starting transfers between devices, hop(): lax.ppermute(value, both, ring_perm(1 if key[1] <= (4 if key[0] == 0 else...  13.8 us
    pallas_call x2, Pallas kernels, pick_half(): pl.pallas_call(functools.partial(pick_kernel, first), out_shape=out_shape...  10.1 us
    pallas_call x2, Pallas kernels, merge(): pl.pallas_call(functools.partial(merge_kernel, first), out_shape=out_shap...  5.63 us
    ppermute x1, starting transfers between devices, symmetric_moment(): one = lax.ppermute(one, both, perm_one)  3.85 us
    ppermute x1, waiting for transfers between devices, symmetric_moment(): one = lax.ppermute(one, both, perm_one)  3.67 us
    pallas_call x2, Pallas kernels, symmetric_moment(): pl.pallas_call(kernel, out_shape=result, in_specs=[smem] + [vmem] * len(a...  3.21 us
  transfers between devices with their start and end apart: 18, of which 11 were waited for; matrix products, arithmetic and copies ran while one was open for 1% of the time, Pallas kernels for 22%

profile of v5, /device:TPU:1, one launch (start us, length us, event | category | flops | bytes accessed | tf_op | source)
XLA Modules:
  0.0 101.0 jit_solution(4758175948647375030)
XLA Ops:
  0.0 0.7 copy-done.5
  0.7 0.7 copy-done.6
  1.4 5.3 %pick_first.1 = (bf16[768,1536]{1,0:T(8,128)(2,1)S(1)}, bf16[1536,256]{1,0:T(8,128)(2,1)S(1)}, s32[16,128]{1,0:T(8,128)S(1)}, f32[768,128]{1,0:T(8,128)S(1)}) custom-call(s32[2,768]{1,0:T(2,128)S(1)} %bitcast.2, f32[2,768]{1,0:T(2,128)S(1)} %bitcast.3, bf16[1536,3072]{1,0:T(8,128)(2,1)} %refs_3_.1), custom_call_target="tpu_custom_call" | custom-call | flops 1207959552 | bytes 7077888 | tf_op jit(solution)/shard_map/pick_first/pallas_call | solution.py:127
  6.7 0.1 collective-permute-start.1
  6.9 4.8 %pick_second.1.ours_ref = bf16[768,1536]{1,0:T(8,128)(2,1)S(1)} custom-call(s32[16,128]{1,0:T(8,128)S(1)} %get-tuple-element.32.refs_0_, bf16[1536,256]{1,0:T(8,128)(2,1)S(1)} %get-tuple-element.33.refs_1_, f32[768,128]{1,0:T(8,128)S(1)} %get-tuple-element.30.refs_2_.coef_ref, bf16[1536,3072]{1,0:T(8,128)(2,1)} %refs_3_.1), custom_call_target="tpu_custom_call" | custom-call | flops 1207959552 | bytes 7077888 | tf_op jit(solution)/shard_map/pick_second/pallas_call | solution.py:127
  11.6 0.5 collective-permute-start
  12.1 0.0 collective-permute-done.1.theirs_ref
  12.1 2.9 %merge_first.1 = (bf16[768,1536]{1,0:T(8,128)(2,1)S(1)}, bf16[3072,768]{1,0:T(8,128)(2,1)S(1)}) custom-call(f32[768,128]{1,0:T(8,128)S(1)} %get-tuple-element.30.refs_2_.coef_ref, bf16[768,1536]{1,0:T(8,128)(2,1)S(1)} %pick_second.1.ours_ref, bf16[768,1536]{1,0:T(8,128)(2,1)S(1)} %collective-permute-done.1.theirs_ref), custom_call_target="tpu_custom_call" | custom-call | flops 4718592 | bytes 7077888 | tf_op jit(solution)/shard_map/merge_first/pallas_call | solution.py:165
  15.1 1.2 %collective-permute-done.theirs_ref = bf16[768,1536]{1,0:T(8,128)(2,1)S(1)} collective-permute-done((bf16[768,1536]{1,0:T(8,128)(2,1)S(1)}, bf16[768,1536]{1,0:T(8,128)(2,1)S(1)}, u32[]{:S(2)}, u32[]{:S(2)}) %collective-permute-start) | collective-permute-done | bytes 2359328 | tf_op jit(solution)/shard_map/ppermute | solution.py:454
  16.3 2.7 %merge_second.1.turned_ref = bf16[3072,768]{1,0:T(8,128)(2,1)S(1)} custom-call(f32[768,128]{1,0:T(8,128)S(1)} %get-tuple-element.30.refs_2_.coef_ref, bf16[768,1536]{1,0:T(8,128)(2,1)S(1)} %get-tuple-element.31.ours_ref, bf16[768,1536]{1,0:T(8,128)(2,1)S(1)} %collective-permute-done.theirs_ref, ...), custom_call_target="tpu_custom_call", output_to_operand_aliasing={{}: (3, {})} | custom-call | flops 4718592 | bytes 7077888 | tf_op jit(solution)/shard_map/merge_second/pallas_call | solution.py:165
  19.0 0.0 copy-start.3
  19.0 3.7 %blocks0.1 = (bf16[480,384]{1,0:T(8,128)(2,1)S(1)}, bf16[480,384]{1,0:T(8,128)(2,1)S(1)}, bf16[480,384]{1,0:T(8,128)(2,1)S(1)}, bf16[480,384]{1,0:T(8,128)(2,1)S(1)}) custom-call(s32[16,16]{1,0:T(8,128)S(1)} %copy-done.4, bf16[3072,768]{1,0:T(8,128)(2,1)S(1)} %merge_second.1.turned_ref, bf16[768,1536]{1,0:T(8,128)(2,1)S(1)} %get-tuple-element.35.mine_ref), custom_call_target="tpu_custom_call" | custom-call | flops 905969664 | bytes 9437184 | tf_op jit(solution)/shard_map/blocks0/pallas_call | solution.py:207
  22.7 2.7 %collective-permute-start.2 = (bf16[480,384]{1,0:T(8,128)(2,1)S(1)}, bf16[480,384]{1,0:T(8,128)(2,1)S(1)}, u32[]{:S(2)}, u32[]{:S(2)}) collective-permute-start(bf16[480,384]{1,0:T(8,128)(2,1)S(1)} %get-tuple-element.36), channel_id=1, source_target_pairs={{0,4},{1,5},{4,8},{5,9},{8,12},{9,13},{12,14},{13,15},{14,10},{15,... | collective-permute-start | bytes 1105928 | tf_op jit(solution)/shard_map/ppermute | solution.py:379
  25.4 0.0 collective-permute-start.6
  25.4 1.5 %collective-permute-start.9 = (bf16[480,384]{1,0:T(8,128)(2,1)S(1)}, bf16[480,384]{1,0:T(8,128)(2,1)S(1)}, u32[]{:S(2)}, u32[]{:S(2)}) collective-permute-start(bf16[480,384]{1,0:T(8,128)(2,1)S(1)} %get-tuple-element.45), channel_id=1, source_target_pairs={{0,4},{1,5},{4,8},{5,9},{8,12},{9,13},{12,14},{13,15},{14,10},{15,... | collective-permute-start | bytes 1105928 | tf_op jit(solution)/shard_map/ppermute | solution.py:379
  26.9 0.0 collective-permute-start.12
  26.9 7.3 %collective-permute-done.2.refs_0_ = bf16[480,384]{1,0:T(8,128)(2,1)S(1)} collective-permute-done((bf16[480,384]{1,0:T(8,128)(2,1)S(1)}, bf16[480,384]{1,0:T(8,128)(2,1)S(1)}, u32[]{:S(2)}, u32[]{:S(2)}) %collective-permute-start.2) | collective-permute-done | bytes 368672 | tf_op jit(solution)/shard_map/ppermute | solution.py:379
  34.2 3.8 %blocks1.1 = (f32[480,384]{1,0:T(8,128)S(1)}, f32[480,384]{1,0:T(8,128)S(1)}, f32[480,384]{1,0:T(8,128)S(1)}, f32[480,384]{1,0:T(8,128)S(1)}) custom-call(s32[16,16]{1,0:T(8,128)S(1)} %copy-done.3, bf16[3072,768]{1,0:T(8,128)(2,1)S(1)} %merge_second.1.turned_ref, bf16[768,1536]{1,0:T(8,128)(2,1)S(1)} %get-tuple-element.35.mine_ref, ...), custom_call_target="tpu_custom_call" | custom-call | flops 905969664 | bytes 9437184 | tf_op jit(solution)/shard_map/blocks1/pallas_call | solution.py:207
  38.0 0.0 collective-permute-done.6
  38.0 0.1 add_convert_fusion.6
  38.1 0.0 copy-start.2
  38.1 1.3 %collective-permute-start.7 = (bf16[480,384]{1,0:T(8,128)(2,1)S(1)}, bf16[480,384]{1,0:T(8,128)(2,1)S(1)}, u32[]{:S(2)}, u32[]{:S(2)}) collective-permute-start(bf16[480,384]{1,0:T(8,128)(2,1)S(1)} %add_convert_fusion.6), channel_id=1, source_target_pairs={{0,2},{1,3},{4,0},{5,1},{8,4},{9,5},{12,8},{13,9},{14,12},{15,13},... | collective-permute-start | bytes 1105928 | tf_op jit(solution)/shard_map/ppermute | solution.py:379
  39.4 0.1 add_convert_fusion.9
  39.5 0.3 collective-permute-start.3
  39.7 2.3 %collective-permute-done.9 = bf16[480,384]{1,0:T(8,128)(2,1)S(1)} collective-permute-done((bf16[480,384]{1,0:T(8,128)(2,1)S(1)}, bf16[480,384]{1,0:T(8,128)(2,1)S(1)}, u32[]{:S(2)}, u32[]{:S(2)}) %collective-permute-start.9) | collective-permute-done | bytes 368672 | tf_op jit(solution)/shard_map/ppermute | solution.py:379
  42.1 0.1 add_convert_fusion.4
  42.2 1.3 %collective-permute-start.10 = (bf16[480,384]{1,0:T(8,128)(2,1)S(1)}, bf16[480,384]{1,0:T(8,128)(2,1)S(1)}, u32[]{:S(2)}, u32[]{:S(2)}) collective-permute-start(bf16[480,384]{1,0:T(8,128)(2,1)S(1)} %add_convert_fusion.4), channel_id=1, source_target_pairs={{0,4},{1,5},{4,8},{5,9},{8,12},{9,13},{12,14},{13,15},{14,10},{15,... | collective-permute-start | bytes 1105928 | tf_op jit(solution)/shard_map/ppermute | solution.py:379
  43.5 0.0 collective-permute-done.12
  43.5 0.1 add_convert_fusion.2
  43.6 0.3 collective-permute-start.13
  43.8 5.2 %collective-permute-done.3.refs_0_ = bf16[480,384]{1,0:T(8,128)(2,1)S(1)} collective-permute-done((bf16[480,384]{1,0:T(8,128)(2,1)S(1)}, bf16[480,384]{1,0:T(8,128)(2,1)S(1)}, u32[]{:S(2)}, u32[]{:S(2)}) %collective-permute-start.3) | collective-permute-done | bytes 368672 | tf_op jit(solution)/shard_map/ppermute | solution.py:379
  49.0 3.6 %blocks2.1 = (f32[480,384]{1,0:T(8,128)S(1)}, f32[480,384]{1,0:T(8,128)S(1)}, f32[480,384]{1,0:T(8,128)S(1)}, f32[480,384]{1,0:T(8,128)S(1)}) custom-call(s32[16,16]{1,0:T(8,128)S(1)} %copy-done.2, bf16[3072,768]{1,0:T(8,128)(2,1)S(1)} %merge_second.1.turned_ref, bf16[768,1536]{1,0:T(8,128)(2,1)S(1)} %get-tuple-element.35.mine_ref, ...), custom_call_target="tpu_custom_call" | custom-call | flops 905969664 | bytes 9437184 | tf_op jit(solution)/shard_map/blocks2/pallas_call | solution.py:207
  52.7 0.0 collective-permute-done.7
  52.7 0.1 add_convert_fusion.5
  52.8 0.0 copy-start.1
  52.8 0.8 collective-permute-start.8
  53.6 0.1 add_convert_fusion.8
  53.7 1.5 %collective-permute-start.4 = (bf16[480,384]{1,0:T(8,128)(2,1)S(1)}, bf16[480,384]{1,0:T(8,128)(2,1)S(1)}, u32[]{:S(2)}, u32[]{:S(2)}) collective-permute-start(bf16[480,384]{1,0:T(8,128)(2,1)S(1)} %add_convert_fusion.8), channel_id=1, source_target_pairs={{0,4},{1,5},{4,8},{5,9},{8,12},{9,13},{12,14},{13,15},{14,10},{15,... | collective-permute-start | bytes 1105928 | tf_op jit(solution)/shard_map/ppermute | solution.py:379
  55.2 3.7 %collective-permute-done.13 = bf16[480,384]{1,0:T(8,128)(2,1)S(1)} collective-permute-done((bf16[480,384]{1,0:T(8,128)(2,1)S(1)}, bf16[480,384]{1,0:T(8,128)(2,1)S(1)}, u32[]{:S(2)}, u32[]{:S(2)}) %collective-permute-start.13) | collective-permute-done | bytes 368672 | tf_op jit(solution)/shard_map/ppermute | solution.py:379
  58.8 0.1 add_convert_fusion.1
  58.9 0.4 collective-permute-start.14
  59.3 0.0 collective-permute-done.10
  59.3 0.1 add_convert_fusion.3
  59.4 1.2 %collective-permute-start.11 = (bf16[480,384]{1,0:T(8,128)(2,1)S(1)}, bf16[480,384]{1,0:T(8,128)(2,1)S(1)}, u32[]{:S(2)}, u32[]{:S(2)}) collective-permute-start(bf16[480,384]{1,0:T(8,128)(2,1)S(1)} %add_convert_fusion.3), channel_id=1, source_target_pairs={{0,4},{1,5},{4,8},{5,9},{8,12},{9,13},{12,14},{13,15},{14,10},{15,... | collective-permute-start | bytes 1105928 | tf_op jit(solution)/shard_map/ppermute | solution.py:379
  60.6 2.9 %collective-permute-done.4.refs_0_ = bf16[480,384]{1,0:T(8,128)(2,1)S(1)} collective-permute-done((bf16[480,384]{1,0:T(8,128)(2,1)S(1)}, bf16[480,384]{1,0:T(8,128)(2,1)S(1)}, u32[]{:S(2)}, u32[]{:S(2)}) %collective-permute-start.4) | collective-permute-done | bytes 368672 | tf_op jit(solution)/shard_map/ppermute | solution.py:379
  63.4 3.6 %blocks3.1 = (f32[480,384]{1,0:T(8,128)S(1)}, f32[480,384]{1,0:T(8,128)S(1)}, f32[480,384]{1,0:T(8,128)S(1)}, f32[480,384]{1,0:T(8,128)S(1)}) custom-call(s32[16,16]{1,0:T(8,128)S(1)} %copy-done.1, bf16[3072,768]{1,0:T(8,128)(2,1)S(1)} %merge_second.1.turned_ref, bf16[768,1536]{1,0:T(8,128)(2,1)S(1)} %get-tuple-element.35.mine_ref, ...), custom_call_target="tpu_custom_call" | custom-call | flops 905969664 | bytes 9437184 | tf_op jit(solution)/shard_map/blocks3/pallas_call | solution.py:207
  67.0 0.0 copy-start
  67.1 0.1 add_convert_fusion.7
  67.1 2.5 %collective-permute-start.5 = (bf16[480,384]{1,0:T(8,128)(2,1)S(1)}, bf16[480,384]{1,0:T(8,128)(2,1)S(1)}, u32[]{:S(2)}, u32[]{:S(2)}) collective-permute-start(bf16[480,384]{1,0:T(8,128)(2,1)S(1)} %add_convert_fusion.7), channel_id=1, source_target_pairs={{0,4},{1,5},{4,8},{5,9},{8,12},{9,13},{12,14},{13,15},{14,10},{15,... | collective-permute-start | bytes 1105928 | tf_op jit(solution)/shard_map/ppermute | solution.py:379
  69.6 5.0 %collective-permute-done.14 = bf16[480,384]{1,0:T(8,128)(2,1)S(1)} collective-permute-done((bf16[480,384]{1,0:T(8,128)(2,1)S(1)}, bf16[480,384]{1,0:T(8,128)(2,1)S(1)}, u32[]{:S(2)}, u32[]{:S(2)}) %collective-permute-start.14) | collective-permute-done | bytes 368672 | tf_op jit(solution)/shard_map/ppermute | solution.py:379
  74.6 0.1 add_convert_fusion
  74.7 0.1 collective-permute-start.15
  74.8 0.0 collective-permute-done.8.left0
  74.8 0.0 collective-permute-done.11.right1
  74.8 4.4 %collective-permute-done.5.right0 = bf16[480,384]{1,0:T(8,128)(2,1)S(1)} collective-permute-done((bf16[480,384]{1,0:T(8,128)(2,1)S(1)}, bf16[480,384]{1,0:T(8,128)(2,1)S(1)}, u32[]{:S(2)}, u32[]{:S(2)}) %collective-permute-start.5) | collective-permute-done | bytes 368672 | tf_op jit(solution)/shard_map/ppermute | solution.py:379
  79.2 4.3 %collective-permute-done.15.left1 = bf16[480,384]{1,0:T(8,128)(2,1)S(1)} collective-permute-done((bf16[480,384]{1,0:T(8,128)(2,1)S(1)}, bf16[480,384]{1,0:T(8,128)(2,1)S(1)}, u32[]{:S(2)}, u32[]{:S(2)}) %collective-permute-start.15) | collective-permute-done | bytes 368672 | tf_op jit(solution)/shard_map/ppermute | solution.py:379
  83.6 1.0 %outgoing.1 = (bf16[384,384]{1,0:T(8,128)(2,1)S(1)}, bf16[192,384]{1,0:T(8,128)(2,1)S(1)}, f32[192,384]{1,0:T(8,128)S(1)}) custom-call(s32[16,5]{1,0:T(8,128)S(1)} %copy-done, f32[480,384]{1,0:T(8,128)S(1)} %get-tuple-element.39.own0, f32[480,384]{1,0:T(8,128)S(1)} %get-tuple-element.40.own1, bf16[480,384]{1,0:T(8,128)(2,1)S(1)} %collective-permute-done.5.right0, ...), custom_call_target="tpu_custom_call" | custom-call | tf_op jit(solution)/shard_map/outgoing/pallas_call | solution.py:406
  84.6 3.8 %collective-permute-start.17 = (bf16[384,384]{1,0:T(8,128)(2,1)S(1)}, bf16[384,384]{1,0:T(8,128)(2,1)S(1)}, u32[]{:S(2)}, u32[]{:S(2)}) collective-permute-start(bf16[384,384]{1,0:T(8,128)(2,1)S(1)} %get-tuple-element.54), channel_id=1, source_target_pairs={{0,2},{1,10},{2,4},{3,12},{4,6},{5,14},{6,0},{7,8},{8,5},{9,11},{1... | collective-permute-start | bytes 884744 | tf_op jit(solution)/shard_map/ppermute | solution.py:419
  88.4 0.6 collective-permute-start.16
  89.1 1.8 %own.1.result_ref = f32[384,1536]{1,0:T(8,128)} custom-call(s32[16,5]{1,0:T(8,128)S(1)} %copy-done, f32[480,384]{1,0:T(8,128)S(1)} %get-tuple-element.39.own0, f32[480,384]{1,0:T(8,128)S(1)} %get-tuple-element.40.own1, bf16[480,384]{1,0:T(8,128)(2,1)S(1)} %collective-permute-done.5.right0, bf16[480,384]{1,0:T(8,128)(2,1)S(1)} %collective-permute-done.8.left0, ...), custom_call_target="tpu_custom_call" | custom-call | tf_op jit(solution)/shard_map/own/pallas_call | solution.py:421
  90.9 3.7 %collective-permute-done.17.one = bf16[384,384]{1,0:T(8,128)(2,1)S(1)} collective-permute-done((bf16[384,384]{1,0:T(8,128)(2,1)S(1)}, bf16[384,384]{1,0:T(8,128)(2,1)S(1)}, u32[]{:S(2)}, u32[]{:S(2)}) %collective-permute-start.17) | collective-permute-done | bytes 294944 | tf_op jit(solution)/shard_map/ppermute | solution.py:419
  94.6 1.7 %one.1.result_ref = f32[384,1536]{1,0:T(8,128)} custom-call(s32[16,5]{1,0:T(8,128)S(1)} %copy-done, bf16[384,384]{1,0:T(8,128)(2,1)S(1)} %collective-permute-done.17.one, f32[384,1536]{1,0:T(8,128)} %own.1.result_ref), custom_call_target="tpu_custom_call", output_to_operand_aliasing={{}: (2, {})} | custom-call | tf_op jit(solution)/shard_map/one/pallas_call | solution.py:431
  96.2 3.1 %collective-permute-done.16.other = bf16[192,384]{1,0:T(8,128)(2,1)S(1)} collective-permute-done((bf16[192,384]{1,0:T(8,128)(2,1)S(1)}, bf16[192,384]{1,0:T(8,128)(2,1)S(1)}, u32[]{:S(2)}, u32[]{:S(2)}) %collective-permute-start.16) | collective-permute-done | bytes 147488 | tf_op jit(solution)/shard_map/ppermute | solution.py:420
  99.3 1.6 %other.1 = f32[384,1536]{1,0:T(8,128)} custom-call(s32[16,5]{1,0:T(8,128)S(1)} %copy-done, f32[192,384]{1,0:T(8,128)S(1)} %get-tuple-element.52.share, bf16[192,384]{1,0:T(8,128)(2,1)S(1)} %collective-permute-done.16.other, f32[384,1536]{1,0:T(8,128)} %one.1.result_ref), custom_call_target="tpu_custom_call", output_to_operand_aliasing={{}: (3, {})} | custom-call | tf_op jit(solution)/shard_map/other/pallas_call | solution.py:431
  (8 shorter events, 0.0 us)
Async XLA Ops:
  0.0 0.7 copy-start.5
  0.7 0.7 copy-start.6
  6.7 5.4 %collective-permute-start.1 = (bf16[768,1536]{1,0:T(8,128)(2,1)S(1)}, bf16[768,1536]{1,0:T(8,128)(2,1)S(1)}, u32[]{:S(2)}, u32[]{:S(2)}) collective-permute-start(bf16[768,1536]{1,0:T(8,128)(2,1)S(1)} %get-tuple-element.31.ours_ref), channel_id=1, source_target_pairs={{0,1},{1,0},{2,3},{3,2},{4,5},{5,4},{6,7},{7,6},{8,9},{9,8},{10,11... | collective-permute-start | bytes 7077896 | tf_op jit(solution)/shard_map/ppermute | solution.py:452
  11.6 4.7 %collective-permute-start = (bf16[768,1536]{1,0:T(8,128)(2,1)S(1)}, bf16[768,1536]{1,0:T(8,128)(2,1)S(1)}, u32[]{:S(2)}, u32[]{:S(2)}) collective-permute-start(bf16[768,1536]{1,0:T(8,128)(2,1)S(1)} %pick_second.1.ours_ref), channel_id=1, source_target_pairs={{0,1},{1,0},{2,3},{3,2},{4,5},{5,4},{6,7},{7,6},{8,9},{9,8},{10,11... | collective-permute-start | bytes 7077896 | tf_op jit(solution)/shard_map/ppermute | solution.py:454
  16.3 2.7 %copy-start.4 = (s32[16,16]{1,0:T(8,128)S(1)}, s32[16,16]{1,0:T(8,128)}, u32[]{:S(2)}) copy-start(s32[16,16]{1,0:T(8,128)} %constant.10.clone.table) | copy-start | bytes 3076
  19.0 15.2 %copy-start.3 = (s32[16,16]{1,0:T(8,128)S(1)}, s32[16,16]{1,0:T(8,128)}, u32[]{:S(2)}) copy-start(s32[16,16]{1,0:T(8,128)} %constant.11.clone.table) | copy-start | bytes 3076
  22.7 11.5 %collective-permute-start.2 = (bf16[480,384]{1,0:T(8,128)(2,1)S(1)}, bf16[480,384]{1,0:T(8,128)(2,1)S(1)}, u32[]{:S(2)}, u32[]{:S(2)}) collective-permute-start(bf16[480,384]{1,0:T(8,128)(2,1)S(1)} %get-tuple-element.36), channel_id=1, source_target_pairs={{0,4},{1,5},{4,8},{5,9},{8,12},{9,13},{12,14},{13,15},{14,10},{15,... | collective-permute-start | bytes 1105928 | tf_op jit(solution)/shard_map/ppermute | solution.py:379
  25.4 12.6 %collective-permute-start.6 = (bf16[480,384]{1,0:T(8,128)(2,1)S(1)}, bf16[480,384]{1,0:T(8,128)(2,1)S(1)}, u32[]{:S(2)}, u32[]{:S(2)}) collective-permute-start(bf16[480,384]{1,0:T(8,128)(2,1)S(1)} %get-tuple-element.42), channel_id=1, source_target_pairs={{0,2},{1,3},{4,0},{5,1},{8,4},{9,5},{12,8},{13,9},{14,12},{15,13},... | collective-permute-start | bytes 1105928 | tf_op jit(solution)/shard_map/ppermute | solution.py:379
  25.4 16.7 %collective-permute-start.9 = (bf16[480,384]{1,0:T(8,128)(2,1)S(1)}, bf16[480,384]{1,0:T(8,128)(2,1)S(1)}, u32[]{:S(2)}, u32[]{:S(2)}) collective-permute-start(bf16[480,384]{1,0:T(8,128)(2,1)S(1)} %get-tuple-element.45), channel_id=1, source_target_pairs={{0,4},{1,5},{4,8},{5,9},{8,12},{9,13},{12,14},{13,15},{14,10},{15,... | collective-permute-start | bytes 1105928 | tf_op jit(solution)/shard_map/ppermute | solution.py:379
  26.9 16.6 %collective-permute-start.12 = (bf16[480,384]{1,0:T(8,128)(2,1)S(1)}, bf16[480,384]{1,0:T(8,128)(2,1)S(1)}, u32[]{:S(2)}, u32[]{:S(2)}) collective-permute-start(bf16[480,384]{1,0:T(8,128)(2,1)S(1)} %get-tuple-element.48), channel_id=1, source_target_pairs={{0,2},{1,3},{4,0},{5,1},{8,4},{9,5},{12,8},{13,9},{14,12},{15,13},... | collective-permute-start | bytes 1105928 | tf_op jit(solution)/shard_map/ppermute | solution.py:379
  38.1 11.0 %copy-start.2 = (s32[16,16]{1,0:T(8,128)S(1)}, s32[16,16]{1,0:T(8,128)}, u32[]{:S(2)}) copy-start(s32[16,16]{1,0:T(8,128)} %constant.12.clone.table) | copy-start | bytes 3076
  38.1 14.6 %collective-permute-start.7 = (bf16[480,384]{1,0:T(8,128)(2,1)S(1)}, bf16[480,384]{1,0:T(8,128)(2,1)S(1)}, u32[]{:S(2)}, u32[]{:S(2)}) collective-permute-start(bf16[480,384]{1,0:T(8,128)(2,1)S(1)} %add_convert_fusion.6), channel_id=1, source_target_pairs={{0,2},{1,3},{4,0},{5,1},{8,4},{9,5},{12,8},{13,9},{14,12},{15,13},... | collective-permute-start | bytes 1105928 | tf_op jit(solution)/shard_map/ppermute | solution.py:379
  39.5 9.6 %collective-permute-start.3 = (bf16[480,384]{1,0:T(8,128)(2,1)S(1)}, bf16[480,384]{1,0:T(8,128)(2,1)S(1)}, u32[]{:S(2)}, u32[]{:S(2)}) collective-permute-start(bf16[480,384]{1,0:T(8,128)(2,1)S(1)} %add_convert_fusion.9), channel_id=1, source_target_pairs={{0,4},{1,5},{4,8},{5,9},{8,12},{9,13},{12,14},{13,15},{14,10},{15,... | collective-permute-start | bytes 1105928 | tf_op jit(solution)/shard_map/ppermute | solution.py:379
  42.2 17.1 %collective-permute-start.10 = (bf16[480,384]{1,0:T(8,128)(2,1)S(1)}, bf16[480,384]{1,0:T(8,128)(2,1)S(1)}, u32[]{:S(2)}, u32[]{:S(2)}) collective-permute-start(bf16[480,384]{1,0:T(8,128)(2,1)S(1)} %add_convert_fusion.4), channel_id=1, source_target_pairs={{0,4},{1,5},{4,8},{5,9},{8,12},{9,13},{12,14},{13,15},{14,10},{15,... | collective-permute-start | bytes 1105928 | tf_op jit(solution)/shard_map/ppermute | solution.py:379
  43.6 15.3 %collective-permute-start.13 = (bf16[480,384]{1,0:T(8,128)(2,1)S(1)}, bf16[480,384]{1,0:T(8,128)(2,1)S(1)}, u32[]{:S(2)}, u32[]{:S(2)}) collective-permute-start(bf16[480,384]{1,0:T(8,128)(2,1)S(1)} %add_convert_fusion.2), channel_id=1, source_target_pairs={{0,2},{1,3},{4,0},{5,1},{8,4},{9,5},{12,8},{13,9},{14,12},{15,13},... | collective-permute-start | bytes 1105928 | tf_op jit(solution)/shard_map/ppermute | solution.py:379
  52.8 10.6 %copy-start.1 = (s32[16,16]{1,0:T(8,128)S(1)}, s32[16,16]{1,0:T(8,128)}, u32[]{:S(2)}) copy-start(s32[16,16]{1,0:T(8,128)} %constant.13.clone.table) | copy-start | bytes 3076
  52.8 22.0 %collective-permute-start.8 = (bf16[480,384]{1,0:T(8,128)(2,1)S(1)}, bf16[480,384]{1,0:T(8,128)(2,1)S(1)}, u32[]{:S(2)}, u32[]{:S(2)}) collective-permute-start(bf16[480,384]{1,0:T(8,128)(2,1)S(1)} %add_convert_fusion.5), channel_id=1, source_target_pairs={{0,2},{1,3},{4,0},{5,1},{8,4},{9,5},{12,8},{13,9},{14,12},{15,13},... | collective-permute-start | bytes 1105928 | tf_op jit(solution)/shard_map/ppermute | solution.py:379
  53.7 9.7 %collective-permute-start.4 = (bf16[480,384]{1,0:T(8,128)(2,1)S(1)}, bf16[480,384]{1,0:T(8,128)(2,1)S(1)}, u32[]{:S(2)}, u32[]{:S(2)}) collective-permute-start(bf16[480,384]{1,0:T(8,128)(2,1)S(1)} %add_convert_fusion.8), channel_id=1, source_target_pairs={{0,4},{1,5},{4,8},{5,9},{8,12},{9,13},{12,14},{13,15},{14,10},{15,... | collective-permute-start | bytes 1105928 | tf_op jit(solution)/shard_map/ppermute | solution.py:379
  58.9 15.7 %collective-permute-start.14 = (bf16[480,384]{1,0:T(8,128)(2,1)S(1)}, bf16[480,384]{1,0:T(8,128)(2,1)S(1)}, u32[]{:S(2)}, u32[]{:S(2)}) collective-permute-start(bf16[480,384]{1,0:T(8,128)(2,1)S(1)} %add_convert_fusion.1), channel_id=1, source_target_pairs={{0,2},{1,3},{4,0},{5,1},{8,4},{9,5},{12,8},{13,9},{14,12},{15,13},... | collective-permute-start | bytes 1105928 | tf_op jit(solution)/shard_map/ppermute | solution.py:379
  59.4 15.4 %collective-permute-start.11 = (bf16[480,384]{1,0:T(8,128)(2,1)S(1)}, bf16[480,384]{1,0:T(8,128)(2,1)S(1)}, u32[]{:S(2)}, u32[]{:S(2)}) collective-permute-start(bf16[480,384]{1,0:T(8,128)(2,1)S(1)} %add_convert_fusion.3), channel_id=1, source_target_pairs={{0,4},{1,5},{4,8},{5,9},{8,12},{9,13},{12,14},{13,15},{14,10},{15,... | collective-permute-start | bytes 1105928 | tf_op jit(solution)/shard_map/ppermute | solution.py:379
  67.0 16.5 %copy-start = (s32[16,5]{1,0:T(8,128)S(1)}, s32[16,5]{1,0:T(8,128)}, u32[]{:S(2)}) copy-start(s32[16,5]{1,0:T(8,128)} %constant.14.clone.place) | copy-start | bytes 964
  67.1 12.1 %collective-permute-start.5 = (bf16[480,384]{1,0:T(8,128)(2,1)S(1)}, bf16[480,384]{1,0:T(8,128)(2,1)S(1)}, u32[]{:S(2)}, u32[]{:S(2)}) collective-permute-start(bf16[480,384]{1,0:T(8,128)(2,1)S(1)} %add_convert_fusion.7), channel_id=1, source_target_pairs={{0,4},{1,5},{4,8},{5,9},{8,12},{9,13},{12,14},{13,15},{14,10},{15,... | collective-permute-start | bytes 1105928 | tf_op jit(solution)/shard_map/ppermute | solution.py:379
  74.7 8.9 %collective-permute-start.15 = (bf16[480,384]{1,0:T(8,128)(2,1)S(1)}, bf16[480,384]{1,0:T(8,128)(2,1)S(1)}, u32[]{:S(2)}, u32[]{:S(2)}) collective-permute-start(bf16[480,384]{1,0:T(8,128)(2,1)S(1)} %add_convert_fusion), channel_id=1, source_target_pairs={{0,2},{1,3},{4,0},{5,1},{8,4},{9,5},{12,8},{13,9},{14,12},{15,13},... | collective-permute-start | bytes 1105928 | tf_op jit(solution)/shard_map/ppermute | solution.py:379
  84.6 10.0 %collective-permute-start.17 = (bf16[384,384]{1,0:T(8,128)(2,1)S(1)}, bf16[384,384]{1,0:T(8,128)(2,1)S(1)}, u32[]{:S(2)}, u32[]{:S(2)}) collective-permute-start(bf16[384,384]{1,0:T(8,128)(2,1)S(1)} %get-tuple-element.54), channel_id=1, source_target_pairs={{0,2},{1,10},{2,4},{3,12},{4,6},{5,14},{6,0},{7,8},{8,5},{9,11},{1... | collective-permute-start | bytes 884744 | tf_op jit(solution)/shard_map/ppermute | solution.py:419
  88.4 10.9 %collective-permute-start.16 = (bf16[192,384]{1,0:T(8,128)(2,1)S(1)}, bf16[192,384]{1,0:T(8,128)(2,1)S(1)}, u32[]{:S(2)}, u32[]{:S(2)}) collective-permute-start(bf16[192,384]{1,0:T(8,128)(2,1)S(1)} %get-tuple-element.53), channel_id=1, source_target_pairs={{0,4},{1,8},{2,6},{3,10},{4,0},{5,12},{6,2},{7,14},{8,3},{9,13},{1... | collective-permute-start | bytes 442376 | tf_op jit(solution)/shard_map/ppermute | solution.py:420

commit v6 on v5

--- a/solution.py
+++ b/solution.py
@@ -59,27 +59,35 @@
 
 def pick_kernel(first, *refs):
     if first:
-        ids_ref, gates_ref, rows_ref, out_ref, pick_ref, starts_ref, coef_ref = refs[:7]
-        held, made, in_sems, out_sems, starts, starts_sem = refs[7:]
+        ids_hbm, gates_hbm, rows_ref, out_ref, pick_ref, starts_ref, coef_ref = refs[:7]
+        held, in_sems, starts, ids_ref, gates_ref, small_sems = refs[7:]
     else:
-        starts, pick_ref, coef_ref, rows_ref, out_ref, held, made, in_sems, out_sems = refs
+        starts, pick_ref, coef_ref, rows_ref, out_ref, held, in_sems = refs
     tokens, width = out_ref.shape
     tiles, _, tile = held.shape
     local = EXPERTS // 2
     member = lax.axis_index("expert")
     base = (1 - member if first else member) * width
 
+    if first:
+        small = [
+            pltpu.make_async_copy(ids_hbm, ids_ref, small_sems.at[0]),
+            pltpu.make_async_copy(gates_hbm, gates_ref, small_sems.at[1]),
+        ]
+        for copy in small:
+            copy.start()
     loads = []
     for j in range(tiles):
         at = pl.ds(pl.multiple_of(base + j * tile, 128), tile)
         loads.append(pltpu.make_async_copy(rows_ref.at[:, at], held.at[j], in_sems.at[j]))
         loads[-1].start()
     if first:
+        for copy in small:
+            copy.wait()
         plan_tokens(ids_ref, gates_ref, pick_ref, starts_ref, coef_ref)
-        copy = pltpu.make_async_copy(starts_ref, starts, starts_sem)
+        copy = pltpu.make_async_copy(starts_ref, starts, small_sems.at[2])
         copy.start()
         copy.wait()
-    stores = []
     for j in range(tiles):
         loads[j].wait()
         for b in range(tokens // BATCH):
@@ -94,82 +102,76 @@
             )
             rows = slice(b * BATCH, (b + 1) * BATCH)
             total = coef_ref[rows, 0:1] * picked[:BATCH] + coef_ref[rows, 1:2] * picked[BATCH:]
-            made[j, rows, :] = total.astype(BF16)
-        stores.append(
-            pltpu.make_async_copy(made.at[j], out_ref.at[:, j * tile : (j + 1) * tile], out_sems.at[j])
-        )
-        stores[-1].start()
-    for store in stores:
-        store.wait()
+            out_ref[rows, j * tile : (j + 1) * tile] = total.astype(BF16)
 
 
 def pick_half(args, rows, tokens, width, first, tile=512):
     tiles = width // tile
     depth = EXPERTS // 2 * WINDOW
     any_, vmem = pl.BlockSpec(memory_space=pl.ANY), pl.BlockSpec(memory_space=pltpu.VMEM)
+    in_hbm = lambda x: pltpu.with_memory_space_constraint(x, pltpu.HBM)
     out_shape = [jax.ShapeDtypeStruct((tokens, width), BF16)]
-    scratch = [
-        pltpu.VMEM((tiles, rows.shape[0], tile), BF16),
-        pltpu.VMEM((tiles, tokens, tile), BF16),
-        pltpu.SemaphoreType.DMA((tiles,)),
-        pltpu.SemaphoreType.DMA((tiles,)),
-    ]
+    scratch = [pltpu.VMEM((tiles, rows.shape[0], tile), BF16), pltpu.SemaphoreType.DMA((tiles,))]
     if first:
         out_shape += [
             jax.ShapeDtypeStruct((2 * tokens, depth), BF16),
             jax.ShapeDtypeStruct((tokens // BATCH, 128), I32),
             jax.ShapeDtypeStruct((tokens, 128), F32),
         ]
-        in_specs = [vmem, vmem, any_]
-        scratch += [pltpu.SMEM((tokens // BATCH, 128), I32), pltpu.SemaphoreType.DMA]
+        args = [in_hbm(x) for x in args]
+        in_specs = [any_] * 3
+        scratch += [
+            pltpu.SMEM((tokens // BATCH, 128), I32),
+            pltpu.VMEM((2, tokens), I32),
+            pltpu.VMEM((2, tokens), F32),
+            pltpu.SemaphoreType.DMA((3,)),
+        ]
     else:
         in_specs = [pl.BlockSpec(memory_space=pltpu.SMEM), vmem, vmem, any_]
     return pl.pallas_call(
         functools.partial(pick_kernel, first),
         out_shape=out_shape,
         in_specs=in_specs,
-        out_specs=[any_] + [vmem] * (len(out_shape) - 1),
+        out_specs=[vmem] * len(out_shape),
         scratch_shapes=scratch,
         cost_estimate=pl.CostEstimate(
             flops=4 * tokens * depth * width, bytes_accessed=2 * (rows.shape[0] + tokens) * width, transcendentals=0
         ),
         compiler_params=pltpu.CompilerParams(vmem_limit_bytes=24 << 20),
         name="pick_first" if first else "pick_second",
-    )(*args, pltpu.with_memory_space_constraint(rows, pltpu.HBM))
+    )(*args, in_hbm(rows))
 
 
 def merge_kernel(first, coef_ref, ours_ref, theirs_ref, *refs):
-    total = coef_ref[:, 2:3] * ours_ref[...].astype(F32) + coef_ref[:, 3:4] * theirs_ref[...].astype(F32)
-    total = total.astype(BF16)
-    if first:
-        refs[0][...] = total
-    refs[-1][...] = total.T
-
-
-def merge(coef, ours, theirs, turned=None, tile=384):
+    tokens, width = ours_ref.shape
+    tile = 384
+    ours = jnp.broadcast_to(coef_ref[:, 2:3], (tokens, tile))
+    theirs = jnp.broadcast_to(coef_ref[:, 3:4], (tokens, tile))
+    for j in range(width // tile):
+        at = slice(j * tile, (j + 1) * tile)
+        total = (ours * ours_ref[:, at].astype(F32) + theirs * theirs_ref[:, at].astype(F32)).astype(BF16)
+        if first:
+            refs[0][:, at] = total
+            refs[-1][at, :] = total.T
+        else:
+            refs[-1][width + j * tile : width + (j + 1) * tile, :] = total.T
+
+
+def merge(coef, ours, theirs, turned=None):
     tokens, width = ours.shape
     first = turned is None
-    steps = width // tile
-    tall = pl.BlockSpec((tokens, tile), lambda j: (0, j))
-    flat = pl.BlockSpec((tile, tokens), lambda j: (j if first else j + steps, 0))
-    in_specs = [pl.BlockSpec(coef.shape, lambda j: (0, 0)), tall, tall]
-    args = [coef, ours, theirs]
+    vmem = pl.BlockSpec(memory_space=pltpu.VMEM)
+    args = [coef, ours, theirs] + ([] if first else [turned])
     out_shape = [jax.ShapeDtypeStruct((2 * width, tokens), BF16)]
-    out_specs = [flat]
     if first:
         out_shape.insert(0, jax.ShapeDtypeStruct((tokens, width), BF16))
-        out_specs.insert(0, tall)
-    else:
-        in_specs.append(pl.BlockSpec(memory_space=pl.ANY))
-        args.append(turned)
     return pl.pallas_call(
         functools.partial(merge_kernel, first),
         out_shape=out_shape,
-        grid=(steps,),
-        in_specs=in_specs,
-        out_specs=out_specs,
+        in_specs=[vmem] * len(args),
+        out_specs=[vmem] * len(out_shape),
         input_output_aliases={} if first else {3: 0},
-        compiler_params=pltpu.CompilerParams(vmem_limit_bytes=32 << 20),
+        compiler_params=pltpu.CompilerParams(vmem_limit_bytes=24 << 20),
         cost_estimate=pl.CostEstimate(flops=4 * ours.size, bytes_accessed=6 * ours.size, transcendentals=0),
         name="merge_first" if first else "merge_second",
     )(*args)
@@ -202,23 +204,19 @@
 
 def moment_blocks(table, turned, mine, width, strip, dtype, name, after=()):
     count = table.shape[1] // 4
-    whole = lambda shape: pl.BlockSpec(shape, lambda i, s: (0, 0))
+    smem, vmem, any_ = [pl.BlockSpec(memory_space=m) for m in (pltpu.SMEM, pltpu.VMEM, pl.ANY)]
     piece = (width + strip, width)
     return pl.pallas_call(
         functools.partial(blocks_kernel, count),
         out_shape=[jax.ShapeDtypeStruct(piece, dtype)] * count,
-        grid_spec=pltpu.PrefetchScalarGridSpec(
-            num_scalar_prefetch=1,
-            grid=(1,),
-            in_specs=[whole(turned.shape), whole(mine.shape)] + [pl.BlockSpec(memory_space=pl.ANY)] * len(after),
-            out_specs=[whole(piece)] * count,
-        ),
+        in_specs=[smem, vmem, vmem] + [any_] * len(after),
+        out_specs=[vmem] * count,
         cost_estimate=pl.CostEstimate(
-            flops=2 * count * mine.shape[0] * width * width,
-            bytes_accessed=2 * turned.size + 2 * mine.size + count * width * width * 4,
+            flops=2 * count * mine.shape[0] * width * piece[0],
+            bytes_accessed=2 * turned.size + 2 * mine.size + count * width * piece[0] * 4,
             transcendentals=0,
         ),
-        compiler_params=pltpu.CompilerParams(vmem_limit_bytes=40 << 20),
+        compiler_params=pltpu.CompilerParams(vmem_limit_bytes=24 << 20),
         name=name,
     )(table, turned, mine, *after)
 
@@ -370,15 +368,15 @@
     both = ("dp", "expert")
     blocks = {}
 
-    def compute(n, dtype, after=()):
-        which = ROUNDS[n]
+    def compute(which, name, dtype, after=()):
         table = jnp.asarray(job_table(which, width))
-        blocks.update(zip(which, moment_blocks(table, turned, mine, width, STRIP, dtype, f"blocks{n}", after)))
+        blocks.update(zip(which, moment_blocks(table, turned, mine, width, STRIP, dtype, name, after)))
 
     def hop(value, key):
         return lax.ppermute(value, both, ring_perm(1 if key[1] <= (4 if key[0] == 0 else 3) else -1))
 
-    compute(0, BF16)
+    compute(ROUNDS[0][:2], "blocks0", BF16)
+    compute(ROUNDS[0][2:], "blocks0b", BF16)
     moving = {key: blocks[key] for key in ROUNDS[0]}
     arrived = {}
     for n in range(4):
@@ -387,7 +385,7 @@
             if key in moving:
                 landed[key] = hop(moving[key], key)
         if n < 3:
-            compute(n + 1, F32, after=(landed[ROUNDS[n][0]],))
+            compute(ROUNDS[n + 1], f"blocks{n + 1}", F32, after=(landed[ROUNDS[n][0]],))
         moving = {}
         for (x, t), value in landed.items():
             rightwards = t <= (4 if x == 0 else 3)

time: 101 us -> 99.2 us (0.982)
  Pallas kernels: 36.5 us -> 33.9 us
  waiting for transfers between devices: 43.2 us -> 45.3 us
  local copies, waits for them, and re-layouts: 1.41 us -> 0.04 us
    pallas_call x2, Pallas kernels: 5.63 us -> 2.41 us  [merge(): pl.pallas_call(functools.partial(merge_kernel, first), out_shape=out_shap...]
    ppermute x1, waiting for transfers between devices: 1.21 us -> 2.9 us  [per_device(): from_peer_too = lax.ppermute(kept, 'expert', swap)]
    unnamed x14 -> x12, local copies, waits for them, and re-layouts: 1.41 us -> 0.04 us
    pallas_call x4 -> x5, Pallas kernels: 14.7 us -> 15.4 us  [moment_blocks(): pl.pallas_call(functools.partial(blocks_kernel, count), out_shape=[jax.Sh...]
  transfers between devices with their start and end apart: 18 -> 18, of which waited for: 11 -> 13; matrix products, arithmetic and copies ran while one was open for 1% -> 1% of each run, Pallas kernels for 22% -> 23%
where the time goes in v6:
time: 99.2 us; the launch traced here: 99 us
  waiting for transfers between devices  45.3 us (46%)
  Pallas kernels  33.9 us (34%)
  starting transfers between devices  18.6 us (19%)
    ppermute x14, waiting for transfers between devices, hop(): lax.ppermute(value, both, ring_perm(1 if key[1] <= (4 if key[0] == 0 else...  35.5 us
    pallas_call x5, Pallas kernels, moment_blocks(): pl.pallas_call(functools.partial(blocks_kernel, count), out_shape=[jax.Sh...  15.4 us
    ppermute x14, starting transfers between devices, hop(): lax.ppermute(value, both, ring_perm(1 if key[1] <= (4 if key[0] == 0 else...  13.5 us
    pallas_call x2, Pallas kernels, pick_half(): pl.pallas_call(functools.partial(pick_kernel, first), out_shape=out_shape...  10.1 us
    ppermute x1, starting transfers between devices, symmetric_moment(): one = lax.ppermute(one, both, perm_one)  4.24 us
    ppermute x1, waiting for transfers between devices, symmetric_moment(): one = lax.ppermute(one, both, perm_one)  3.67 us
    pallas_call x2, Pallas kernels, symmetric_moment(): pl.pallas_call(kernel, out_shape=result, in_specs=[smem] + [vmem] * len(a...  3.21 us
    ppermute x1, waiting for transfers between devices, symmetric_moment(): other = lax.ppermute(other, both, perm_other)  3.2 us
  transfers between devices with their start and end apart: 18, of which 13 were waited for; matrix products, arithmetic and copies ran while one was open for 1% of the time, Pallas kernels for 23%

profile of v6, /device:TPU:1, one launch (start us, length us, event | category | flops | bytes accessed | tf_op | source)
XLA Modules:
  0.0 99.0 jit_solution(9090155926918386587)
XLA Ops:
  0.0 5.5 %pick_first.1 = (bf16[768,1536]{1,0:T(8,128)(2,1)S(1)}, bf16[1536,256]{1,0:T(8,128)(2,1)S(1)}, s32[16,128]{1,0:T(8,128)S(1)}, f32[768,128]{1,0:T(8,128)S(1)}) custom-call(s32[2,768]{1,0:T(2,128)} %bitcast.2, f32[2,768]{1,0:T(2,128)} %bitcast.3, bf16[1536,3072]{1,0:T(8,128)(2,1)} %refs_3_.1), custom_call_target="tpu_custom_call" | custom-call | flops 1207959552 | bytes 7077888 | tf_op jit(solution)/shard_map/pick_first/pallas_call | solution.py:131
  5.6 0.1 collective-permute-start.1
  5.7 4.6 %pick_second.1.ours_ref = bf16[768,1536]{1,0:T(8,128)(2,1)S(1)} custom-call(s32[16,128]{1,0:T(8,128)S(1)} %get-tuple-element.32.refs_0_, bf16[1536,256]{1,0:T(8,128)(2,1)S(1)} %get-tuple-element.33.refs_1_, f32[768,128]{1,0:T(8,128)S(1)} %get-tuple-element.30.refs_2_.coef_ref, bf16[1536,3072]{1,0:T(8,128)(2,1)} %refs_3_.1), custom_call_target="tpu_custom_call" | custom-call | flops 1207959552 | bytes 7077888 | tf_op jit(solution)/shard_map/pick_second/pallas_call | solution.py:131
  10.2 0.5 collective-permute-start
  10.8 0.0 collective-permute-done.1.theirs_ref
  10.8 1.3 %merge_first.1 = (bf16[768,1536]{1,0:T(8,128)(2,1)S(1)}, bf16[3072,768]{1,0:T(8,128)(2,1)S(1)}) custom-call(f32[768,128]{1,0:T(8,128)S(1)} %get-tuple-element.30.refs_2_.coef_ref, bf16[768,1536]{1,0:T(8,128)(2,1)S(1)} %pick_second.1.ours_ref, bf16[768,1536]{1,0:T(8,128)(2,1)S(1)} %collective-permute-done.1.theirs_ref), custom_call_target="tpu_custom_call" | custom-call | flops 4718592 | bytes 7077888 | tf_op jit(solution)/shard_map/merge_first/pallas_call | solution.py:168
  12.0 2.9 %collective-permute-done.theirs_ref = bf16[768,1536]{1,0:T(8,128)(2,1)S(1)} collective-permute-done((bf16[768,1536]{1,0:T(8,128)(2,1)S(1)}, bf16[768,1536]{1,0:T(8,128)(2,1)S(1)}, u32[]{:S(2)}, u32[]{:S(2)}) %collective-permute-start) | collective-permute-done | bytes 2359328 | tf_op jit(solution)/shard_map/ppermute | solution.py:452
  14.9 1.2 %merge_second.1.turned_ref = bf16[3072,768]{1,0:T(8,128)(2,1)S(1)} custom-call(f32[768,128]{1,0:T(8,128)S(1)} %get-tuple-element.30.refs_2_.coef_ref, bf16[768,1536]{1,0:T(8,128)(2,1)S(1)} %get-tuple-element.31.ours_ref, bf16[768,1536]{1,0:T(8,128)(2,1)S(1)} %collective-permute-done.theirs_ref, ...), custom_call_target="tpu_custom_call", output_to_operand_aliasing={{}: (3, {})} | custom-call | flops 4718592 | bytes 7077888 | tf_op jit(solution)/shard_map/merge_second/pallas_call | solution.py:168
  16.1 0.0 copy-start.4
  16.1 2.2 %blocks0.1 = (bf16[480,384]{1,0:T(8,128)(2,1)S(1)}, bf16[480,384]{1,0:T(8,128)(2,1)S(1)}) custom-call(s32[16,8]{1,0:T(8,128)S(1)} %copy-done.5, bf16[3072,768]{1,0:T(8,128)(2,1)S(1)} %merge_second.1.turned_ref, bf16[768,1536]{1,0:T(8,128)(2,1)S(1)} %get-tuple-element.35.mine_ref), custom_call_target="tpu_custom_call" | custom-call | flops 566231040 | bytes 8552448 | tf_op jit(solution)/shard_map/blocks0/pallas_call | solution.py:209
  18.3 0.0 copy-start.3
  18.3 2.7 %collective-permute-start.2 = (bf16[480,384]{1,0:T(8,128)(2,1)S(1)}, bf16[480,384]{1,0:T(8,128)(2,1)S(1)}, u32[]{:S(2)}, u32[]{:S(2)}) collective-permute-start(bf16[480,384]{1,0:T(8,128)(2,1)S(1)} %get-tuple-element.36), channel_id=1, source_target_pairs={{0,4},{1,5},{4,8},{5,9},{8,12},{9,13},{12,14},{13,15},{14,10},{15,... | collective-permute-start | bytes 1105928 | tf_op jit(solution)/shard_map/ppermute | solution.py:376
  21.0 2.2 %blocks0b.1 = (bf16[480,384]{1,0:T(8,128)(2,1)S(1)}, bf16[480,384]{1,0:T(8,128)(2,1)S(1)}) custom-call(s32[16,8]{1,0:T(8,128)S(1)} %copy-done.4, bf16[3072,768]{1,0:T(8,128)(2,1)S(1)} %merge_second.1.turned_ref, bf16[768,1536]{1,0:T(8,128)(2,1)S(1)} %get-tuple-element.35.mine_ref), custom_call_target="tpu_custom_call" | custom-call | flops 566231040 | bytes 8552448 | tf_op jit(solution)/shard_map/blocks0b/pallas_call | solution.py:209
  23.2 0.1 collective-permute-start.6
  23.3 1.5 %collective-permute-start.9 = (bf16[480,384]{1,0:T(8,128)(2,1)S(1)}, bf16[480,384]{1,0:T(8,128)(2,1)S(1)}, u32[]{:S(2)}, u32[]{:S(2)}) collective-permute-start(bf16[480,384]{1,0:T(8,128)(2,1)S(1)} %get-tuple-element.45), channel_id=1, source_target_pairs={{0,4},{1,5},{4,8},{5,9},{8,12},{9,13},{12,14},{13,15},{14,10},{15,... | collective-permute-start | bytes 1105928 | tf_op jit(solution)/shard_map/ppermute | solution.py:376
  24.7 0.1 collective-permute-start.12
  24.8 5.0 %collective-permute-done.2.refs_0_ = bf16[480,384]{1,0:T(8,128)(2,1)S(1)} collective-permute-done((bf16[480,384]{1,0:T(8,128)(2,1)S(1)}, bf16[480,384]{1,0:T(8,128)(2,1)S(1)}, u32[]{:S(2)}, u32[]{:S(2)}) %collective-permute-start.2) | collective-permute-done | bytes 368672 | tf_op jit(solution)/shard_map/ppermute | solution.py:376
  29.8 3.8 %blocks1.1 = (f32[480,384]{1,0:T(8,128)S(1)}, f32[480,384]{1,0:T(8,128)S(1)}, f32[480,384]{1,0:T(8,128)S(1)}, f32[480,384]{1,0:T(8,128)S(1)}) custom-call(s32[16,16]{1,0:T(8,128)S(1)} %copy-done.3, bf16[3072,768]{1,0:T(8,128)(2,1)S(1)} %merge_second.1.turned_ref, bf16[768,1536]{1,0:T(8,128)(2,1)S(1)} %get-tuple-element.35.mine_ref, ...), custom_call_target="tpu_custom_call" | custom-call | flops 1132462080 | bytes 10027008 | tf_op jit(solution)/shard_map/blocks1/pallas_call | solution.py:209
  33.6 0.0 collective-permute-done.6
  33.6 0.1 add_convert_fusion.6
  33.7 0.0 copy-start.2
  33.7 1.3 %collective-permute-start.7 = (bf16[480,384]{1,0:T(8,128)(2,1)S(1)}, bf16[480,384]{1,0:T(8,128)(2,1)S(1)}, u32[]{:S(2)}, u32[]{:S(2)}) collective-permute-start(bf16[480,384]{1,0:T(8,128)(2,1)S(1)} %add_convert_fusion.6), channel_id=1, source_target_pairs={{0,2},{1,3},{4,0},{5,1},{8,4},{9,5},{12,8},{13,9},{14,12},{15,13},... | collective-permute-start | bytes 1105928 | tf_op jit(solution)/shard_map/ppermute | solution.py:376
  35.0 0.1 add_convert_fusion.9
  35.0 0.3 collective-permute-start.3
  35.3 2.3 %collective-permute-done.9 = bf16[480,384]{1,0:T(8,128)(2,1)S(1)} collective-permute-done((bf16[480,384]{1,0:T(8,128)(2,1)S(1)}, bf16[480,384]{1,0:T(8,128)(2,1)S(1)}, u32[]{:S(2)}, u32[]{:S(2)}) %collective-permute-start.9) | collective-permute-done | bytes 368672 | tf_op jit(solution)/shard_map/ppermute | solution.py:376
  37.7 0.1 add_convert_fusion.4
  37.8 1.3 %collective-permute-start.10 = (bf16[480,384]{1,0:T(8,128)(2,1)S(1)}, bf16[480,384]{1,0:T(8,128)(2,1)S(1)}, u32[]{:S(2)}, u32[]{:S(2)}) collective-permute-start(bf16[480,384]{1,0:T(8,128)(2,1)S(1)} %add_convert_fusion.4), channel_id=1, source_target_pairs={{0,4},{1,5},{4,8},{5,9},{8,12},{9,13},{12,14},{13,15},{14,10},{15,... | collective-permute-start | bytes 1105928 | tf_op jit(solution)/shard_map/ppermute | solution.py:376
  39.1 1.8 %collective-permute-done.12 = bf16[480,384]{1,0:T(8,128)(2,1)S(1)} collective-permute-done((bf16[480,384]{1,0:T(8,128)(2,1)S(1)}, bf16[480,384]{1,0:T(8,128)(2,1)S(1)}, u32[]{:S(2)}, u32[]{:S(2)}) %collective-permute-start.12) | collective-permute-done | bytes 368672 | tf_op jit(solution)/shard_map/ppermute | solution.py:376
  40.9 0.1 add_convert_fusion.2
  41.0 0.4 collective-permute-start.13
  41.3 3.0 %collective-permute-done.3.refs_0_ = bf16[480,384]{1,0:T(8,128)(2,1)S(1)} collective-permute-done((bf16[480,384]{1,0:T(8,128)(2,1)S(1)}, bf16[480,384]{1,0:T(8,128)(2,1)S(1)}, u32[]{:S(2)}, u32[]{:S(2)}) %collective-permute-start.3) | collective-permute-done | bytes 368672 | tf_op jit(solution)/shard_map/ppermute | solution.py:376
  44.4 3.6 %blocks2.1 = (f32[480,384]{1,0:T(8,128)S(1)}, f32[480,384]{1,0:T(8,128)S(1)}, f32[480,384]{1,0:T(8,128)S(1)}, f32[480,384]{1,0:T(8,128)S(1)}) custom-call(s32[16,16]{1,0:T(8,128)S(1)} %copy-done.2, bf16[3072,768]{1,0:T(8,128)(2,1)S(1)} %merge_second.1.turned_ref, bf16[768,1536]{1,0:T(8,128)(2,1)S(1)} %get-tuple-element.35.mine_ref, ...), custom_call_target="tpu_custom_call" | custom-call | flops 1132462080 | bytes 10027008 | tf_op jit(solution)/shard_map/blocks2/pallas_call | solution.py:209
  48.0 0.8 collective-permute-done.7
  48.8 0.1 add_convert_fusion.5
  48.9 0.0 copy-start.1
  48.9 0.4 collective-permute-start.8
  49.3 0.1 add_convert_fusion.8
  49.3 1.2 %collective-permute-start.4 = (bf16[480,384]{1,0:T(8,128)(2,1)S(1)}, bf16[480,384]{1,0:T(8,128)(2,1)S(1)}, u32[]{:S(2)}, u32[]{:S(2)}) collective-permute-start(bf16[480,384]{1,0:T(8,128)(2,1)S(1)} %add_convert_fusion.8), channel_id=1, source_target_pairs={{0,4},{1,5},{4,8},{5,9},{8,12},{9,13},{12,14},{13,15},{14,10},{15,... | collective-permute-start | bytes 1105928 | tf_op jit(solution)/shard_map/ppermute | solution.py:376
  50.5 6.2 %collective-permute-done.13 = bf16[480,384]{1,0:T(8,128)(2,1)S(1)} collective-permute-done((bf16[480,384]{1,0:T(8,128)(2,1)S(1)}, bf16[480,384]{1,0:T(8,128)(2,1)S(1)}, u32[]{:S(2)}, u32[]{:S(2)}) %collective-permute-start.13) | collective-permute-done | bytes 368672 | tf_op jit(solution)/shard_map/ppermute | solution.py:376
  56.7 0.1 add_convert_fusion.1
  56.8 0.4 collective-permute-start.14
  57.1 0.0 collective-permute-done.10
  57.1 0.1 add_convert_fusion.3
  57.2 1.2 %collective-permute-start.11 = (bf16[480,384]{1,0:T(8,128)(2,1)S(1)}, bf16[480,384]{1,0:T(8,128)(2,1)S(1)}, u32[]{:S(2)}, u32[]{:S(2)}) collective-permute-start(bf16[480,384]{1,0:T(8,128)(2,1)S(1)} %add_convert_fusion.3), channel_id=1, source_target_pairs={{0,4},{1,5},{4,8},{5,9},{8,12},{9,13},{12,14},{13,15},{14,10},{15,... | collective-permute-start | bytes 1105928 | tf_op jit(solution)/shard_map/ppermute | solution.py:376
  58.4 0.6 collective-permute-done.4.refs_0_
  59.0 3.6 %blocks3.1 = (f32[480,384]{1,0:T(8,128)S(1)}, f32[480,384]{1,0:T(8,128)S(1)}, f32[480,384]{1,0:T(8,128)S(1)}, f32[480,384]{1,0:T(8,128)S(1)}) custom-call(s32[16,16]{1,0:T(8,128)S(1)} %copy-done.1, bf16[3072,768]{1,0:T(8,128)(2,1)S(1)} %merge_second.1.turned_ref, bf16[768,1536]{1,0:T(8,128)(2,1)S(1)} %get-tuple-element.35.mine_ref, ...), custom_call_target="tpu_custom_call" | custom-call | flops 1132462080 | bytes 10027008 | tf_op jit(solution)/shard_map/blocks3/pallas_call | solution.py:209
  62.6 0.0 copy-start
  62.7 0.1 add_convert_fusion.7
  62.7 2.4 %collective-permute-start.5 = (bf16[480,384]{1,0:T(8,128)(2,1)S(1)}, bf16[480,384]{1,0:T(8,128)(2,1)S(1)}, u32[]{:S(2)}, u32[]{:S(2)}) collective-permute-start(bf16[480,384]{1,0:T(8,128)(2,1)S(1)} %add_convert_fusion.7), channel_id=1, source_target_pairs={{0,4},{1,5},{4,8},{5,9},{8,12},{9,13},{12,14},{13,15},{14,10},{15,... | collective-permute-start | bytes 1105928 | tf_op jit(solution)/shard_map/ppermute | solution.py:376
  65.2 7.3 %collective-permute-done.14 = bf16[480,384]{1,0:T(8,128)(2,1)S(1)} collective-permute-done((bf16[480,384]{1,0:T(8,128)(2,1)S(1)}, bf16[480,384]{1,0:T(8,128)(2,1)S(1)}, u32[]{:S(2)}, u32[]{:S(2)}) %collective-permute-start.14) | collective-permute-done | bytes 368672 | tf_op jit(solution)/shard_map/ppermute | solution.py:376
  72.5 0.1 add_convert_fusion
  72.6 0.4 collective-permute-start.15
  72.9 0.0 collective-permute-done.8.left0
  72.9 0.0 collective-permute-done.11.right1
  72.9 2.9 %collective-permute-done.5.right0 = bf16[480,384]{1,0:T(8,128)(2,1)S(1)} collective-permute-done((bf16[480,384]{1,0:T(8,128)(2,1)S(1)}, bf16[480,384]{1,0:T(8,128)(2,1)S(1)}, u32[]{:S(2)}, u32[]{:S(2)}) %collective-permute-start.5) | collective-permute-done | bytes 368672 | tf_op jit(solution)/shard_map/ppermute | solution.py:376
  75.8 5.6 %collective-permute-done.15.left1 = bf16[480,384]{1,0:T(8,128)(2,1)S(1)} collective-permute-done((bf16[480,384]{1,0:T(8,128)(2,1)S(1)}, bf16[480,384]{1,0:T(8,128)(2,1)S(1)}, u32[]{:S(2)}, u32[]{:S(2)}) %collective-permute-start.15) | collective-permute-done | bytes 368672 | tf_op jit(solution)/shard_map/ppermute | solution.py:376
  81.4 1.0 %outgoing.1 = (bf16[384,384]{1,0:T(8,128)(2,1)S(1)}, bf16[192,384]{1,0:T(8,128)(2,1)S(1)}, f32[192,384]{1,0:T(8,128)S(1)}) custom-call(s32[16,5]{1,0:T(8,128)S(1)} %copy-done, f32[480,384]{1,0:T(8,128)S(1)} %get-tuple-element.39.own0, f32[480,384]{1,0:T(8,128)S(1)} %get-tuple-element.40.own1, bf16[480,384]{1,0:T(8,128)(2,1)S(1)} %collective-permute-done.5.right0, ...), custom_call_target="tpu_custom_call" | custom-call | tf_op jit(solution)/shard_map/outgoing/pallas_call | solution.py:404
  82.4 4.2 %collective-permute-start.17 = (bf16[384,384]{1,0:T(8,128)(2,1)S(1)}, bf16[384,384]{1,0:T(8,128)(2,1)S(1)}, u32[]{:S(2)}, u32[]{:S(2)}) collective-permute-start(bf16[384,384]{1,0:T(8,128)(2,1)S(1)} %get-tuple-element.54), channel_id=1, source_target_pairs={{0,2},{1,10},{2,4},{3,12},{4,6},{5,14},{6,0},{7,8},{8,5},{9,11},{1... | collective-permute-start | bytes 884744 | tf_op jit(solution)/shard_map/ppermute | solution.py:417
  86.7 0.2 collective-permute-start.16
  86.9 1.8 %own.1.result_ref = f32[384,1536]{1,0:T(8,128)} custom-call(s32[16,5]{1,0:T(8,128)S(1)} %copy-done, f32[480,384]{1,0:T(8,128)S(1)} %get-tuple-element.39.own0, f32[480,384]{1,0:T(8,128)S(1)} %get-tuple-element.40.own1, bf16[480,384]{1,0:T(8,128)(2,1)S(1)} %collective-permute-done.5.right0, bf16[480,384]{1,0:T(8,128)(2,1)S(1)} %collective-permute-done.8.left0, ...), custom_call_target="tpu_custom_call" | custom-call | tf_op jit(solution)/shard_map/own/pallas_call | solution.py:419
  88.7 3.7 %collective-permute-done.17.one = bf16[384,384]{1,0:T(8,128)(2,1)S(1)} collective-permute-done((bf16[384,384]{1,0:T(8,128)(2,1)S(1)}, bf16[384,384]{1,0:T(8,128)(2,1)S(1)}, u32[]{:S(2)}, u32[]{:S(2)}) %collective-permute-start.17) | collective-permute-done | bytes 294944 | tf_op jit(solution)/shard_map/ppermute | solution.py:417
  92.4 1.7 %one.1.result_ref = f32[384,1536]{1,0:T(8,128)} custom-call(s32[16,5]{1,0:T(8,128)S(1)} %copy-done, bf16[384,384]{1,0:T(8,128)(2,1)S(1)} %collective-permute-done.17.one, f32[384,1536]{1,0:T(8,128)} %own.1.result_ref), custom_call_target="tpu_custom_call", output_to_operand_aliasing={{}: (2, {})} | custom-call | tf_op jit(solution)/shard_map/one/pallas_call | solution.py:429
  94.1 3.2 %collective-permute-done.16.other = bf16[192,384]{1,0:T(8,128)(2,1)S(1)} collective-permute-done((bf16[192,384]{1,0:T(8,128)(2,1)S(1)}, bf16[192,384]{1,0:T(8,128)(2,1)S(1)}, u32[]{:S(2)}, u32[]{:S(2)}) %collective-permute-start.16) | collective-permute-done | bytes 147488 | tf_op jit(solution)/shard_map/ppermute | solution.py:418
  97.3 1.6 %other.1 = f32[384,1536]{1,0:T(8,128)} custom-call(s32[16,5]{1,0:T(8,128)S(1)} %copy-done, f32[192,384]{1,0:T(8,128)S(1)} %get-tuple-element.52.share, bf16[192,384]{1,0:T(8,128)(2,1)S(1)} %collective-permute-done.16.other, f32[384,1536]{1,0:T(8,128)} %one.1.result_ref), custom_call_target="tpu_custom_call", output_to_operand_aliasing={{}: (3, {})} | custom-call | tf_op jit(solution)/shard_map/other/pallas_call | solution.py:429
  (7 shorter events, 0.0 us)
Async XLA Ops:
  5.6 5.2 %collective-permute-start.1 = (bf16[768,1536]{1,0:T(8,128)(2,1)S(1)}, bf16[768,1536]{1,0:T(8,128)(2,1)S(1)}, u32[]{:S(2)}, u32[]{:S(2)}) collective-permute-start(bf16[768,1536]{1,0:T(8,128)(2,1)S(1)} %get-tuple-element.31.ours_ref), channel_id=1, source_target_pairs={{0,1},{1,0},{2,3},{3,2},{4,5},{5,4},{6,7},{7,6},{8,9},{9,8},{10,11... | collective-permute-start | bytes 7077896 | tf_op jit(solution)/shard_map/ppermute | solution.py:450
  10.2 4.7 %collective-permute-start = (bf16[768,1536]{1,0:T(8,128)(2,1)S(1)}, bf16[768,1536]{1,0:T(8,128)(2,1)S(1)}, u32[]{:S(2)}, u32[]{:S(2)}) collective-permute-start(bf16[768,1536]{1,0:T(8,128)(2,1)S(1)} %pick_second.1.ours_ref), channel_id=1, source_target_pairs={{0,1},{1,0},{2,3},{3,2},{4,5},{5,4},{6,7},{7,6},{8,9},{9,8},{10,11... | collective-permute-start | bytes 7077896 | tf_op jit(solution)/shard_map/ppermute | solution.py:452
  14.9 1.2 %copy-start.5 = (s32[16,8]{1,0:T(8,128)S(1)}, s32[16,8]{1,0:T(8,128)}, u32[]{:S(2)}) copy-start(s32[16,8]{1,0:T(8,128)} %constant.12.clone.table) | copy-start | bytes 1540
  16.1 4.9 %copy-start.4 = (s32[16,8]{1,0:T(8,128)S(1)}, s32[16,8]{1,0:T(8,128)}, u32[]{:S(2)}) copy-start(s32[16,8]{1,0:T(8,128)} %constant.13.clone.table) | copy-start | bytes 1540
  18.3 11.5 %copy-start.3 = (s32[16,16]{1,0:T(8,128)S(1)}, s32[16,16]{1,0:T(8,128)}, u32[]{:S(2)}) copy-start(s32[16,16]{1,0:T(8,128)} %constant.14.clone.table) | copy-start | bytes 3076
  18.3 11.5 %collective-permute-start.2 = (bf16[480,384]{1,0:T(8,128)(2,1)S(1)}, bf16[480,384]{1,0:T(8,128)(2,1)S(1)}, u32[]{:S(2)}, u32[]{:S(2)}) collective-permute-start(bf16[480,384]{1,0:T(8,128)(2,1)S(1)} %get-tuple-element.36), channel_id=1, source_target_pairs={{0,4},{1,5},{4,8},{5,9},{8,12},{9,13},{12,14},{13,15},{14,10},{15,... | collective-permute-start | bytes 1105928 | tf_op jit(solution)/shard_map/ppermute | solution.py:376
  23.2 10.4 %collective-permute-start.6 = (bf16[480,384]{1,0:T(8,128)(2,1)S(1)}, bf16[480,384]{1,0:T(8,128)(2,1)S(1)}, u32[]{:S(2)}, u32[]{:S(2)}) collective-permute-start(bf16[480,384]{1,0:T(8,128)(2,1)S(1)} %get-tuple-element.42), channel_id=1, source_target_pairs={{0,2},{1,3},{4,0},{5,1},{8,4},{9,5},{12,8},{13,9},{14,12},{15,13},... | collective-permute-start | bytes 1105928 | tf_op jit(solution)/shard_map/ppermute | solution.py:376
  23.3 14.4 %collective-permute-start.9 = (bf16[480,384]{1,0:T(8,128)(2,1)S(1)}, bf16[480,384]{1,0:T(8,128)(2,1)S(1)}, u32[]{:S(2)}, u32[]{:S(2)}) collective-permute-start(bf16[480,384]{1,0:T(8,128)(2,1)S(1)} %get-tuple-element.45), channel_id=1, source_target_pairs={{0,4},{1,5},{4,8},{5,9},{8,12},{9,13},{12,14},{13,15},{14,10},{15,... | collective-permute-start | bytes 1105928 | tf_op jit(solution)/shard_map/ppermute | solution.py:376
  24.7 16.2 %collective-permute-start.12 = (bf16[480,384]{1,0:T(8,128)(2,1)S(1)}, bf16[480,384]{1,0:T(8,128)(2,1)S(1)}, u32[]{:S(2)}, u32[]{:S(2)}) collective-permute-start(bf16[480,384]{1,0:T(8,128)(2,1)S(1)} %get-tuple-element.48), channel_id=1, source_target_pairs={{0,2},{1,3},{4,0},{5,1},{8,4},{9,5},{12,8},{13,9},{14,12},{15,13},... | collective-permute-start | bytes 1105928 | tf_op jit(solution)/shard_map/ppermute | solution.py:376
  33.7 10.7 %copy-start.2 = (s32[16,16]{1,0:T(8,128)S(1)}, s32[16,16]{1,0:T(8,128)}, u32[]{:S(2)}) copy-start(s32[16,16]{1,0:T(8,128)} %constant.15.clone.table) | copy-start | bytes 3076
  33.7 15.1 %collective-permute-start.7 = (bf16[480,384]{1,0:T(8,128)(2,1)S(1)}, bf16[480,384]{1,0:T(8,128)(2,1)S(1)}, u32[]{:S(2)}, u32[]{:S(2)}) collective-permute-start(bf16[480,384]{1,0:T(8,128)(2,1)S(1)} %add_convert_fusion.6), channel_id=1, source_target_pairs={{0,2},{1,3},{4,0},{5,1},{8,4},{9,5},{12,8},{13,9},{14,12},{15,13},... | collective-permute-start | bytes 1105928 | tf_op jit(solution)/shard_map/ppermute | solution.py:376
  35.0 9.3 %collective-permute-start.3 = (bf16[480,384]{1,0:T(8,128)(2,1)S(1)}, bf16[480,384]{1,0:T(8,128)(2,1)S(1)}, u32[]{:S(2)}, u32[]{:S(2)}) collective-permute-start(bf16[480,384]{1,0:T(8,128)(2,1)S(1)} %add_convert_fusion.9), channel_id=1, source_target_pairs={{0,4},{1,5},{4,8},{5,9},{8,12},{9,13},{12,14},{13,15},{14,10},{15,... | collective-permute-start | bytes 1105928 | tf_op jit(solution)/shard_map/ppermute | solution.py:376
  37.8 19.4 %collective-permute-start.10 = (bf16[480,384]{1,0:T(8,128)(2,1)S(1)}, bf16[480,384]{1,0:T(8,128)(2,1)S(1)}, u32[]{:S(2)}, u32[]{:S(2)}) collective-permute-start(bf16[480,384]{1,0:T(8,128)(2,1)S(1)} %add_convert_fusion.4), channel_id=1, source_target_pairs={{0,4},{1,5},{4,8},{5,9},{8,12},{9,13},{12,14},{13,15},{14,10},{15,... | collective-permute-start | bytes 1105928 | tf_op jit(solution)/shard_map/ppermute | solution.py:376
  41.0 15.7 %collective-permute-start.13 = (bf16[480,384]{1,0:T(8,128)(2,1)S(1)}, bf16[480,384]{1,0:T(8,128)(2,1)S(1)}, u32[]{:S(2)}, u32[]{:S(2)}) collective-permute-start(bf16[480,384]{1,0:T(8,128)(2,1)S(1)} %add_convert_fusion.2), channel_id=1, source_target_pairs={{0,2},{1,3},{4,0},{5,1},{8,4},{9,5},{12,8},{13,9},{14,12},{15,13},... | collective-permute-start | bytes 1105928 | tf_op jit(solution)/shard_map/ppermute | solution.py:376
  48.9 10.2 %copy-start.1 = (s32[16,16]{1,0:T(8,128)S(1)}, s32[16,16]{1,0:T(8,128)}, u32[]{:S(2)}) copy-start(s32[16,16]{1,0:T(8,128)} %constant.16.clone.table) | copy-start | bytes 3076
  48.9 24.1 %collective-permute-start.8 = (bf16[480,384]{1,0:T(8,128)(2,1)S(1)}, bf16[480,384]{1,0:T(8,128)(2,1)S(1)}, u32[]{:S(2)}, u32[]{:S(2)}) collective-permute-start(bf16[480,384]{1,0:T(8,128)(2,1)S(1)} %add_convert_fusion.5), channel_id=1, source_target_pairs={{0,2},{1,3},{4,0},{5,1},{8,4},{9,5},{12,8},{13,9},{14,12},{15,13},... | collective-permute-start | bytes 1105928 | tf_op jit(solution)/shard_map/ppermute | solution.py:376
  49.3 9.7 %collective-permute-start.4 = (bf16[480,384]{1,0:T(8,128)(2,1)S(1)}, bf16[480,384]{1,0:T(8,128)(2,1)S(1)}, u32[]{:S(2)}, u32[]{:S(2)}) collective-permute-start(bf16[480,384]{1,0:T(8,128)(2,1)S(1)} %add_convert_fusion.8), channel_id=1, source_target_pairs={{0,4},{1,5},{4,8},{5,9},{8,12},{9,13},{12,14},{13,15},{14,10},{15,... | collective-permute-start | bytes 1105928 | tf_op jit(solution)/shard_map/ppermute | solution.py:376
  56.8 15.7 %collective-permute-start.14 = (bf16[480,384]{1,0:T(8,128)(2,1)S(1)}, bf16[480,384]{1,0:T(8,128)(2,1)S(1)}, u32[]{:S(2)}, u32[]{:S(2)}) collective-permute-start(bf16[480,384]{1,0:T(8,128)(2,1)S(1)} %add_convert_fusion.1), channel_id=1, source_target_pairs={{0,2},{1,3},{4,0},{5,1},{8,4},{9,5},{12,8},{13,9},{14,12},{15,13},... | collective-permute-start | bytes 1105928 | tf_op jit(solution)/shard_map/ppermute | solution.py:376
  57.2 15.7 %collective-permute-start.11 = (bf16[480,384]{1,0:T(8,128)(2,1)S(1)}, bf16[480,384]{1,0:T(8,128)(2,1)S(1)}, u32[]{:S(2)}, u32[]{:S(2)}) collective-permute-start(bf16[480,384]{1,0:T(8,128)(2,1)S(1)} %add_convert_fusion.3), channel_id=1, source_target_pairs={{0,4},{1,5},{4,8},{5,9},{8,12},{9,13},{12,14},{13,15},{14,10},{15,... | collective-permute-start | bytes 1105928 | tf_op jit(solution)/shard_map/ppermute | solution.py:376
  62.6 18.8 %copy-start = (s32[16,5]{1,0:T(8,128)S(1)}, s32[16,5]{1,0:T(8,128)}, u32[]{:S(2)}) copy-start(s32[16,5]{1,0:T(8,128)} %constant.17.clone.place) | copy-start | bytes 964
  62.7 13.1 %collective-permute-start.5 = (bf16[480,384]{1,0:T(8,128)(2,1)S(1)}, bf16[480,384]{1,0:T(8,128)(2,1)S(1)}, u32[]{:S(2)}, u32[]{:S(2)}) collective-permute-start(bf16[480,384]{1,0:T(8,128)(2,1)S(1)} %add_convert_fusion.7), channel_id=1, source_target_pairs={{0,4},{1,5},{4,8},{5,9},{8,12},{9,13},{12,14},{13,15},{14,10},{15,... | collective-permute-start | bytes 1105928 | tf_op jit(solution)/shard_map/ppermute | solution.py:376
  72.6 8.9 %collective-permute-start.15 = (bf16[480,384]{1,0:T(8,128)(2,1)S(1)}, bf16[480,384]{1,0:T(8,128)(2,1)S(1)}, u32[]{:S(2)}, u32[]{:S(2)}) collective-permute-start(bf16[480,384]{1,0:T(8,128)(2,1)S(1)} %add_convert_fusion), channel_id=1, source_target_pairs={{0,2},{1,3},{4,0},{5,1},{8,4},{9,5},{12,8},{13,9},{14,12},{15,13},... | collective-permute-start | bytes 1105928 | tf_op jit(solution)/shard_map/ppermute | solution.py:376
  82.4 9.9 %collective-permute-start.17 = (bf16[384,384]{1,0:T(8,128)(2,1)S(1)}, bf16[384,384]{1,0:T(8,128)(2,1)S(1)}, u32[]{:S(2)}, u32[]{:S(2)}) collective-permute-start(bf16[384,384]{1,0:T(8,128)(2,1)S(1)} %get-tuple-element.54), channel_id=1, source_target_pairs={{0,2},{1,10},{2,4},{3,12},{4,6},{5,14},{6,0},{7,8},{8,5},{9,11},{1... | collective-permute-start | bytes 884744 | tf_op jit(solution)/shard_map/ppermute | solution.py:417
  86.7 10.6 %collective-permute-start.16 = (bf16[192,384]{1,0:T(8,128)(2,1)S(1)}, bf16[192,384]{1,0:T(8,128)(2,1)S(1)}, u32[]{:S(2)}, u32[]{:S(2)}) collective-permute-start(bf16[192,384]{1,0:T(8,128)(2,1)S(1)} %get-tuple-element.53), channel_id=1, source_target_pairs={{0,4},{1,8},{2,6},{3,10},{4,0},{5,12},{6,2},{7,14},{8,3},{9,13},{1... | collective-permute-start | bytes 442376 | tf_op jit(solution)/shard_map/ppermute | solution.py:418

commit v7 on v6

--- a/solution.py
+++ b/solution.py
@@ -304,7 +304,7 @@
     return own[rows, :] + right[rows, :].astype(F32) + left[rows, :].astype(F32)
 
 
-def outgoing_kernel(scale, place, own0, own1, right0, left0, right1, left1, one, other, share):
+def outgoing_kernel(scale, place, own0, own1, right0, left1, right1, left0, one, other, share):
     width = one.shape[0]
     kind = place[my_row(), 4]
     block, strip = slice(0, width), slice(width, width + STRIP)
@@ -327,7 +327,7 @@
     return pltpu.make_async_copy(made, out_ref.at[:, at], sem)
 
 
-def own_kernel(scale, place, own0, own1, right0, left0, right1, left1, out_ref, made, sems):
+def own_kernel(scale, place, own0, own1, right0, left1, right1, left0, out_ref, made, sems):
     block = slice(0, made.shape[1])
     copies = []
     for n, parts in enumerate(((own0, right0, left0), (own1, right1, left1))):
@@ -377,6 +377,7 @@
 
     compute(ROUNDS[0][:2], "blocks0", BF16)
     compute(ROUNDS[0][2:], "blocks0b", BF16)
+    compute(ROUNDS[1], "blocks1", F32)
     moving = {key: blocks[key] for key in ROUNDS[0]}
     arrived = {}
     for n in range(4):
@@ -384,8 +385,8 @@
         for key in ROUNDS[n]:
             if key in moving:
                 landed[key] = hop(moving[key], key)
-        if n < 3:
-            compute(ROUNDS[n + 1], f"blocks{n + 1}", F32, after=(landed[ROUNDS[n][0]],))
+        if n < 2:
+            compute(ROUNDS[n + 2], f"blocks{n + 2}", F32, after=(landed[ROUNDS[n][0]],))
         moving = {}
         for (x, t), value in landed.items():
             rightwards = t <= (4 if x == 0 else 3)
@@ -399,7 +400,7 @@
     smem, vmem, any_ = [pl.BlockSpec(memory_space=m) for m in (pltpu.SMEM, pltpu.VMEM, pl.ANY)]
     result = jax.ShapeDtypeStruct((width, 4 * width), F32)
     params = pltpu.CompilerParams(vmem_limit_bytes=24 << 20)
-    sums = (blocks[0, 0], blocks[1, 0], arrived[0, True], arrived[0, False], arrived[1, True], arrived[1, False])
+    sums = (blocks[0, 0], blocks[1, 0], arrived[0, True], arrived[1, False], arrived[1, True], arrived[0, False])
     scale = 1.0 / total_tokens
     one, other, share = pl.pallas_call(
         functools.partial(outgoing_kernel, scale),

time: 99.2 us -> 95 us (0.958)
  waiting for transfers between devices: 45.3 us -> 42.4 us
  starting transfers between devices: 18.6 us -> 17.3 us
    ppermute x14, waiting for transfers between devices: 35.5 us -> 33.5 us  [hop(): lax.ppermute(value, both, ring_perm(1 if key[1] <= (4 if key[0] == 0 else...]
    ppermute x14, starting transfers between devices: 13.5 us -> 12.2 us  [hop(): lax.ppermute(value, both, ring_perm(1 if key[1] <= (4 if key[0] == 0 else...]
  transfers between devices with their start and end apart: 18 -> 18, of which waited for: 13 -> 11; matrix products, arithmetic and copies ran while one was open for 1% -> 1% of each run, Pallas kernels for 23% -> 24%
where the time goes in v7:
time: 95 us; the launch traced here: 94.8 us
  waiting for transfers between devices  42.4 us (45%)
  Pallas kernels  33.9 us (36%)
  starting transfers between devices  17.3 us (18%)
    ppermute x14, waiting for transfers between devices, hop(): lax.ppermute(value, both, ring_perm(1 if key[1] <= (4 if key[0] == 0 else...  33.5 us
    pallas_call x5, Pallas kernels, moment_blocks(): pl.pallas_call(functools.partial(blocks_kernel, count), out_shape=[jax.Sh...  15.4 us
    ppermute x14, starting transfers between devices, hop(): lax.ppermute(value, both, ring_perm(1 if key[1] <= (4 if key[0] == 0 else...  12.2 us
    pallas_call x2, Pallas kernels, pick_half(): pl.pallas_call(functools.partial(pick_kernel, first), out_shape=out_shape...  10.1 us
    ppermute x1, starting transfers between devices, symmetric_moment(): one = lax.ppermute(one, both, perm_one)  4.54 us
    ppermute x1, waiting for transfers between devices, symmetric_moment(): one = lax.ppermute(one, both, perm_one)  3.45 us
    pallas_call x2, Pallas kernels, symmetric_moment(): pl.pallas_call(kernel, out_shape=result, in_specs=[smem] + [vmem] * len(a...  3.21 us
    ppermute x1, waiting for transfers between devices, per_device(): from_peer_too = lax.ppermute(kept, 'expert', swap)  2.9 us
  transfers between devices with their start and end apart: 18, of which 11 were waited for; matrix products, arithmetic and copies ran while one was open for 1% of the time, Pallas kernels for 24%

profile of v7, /device:TPU:1, one launch (start us, length us, event | category | flops | bytes accessed | tf_op | source)
XLA Modules:
  0.0 94.8 jit_solution(4359354523669129727)
XLA Ops:
  0.0 5.5 %pick_first.1 = (bf16[768,1536]{1,0:T(8,128)(2,1)S(1)}, bf16[1536,256]{1,0:T(8,128)(2,1)S(1)}, s32[16,128]{1,0:T(8,128)S(1)}, f32[768,128]{1,0:T(8,128)S(1)}) custom-call(s32[2,768]{1,0:T(2,128)} %bitcast.2, f32[2,768]{1,0:T(2,128)} %bitcast.3, bf16[1536,3072]{1,0:T(8,128)(2,1)} %refs_3_.1), custom_call_target="tpu_custom_call" | custom-call | flops 1207959552 | bytes 7077888 | tf_op jit(solution)/shard_map/pick_first/pallas_call | solution.py:131
  5.6 0.1 collective-permute-start.1
  5.7 4.6 %pick_second.1.ours_ref = bf16[768,1536]{1,0:T(8,128)(2,1)S(1)} custom-call(s32[16,128]{1,0:T(8,128)S(1)} %get-tuple-element.32.refs_0_, bf16[1536,256]{1,0:T(8,128)(2,1)S(1)} %get-tuple-element.33.refs_1_, f32[768,128]{1,0:T(8,128)S(1)} %get-tuple-element.30.refs_2_.coef_ref, bf16[1536,3072]{1,0:T(8,128)(2,1)} %refs_3_.1), custom_call_target="tpu_custom_call" | custom-call | flops 1207959552 | bytes 7077888 | tf_op jit(solution)/shard_map/pick_second/pallas_call | solution.py:131
  10.2 0.5 collective-permute-start
  10.8 0.0 collective-permute-done.1.theirs_ref
  10.8 1.3 %merge_first.1 = (bf16[768,1536]{1,0:T(8,128)(2,1)S(1)}, bf16[3072,768]{1,0:T(8,128)(2,1)S(1)}) custom-call(f32[768,128]{1,0:T(8,128)S(1)} %get-tuple-element.30.refs_2_.coef_ref, bf16[768,1536]{1,0:T(8,128)(2,1)S(1)} %pick_second.1.ours_ref, bf16[768,1536]{1,0:T(8,128)(2,1)S(1)} %collective-permute-done.1.theirs_ref), custom_call_target="tpu_custom_call" | custom-call | flops 4718592 | bytes 7077888 | tf_op jit(solution)/shard_map/merge_first/pallas_call | solution.py:168
  12.0 2.9 %collective-permute-done.theirs_ref = bf16[768,1536]{1,0:T(8,128)(2,1)S(1)} collective-permute-done((bf16[768,1536]{1,0:T(8,128)(2,1)S(1)}, bf16[768,1536]{1,0:T(8,128)(2,1)S(1)}, u32[]{:S(2)}, u32[]{:S(2)}) %collective-permute-start) | collective-permute-done | bytes 2359328 | tf_op jit(solution)/shard_map/ppermute | solution.py:453
  14.9 1.2 %merge_second.1.turned_ref = bf16[3072,768]{1,0:T(8,128)(2,1)S(1)} custom-call(f32[768,128]{1,0:T(8,128)S(1)} %get-tuple-element.30.refs_2_.coef_ref, bf16[768,1536]{1,0:T(8,128)(2,1)S(1)} %get-tuple-element.31.ours_ref, bf16[768,1536]{1,0:T(8,128)(2,1)S(1)} %collective-permute-done.theirs_ref, ...), custom_call_target="tpu_custom_call", output_to_operand_aliasing={{}: (3, {})} | custom-call | flops 4718592 | bytes 7077888 | tf_op jit(solution)/shard_map/merge_second/pallas_call | solution.py:168
  16.1 0.0 copy-done.5
  16.1 0.0 copy-start.4
  16.1 2.2 %blocks0.1 = (bf16[480,384]{1,0:T(8,128)(2,1)S(1)}, bf16[480,384]{1,0:T(8,128)(2,1)S(1)}) custom-call(s32[16,8]{1,0:T(8,128)S(1)} %copy-done.5, bf16[3072,768]{1,0:T(8,128)(2,1)S(1)} %merge_second.1.turned_ref, bf16[768,1536]{1,0:T(8,128)(2,1)S(1)} %get-tuple-element.35.mine_ref), custom_call_target="tpu_custom_call" | custom-call | flops 566231040 | bytes 8552448 | tf_op jit(solution)/shard_map/blocks0/pallas_call | solution.py:209
  18.3 2.7 %collective-permute-start.6 = (bf16[480,384]{1,0:T(8,128)(2,1)S(1)}, bf16[480,384]{1,0:T(8,128)(2,1)S(1)}, u32[]{:S(2)}, u32[]{:S(2)}) collective-permute-start(bf16[480,384]{1,0:T(8,128)(2,1)S(1)} %get-tuple-element.42), channel_id=1, source_target_pairs={{0,2},{1,3},{4,0},{5,1},{8,4},{9,5},{12,8},{13,9},{14,12},{15,13},... | collective-permute-start | bytes 1105928 | tf_op jit(solution)/shard_map/ppermute | solution.py:376
  20.9 0.1 collective-permute-start.2
  21.1 2.2 %blocks0b.1 = (bf16[480,384]{1,0:T(8,128)(2,1)S(1)}, bf16[480,384]{1,0:T(8,128)(2,1)S(1)}) custom-call(s32[16,8]{1,0:T(8,128)S(1)} %copy-done.4, bf16[3072,768]{1,0:T(8,128)(2,1)S(1)} %merge_second.1.turned_ref, bf16[768,1536]{1,0:T(8,128)(2,1)S(1)} %get-tuple-element.35.mine_ref), custom_call_target="tpu_custom_call" | custom-call | flops 566231040 | bytes 8552448 | tf_op jit(solution)/shard_map/blocks0b/pallas_call | solution.py:209
  23.3 1.4 %collective-permute-start.10 = (bf16[480,384]{1,0:T(8,128)(2,1)S(1)}, bf16[480,384]{1,0:T(8,128)(2,1)S(1)}, u32[]{:S(2)}, u32[]{:S(2)}) collective-permute-start(bf16[480,384]{1,0:T(8,128)(2,1)S(1)} %get-tuple-element.46), channel_id=1, source_target_pairs={{0,4},{1,5},{4,8},{5,9},{8,12},{9,13},{12,14},{13,15},{14,10},{15,... | collective-permute-start | bytes 1105928 | tf_op jit(solution)/shard_map/ppermute | solution.py:376
  24.7 0.1 collective-permute-start.13
  24.8 3.8 %blocks1.1 = (f32[480,384]{1,0:T(8,128)S(1)}, f32[480,384]{1,0:T(8,128)S(1)}, f32[480,384]{1,0:T(8,128)S(1)}, f32[480,384]{1,0:T(8,128)S(1)}) custom-call(s32[16,16]{1,0:T(8,128)S(1)} %copy-done.3, bf16[3072,768]{1,0:T(8,128)(2,1)S(1)} %merge_second.1.turned_ref, bf16[768,1536]{1,0:T(8,128)(2,1)S(1)} %get-tuple-element.35.mine_ref), custom_call_target="tpu_custom_call" | custom-call | flops 1132462080 | bytes 10027008 | tf_op jit(solution)/shard_map/blocks1/pallas_call | solution.py:209
  28.6 1.2 %collective-permute-done.6 = bf16[480,384]{1,0:T(8,128)(2,1)S(1)} collective-permute-done((bf16[480,384]{1,0:T(8,128)(2,1)S(1)}, bf16[480,384]{1,0:T(8,128)(2,1)S(1)}, u32[]{:S(2)}, u32[]{:S(2)}) %collective-permute-start.6) | collective-permute-done | bytes 368672 | tf_op jit(solution)/shard_map/ppermute | solution.py:376
  29.8 0.1 add_convert_fusion.6
  29.9 0.0 copy-start.2
  29.9 1.2 %collective-permute-start.7 = (bf16[480,384]{1,0:T(8,128)(2,1)S(1)}, bf16[480,384]{1,0:T(8,128)(2,1)S(1)}, u32[]{:S(2)}, u32[]{:S(2)}) collective-permute-start(bf16[480,384]{1,0:T(8,128)(2,1)S(1)} %add_convert_fusion.6), channel_id=1, source_target_pairs={{0,2},{1,3},{4,0},{5,1},{8,4},{9,5},{12,8},{13,9},{14,12},{15,13},... | collective-permute-start | bytes 1105928 | tf_op jit(solution)/shard_map/ppermute | solution.py:376
  31.1 0.0 collective-permute-done.2.refs_0_
  31.1 0.1 add_convert_fusion.9
  31.2 0.4 collective-permute-start.3
  31.6 7.0 %collective-permute-done.10 = bf16[480,384]{1,0:T(8,128)(2,1)S(1)} collective-permute-done((bf16[480,384]{1,0:T(8,128)(2,1)S(1)}, bf16[480,384]{1,0:T(8,128)(2,1)S(1)}, u32[]{:S(2)}, u32[]{:S(2)}) %collective-permute-start.10) | collective-permute-done | bytes 368672 | tf_op jit(solution)/shard_map/ppermute | solution.py:376
  38.6 0.1 add_convert_fusion.3
  38.6 0.5 collective-permute-start.11
  39.2 0.0 collective-permute-done.13
  39.2 0.1 add_convert_fusion.1
  39.2 1.1 %collective-permute-start.14 = (bf16[480,384]{1,0:T(8,128)(2,1)S(1)}, bf16[480,384]{1,0:T(8,128)(2,1)S(1)}, u32[]{:S(2)}, u32[]{:S(2)}) collective-permute-start(bf16[480,384]{1,0:T(8,128)(2,1)S(1)} %add_convert_fusion.1), channel_id=1, source_target_pairs={{0,2},{1,3},{4,0},{5,1},{8,4},{9,5},{12,8},{13,9},{14,12},{15,13},... | collective-permute-start | bytes 1105928 | tf_op jit(solution)/shard_map/ppermute | solution.py:376
  40.3 3.6 %blocks2.1 = (f32[480,384]{1,0:T(8,128)S(1)}, f32[480,384]{1,0:T(8,128)S(1)}, f32[480,384]{1,0:T(8,128)S(1)}, f32[480,384]{1,0:T(8,128)S(1)}) custom-call(s32[16,16]{1,0:T(8,128)S(1)} %copy-done.2, bf16[3072,768]{1,0:T(8,128)(2,1)S(1)} %merge_second.1.turned_ref, bf16[768,1536]{1,0:T(8,128)(2,1)S(1)} %get-tuple-element.35.mine_ref, ...), custom_call_target="tpu_custom_call" | custom-call | flops 1132462080 | bytes 10027008 | tf_op jit(solution)/shard_map/blocks2/pallas_call | solution.py:209
  43.9 1.7 %collective-permute-done.7 = bf16[480,384]{1,0:T(8,128)(2,1)S(1)} collective-permute-done((bf16[480,384]{1,0:T(8,128)(2,1)S(1)}, bf16[480,384]{1,0:T(8,128)(2,1)S(1)}, u32[]{:S(2)}, u32[]{:S(2)}) %collective-permute-start.7) | collective-permute-done | bytes 368672 | tf_op jit(solution)/shard_map/ppermute | solution.py:376
  45.6 0.1 add_convert_fusion.5
  45.7 0.0 copy-start.1
  45.7 1.2 %collective-permute-start.8 = (bf16[480,384]{1,0:T(8,128)(2,1)S(1)}, bf16[480,384]{1,0:T(8,128)(2,1)S(1)}, u32[]{:S(2)}, u32[]{:S(2)}) collective-permute-start(bf16[480,384]{1,0:T(8,128)(2,1)S(1)} %add_convert_fusion.5), channel_id=1, source_target_pairs={{0,2},{1,3},{4,0},{5,1},{8,4},{9,5},{12,8},{13,9},{14,12},{15,13},... | collective-permute-start | bytes 1105928 | tf_op jit(solution)/shard_map/ppermute | solution.py:376
  46.9 0.0 collective-permute-done.3.refs_0_
  46.9 0.1 add_convert_fusion.8
  47.0 0.4 collective-permute-start.4
  47.4 7.0 %collective-permute-done.11 = bf16[480,384]{1,0:T(8,128)(2,1)S(1)} collective-permute-done((bf16[480,384]{1,0:T(8,128)(2,1)S(1)}, bf16[480,384]{1,0:T(8,128)(2,1)S(1)}, u32[]{:S(2)}, u32[]{:S(2)}) %collective-permute-start.11) | collective-permute-done | bytes 368672 | tf_op jit(solution)/shard_map/ppermute | solution.py:376
  54.4 0.1 add_convert_fusion.2
  54.4 0.5 collective-permute-start.12
  55.0 0.0 collective-permute-done.14
  55.0 0.1 add_convert_fusion
  55.0 1.1 %collective-permute-start.15 = (bf16[480,384]{1,0:T(8,128)(2,1)S(1)}, bf16[480,384]{1,0:T(8,128)(2,1)S(1)}, u32[]{:S(2)}, u32[]{:S(2)}) collective-permute-start(bf16[480,384]{1,0:T(8,128)(2,1)S(1)} %add_convert_fusion), channel_id=1, source_target_pairs={{0,2},{1,3},{4,0},{5,1},{8,4},{9,5},{12,8},{13,9},{14,12},{15,13},... | collective-permute-start | bytes 1105928 | tf_op jit(solution)/shard_map/ppermute | solution.py:376
  56.1 3.6 %blocks3.1 = (f32[480,384]{1,0:T(8,128)S(1)}, f32[480,384]{1,0:T(8,128)S(1)}, f32[480,384]{1,0:T(8,128)S(1)}, f32[480,384]{1,0:T(8,128)S(1)}) custom-call(s32[16,16]{1,0:T(8,128)S(1)} %copy-done.1, bf16[3072,768]{1,0:T(8,128)(2,1)S(1)} %merge_second.1.turned_ref, bf16[768,1536]{1,0:T(8,128)(2,1)S(1)} %get-tuple-element.35.mine_ref, ...), custom_call_target="tpu_custom_call" | custom-call | flops 1132462080 | bytes 10027008 | tf_op jit(solution)/shard_map/blocks3/pallas_call | solution.py:209
  59.7 0.0 copy-start
  59.7 1.7 %collective-permute-done.8 = bf16[480,384]{1,0:T(8,128)(2,1)S(1)} collective-permute-done((bf16[480,384]{1,0:T(8,128)(2,1)S(1)}, bf16[480,384]{1,0:T(8,128)(2,1)S(1)}, u32[]{:S(2)}, u32[]{:S(2)}) %collective-permute-start.8) | collective-permute-done | bytes 368672 | tf_op jit(solution)/shard_map/ppermute | solution.py:376
  61.4 0.1 add_convert_fusion.4
  61.5 1.2 %collective-permute-start.9 = (bf16[480,384]{1,0:T(8,128)(2,1)S(1)}, bf16[480,384]{1,0:T(8,128)(2,1)S(1)}, u32[]{:S(2)}, u32[]{:S(2)}) collective-permute-start(bf16[480,384]{1,0:T(8,128)(2,1)S(1)} %add_convert_fusion.4), channel_id=1, source_target_pairs={{0,2},{1,3},{4,0},{5,1},{8,4},{9,5},{12,8},{13,9},{14,12},{15,13},... | collective-permute-start | bytes 1105928 | tf_op jit(solution)/shard_map/ppermute | solution.py:376
  62.7 0.0 collective-permute-done.4
  62.7 0.1 add_convert_fusion.7
  62.8 0.4 collective-permute-start.5
  63.1 7.0 %collective-permute-done.12.right1 = bf16[480,384]{1,0:T(8,128)(2,1)S(1)} collective-permute-done((bf16[480,384]{1,0:T(8,128)(2,1)S(1)}, bf16[480,384]{1,0:T(8,128)(2,1)S(1)}, u32[]{:S(2)}, u32[]{:S(2)}) %collective-permute-start.12) | collective-permute-done | bytes 368672 | tf_op jit(solution)/shard_map/ppermute | solution.py:376
  70.2 0.0 collective-permute-done.15.left0
  70.2 7.0 %collective-permute-done.9.left1 = bf16[480,384]{1,0:T(8,128)(2,1)S(1)} collective-permute-done((bf16[480,384]{1,0:T(8,128)(2,1)S(1)}, bf16[480,384]{1,0:T(8,128)(2,1)S(1)}, u32[]{:S(2)}, u32[]{:S(2)}) %collective-permute-start.9) | collective-permute-done | bytes 368672 | tf_op jit(solution)/shard_map/ppermute | solution.py:376
  77.2 0.8 collective-permute-done.5.right0
  78.1 1.0 %outgoing.1 = (bf16[384,384]{1,0:T(8,128)(2,1)S(1)}, bf16[192,384]{1,0:T(8,128)(2,1)S(1)}, f32[192,384]{1,0:T(8,128)S(1)}) custom-call(s32[16,5]{1,0:T(8,128)S(1)} %copy-done, f32[480,384]{1,0:T(8,128)S(1)} %get-tuple-element.38.own0, f32[480,384]{1,0:T(8,128)S(1)} %get-tuple-element.39.own1, bf16[480,384]{1,0:T(8,128)(2,1)S(1)} %collective-permute-done.5.right0, ...), custom_call_target="tpu_custom_call" | custom-call | tf_op jit(solution)/shard_map/outgoing/pallas_call | solution.py:405
  79.1 4.5 %collective-permute-start.17 = (bf16[384,384]{1,0:T(8,128)(2,1)S(1)}, bf16[384,384]{1,0:T(8,128)(2,1)S(1)}, u32[]{:S(2)}, u32[]{:S(2)}) collective-permute-start(bf16[384,384]{1,0:T(8,128)(2,1)S(1)} %get-tuple-element.54), channel_id=1, source_target_pairs={{0,2},{1,10},{2,4},{3,12},{4,6},{5,14},{6,0},{7,8},{8,5},{9,11},{1... | collective-permute-start | bytes 884744 | tf_op jit(solution)/shard_map/ppermute | solution.py:418
  83.6 0.0 collective-permute-start.16
  83.6 1.8 %own.1.result_ref = f32[384,1536]{1,0:T(8,128)} custom-call(s32[16,5]{1,0:T(8,128)S(1)} %copy-done, f32[480,384]{1,0:T(8,128)S(1)} %get-tuple-element.38.own0, f32[480,384]{1,0:T(8,128)S(1)} %get-tuple-element.39.own1, bf16[480,384]{1,0:T(8,128)(2,1)S(1)} %collective-permute-done.5.right0, bf16[480,384]{1,0:T(8,128)(2,1)S(1)} %collective-permute-done.9.left1, ...), custom_call_target="tpu_custom_call" | custom-call | tf_op jit(solution)/shard_map/own/pallas_call | solution.py:420
  85.4 3.5 %collective-permute-done.17.one = bf16[384,384]{1,0:T(8,128)(2,1)S(1)} collective-permute-done((bf16[384,384]{1,0:T(8,128)(2,1)S(1)}, bf16[384,384]{1,0:T(8,128)(2,1)S(1)}, u32[]{:S(2)}, u32[]{:S(2)}) %collective-permute-start.17) | collective-permute-done | bytes 294944 | tf_op jit(solution)/shard_map/ppermute | solution.py:418
  88.9 1.7 %one.1.result_ref = f32[384,1536]{1,0:T(8,128)} custom-call(s32[16,5]{1,0:T(8,128)S(1)} %copy-done, bf16[384,384]{1,0:T(8,128)(2,1)S(1)} %collective-permute-done.17.one, f32[384,1536]{1,0:T(8,128)} %own.1.result_ref), custom_call_target="tpu_custom_call", output_to_operand_aliasing={{}: (2, {})} | custom-call | tf_op jit(solution)/shard_map/one/pallas_call | solution.py:430
  90.6 2.5 %collective-permute-done.16.other = bf16[192,384]{1,0:T(8,128)(2,1)S(1)} collective-permute-done((bf16[192,384]{1,0:T(8,128)(2,1)S(1)}, bf16[192,384]{1,0:T(8,128)(2,1)S(1)}, u32[]{:S(2)}, u32[]{:S(2)}) %collective-permute-start.16) | collective-permute-done | bytes 147488 | tf_op jit(solution)/shard_map/ppermute | solution.py:419
  93.0 1.6 %other.1 = f32[384,1536]{1,0:T(8,128)} custom-call(s32[16,5]{1,0:T(8,128)S(1)} %copy-done, f32[192,384]{1,0:T(8,128)S(1)} %get-tuple-element.52.share, bf16[192,384]{1,0:T(8,128)(2,1)S(1)} %collective-permute-done.16.other, f32[384,1536]{1,0:T(8,128)} %one.1.result_ref), custom_call_target="tpu_custom_call", output_to_operand_aliasing={{}: (3, {})} | custom-call | tf_op jit(solution)/shard_map/other/pallas_call | solution.py:430
  (7 shorter events, 0.0 us)
Async XLA Ops:
  5.6 5.2 %collective-permute-start.1 = (bf16[768,1536]{1,0:T(8,128)(2,1)S(1)}, bf16[768,1536]{1,0:T(8,128)(2,1)S(1)}, u32[]{:S(2)}, u32[]{:S(2)}) collective-permute-start(bf16[768,1536]{1,0:T(8,128)(2,1)S(1)} %get-tuple-element.31.ours_ref), channel_id=1, source_target_pairs={{0,1},{1,0},{2,3},{3,2},{4,5},{5,4},{6,7},{7,6},{8,9},{9,8},{10,11... | collective-permute-start | bytes 7077896 | tf_op jit(solution)/shard_map/ppermute | solution.py:451
  10.2 4.7 %collective-permute-start = (bf16[768,1536]{1,0:T(8,128)(2,1)S(1)}, bf16[768,1536]{1,0:T(8,128)(2,1)S(1)}, u32[]{:S(2)}, u32[]{:S(2)}) collective-permute-start(bf16[768,1536]{1,0:T(8,128)(2,1)S(1)} %pick_second.1.ours_ref), channel_id=1, source_target_pairs={{0,1},{1,0},{2,3},{3,2},{4,5},{5,4},{6,7},{7,6},{8,9},{9,8},{10,11... | collective-permute-start | bytes 7077896 | tf_op jit(solution)/shard_map/ppermute | solution.py:453
  14.9 1.2 %copy-start.5 = (s32[16,8]{1,0:T(8,128)S(1)}, s32[16,8]{1,0:T(8,128)}, u32[]{:S(2)}) copy-start(s32[16,8]{1,0:T(8,128)} %constant.12.clone.table) | copy-start | bytes 1540
  16.1 5.0 %copy-start.4 = (s32[16,8]{1,0:T(8,128)S(1)}, s32[16,8]{1,0:T(8,128)}, u32[]{:S(2)}) copy-start(s32[16,8]{1,0:T(8,128)} %constant.13.clone.table) | copy-start | bytes 1540
  18.3 11.5 %collective-permute-start.6 = (bf16[480,384]{1,0:T(8,128)(2,1)S(1)}, bf16[480,384]{1,0:T(8,128)(2,1)S(1)}, u32[]{:S(2)}, u32[]{:S(2)}) collective-permute-start(bf16[480,384]{1,0:T(8,128)(2,1)S(1)} %get-tuple-element.42), channel_id=1, source_target_pairs={{0,2},{1,3},{4,0},{5,1},{8,4},{9,5},{12,8},{13,9},{14,12},{15,13},... | collective-permute-start | bytes 1105928 | tf_op jit(solution)/shard_map/ppermute | solution.py:376
  20.9 3.8 %copy-start.3 = (s32[16,16]{1,0:T(8,128)S(1)}, s32[16,16]{1,0:T(8,128)}, u32[]{:S(2)}) copy-start(s32[16,16]{1,0:T(8,128)} %constant.14.clone.table) | copy-start | bytes 3076
  20.9 10.2 %collective-permute-start.2 = (bf16[480,384]{1,0:T(8,128)(2,1)S(1)}, bf16[480,384]{1,0:T(8,128)(2,1)S(1)}, u32[]{:S(2)}, u32[]{:S(2)}) collective-permute-start(bf16[480,384]{1,0:T(8,128)(2,1)S(1)} %get-tuple-element.36), channel_id=1, source_target_pairs={{0,4},{1,5},{4,8},{5,9},{8,12},{9,13},{12,14},{13,15},{14,10},{15,... | collective-permute-start | bytes 1105928 | tf_op jit(solution)/shard_map/ppermute | solution.py:376
  23.3 15.3 %collective-permute-start.10 = (bf16[480,384]{1,0:T(8,128)(2,1)S(1)}, bf16[480,384]{1,0:T(8,128)(2,1)S(1)}, u32[]{:S(2)}, u32[]{:S(2)}) collective-permute-start(bf16[480,384]{1,0:T(8,128)(2,1)S(1)} %get-tuple-element.46), channel_id=1, source_target_pairs={{0,4},{1,5},{4,8},{5,9},{8,12},{9,13},{12,14},{13,15},{14,10},{15,... | collective-permute-start | bytes 1105928 | tf_op jit(solution)/shard_map/ppermute | solution.py:376
  24.7 14.5 %collective-permute-start.13 = (bf16[480,384]{1,0:T(8,128)(2,1)S(1)}, bf16[480,384]{1,0:T(8,128)(2,1)S(1)}, u32[]{:S(2)}, u32[]{:S(2)}) collective-permute-start(bf16[480,384]{1,0:T(8,128)(2,1)S(1)} %get-tuple-element.49), channel_id=1, source_target_pairs={{0,2},{1,3},{4,0},{5,1},{8,4},{9,5},{12,8},{13,9},{14,12},{15,13},... | collective-permute-start | bytes 1105928 | tf_op jit(solution)/shard_map/ppermute | solution.py:376
  29.9 10.4 %copy-start.2 = (s32[16,16]{1,0:T(8,128)S(1)}, s32[16,16]{1,0:T(8,128)}, u32[]{:S(2)}) copy-start(s32[16,16]{1,0:T(8,128)} %constant.15.clone.table) | copy-start | bytes 3076
  29.9 15.7 %collective-permute-start.7 = (bf16[480,384]{1,0:T(8,128)(2,1)S(1)}, bf16[480,384]{1,0:T(8,128)(2,1)S(1)}, u32[]{:S(2)}, u32[]{:S(2)}) collective-permute-start(bf16[480,384]{1,0:T(8,128)(2,1)S(1)} %add_convert_fusion.6), channel_id=1, source_target_pairs={{0,2},{1,3},{4,0},{5,1},{8,4},{9,5},{12,8},{13,9},{14,12},{15,13},... | collective-permute-start | bytes 1105928 | tf_op jit(solution)/shard_map/ppermute | solution.py:376
  31.2 15.7 %collective-permute-start.3 = (bf16[480,384]{1,0:T(8,128)(2,1)S(1)}, bf16[480,384]{1,0:T(8,128)(2,1)S(1)}, u32[]{:S(2)}, u32[]{:S(2)}) collective-permute-start(bf16[480,384]{1,0:T(8,128)(2,1)S(1)} %add_convert_fusion.9), channel_id=1, source_target_pairs={{0,4},{1,5},{4,8},{5,9},{8,12},{9,13},{12,14},{13,15},{14,10},{15,... | collective-permute-start | bytes 1105928 | tf_op jit(solution)/shard_map/ppermute | solution.py:376
  38.6 15.7 %collective-permute-start.11 = (bf16[480,384]{1,0:T(8,128)(2,1)S(1)}, bf16[480,384]{1,0:T(8,128)(2,1)S(1)}, u32[]{:S(2)}, u32[]{:S(2)}) collective-permute-start(bf16[480,384]{1,0:T(8,128)(2,1)S(1)} %add_convert_fusion.3), channel_id=1, source_target_pairs={{0,4},{1,5},{4,8},{5,9},{8,12},{9,13},{12,14},{13,15},{14,10},{15,... | collective-permute-start | bytes 1105928 | tf_op jit(solution)/shard_map/ppermute | solution.py:376
  39.2 15.7 %collective-permute-start.14 = (bf16[480,384]{1,0:T(8,128)(2,1)S(1)}, bf16[480,384]{1,0:T(8,128)(2,1)S(1)}, u32[]{:S(2)}, u32[]{:S(2)}) collective-permute-start(bf16[480,384]{1,0:T(8,128)(2,1)S(1)} %add_convert_fusion.1), channel_id=1, source_target_pairs={{0,2},{1,3},{4,0},{5,1},{8,4},{9,5},{12,8},{13,9},{14,12},{15,13},... | collective-permute-start | bytes 1105928 | tf_op jit(solution)/shard_map/ppermute | solution.py:376
  45.7 10.4 %copy-start.1 = (s32[16,16]{1,0:T(8,128)S(1)}, s32[16,16]{1,0:T(8,128)}, u32[]{:S(2)}) copy-start(s32[16,16]{1,0:T(8,128)} %constant.16.clone.table) | copy-start | bytes 3076
  45.7 15.7 %collective-permute-start.8 = (bf16[480,384]{1,0:T(8,128)(2,1)S(1)}, bf16[480,384]{1,0:T(8,128)(2,1)S(1)}, u32[]{:S(2)}, u32[]{:S(2)}) collective-permute-start(bf16[480,384]{1,0:T(8,128)(2,1)S(1)} %add_convert_fusion.5), channel_id=1, source_target_pairs={{0,2},{1,3},{4,0},{5,1},{8,4},{9,5},{12,8},{13,9},{14,12},{15,13},... | collective-permute-start | bytes 1105928 | tf_op jit(solution)/shard_map/ppermute | solution.py:376
  47.0 15.7 %collective-permute-start.4 = (bf16[480,384]{1,0:T(8,128)(2,1)S(1)}, bf16[480,384]{1,0:T(8,128)(2,1)S(1)}, u32[]{:S(2)}, u32[]{:S(2)}) collective-permute-start(bf16[480,384]{1,0:T(8,128)(2,1)S(1)} %add_convert_fusion.8), channel_id=1, source_target_pairs={{0,4},{1,5},{4,8},{5,9},{8,12},{9,13},{12,14},{13,15},{14,10},{15,... | collective-permute-start | bytes 1105928 | tf_op jit(solution)/shard_map/ppermute | solution.py:376
  54.4 15.7 %collective-permute-start.12 = (bf16[480,384]{1,0:T(8,128)(2,1)S(1)}, bf16[480,384]{1,0:T(8,128)(2,1)S(1)}, u32[]{:S(2)}, u32[]{:S(2)}) collective-permute-start(bf16[480,384]{1,0:T(8,128)(2,1)S(1)} %add_convert_fusion.2), channel_id=1, source_target_pairs={{0,4},{1,5},{4,8},{5,9},{8,12},{9,13},{12,14},{13,15},{14,10},{15,... | collective-permute-start | bytes 1105928 | tf_op jit(solution)/shard_map/ppermute | solution.py:376
  55.0 15.1 %collective-permute-start.15 = (bf16[480,384]{1,0:T(8,128)(2,1)S(1)}, bf16[480,384]{1,0:T(8,128)(2,1)S(1)}, u32[]{:S(2)}, u32[]{:S(2)}) collective-permute-start(bf16[480,384]{1,0:T(8,128)(2,1)S(1)} %add_convert_fusion), channel_id=1, source_target_pairs={{0,2},{1,3},{4,0},{5,1},{8,4},{9,5},{12,8},{13,9},{14,12},{15,13},... | collective-permute-start | bytes 1105928 | tf_op jit(solution)/shard_map/ppermute | solution.py:376
  59.7 18.3 %copy-start = (s32[16,5]{1,0:T(8,128)S(1)}, s32[16,5]{1,0:T(8,128)}, u32[]{:S(2)}) copy-start(s32[16,5]{1,0:T(8,128)} %constant.17.clone.place) | copy-start | bytes 964
  61.5 15.7 %collective-permute-start.9 = (bf16[480,384]{1,0:T(8,128)(2,1)S(1)}, bf16[480,384]{1,0:T(8,128)(2,1)S(1)}, u32[]{:S(2)}, u32[]{:S(2)}) collective-permute-start(bf16[480,384]{1,0:T(8,128)(2,1)S(1)} %add_convert_fusion.4), channel_id=1, source_target_pairs={{0,2},{1,3},{4,0},{5,1},{8,4},{9,5},{12,8},{13,9},{14,12},{15,13},... | collective-permute-start | bytes 1105928 | tf_op jit(solution)/shard_map/ppermute | solution.py:376
  62.8 15.3 %collective-permute-start.5 = (bf16[480,384]{1,0:T(8,128)(2,1)S(1)}, bf16[480,384]{1,0:T(8,128)(2,1)S(1)}, u32[]{:S(2)}, u32[]{:S(2)}) collective-permute-start(bf16[480,384]{1,0:T(8,128)(2,1)S(1)} %add_convert_fusion.7), channel_id=1, source_target_pairs={{0,4},{1,5},{4,8},{5,9},{8,12},{9,13},{12,14},{13,15},{14,10},{15,... | collective-permute-start | bytes 1105928 | tf_op jit(solution)/shard_map/ppermute | solution.py:376
  79.1 9.8 %collective-permute-start.17 = (bf16[384,384]{1,0:T(8,128)(2,1)S(1)}, bf16[384,384]{1,0:T(8,128)(2,1)S(1)}, u32[]{:S(2)}, u32[]{:S(2)}) collective-permute-start(bf16[384,384]{1,0:T(8,128)(2,1)S(1)} %get-tuple-element.54), channel_id=1, source_target_pairs={{0,2},{1,10},{2,4},{3,12},{4,6},{5,14},{6,0},{7,8},{8,5},{9,11},{1... | collective-permute-start | bytes 884744 | tf_op jit(solution)/shard_map/ppermute | solution.py:418
  83.6 9.4 %collective-permute-start.16 = (bf16[192,384]{1,0:T(8,128)(2,1)S(1)}, bf16[192,384]{1,0:T(8,128)(2,1)S(1)}, u32[]{:S(2)}, u32[]{:S(2)}) collective-permute-start(bf16[192,384]{1,0:T(8,128)(2,1)S(1)} %get-tuple-element.53), channel_id=1, source_target_pairs={{0,4},{1,8},{2,6},{3,10},{4,0},{5,12},{6,2},{7,14},{8,3},{9,13},{1... | collective-permute-start | bytes 442376 | tf_op jit(solution)/shard_map/ppermute | solution.py:419

commit v8 on v7

--- a/solution.py
+++ b/solution.py
@@ -181,39 +181,46 @@
     return lax.axis_index("dp") * 2 + lax.axis_index("expert")
 
 
-def blocks_kernel(count, table, turned_ref, mine_ref, *refs):
-    tall, width = refs[-1].shape
-    strip = tall - width
+def blocks_kernel(pieces, width, table, turned_ref, mine_ref, *refs):
+    third = width // 3
     me = my_row()
-    for n, out_ref in enumerate(refs[-count:]):
-        jobs = [table[me, 4 * n + k] for k in range(4)]
-        parts = ((0, width, width), (width, strip, strip))
-        for k, (at, rows, unit) in enumerate(parts):
-
-            @pl.when(jobs[2 * k] >= 0)
-            def _(jobs=jobs, k=k, out_ref=out_ref, at=at, rows=rows, unit=unit):
-                down = pl.ds(pl.multiple_of(jobs[2 * k] * unit, 32), rows)
-                along = pl.ds(pl.multiple_of(jobs[2 * k + 1] * width, 128), width)
-                block = jnp.dot(turned_ref[down, :], mine_ref[:, along], preferred_element_type=F32)
-                out_ref[at : at + rows, :] = block.astype(out_ref.dtype)
-
-        @pl.when(jobs[2] < 0)
-        def _(out_ref=out_ref):
-            out_ref[width:, :] = jnp.zeros((strip, width), out_ref.dtype)
-
-
-def moment_blocks(table, turned, mine, width, strip, dtype, name, after=()):
-    count = table.shape[1] // 4
+    for n, (x, out_ref) in enumerate(zip(pieces, refs[-len(pieces) :])):
+        tall = out_ref.shape[0]
+        row, column, strip, strip_column, diagonal = [table[me, FIELDS * n + k] for k in range(FIELDS)]
+
+        def part(out_ref, at, lane, first_row, rows, first_column, columns):
+            down = pl.ds(pl.multiple_of(first_row, STRIP), rows)
+            along = pl.ds(pl.multiple_of(first_column, 128), columns)
+            block = jnp.dot(turned_ref[down, :], mine_ref[:, along], preferred_element_type=F32)
+            out_ref[at : at + rows, lane : lane + columns] = block.astype(out_ref.dtype)
+
+        @pl.when(diagonal == 0 if x == 0 else True)
+        def _(o=out_ref, r=row * width, c=column * width, s=strip * STRIP, sc=strip_column * width, tall=tall):
+            part(o, 0, 0, r, width, c, width)
+            part(o, width, 0, s, tall - width, sc, width)
+
+        if x == 0:
+
+            @pl.when(diagonal == 1)
+            def _(o=out_ref, r=row * width, c=column * width, s=strip * STRIP, sc=strip_column * width, tall=tall):
+                part(o, 0, 0, r, third, c, width)
+                part(o, third, 0, r + third, third, c + third, 2 * third)
+                part(o, third, 2 * third, r + 2 * third, third, c + 2 * third, third)
+                part(o, 2 * third, 0, s, tall - 2 * third, sc, width)
+
+
+def moment_blocks(table, pieces, turned, mine, width, dtype, name, after=()):
+    count = len(pieces)
     smem, vmem, any_ = [pl.BlockSpec(memory_space=m) for m in (pltpu.SMEM, pltpu.VMEM, pl.ANY)]
-    piece = (width + strip, width)
+    piece = (width + STRIP, width)
     return pl.pallas_call(
-        functools.partial(blocks_kernel, count),
+        functools.partial(blocks_kernel, pieces, width),
         out_shape=[jax.ShapeDtypeStruct(piece, dtype)] * count,
         in_specs=[smem, vmem, vmem] + [any_] * len(after),
         out_specs=[vmem] * count,
         cost_estimate=pl.CostEstimate(
             flops=2 * count * mine.shape[0] * width * piece[0],
-            bytes_accessed=2 * turned.size + 2 * mine.size + count * width * piece[0] * 4,
+            bytes_accessed=0,
             transcendentals=0,
         ),
         compiler_params=pltpu.CompilerParams(vmem_limit_bytes=24 << 20),
@@ -221,7 +228,8 @@
     )(table, turned, mine, *after)
 
 
-STRIP = 96
+STRIP = 32
+FIELDS = 5
 
 
 def is_diagonal(b, e):
@@ -252,18 +260,18 @@
 
 
 def job_table(which, width):
-    table = np.full((8, 2, len(which), 4), -1, np.int32)
+    table = np.zeros((8, 2, len(which), FIELDS), np.int32)
     for p, b in enumerate(SNAKE):
         for e in range(2):
             for n, (x, t) in enumerate(which):
                 q = SNAKE[(p + t) % 8]
-                table[b, e, n, :2] = (q % 4 + (0 if q // 4 == e else 4), owned_columns(q, e)[x])
+                row, column = q % 4 + (0 if q // 4 == e else 4), owned_columns(q, e)[x]
                 if is_diagonal(q, e):
                     lead, other = (q % 4, (q + 2) % 4) if leads(q) else ((q + 2) % 4, q % 4)
-                    first = lead * width + (0 if leads(q) else width // 2)
+                    first = lead * width + (0 if leads(q) else width // 2) + x * (width // 3 + STRIP)
                 else:
-                    first, other = (4 + q % 4) * width, fourth_column(q, e)
-                table[b, e, n, 2:] = (first // STRIP + x, other)
+                    first, other = row * width + x * STRIP, fourth_column(q, e)
+                table[b, e, n] = (row, column, first // STRIP, other, is_diagonal(q, e))
     return table.reshape(16, -1)
 
 
@@ -306,19 +314,26 @@
 
 def outgoing_kernel(scale, place, own0, own1, right0, left1, right1, left0, one, other, share):
     width = one.shape[0]
+    third, half = width // 3, width // 2
+    tall = width + STRIP
     kind = place[my_row(), 4]
-    block, strip = slice(0, width), slice(width, width + STRIP)
-    one[...] = (total(own1, right1, left1, block) * scale).astype(BF16)
-    share[:STRIP, :] = total(own0, right0, left0, strip) * scale
-    share[STRIP:, :] = total(own1, right1, left1, strip) * scale
+    one[...] = (total(own1, right1, left1, slice(0, width)) * scale).astype(BF16)
+    tail = total(own1, right1, left1, slice(width, tall)) * scale
 
     @pl.when(kind == 0)
     def _():
-        other[...] = ((total(own0, right0, left0, block) * scale).T[width // 2 :, :]).astype(BF16)
+        share[:STRIP, :] = total(own0, right0, left0, slice(width, tall)) * scale
+        share[STRIP : 2 * STRIP, :] = tail
+        share[2 * STRIP :, :] = jnp.zeros((half - 2 * STRIP, width), F32)
+        turned = (total(own0, right0, left0, slice(0, width)) * scale).T
+        other[...] = turned[2 * STRIP :, :].astype(BF16)
 
     @pl.when(kind > 0)
     def _():
-        other[...] = share[...].astype(BF16)
+        share[: half - STRIP, :] = total(own0, right0, left0, slice(2 * third, tall)) * scale
+        share[half - STRIP :, :] = tail
+        other[:half, :] = share[...].astype(BF16)
+        other[half:, :] = jnp.zeros((width - 2 * STRIP - half, width), BF16)
 
 
 def put(place, n, made, out_ref, sem):
@@ -328,12 +343,27 @@
 
 
 def own_kernel(scale, place, own0, own1, right0, left1, right1, left0, out_ref, made, sems):
-    block = slice(0, made.shape[1])
-    copies = []
-    for n, parts in enumerate(((own0, right0, left0), (own1, right1, left1))):
-        made[n] = total(*parts, block) * scale
-        copies.append(put(place, n, made.at[n], out_ref, sems.at[n]))
-        copies[-1].start()
+    width = made.shape[1]
+    third = width // 3
+    made[1] = total(own1, right1, left1, slice(0, width)) * scale
+    copies = [put(place, n, made.at[n], out_ref, sems.at[n]) for n in range(2)]
+    copies[1].start()
+
+    @pl.when(place[my_row(), 4] == 0)
+    def _():
+        made[0] = total(own0, right0, left0, slice(0, width)) * scale
+
+    @pl.when(place[my_row(), 4] > 0)
+    def _():
+        tiles = total(own0, right0, left0, slice(0, 2 * third)) * scale
+        upper = {(0, 0): (0, 0), (0, 1): (0, 1), (0, 2): (0, 2), (1, 1): (1, 0), (1, 2): (1, 1), (2, 2): (1, 2)}
+        for (i, j), (r, c) in upper.items():
+            tile = tiles[r * third : (r + 1) * third, c * third : (c + 1) * third]
+            made[0, i * third : (i + 1) * third, j * third : (j + 1) * third] = tile
+            if i != j:
+                made[0, j * third : (j + 1) * third, i * third : (i + 1) * third] = tile.T
+
+    copies[0].start()
     for copy in copies:
         copy.wait()
 
@@ -347,16 +377,21 @@
 
 def other_kernel(place, share, other, result_ref, out_ref, made, sem):
     kind = place[my_row(), 4]
-    half = other.shape[0]
-
-    @pl.when(kind < 2)
+    half = share.shape[0]
+
+    @pl.when(kind == 0)
+    def _():
+        made[: 2 * STRIP, :] = share[: 2 * STRIP, :]
+        made[2 * STRIP :, :] = other[...].astype(F32)
+
+    @pl.when(kind == 1)
     def _():
         made[:half, :] = share[...]
-        made[half:, :] = other[...].astype(F32)
+        made[half:, :] = other[:half, :].astype(F32)
 
     @pl.when(kind == 2)
     def _():
-        made[...] = jnp.concatenate([other[...].astype(F32), share[...]], axis=0).T
+        made[...] = jnp.concatenate([other[:half, :].astype(F32), share[...]], axis=0).T
 
     copy = put(place, 3, made, out_ref, sem)
     copy.start()
@@ -370,7 +405,8 @@
 
     def compute(which, name, dtype, after=()):
         table = jnp.asarray(job_table(which, width))
-        blocks.update(zip(which, moment_blocks(table, turned, mine, width, STRIP, dtype, name, after)))
+        pieces = tuple(x for x, _ in which)
+        blocks.update(zip(which, moment_blocks(table, pieces, turned, mine, width, dtype, name, after)))
 
     def hop(value, key):
         return lax.ppermute(value, both, ring_perm(1 if key[1] <= (4 if key[0] == 0 else 3) else -1))
@@ -406,8 +442,8 @@
         functools.partial(outgoing_kernel, scale),
         out_shape=[
             jax.ShapeDtypeStruct((width, width), BF16),
-            jax.ShapeDtypeStruct((2 * STRIP, width), BF16),
-            jax.ShapeDtypeStruct((2 * STRIP, width), F32),
+            jax.ShapeDtypeStruct((width - 2 * STRIP, width), BF16),
+            jax.ShapeDtypeStruct((width // 2, width), F32),
         ],
         in_specs=[smem] + [vmem] * 6,
         out_specs=[vmem] * 3,

time: 95 us -> 92.6 us (0.975)
  Pallas kernels: 33.9 us -> 30 us
  starting transfers between devices: 17.3 us -> 19.4 us
  waiting for transfers between devices: 42.4 us -> 41.2 us
    pallas_call x5, Pallas kernels: 15.4 us -> 11.5 us  [moment_blocks(): pl.pallas_call(functools.partial(blocks_kernel, pieces, width), out_shape...]
    ppermute x14, waiting for transfers between devices: 33.5 us -> 31.4 us  [hop(): lax.ppermute(value, both, ring_perm(1 if key[1] <= (4 if key[0] == 0 else...]
    ppermute x1, starting transfers between devices: 4.54 us -> 5.6 us  [symmetric_moment(): one = lax.ppermute(one, both, perm_one)]
    ppermute x1, waiting for transfers between devices: 3.45 us -> 4.49 us  [symmetric_moment(): one = lax.ppermute(one, both, perm_one)]
    ppermute x14, starting transfers between devices: 12.2 us -> 13.2 us  [hop(): lax.ppermute(value, both, ring_perm(1 if key[1] <= (4 if key[0] == 0 else...]
  transfers between devices with their start and end apart: 18 -> 18, of which waited for: 11 -> 11; matrix products, arithmetic and copies ran while one was open for 1% -> 1% of each run, Pallas kernels for 24% -> 21%
where the time goes in v8:
time: 92.6 us; the launch traced here: 91.7 us
  waiting for transfers between devices  41.2 us (44%)
  Pallas kernels  30 us (32%)
  starting transfers between devices  19.4 us (21%)
    ppermute x14, waiting for transfers between devices, hop(): lax.ppermute(value, both, ring_perm(1 if key[1] <= (4 if key[0] == 0 else...  31.4 us
    ppermute x14, starting transfers between devices, hop(): lax.ppermute(value, both, ring_perm(1 if key[1] <= (4 if key[0] == 0 else...  13.2 us
    pallas_call x5, Pallas kernels, moment_blocks(): pl.pallas_call(functools.partial(blocks_kernel, pieces, width), out_shape...  11.5 us
    pallas_call x2, Pallas kernels, pick_half(): pl.pallas_call(functools.partial(pick_kernel, first), out_shape=out_shape...  10.1 us
    ppermute x1, starting transfers between devices, symmetric_moment(): one = lax.ppermute(one, both, perm_one)  5.6 us
    ppermute x1, waiting for transfers between devices, symmetric_moment(): one = lax.ppermute(one, both, perm_one)  4.49 us
    pallas_call x2, Pallas kernels, symmetric_moment(): pl.pallas_call(kernel, out_shape=result, in_specs=[smem] + [vmem] * len(a...  3.22 us
    ppermute x1, waiting for transfers between devices, per_device(): from_peer_too = lax.ppermute(kept, 'expert', swap)  2.9 us
  transfers between devices with their start and end apart: 18, of which 11 were waited for; matrix products, arithmetic and copies ran while one was open for 1% of the time, Pallas kernels for 21%

profile of v8, /device:TPU:1, one launch (start us, length us, event | category | flops | bytes accessed | tf_op | source)
XLA Modules:
  0.0 91.7 jit_solution(3254531199773509145)
XLA Ops:
  0.0 5.5 %pick_first.1 = (bf16[768,1536]{1,0:T(8,128)(2,1)S(1)}, bf16[1536,256]{1,0:T(8,128)(2,1)S(1)}, s32[16,128]{1,0:T(8,128)S(1)}, f32[768,128]{1,0:T(8,128)S(1)}) custom-call(s32[2,768]{1,0:T(2,128)} %bitcast.2, f32[2,768]{1,0:T(2,128)} %bitcast.3, bf16[1536,3072]{1,0:T(8,128)(2,1)} %refs_3_.1), custom_call_target="tpu_custom_call" | custom-call | flops 1207959552 | bytes 7077888 | tf_op jit(solution)/shard_map/pick_first/pallas_call | solution.py:131
  5.6 0.1 collective-permute-start.1
  5.7 4.6 %pick_second.1.ours_ref = bf16[768,1536]{1,0:T(8,128)(2,1)S(1)} custom-call(s32[16,128]{1,0:T(8,128)S(1)} %get-tuple-element.32.refs_0_, bf16[1536,256]{1,0:T(8,128)(2,1)S(1)} %get-tuple-element.33.refs_1_, f32[768,128]{1,0:T(8,128)S(1)} %get-tuple-element.30.refs_2_.coef_ref, bf16[1536,3072]{1,0:T(8,128)(2,1)} %refs_3_.1), custom_call_target="tpu_custom_call" | custom-call | flops 1207959552 | bytes 7077888 | tf_op jit(solution)/shard_map/pick_second/pallas_call | solution.py:131
  10.2 0.5 collective-permute-start
  10.8 0.0 collective-permute-done.1.theirs_ref
  10.8 1.2 %merge_first.1 = (bf16[768,1536]{1,0:T(8,128)(2,1)S(1)}, bf16[3072,768]{1,0:T(8,128)(2,1)S(1)}) custom-call(f32[768,128]{1,0:T(8,128)S(1)} %get-tuple-element.30.refs_2_.coef_ref, bf16[768,1536]{1,0:T(8,128)(2,1)S(1)} %pick_second.1.ours_ref, bf16[768,1536]{1,0:T(8,128)(2,1)S(1)} %collective-permute-done.1.theirs_ref), custom_call_target="tpu_custom_call" | custom-call | flops 4718592 | bytes 7077888 | tf_op jit(solution)/shard_map/merge_first/pallas_call | solution.py:168
  12.0 2.9 %collective-permute-done.theirs_ref = bf16[768,1536]{1,0:T(8,128)(2,1)S(1)} collective-permute-done((bf16[768,1536]{1,0:T(8,128)(2,1)S(1)}, bf16[768,1536]{1,0:T(8,128)(2,1)S(1)}, u32[]{:S(2)}, u32[]{:S(2)}) %collective-permute-start) | collective-permute-done | bytes 2359328 | tf_op jit(solution)/shard_map/ppermute | solution.py:489
  14.9 1.2 %merge_second.1.turned_ref = bf16[3072,768]{1,0:T(8,128)(2,1)S(1)} custom-call(f32[768,128]{1,0:T(8,128)S(1)} %get-tuple-element.30.refs_2_.coef_ref, bf16[768,1536]{1,0:T(8,128)(2,1)S(1)} %get-tuple-element.31.ours_ref, bf16[768,1536]{1,0:T(8,128)(2,1)S(1)} %collective-permute-done.theirs_ref, ...), custom_call_target="tpu_custom_call", output_to_operand_aliasing={{}: (3, {})} | custom-call | flops 4718592 | bytes 7077888 | tf_op jit(solution)/shard_map/merge_second/pallas_call | solution.py:168
  16.1 0.0 copy-start.4
  16.1 1.7 %blocks0.1 = (bf16[416,384]{1,0:T(8,128)(2,1)S(1)}, bf16[416,384]{1,0:T(8,128)(2,1)S(1)}) custom-call(s32[16,10]{1,0:T(8,128)S(1)} %copy-done.5, bf16[3072,768]{1,0:T(8,128)(2,1)S(1)} %merge_second.1.turned_ref, bf16[768,1536]{1,0:T(8,128)(2,1)S(1)} %get-tuple-element.35.mine_ref), custom_call_target="tpu_custom_call" | custom-call | flops 490733568 | tf_op jit(solution)/shard_map/blocks0/pallas_call | solution.py:216
  17.8 0.0 copy-start.3
  17.8 2.7 %collective-permute-start.6 = (bf16[416,384]{1,0:T(8,128)(2,1)S(1)}, bf16[416,384]{1,0:T(8,128)(2,1)S(1)}, u32[]{:S(2)}, u32[]{:S(2)}) collective-permute-start(bf16[416,384]{1,0:T(8,128)(2,1)S(1)} %get-tuple-element.42), channel_id=1, source_target_pairs={{0,2},{1,3},{4,0},{5,1},{8,4},{9,5},{12,8},{13,9},{14,12},{15,13},... | collective-permute-start | bytes 958472 | tf_op jit(solution)/shard_map/ppermute | solution.py:412
  20.5 0.0 copy-done.4
  20.5 1.7 %blocks0b.1 = (bf16[416,384]{1,0:T(8,128)(2,1)S(1)}, bf16[416,384]{1,0:T(8,128)(2,1)S(1)}) custom-call(s32[16,10]{1,0:T(8,128)S(1)} %copy-done.4, bf16[3072,768]{1,0:T(8,128)(2,1)S(1)} %merge_second.1.turned_ref, bf16[768,1536]{1,0:T(8,128)(2,1)S(1)} %get-tuple-element.35.mine_ref), custom_call_target="tpu_custom_call" | custom-call | flops 490733568 | tf_op jit(solution)/shard_map/blocks0b/pallas_call | solution.py:216
  22.2 0.1 collective-permute-start.10
  22.4 1.4 %collective-permute-start.13 = (bf16[416,384]{1,0:T(8,128)(2,1)S(1)}, bf16[416,384]{1,0:T(8,128)(2,1)S(1)}, u32[]{:S(2)}, u32[]{:S(2)}) collective-permute-start(bf16[416,384]{1,0:T(8,128)(2,1)S(1)} %get-tuple-element.49), channel_id=1, source_target_pairs={{0,2},{1,3},{4,0},{5,1},{8,4},{9,5},{12,8},{13,9},{14,12},{15,13},... | collective-permute-start | bytes 958472 | tf_op jit(solution)/shard_map/ppermute | solution.py:412
  23.8 0.1 collective-permute-start.2
  23.8 2.6 %blocks1.1 = (f32[416,384]{1,0:T(8,128)S(1)}, f32[416,384]{1,0:T(8,128)S(1)}, f32[416,384]{1,0:T(8,128)S(1)}, f32[416,384]{1,0:T(8,128)S(1)}) custom-call(s32[16,20]{1,0:T(8,128)S(1)} %copy-done.3, bf16[3072,768]{1,0:T(8,128)(2,1)S(1)} %merge_second.1.turned_ref, bf16[768,1536]{1,0:T(8,128)(2,1)S(1)} %get-tuple-element.35.mine_ref), custom_call_target="tpu_custom_call" | custom-call | flops 981467136 | tf_op jit(solution)/shard_map/blocks1/pallas_call | solution.py:216
  26.5 1.8 %collective-permute-done.6 = bf16[416,384]{1,0:T(8,128)(2,1)S(1)} collective-permute-done((bf16[416,384]{1,0:T(8,128)(2,1)S(1)}, bf16[416,384]{1,0:T(8,128)(2,1)S(1)}, u32[]{:S(2)}, u32[]{:S(2)}) %collective-permute-start.6) | collective-permute-done | bytes 319520 | tf_op jit(solution)/shard_map/ppermute | solution.py:412
  28.3 0.1 add_convert_fusion.6
  28.4 1.2 %collective-permute-start.7 = (bf16[416,384]{1,0:T(8,128)(2,1)S(1)}, bf16[416,384]{1,0:T(8,128)(2,1)S(1)}, u32[]{:S(2)}, u32[]{:S(2)}) collective-permute-start(bf16[416,384]{1,0:T(8,128)(2,1)S(1)} %add_convert_fusion.6), channel_id=1, source_target_pairs={{0,2},{1,3},{4,0},{5,1},{8,4},{9,5},{12,8},{13,9},{14,12},{15,13},... | collective-permute-start | bytes 958472 | tf_op jit(solution)/shard_map/ppermute | solution.py:412
  29.6 8.2 %collective-permute-done.2.refs_0_ = bf16[416,384]{1,0:T(8,128)(2,1)S(1)} collective-permute-done((bf16[416,384]{1,0:T(8,128)(2,1)S(1)}, bf16[416,384]{1,0:T(8,128)(2,1)S(1)}, u32[]{:S(2)}, u32[]{:S(2)}) %collective-permute-start.2) | collective-permute-done | bytes 319520 | tf_op jit(solution)/shard_map/ppermute | solution.py:412
  37.8 0.1 add_convert_fusion.9
  37.9 0.4 collective-permute-start.3
  38.3 0.0 collective-permute-done.10
  38.3 0.1 add_convert_fusion.3
  38.4 1.2 %collective-permute-start.11 = (bf16[416,384]{1,0:T(8,128)(2,1)S(1)}, bf16[416,384]{1,0:T(8,128)(2,1)S(1)}, u32[]{:S(2)}, u32[]{:S(2)}) collective-permute-start(bf16[416,384]{1,0:T(8,128)(2,1)S(1)} %add_convert_fusion.3), channel_id=1, source_target_pairs={{0,4},{1,5},{4,8},{5,9},{8,12},{9,13},{12,14},{13,15},{14,10},{15,... | collective-permute-start | bytes 958472 | tf_op jit(solution)/shard_map/ppermute | solution.py:412
  39.6 0.0 collective-permute-done.13
  39.6 0.1 add_convert_fusion.1
  39.7 0.4 collective-permute-start.14
  40.1 2.6 %blocks2.1 = (f32[416,384]{1,0:T(8,128)S(1)}, f32[416,384]{1,0:T(8,128)S(1)}, f32[416,384]{1,0:T(8,128)S(1)}, f32[416,384]{1,0:T(8,128)S(1)}) custom-call(s32[16,20]{1,0:T(8,128)S(1)} %copy-done.2, bf16[3072,768]{1,0:T(8,128)(2,1)S(1)} %merge_second.1.turned_ref, bf16[768,1536]{1,0:T(8,128)(2,1)S(1)} %get-tuple-element.35.mine_ref, ...), custom_call_target="tpu_custom_call" | custom-call | flops 981467136 | tf_op jit(solution)/shard_map/blocks2/pallas_call | solution.py:216
  42.7 0.0 collective-permute-done.7
  42.7 0.0 copy-start.1
  42.7 0.1 add_convert_fusion.5
  42.8 1.1 %collective-permute-start.8 = (bf16[416,384]{1,0:T(8,128)(2,1)S(1)}, bf16[416,384]{1,0:T(8,128)(2,1)S(1)}, u32[]{:S(2)}, u32[]{:S(2)}) collective-permute-start(bf16[416,384]{1,0:T(8,128)(2,1)S(1)} %add_convert_fusion.5), channel_id=1, source_target_pairs={{0,2},{1,3},{4,0},{5,1},{8,4},{9,5},{12,8},{13,9},{14,12},{15,13},... | collective-permute-start | bytes 958472 | tf_op jit(solution)/shard_map/ppermute | solution.py:412
  44.0 1.7 %collective-permute-done.3.refs_0_ = bf16[416,384]{1,0:T(8,128)(2,1)S(1)} collective-permute-done((bf16[416,384]{1,0:T(8,128)(2,1)S(1)}, bf16[416,384]{1,0:T(8,128)(2,1)S(1)}, u32[]{:S(2)}, u32[]{:S(2)}) %collective-permute-start.3) | collective-permute-done | bytes 319520 | tf_op jit(solution)/shard_map/ppermute | solution.py:412
  45.7 0.1 add_convert_fusion.8
  45.8 0.8 collective-permute-start.4
  46.5 6.0 %collective-permute-done.11 = bf16[416,384]{1,0:T(8,128)(2,1)S(1)} collective-permute-done((bf16[416,384]{1,0:T(8,128)(2,1)S(1)}, bf16[416,384]{1,0:T(8,128)(2,1)S(1)}, u32[]{:S(2)}, u32[]{:S(2)}) %collective-permute-start.11) | collective-permute-done | bytes 319520 | tf_op jit(solution)/shard_map/ppermute | solution.py:412
  52.5 0.1 add_convert_fusion.2
  52.6 0.8 collective-permute-start.12
  53.4 0.0 collective-permute-done.14
  53.4 0.1 add_convert_fusion
  53.5 0.8 collective-permute-start.15
  54.3 2.8 %blocks3.1 = (f32[416,384]{1,0:T(8,128)S(1)}, f32[416,384]{1,0:T(8,128)S(1)}, f32[416,384]{1,0:T(8,128)S(1)}, f32[416,384]{1,0:T(8,128)S(1)}) custom-call(s32[16,20]{1,0:T(8,128)S(1)} %copy-done.1, bf16[3072,768]{1,0:T(8,128)(2,1)S(1)} %merge_second.1.turned_ref, bf16[768,1536]{1,0:T(8,128)(2,1)S(1)} %get-tuple-element.35.mine_ref, ...), custom_call_target="tpu_custom_call" | custom-call | flops 981467136 | tf_op jit(solution)/shard_map/blocks3/pallas_call | solution.py:216
  57.1 0.0 copy-start
  57.1 0.0 collective-permute-done.8
  57.1 0.1 add_convert_fusion.4
  57.2 1.4 %collective-permute-start.9 = (bf16[416,384]{1,0:T(8,128)(2,1)S(1)}, bf16[416,384]{1,0:T(8,128)(2,1)S(1)}, u32[]{:S(2)}, u32[]{:S(2)}) collective-permute-start(bf16[416,384]{1,0:T(8,128)(2,1)S(1)} %add_convert_fusion.4), channel_id=1, source_target_pairs={{0,2},{1,3},{4,0},{5,1},{8,4},{9,5},{12,8},{13,9},{14,12},{15,13},... | collective-permute-start | bytes 958472 | tf_op jit(solution)/shard_map/ppermute | solution.py:412
  58.6 0.8 collective-permute-done.4
  59.4 0.1 add_convert_fusion.7
  59.5 0.8 collective-permute-start.5
  60.2 6.0 %collective-permute-done.12.right1 = bf16[416,384]{1,0:T(8,128)(2,1)S(1)} collective-permute-done((bf16[416,384]{1,0:T(8,128)(2,1)S(1)}, bf16[416,384]{1,0:T(8,128)(2,1)S(1)}, u32[]{:S(2)}, u32[]{:S(2)}) %collective-permute-start.12) | collective-permute-done | bytes 319520 | tf_op jit(solution)/shard_map/ppermute | solution.py:412
  66.2 0.0 collective-permute-done.15.left0
  66.2 0.2 collective-permute-done.9.left1
  66.5 6.6 %collective-permute-done.5.right0 = bf16[416,384]{1,0:T(8,128)(2,1)S(1)} collective-permute-done((bf16[416,384]{1,0:T(8,128)(2,1)S(1)}, bf16[416,384]{1,0:T(8,128)(2,1)S(1)}, u32[]{:S(2)}, u32[]{:S(2)}) %collective-permute-start.5) | collective-permute-done | bytes 319520 | tf_op jit(solution)/shard_map/ppermute | solution.py:412
  73.1 1.0 %outgoing.1 = (bf16[384,384]{1,0:T(8,128)(2,1)S(1)}, bf16[320,384]{1,0:T(8,128)(2,1)S(1)}, f32[192,384]{1,0:T(8,128)S(1)}) custom-call(s32[16,5]{1,0:T(8,128)S(1)} %copy-done, f32[416,384]{1,0:T(8,128)S(1)} %get-tuple-element.38.own0, f32[416,384]{1,0:T(8,128)S(1)} %get-tuple-element.39.own1, bf16[416,384]{1,0:T(8,128)(2,1)S(1)} %collective-permute-done.5.right0, ...), custom_call_target="tpu_custom_call" | custom-call | tf_op jit(solution)/shard_map/outgoing/pallas_call | solution.py:441
  74.1 5.6 %collective-permute-start.17 = (bf16[384,384]{1,0:T(8,128)(2,1)S(1)}, bf16[384,384]{1,0:T(8,128)(2,1)S(1)}, u32[]{:S(2)}, u32[]{:S(2)}) collective-permute-start(bf16[384,384]{1,0:T(8,128)(2,1)S(1)} %get-tuple-element.54), channel_id=1, source_target_pairs={{0,2},{1,10},{2,4},{3,12},{4,6},{5,14},{6,0},{7,8},{8,5},{9,11},{1... | collective-permute-start | bytes 884744 | tf_op jit(solution)/shard_map/ppermute | solution.py:454
  79.7 0.0 collective-permute-start.16
  79.7 1.8 %own.1.result_ref = f32[384,1536]{1,0:T(8,128)} custom-call(s32[16,5]{1,0:T(8,128)S(1)} %copy-done, f32[416,384]{1,0:T(8,128)S(1)} %get-tuple-element.38.own0, f32[416,384]{1,0:T(8,128)S(1)} %get-tuple-element.39.own1, bf16[416,384]{1,0:T(8,128)(2,1)S(1)} %collective-permute-done.5.right0, bf16[416,384]{1,0:T(8,128)(2,1)S(1)} %collective-permute-done.9.left1, ...), custom_call_target="tpu_custom_call" | custom-call | tf_op jit(solution)/shard_map/own/pallas_call | solution.py:456
  81.5 4.5 %collective-permute-done.17.one = bf16[384,384]{1,0:T(8,128)(2,1)S(1)} collective-permute-done((bf16[384,384]{1,0:T(8,128)(2,1)S(1)}, bf16[384,384]{1,0:T(8,128)(2,1)S(1)}, u32[]{:S(2)}, u32[]{:S(2)}) %collective-permute-start.17) | collective-permute-done | bytes 294944 | tf_op jit(solution)/shard_map/ppermute | solution.py:454
  86.0 1.7 %one.1.result_ref = f32[384,1536]{1,0:T(8,128)} custom-call(s32[16,5]{1,0:T(8,128)S(1)} %copy-done, bf16[384,384]{1,0:T(8,128)(2,1)S(1)} %collective-permute-done.17.one, f32[384,1536]{1,0:T(8,128)} %own.1.result_ref), custom_call_target="tpu_custom_call", output_to_operand_aliasing={{}: (2, {})} | custom-call | tf_op jit(solution)/shard_map/one/pallas_call | solution.py:466
  87.7 2.4 %collective-permute-done.16.other = bf16[320,384]{1,0:T(8,128)(2,1)S(1)} collective-permute-done((bf16[320,384]{1,0:T(8,128)(2,1)S(1)}, bf16[320,384]{1,0:T(8,128)(2,1)S(1)}, u32[]{:S(2)}, u32[]{:S(2)}) %collective-permute-start.16) | collective-permute-done | bytes 245792 | tf_op jit(solution)/shard_map/ppermute | solution.py:455
  90.0 1.6 %other.1 = f32[384,1536]{1,0:T(8,128)} custom-call(s32[16,5]{1,0:T(8,128)S(1)} %copy-done, f32[192,384]{1,0:T(8,128)S(1)} %get-tuple-element.52.share, bf16[320,384]{1,0:T(8,128)(2,1)S(1)} %collective-permute-done.16.other, f32[384,1536]{1,0:T(8,128)} %one.1.result_ref), custom_call_target="tpu_custom_call", output_to_operand_aliasing={{}: (3, {})} | custom-call | tf_op jit(solution)/shard_map/other/pallas_call | solution.py:466
  (7 shorter events, 0.0 us)
Async XLA Ops:
  5.6 5.2 %collective-permute-start.1 = (bf16[768,1536]{1,0:T(8,128)(2,1)S(1)}, bf16[768,1536]{1,0:T(8,128)(2,1)S(1)}, u32[]{:S(2)}, u32[]{:S(2)}) collective-permute-start(bf16[768,1536]{1,0:T(8,128)(2,1)S(1)} %get-tuple-element.31.ours_ref), channel_id=1, source_target_pairs={{0,1},{1,0},{2,3},{3,2},{4,5},{5,4},{6,7},{7,6},{8,9},{9,8},{10,11... | collective-permute-start | bytes 7077896 | tf_op jit(solution)/shard_map/ppermute | solution.py:487
  10.2 4.7 %collective-permute-start = (bf16[768,1536]{1,0:T(8,128)(2,1)S(1)}, bf16[768,1536]{1,0:T(8,128)(2,1)S(1)}, u32[]{:S(2)}, u32[]{:S(2)}) collective-permute-start(bf16[768,1536]{1,0:T(8,128)(2,1)S(1)} %pick_second.1.ours_ref), channel_id=1, source_target_pairs={{0,1},{1,0},{2,3},{3,2},{4,5},{5,4},{6,7},{7,6},{8,9},{9,8},{10,11... | collective-permute-start | bytes 7077896 | tf_op jit(solution)/shard_map/ppermute | solution.py:489
  14.9 1.2 %copy-start.5 = (s32[16,10]{1,0:T(8,128)S(1)}, s32[16,10]{1,0:T(8,128)}, u32[]{:S(2)}) copy-start(s32[16,10]{1,0:T(8,128)} %constant.12.clone.table) | copy-start | bytes 1924
  16.1 4.4 %copy-start.4 = (s32[16,10]{1,0:T(8,128)S(1)}, s32[16,10]{1,0:T(8,128)}, u32[]{:S(2)}) copy-start(s32[16,10]{1,0:T(8,128)} %constant.13.clone.table) | copy-start | bytes 1924
  17.8 6.0 %copy-start.3 = (s32[16,20]{1,0:T(8,128)S(1)}, s32[16,20]{1,0:T(8,128)}, u32[]{:S(2)}) copy-start(s32[16,20]{1,0:T(8,128)} %constant.14.clone.table) | copy-start | bytes 3844
  17.8 10.5 %collective-permute-start.6 = (bf16[416,384]{1,0:T(8,128)(2,1)S(1)}, bf16[416,384]{1,0:T(8,128)(2,1)S(1)}, u32[]{:S(2)}, u32[]{:S(2)}) collective-permute-start(bf16[416,384]{1,0:T(8,128)(2,1)S(1)} %get-tuple-element.42), channel_id=1, source_target_pairs={{0,2},{1,3},{4,0},{5,1},{8,4},{9,5},{12,8},{13,9},{14,12},{15,13},... | collective-permute-start | bytes 958472 | tf_op jit(solution)/shard_map/ppermute | solution.py:412
  22.2 16.1 %collective-permute-start.10 = (bf16[416,384]{1,0:T(8,128)(2,1)S(1)}, bf16[416,384]{1,0:T(8,128)(2,1)S(1)}, u32[]{:S(2)}, u32[]{:S(2)}) collective-permute-start(bf16[416,384]{1,0:T(8,128)(2,1)S(1)} %get-tuple-element.46), channel_id=1, source_target_pairs={{0,4},{1,5},{4,8},{5,9},{8,12},{9,13},{12,14},{13,15},{14,10},{15,... | collective-permute-start | bytes 958472 | tf_op jit(solution)/shard_map/ppermute | solution.py:412
  22.4 17.2 %collective-permute-start.13 = (bf16[416,384]{1,0:T(8,128)(2,1)S(1)}, bf16[416,384]{1,0:T(8,128)(2,1)S(1)}, u32[]{:S(2)}, u32[]{:S(2)}) collective-permute-start(bf16[416,384]{1,0:T(8,128)(2,1)S(1)} %get-tuple-element.49), channel_id=1, source_target_pairs={{0,2},{1,3},{4,0},{5,1},{8,4},{9,5},{12,8},{13,9},{14,12},{15,13},... | collective-permute-start | bytes 958472 | tf_op jit(solution)/shard_map/ppermute | solution.py:412
  23.8 14.1 %collective-permute-start.2 = (bf16[416,384]{1,0:T(8,128)(2,1)S(1)}, bf16[416,384]{1,0:T(8,128)(2,1)S(1)}, u32[]{:S(2)}, u32[]{:S(2)}) collective-permute-start(bf16[416,384]{1,0:T(8,128)(2,1)S(1)} %get-tuple-element.36), channel_id=1, source_target_pairs={{0,4},{1,5},{4,8},{5,9},{8,12},{9,13},{12,14},{13,15},{14,10},{15,... | collective-permute-start | bytes 958472 | tf_op jit(solution)/shard_map/ppermute | solution.py:412
  28.3 11.7 %copy-start.2 = (s32[16,20]{1,0:T(8,128)S(1)}, s32[16,20]{1,0:T(8,128)}, u32[]{:S(2)}) copy-start(s32[16,20]{1,0:T(8,128)} %constant.15.clone.table) | copy-start | bytes 3844
  28.4 14.3 %collective-permute-start.7 = (bf16[416,384]{1,0:T(8,128)(2,1)S(1)}, bf16[416,384]{1,0:T(8,128)(2,1)S(1)}, u32[]{:S(2)}, u32[]{:S(2)}) collective-permute-start(bf16[416,384]{1,0:T(8,128)(2,1)S(1)} %add_convert_fusion.6), channel_id=1, source_target_pairs={{0,2},{1,3},{4,0},{5,1},{8,4},{9,5},{12,8},{13,9},{14,12},{15,13},... | collective-permute-start | bytes 958472 | tf_op jit(solution)/shard_map/ppermute | solution.py:412
  37.9 7.8 %collective-permute-start.3 = (bf16[416,384]{1,0:T(8,128)(2,1)S(1)}, bf16[416,384]{1,0:T(8,128)(2,1)S(1)}, u32[]{:S(2)}, u32[]{:S(2)}) collective-permute-start(bf16[416,384]{1,0:T(8,128)(2,1)S(1)} %add_convert_fusion.9), channel_id=1, source_target_pairs={{0,4},{1,5},{4,8},{5,9},{8,12},{9,13},{12,14},{13,15},{14,10},{15,... | collective-permute-start | bytes 958472 | tf_op jit(solution)/shard_map/ppermute | solution.py:412
  38.4 14.1 %collective-permute-start.11 = (bf16[416,384]{1,0:T(8,128)(2,1)S(1)}, bf16[416,384]{1,0:T(8,128)(2,1)S(1)}, u32[]{:S(2)}, u32[]{:S(2)}) collective-permute-start(bf16[416,384]{1,0:T(8,128)(2,1)S(1)} %add_convert_fusion.3), channel_id=1, source_target_pairs={{0,4},{1,5},{4,8},{5,9},{8,12},{9,13},{12,14},{13,15},{14,10},{15,... | collective-permute-start | bytes 958472 | tf_op jit(solution)/shard_map/ppermute | solution.py:412
  39.7 13.7 %collective-permute-start.14 = (bf16[416,384]{1,0:T(8,128)(2,1)S(1)}, bf16[416,384]{1,0:T(8,128)(2,1)S(1)}, u32[]{:S(2)}, u32[]{:S(2)}) collective-permute-start(bf16[416,384]{1,0:T(8,128)(2,1)S(1)} %add_convert_fusion.1), channel_id=1, source_target_pairs={{0,2},{1,3},{4,0},{5,1},{8,4},{9,5},{12,8},{13,9},{14,12},{15,13},... | collective-permute-start | bytes 958472 | tf_op jit(solution)/shard_map/ppermute | solution.py:412
  42.7 11.5 %copy-start.1 = (s32[16,20]{1,0:T(8,128)S(1)}, s32[16,20]{1,0:T(8,128)}, u32[]{:S(2)}) copy-start(s32[16,20]{1,0:T(8,128)} %constant.16.clone.table) | copy-start | bytes 3844
  42.8 14.3 %collective-permute-start.8 = (bf16[416,384]{1,0:T(8,128)(2,1)S(1)}, bf16[416,384]{1,0:T(8,128)(2,1)S(1)}, u32[]{:S(2)}, u32[]{:S(2)}) collective-permute-start(bf16[416,384]{1,0:T(8,128)(2,1)S(1)} %add_convert_fusion.5), channel_id=1, source_target_pairs={{0,2},{1,3},{4,0},{5,1},{8,4},{9,5},{12,8},{13,9},{14,12},{15,13},... | collective-permute-start | bytes 958472 | tf_op jit(solution)/shard_map/ppermute | solution.py:412
  45.8 13.6 %collective-permute-start.4 = (bf16[416,384]{1,0:T(8,128)(2,1)S(1)}, bf16[416,384]{1,0:T(8,128)(2,1)S(1)}, u32[]{:S(2)}, u32[]{:S(2)}) collective-permute-start(bf16[416,384]{1,0:T(8,128)(2,1)S(1)} %add_convert_fusion.8), channel_id=1, source_target_pairs={{0,4},{1,5},{4,8},{5,9},{8,12},{9,13},{12,14},{13,15},{14,10},{15,... | collective-permute-start | bytes 958472 | tf_op jit(solution)/shard_map/ppermute | solution.py:412
  52.6 13.6 %collective-permute-start.12 = (bf16[416,384]{1,0:T(8,128)(2,1)S(1)}, bf16[416,384]{1,0:T(8,128)(2,1)S(1)}, u32[]{:S(2)}, u32[]{:S(2)}) collective-permute-start(bf16[416,384]{1,0:T(8,128)(2,1)S(1)} %add_convert_fusion.2), channel_id=1, source_target_pairs={{0,4},{1,5},{4,8},{5,9},{8,12},{9,13},{12,14},{13,15},{14,10},{15,... | collective-permute-start | bytes 958472 | tf_op jit(solution)/shard_map/ppermute | solution.py:412
  53.5 12.8 %collective-permute-start.15 = (bf16[416,384]{1,0:T(8,128)(2,1)S(1)}, bf16[416,384]{1,0:T(8,128)(2,1)S(1)}, u32[]{:S(2)}, u32[]{:S(2)}) collective-permute-start(bf16[416,384]{1,0:T(8,128)(2,1)S(1)} %add_convert_fusion), channel_id=1, source_target_pairs={{0,2},{1,3},{4,0},{5,1},{8,4},{9,5},{12,8},{13,9},{14,12},{15,13},... | collective-permute-start | bytes 958472 | tf_op jit(solution)/shard_map/ppermute | solution.py:412
  57.1 16.0 %copy-start = (s32[16,5]{1,0:T(8,128)S(1)}, s32[16,5]{1,0:T(8,128)}, u32[]{:S(2)}) copy-start(s32[16,5]{1,0:T(8,128)} %constant.17.clone.place) | copy-start | bytes 964
  57.2 9.3 %collective-permute-start.9 = (bf16[416,384]{1,0:T(8,128)(2,1)S(1)}, bf16[416,384]{1,0:T(8,128)(2,1)S(1)}, u32[]{:S(2)}, u32[]{:S(2)}) collective-permute-start(bf16[416,384]{1,0:T(8,128)(2,1)S(1)} %add_convert_fusion.4), channel_id=1, source_target_pairs={{0,2},{1,3},{4,0},{5,1},{8,4},{9,5},{12,8},{13,9},{14,12},{15,13},... | collective-permute-start | bytes 958472 | tf_op jit(solution)/shard_map/ppermute | solution.py:412
  59.5 13.6 %collective-permute-start.5 = (bf16[416,384]{1,0:T(8,128)(2,1)S(1)}, bf16[416,384]{1,0:T(8,128)(2,1)S(1)}, u32[]{:S(2)}, u32[]{:S(2)}) collective-permute-start(bf16[416,384]{1,0:T(8,128)(2,1)S(1)} %add_convert_fusion.7), channel_id=1, source_target_pairs={{0,4},{1,5},{4,8},{5,9},{8,12},{9,13},{12,14},{13,15},{14,10},{15,... | collective-permute-start | bytes 958472 | tf_op jit(solution)/shard_map/ppermute | solution.py:412
  74.1 11.9 %collective-permute-start.17 = (bf16[384,384]{1,0:T(8,128)(2,1)S(1)}, bf16[384,384]{1,0:T(8,128)(2,1)S(1)}, u32[]{:S(2)}, u32[]{:S(2)}) collective-permute-start(bf16[384,384]{1,0:T(8,128)(2,1)S(1)} %get-tuple-element.54), channel_id=1, source_target_pairs={{0,2},{1,10},{2,4},{3,12},{4,6},{5,14},{6,0},{7,8},{8,5},{9,11},{1... | collective-permute-start | bytes 884744 | tf_op jit(solution)/shard_map/ppermute | solution.py:454
  79.7 10.3 %collective-permute-start.16 = (bf16[320,384]{1,0:T(8,128)(2,1)S(1)}, bf16[320,384]{1,0:T(8,128)(2,1)S(1)}, u32[]{:S(2)}, u32[]{:S(2)}) collective-permute-start(bf16[320,384]{1,0:T(8,128)(2,1)S(1)} %get-tuple-element.53), channel_id=1, source_target_pairs={{0,4},{1,8},{2,6},{3,10},{4,0},{5,12},{6,2},{7,14},{8,3},{9,13},{1... | collective-permute-start | bytes 737288 | tf_op jit(solution)/shard_map/ppermute | solution.py:455

commit v9 on v8

--- a/solution.py
+++ b/solution.py
@@ -57,18 +57,19 @@
             pick_ref[(2 * b + k) * BATCH : (2 * b + k + 1) * BATCH, :] = jnp.where(columns == at, 1.0, 0.0).astype(BF16)
 
 
-def pick_kernel(first, *refs):
+def pick_kernel(first, tiles, *refs):
     if first:
-        ids_hbm, gates_hbm, rows_ref, out_ref, pick_ref, starts_ref, coef_ref = refs[:7]
-        held, in_sems, starts, ids_ref, gates_ref, small_sems = refs[7:]
+        ids_hbm, gates_hbm, rows_ref, out_ref, held, pick_ref, starts_ref, coef_ref = refs[:8]
+        in_sems, starts, ids_ref, gates_ref, small_sems = refs[8:]
     else:
-        starts, pick_ref, coef_ref, rows_ref, out_ref, held, in_sems = refs
-    tokens, width = out_ref.shape
-    tiles, _, tile = held.shape
+        starts, pick_ref, coef_ref, held = refs[:4]
+        out_ref = refs[-1]
+    tokens = out_ref.shape[0]
+    count, _, tile = held.shape
     local = EXPERTS // 2
     member = lax.axis_index("expert")
-    base = (1 - member if first else member) * width
-
+
+    loads = []
     if first:
         small = [
             pltpu.make_async_copy(ids_hbm, ids_ref, small_sems.at[0]),
@@ -76,20 +77,21 @@
         ]
         for copy in small:
             copy.start()
-    loads = []
-    for j in range(tiles):
-        at = pl.ds(pl.multiple_of(base + j * tile, 128), tile)
-        loads.append(pltpu.make_async_copy(rows_ref.at[:, at], held.at[j], in_sems.at[j]))
-        loads[-1].start()
-    if first:
+        for j in range(count):
+            side = 1 - member if j < count // 2 else member
+            at = side * (count // 2 * tile) + j % (count // 2) * tile
+            at = pl.ds(pl.multiple_of(at, 128), tile)
+            loads.append(pltpu.make_async_copy(rows_ref.at[:, at], held.at[j], in_sems.at[j]))
+            loads[-1].start()
         for copy in small:
             copy.wait()
         plan_tokens(ids_ref, gates_ref, pick_ref, starts_ref, coef_ref)
         copy = pltpu.make_async_copy(starts_ref, starts, small_sems.at[2])
         copy.start()
         copy.wait()
-    for j in range(tiles):
-        loads[j].wait()
+    for n, j in enumerate(tiles):
+        if first:
+            loads[j].wait()
         for b in range(tokens // BATCH):
             windows = []
             for k in range(local):
@@ -102,77 +104,93 @@
             )
             rows = slice(b * BATCH, (b + 1) * BATCH)
             total = coef_ref[rows, 0:1] * picked[:BATCH] + coef_ref[rows, 1:2] * picked[BATCH:]
-            out_ref[rows, j * tile : (j + 1) * tile] = total.astype(BF16)
-
-
-def pick_half(args, rows, tokens, width, first, tile=512):
-    tiles = width // tile
-    depth = EXPERTS // 2 * WINDOW
-    any_, vmem = pl.BlockSpec(memory_space=pl.ANY), pl.BlockSpec(memory_space=pltpu.VMEM)
-    in_hbm = lambda x: pltpu.with_memory_space_constraint(x, pltpu.HBM)
-    out_shape = [jax.ShapeDtypeStruct((tokens, width), BF16)]
-    scratch = [pltpu.VMEM((tiles, rows.shape[0], tile), BF16), pltpu.SemaphoreType.DMA((tiles,))]
-    if first:
-        out_shape += [
-            jax.ShapeDtypeStruct((2 * tokens, depth), BF16),
-            jax.ShapeDtypeStruct((tokens // BATCH, 128), I32),
-            jax.ShapeDtypeStruct((tokens, 128), F32),
-        ]
-        args = [in_hbm(x) for x in args]
-        in_specs = [any_] * 3
-        scratch += [
-            pltpu.SMEM((tokens // BATCH, 128), I32),
-            pltpu.VMEM((2, tokens), I32),
-            pltpu.VMEM((2, tokens), F32),
-            pltpu.SemaphoreType.DMA((3,)),
-        ]
-    else:
-        in_specs = [pl.BlockSpec(memory_space=pltpu.SMEM), vmem, vmem, any_]
+            out_ref[rows, n * tile : (n + 1) * tile] = total.astype(BF16)
+    for j, load in enumerate(loads):
+        if j not in tiles:
+            load.wait()
+
+
+def pick_call(first, tiles, args, out_shape, in_specs, scratch, tile):
+    tokens = out_shape[0].shape[0]
+    vmem = pl.BlockSpec(memory_space=pltpu.VMEM)
     return pl.pallas_call(
-        functools.partial(pick_kernel, first),
+        functools.partial(pick_kernel, first, tiles),
         out_shape=out_shape,
         in_specs=in_specs,
         out_specs=[vmem] * len(out_shape),
         scratch_shapes=scratch,
         cost_estimate=pl.CostEstimate(
-            flops=4 * tokens * depth * width, bytes_accessed=2 * (rows.shape[0] + tokens) * width, transcendentals=0
+            flops=tokens * EXPERTS * WINDOW * len(tiles) * tile, bytes_accessed=0, transcendentals=0
         ),
         compiler_params=pltpu.CompilerParams(vmem_limit_bytes=24 << 20),
-        name="pick_first" if first else "pick_second",
-    )(*args, in_hbm(rows))
-
-
-def merge_kernel(first, coef_ref, ours_ref, theirs_ref, *refs):
-    tokens, width = ours_ref.shape
-    tile = 384
+        name="pick_first" if first else "pick",
+    )(*args)
+
+
+def pick_rows(ids, gates, rows, tile):
+    tokens, (depth, channels) = ids.shape[1], rows.shape
+    count = channels // tile
+    out_shape = [
+        jax.ShapeDtypeStruct((tokens, tile), BF16),
+        jax.ShapeDtypeStruct((count, depth, tile), BF16),
+        jax.ShapeDtypeStruct((2 * tokens, EXPERTS // 2 * WINDOW), BF16),
+        jax.ShapeDtypeStruct((tokens // BATCH, 128), I32),
+        jax.ShapeDtypeStruct((tokens, 128), F32),
+    ]
+    scratch = [
+        pltpu.SemaphoreType.DMA((count,)),
+        pltpu.SMEM((tokens // BATCH, 128), I32),
+        pltpu.VMEM((2, tokens), I32),
+        pltpu.VMEM((2, tokens), F32),
+        pltpu.SemaphoreType.DMA((3,)),
+    ]
+    args = [pltpu.with_memory_space_constraint(x, pltpu.HBM) for x in (ids, gates, rows)]
+    return pick_call(True, (0,), args, out_shape, [pl.BlockSpec(memory_space=pl.ANY)] * 3, scratch, tile)
+
+
+def pick_more(tiles, starts, pick, coef, held, after=()):
+    tokens, tile = coef.shape[0], held.shape[2]
+    vmem = pl.BlockSpec(memory_space=pltpu.VMEM)
+    out_shape = [jax.ShapeDtypeStruct((tokens, len(tiles) * tile), BF16)]
+    in_specs = [pl.BlockSpec(memory_space=pltpu.SMEM)] + [vmem] * 3
+    in_specs += [pl.BlockSpec(memory_space=pl.ANY)] * len(after)
+    return pick_call(False, tiles, (starts, pick, coef, held, *after), out_shape, in_specs, [], tile)[0]
+
+
+def merge_kernel(first, tile, pieces, coef_ref, *refs):
+    tokens = coef_ref.shape[0]
+    sides = []
+    for count in pieces:
+        sides.append([ref.at[:, j : j + tile] for ref in refs[:count] for j in range(0, ref.shape[1], tile)])
+        refs = refs[count:]
+    width = len(sides[0]) * tile
     ours = jnp.broadcast_to(coef_ref[:, 2:3], (tokens, tile))
     theirs = jnp.broadcast_to(coef_ref[:, 3:4], (tokens, tile))
-    for j in range(width // tile):
-        at = slice(j * tile, (j + 1) * tile)
-        total = (ours * ours_ref[:, at].astype(F32) + theirs * theirs_ref[:, at].astype(F32)).astype(BF16)
+    for j, (a, b) in enumerate(zip(*sides)):
+        total = (ours * a[...].astype(F32) + theirs * b[...].astype(F32)).astype(BF16)
         if first:
-            refs[0][:, at] = total
-            refs[-1][at, :] = total.T
+            refs[0][:, j * tile : (j + 1) * tile] = total
+            refs[-1][j * tile : (j + 1) * tile, :] = total.T
         else:
             refs[-1][width + j * tile : width + (j + 1) * tile, :] = total.T
 
 
-def merge(coef, ours, theirs, turned=None):
-    tokens, width = ours.shape
+def merge(coef, ours, theirs, width, turned=None, tile=256):
+    tokens = coef.shape[0]
     first = turned is None
     vmem = pl.BlockSpec(memory_space=pltpu.VMEM)
-    args = [coef, ours, theirs] + ([] if first else [turned])
+    args = [coef, *ours, *theirs] + ([] if first else [turned])
     out_shape = [jax.ShapeDtypeStruct((2 * width, tokens), BF16)]
     if first:
         out_shape.insert(0, jax.ShapeDtypeStruct((tokens, width), BF16))
     return pl.pallas_call(
-        functools.partial(merge_kernel, first),
+        functools.partial(merge_kernel, first, tile, (len(ours), len(theirs))),
         out_shape=out_shape,
         in_specs=[vmem] * len(args),
         out_specs=[vmem] * len(out_shape),
-        input_output_aliases={} if first else {3: 0},
+        input_output_aliases={} if first else {len(args) - 1: 0},
         compiler_params=pltpu.CompilerParams(vmem_limit_bytes=24 << 20),
-        cost_estimate=pl.CostEstimate(flops=4 * ours.size, bytes_accessed=6 * ours.size, transcendentals=0),
+        cost_estimate=pl.CostEstimate(flops=4 * tokens * width, bytes_accessed=0, transcendentals=0),
         name="merge_first" if first else "merge_second",
     )(*args)
 
@@ -219,7 +237,7 @@
         in_specs=[smem, vmem, vmem] + [any_] * len(after),
         out_specs=[vmem] * count,
         cost_estimate=pl.CostEstimate(
-            flops=2 * count * mine.shape[0] * width * piece[0],
+            flops=count * mine.shape[0] * width * width,
             bytes_accessed=0,
             transcendentals=0,
         ),
@@ -412,8 +430,7 @@
         return lax.ppermute(value, both, ring_perm(1 if key[1] <= (4 if key[0] == 0 else 3) else -1))
 
     compute(ROUNDS[0][:2], "blocks0", BF16)
-    compute(ROUNDS[0][2:], "blocks0b", BF16)
-    compute(ROUNDS[1], "blocks1", F32)
+    compute(ROUNDS[0][2:], "blocks0b", BF16, after=(blocks[0, 4],))
     moving = {key: blocks[key] for key in ROUNDS[0]}
     arrived = {}
     for n in range(4):
@@ -421,8 +438,9 @@
         for key in ROUNDS[n]:
             if key in moving:
                 landed[key] = hop(moving[key], key)
-        if n < 2:
-            compute(ROUNDS[n + 2], f"blocks{n + 2}", F32, after=(landed[ROUNDS[n][0]],))
+        if n < 3:
+            early = [landed[key] for key in ROUNDS[n][:2]]
+            compute(ROUNDS[n + 1], f"blocks{n + 1}", F32, after=early)
         moving = {}
         for (x, t), value in landed.items():
             rightwards = t <= (4 if x == 0 else 3)
@@ -483,12 +501,14 @@
     half = channels // 2
     swap = [(0, 1), (1, 0)]
 
-    sent, pick, starts, coef = pick_half((expert_ids.T, gates.T), expert_out, tokens, half, True)
-    from_peer = lax.ppermute(sent, "expert", swap)
-    (kept,) = pick_half((starts, pick, coef), expert_out, tokens, half, False)
-    from_peer_too = lax.ppermute(kept, "expert", swap)
-    rows, turned = merge(coef, kept, from_peer)
-    (turned,) = merge(coef, sent, from_peer_too, turned)
+    picked, held, pick, starts, coef = pick_rows(expert_ids.T, gates.T, expert_out, half // 3)
+    picked, arrived = [picked], [lax.ppermute(picked, "expert", swap)]
+    for tiles in ((1, 2), (3, 4), (5,)):
+        after = arrived[:1] if len(picked) == 2 else ()
+        picked.append(pick_more(tiles, starts, pick, coef, held, after))
+        arrived.append(lax.ppermute(picked[-1], "expert", swap))
+    rows, turned = merge(coef, picked[2:], arrived[:2], half)
+    (turned,) = merge(coef, picked[:2], arrived[2:], half, turned)
 
     total_tokens = tokens * dp_size
     if dp_size == 8 and channels == 8 * 384:

time: 92.6 us -> 90.6 us (0.978)
  waiting for transfers between devices: 41.2 us -> 38.9 us
  Pallas kernels: 30 us -> 32.1 us
  starting transfers between devices: 19.4 us -> 18.3 us
    ppermute x14, waiting for transfers between devices: 31.4 us -> 28.5 us  [hop(): lax.ppermute(value, both, ring_perm(1 if key[1] <= (4 if key[0] == 0 else...]
    ppermute x1, waiting for transfers between devices: 2.36 us -> 4.64 us  [symmetric_moment(): other = lax.ppermute(other, both, perm_other)]
    pallas_call x4 -> x6, Pallas kernels: 12.5 us -> 14.6 us  [the longest x4 12.1 us: pick_call(): pl.pallas_call(functools.partial(pick_kernel, first, tiles), out_shape=ou...]
    ppermute x2 -> x4, waiting for transfers between devices: 2.9 us -> 1.26 us  [the longest x3 1.26 us: per_device(): arrived.append(lax.ppermute(picked[-1], 'expert', swap))]
    ppermute x14, starting transfers between devices: 13.2 us -> 12.1 us  [hop(): lax.ppermute(value, both, ring_perm(1 if key[1] <= (4 if key[0] == 0 else...]
  transfers between devices with their start and end apart: 18 -> 20, of which waited for: 11 -> 11; matrix products, arithmetic and copies ran while one was open for 1% -> 1% of each run, Pallas kernels for 21% -> 22%
where the time goes in v9:
time: 90.6 us; the launch traced here: 90.5 us
  waiting for transfers between devices  38.9 us (43%)
  Pallas kernels  32.1 us (35%)
  starting transfers between devices  18.3 us (20%)
    ppermute x14, waiting for transfers between devices, hop(): lax.ppermute(value, both, ring_perm(1 if key[1] <= (4 if key[0] == 0 else...  28.5 us
    ppermute x14, starting transfers between devices, hop(): lax.ppermute(value, both, ring_perm(1 if key[1] <= (4 if key[0] == 0 else...  12.1 us
    pallas_call x4, Pallas kernels, pick_call(): pl.pallas_call(functools.partial(pick_kernel, first, tiles), out_shape=ou...  12.1 us
    pallas_call x5, Pallas kernels, moment_blocks(): pl.pallas_call(functools.partial(blocks_kernel, pieces, width), out_shape...  11.5 us
    ppermute x1, starting transfers between devices, symmetric_moment(): one = lax.ppermute(one, both, perm_one)  4.9 us
    ppermute x1, waiting for transfers between devices, symmetric_moment(): other = lax.ppermute(other, both, perm_other)  4.64 us
    ppermute x1, waiting for transfers between devices, symmetric_moment(): one = lax.ppermute(one, both, perm_one)  4.48 us
    pallas_call x2, Pallas kernels, symmetric_moment(): pl.pallas_call(kernel, out_shape=result, in_specs=[smem] + [vmem] * len(a...  3.22 us
  transfers between devices with their start and end apart: 20, of which 11 were waited for; matrix products, arithmetic and copies ran while one was open for 1% of the time, Pallas kernels for 22%

profile of v9, /device:TPU:1, one launch (start us, length us, event | category | flops | bytes accessed | tf_op | source)
XLA Modules:
  0.0 90.5 jit_solution(6070812636347890815)
XLA Ops:
  0.0 6.3 %pick_first.1 = (bf16[768,512]{1,0:T(8,128)(2,1)S(1)}, bf16[6,1536,512]{2,1,0:T(8,128)(2,1)S(1)}, bf16[1536,256]{1,0:T(8,128)(2,1)S(1)}, s32[16,128]{1,0:T(8,128)S(1)}, f32[768,128]{1,0:T(8,128)S(1)}) custom-call(s32[2,768]{1,0:T(2,128)} %bitcast.2, f32[2,768]{1,0:T(2,128)} %bitcast.3, bf16[1536,3072]{1,0:T(8,128)(2,1)} %refs_2_.1), custom_call_target="tpu_custom_call" | custom-call | flops 201326592 | tf_op jit(solution)/shard_map/pick_first/pallas_call | solution.py:116
  6.3 0.1 collective-permute-start
  6.5 2.1 %pick.3.refs_1_ = bf16[768,1024]{1,0:T(8,128)(2,1)S(1)} custom-call(s32[16,128]{1,0:T(8,128)S(1)} %get-tuple-element.33.refs_0_, bf16[1536,256]{1,0:T(8,128)(2,1)S(1)} %get-tuple-element.34.refs_1_, f32[768,128]{1,0:T(8,128)S(1)} %get-tuple-element.31.refs_2_.coef_ref, bf16[6,1536,512]{2,1,0:T(8,128)(2,1)S(1)} %get-tuple-element.35.refs_3_), custom_call_target="tpu_custom_call" | custom-call | flops 402653184 | tf_op jit(solution)/shard_map/pick/pallas_call | solution.py:116
  8.6 0.5 collective-permute-start.3
  9.1 0.0 collective-permute-done.refs_4_.refs_2_
  9.1 2.1 %pick.4.refs_0_ = bf16[768,1024]{1,0:T(8,128)(2,1)S(1)} custom-call(s32[16,128]{1,0:T(8,128)S(1)} %get-tuple-element.33.refs_0_, bf16[1536,256]{1,0:T(8,128)(2,1)S(1)} %get-tuple-element.34.refs_1_, f32[768,128]{1,0:T(8,128)S(1)} %get-tuple-element.31.refs_2_.coef_ref, bf16[6,1536,512]{2,1,0:T(8,128)(2,1)S(1)} %get-tuple-element.35.refs_3_, ...), custom_call_target="tpu_custom_call" | custom-call | flops 402653184 | tf_op jit(solution)/shard_map/pick/pallas_call | solution.py:116
  11.3 0.1 collective-permute-start.1
  11.4 1.5 %pick.5.refs_1_ = bf16[768,512]{1,0:T(8,128)(2,1)S(1)} custom-call(s32[16,128]{1,0:T(8,128)S(1)} %get-tuple-element.33.refs_0_, bf16[1536,256]{1,0:T(8,128)(2,1)S(1)} %get-tuple-element.34.refs_1_, f32[768,128]{1,0:T(8,128)S(1)} %get-tuple-element.31.refs_2_.coef_ref, bf16[6,1536,512]{2,1,0:T(8,128)(2,1)S(1)} %get-tuple-element.35.refs_3_), custom_call_target="tpu_custom_call" | custom-call | flops 201326592 | tf_op jit(solution)/shard_map/pick/pallas_call | solution.py:116
  12.9 0.5 collective-permute-start.2
  13.4 0.0 collective-permute-done.3.refs_3_
  13.4 1.2 %merge_first.1 = (bf16[768,1536]{1,0:T(8,128)(2,1)S(1)}, bf16[3072,768]{1,0:T(8,128)(2,1)S(1)}) custom-call(f32[768,128]{1,0:T(8,128)S(1)} %get-tuple-element.31.refs_2_.coef_ref, bf16[768,1024]{1,0:T(8,128)(2,1)S(1)} %pick.4.refs_0_, bf16[768,512]{1,0:T(8,128)(2,1)S(1)} %pick.5.refs_1_, bf16[768,512]{1,0:T(8,128)(2,1)S(1)} %collective-permute-done.refs_4_.refs_2_, ...), custom_call_target="tpu_custom_call" | custom-call | flops 4718592 | tf_op jit(solution)/shard_map/merge_first/pallas_call | solution.py:186
  14.6 1.3 %collective-permute-done.2.refs_3_ = bf16[768,512]{1,0:T(8,128)(2,1)S(1)} collective-permute-done((bf16[768,512]{1,0:T(8,128)(2,1)S(1)}, bf16[768,512]{1,0:T(8,128)(2,1)S(1)}, u32[]{:S(2)}, u32[]{:S(2)}) %collective-permute-start.2) | collective-permute-done | bytes 786464 | tf_op jit(solution)/shard_map/ppermute | solution.py:509
  15.9 1.3 %merge_second.1.turned_ref = bf16[3072,768]{1,0:T(8,128)(2,1)S(1)} custom-call(f32[768,128]{1,0:T(8,128)S(1)} %get-tuple-element.31.refs_2_.coef_ref, bf16[768,512]{1,0:T(8,128)(2,1)S(1)} %get-tuple-element.32.refs_0_, bf16[768,1024]{1,0:T(8,128)(2,1)S(1)} %pick.3.refs_1_, ...), custom_call_target="tpu_custom_call", output_to_operand_aliasing={{}: (5, {})} | custom-call | flops 4718592 | tf_op jit(solution)/shard_map/merge_second/pallas_call | solution.py:186
  17.2 0.0 copy-start.4
  17.2 1.7 %blocks0.1 = (bf16[416,384]{1,0:T(8,128)(2,1)S(1)}, bf16[416,384]{1,0:T(8,128)(2,1)S(1)}) custom-call(s32[16,10]{1,0:T(8,128)S(1)} %copy-done.5, bf16[3072,768]{1,0:T(8,128)(2,1)S(1)} %merge_second.1.turned_ref, bf16[768,1536]{1,0:T(8,128)(2,1)S(1)} %get-tuple-element.37.mine_ref), custom_call_target="tpu_custom_call" | custom-call | flops 226492416 | tf_op jit(solution)/shard_map/blocks0/pallas_call | solution.py:234
  18.9 2.5 %collective-permute-start.4 = (bf16[416,384]{1,0:T(8,128)(2,1)S(1)}, bf16[416,384]{1,0:T(8,128)(2,1)S(1)}, u32[]{:S(2)}, u32[]{:S(2)}) collective-permute-start(bf16[416,384]{1,0:T(8,128)(2,1)S(1)} %get-tuple-element.38.refs_0_), channel_id=1, source_target_pairs={{0,4},{1,5},{4,8},{5,9},{8,12},{9,13},{12,14},{13,15},{14,10},{15,... | collective-permute-start | bytes 958472 | tf_op jit(solution)/shard_map/ppermute | solution.py:430
  21.4 0.0 collective-permute-start.5
  21.4 1.7 %blocks0b.1 = (bf16[416,384]{1,0:T(8,128)(2,1)S(1)}, bf16[416,384]{1,0:T(8,128)(2,1)S(1)}) custom-call(s32[16,10]{1,0:T(8,128)S(1)} %copy-done.4, bf16[3072,768]{1,0:T(8,128)(2,1)S(1)} %merge_second.1.turned_ref, bf16[768,1536]{1,0:T(8,128)(2,1)S(1)} %get-tuple-element.37.mine_ref, bf16[416,384]{1,0:T(8,128)(2,1)S(1)} %get-tuple-element.38.refs_0_), custom_call_target="tpu_custom_call" | custom-call | flops 226492416 | tf_op jit(solution)/shard_map/blocks0b/pallas_call | solution.py:234
  23.1 1.4 %collective-permute-start.15 = (bf16[416,384]{1,0:T(8,128)(2,1)S(1)}, bf16[416,384]{1,0:T(8,128)(2,1)S(1)}, u32[]{:S(2)}, u32[]{:S(2)}) collective-permute-start(bf16[416,384]{1,0:T(8,128)(2,1)S(1)} %get-tuple-element.51), channel_id=1, source_target_pairs={{0,2},{1,3},{4,0},{5,1},{8,4},{9,5},{12,8},{13,9},{14,12},{15,13},... | collective-permute-start | bytes 958472 | tf_op jit(solution)/shard_map/ppermute | solution.py:430
  24.6 0.3 collective-permute-start.12
  24.9 4.0 %collective-permute-done.4.refs_0_ = bf16[416,384]{1,0:T(8,128)(2,1)S(1)} collective-permute-done((bf16[416,384]{1,0:T(8,128)(2,1)S(1)}, bf16[416,384]{1,0:T(8,128)(2,1)S(1)}, u32[]{:S(2)}, u32[]{:S(2)}) %collective-permute-start.4) | collective-permute-done | bytes 319520 | tf_op jit(solution)/shard_map/ppermute | solution.py:430
  28.9 0.9 collective-permute-done.5.refs_1_
  29.8 2.6 %blocks1.1 = (f32[416,384]{1,0:T(8,128)S(1)}, f32[416,384]{1,0:T(8,128)S(1)}, f32[416,384]{1,0:T(8,128)S(1)}, f32[416,384]{1,0:T(8,128)S(1)}) custom-call(s32[16,20]{1,0:T(8,128)S(1)} %copy-done.3, bf16[3072,768]{1,0:T(8,128)(2,1)S(1)} %merge_second.1.turned_ref, bf16[768,1536]{1,0:T(8,128)(2,1)S(1)} %get-tuple-element.37.mine_ref, ...), custom_call_target="tpu_custom_call" | custom-call | flops 452984832 | tf_op jit(solution)/shard_map/blocks1/pallas_call | solution.py:234
  32.5 0.0 copy-start.2
  32.5 0.1 add_convert_fusion.8
  32.6 0.4 collective-permute-start.7
  32.9 0.1 add_convert_fusion.9
  33.0 1.2 %collective-permute-start.6 = (bf16[416,384]{1,0:T(8,128)(2,1)S(1)}, bf16[416,384]{1,0:T(8,128)(2,1)S(1)}, u32[]{:S(2)}, u32[]{:S(2)}) collective-permute-start(bf16[416,384]{1,0:T(8,128)(2,1)S(1)} %add_convert_fusion.9), channel_id=1, source_target_pairs={{0,4},{1,5},{4,8},{5,9},{8,12},{9,13},{12,14},{13,15},{14,10},{15,... | collective-permute-start | bytes 958472 | tf_op jit(solution)/shard_map/ppermute | solution.py:430
  34.2 2.5 %collective-permute-done.15 = bf16[416,384]{1,0:T(8,128)(2,1)S(1)} collective-permute-done((bf16[416,384]{1,0:T(8,128)(2,1)S(1)}, bf16[416,384]{1,0:T(8,128)(2,1)S(1)}, u32[]{:S(2)}, u32[]{:S(2)}) %collective-permute-start.15) | collective-permute-done | bytes 319520 | tf_op jit(solution)/shard_map/ppermute | solution.py:430
  36.7 0.1 add_convert_fusion.1
  36.7 0.4 collective-permute-start.16
  37.1 0.1 add_convert_fusion.3
  37.2 1.2 %collective-permute-start.13 = (bf16[416,384]{1,0:T(8,128)(2,1)S(1)}, bf16[416,384]{1,0:T(8,128)(2,1)S(1)}, u32[]{:S(2)}, u32[]{:S(2)}) collective-permute-start(bf16[416,384]{1,0:T(8,128)(2,1)S(1)} %add_convert_fusion.3), channel_id=1, source_target_pairs={{0,4},{1,5},{4,8},{5,9},{8,12},{9,13},{12,14},{13,15},{14,10},{15,... | collective-permute-start | bytes 958472 | tf_op jit(solution)/shard_map/ppermute | solution.py:430
  38.4 5.1 %collective-permute-done.7.refs_1_ = bf16[416,384]{1,0:T(8,128)(2,1)S(1)} collective-permute-done((bf16[416,384]{1,0:T(8,128)(2,1)S(1)}, bf16[416,384]{1,0:T(8,128)(2,1)S(1)}, u32[]{:S(2)}, u32[]{:S(2)}) %collective-permute-start.7) | collective-permute-done | bytes 319520 | tf_op jit(solution)/shard_map/ppermute | solution.py:430
  43.5 2.6 %blocks2.1 = (f32[416,384]{1,0:T(8,128)S(1)}, f32[416,384]{1,0:T(8,128)S(1)}, f32[416,384]{1,0:T(8,128)S(1)}, f32[416,384]{1,0:T(8,128)S(1)}) custom-call(s32[16,20]{1,0:T(8,128)S(1)} %copy-done.2, bf16[3072,768]{1,0:T(8,128)(2,1)S(1)} %merge_second.1.turned_ref, bf16[768,1536]{1,0:T(8,128)(2,1)S(1)} %get-tuple-element.37.mine_ref, ...), custom_call_target="tpu_custom_call" | custom-call | flops 452984832 | tf_op jit(solution)/shard_map/blocks2/pallas_call | solution.py:234
  46.2 0.0 copy-start.1
  46.2 0.1 add_convert_fusion.6
  46.3 0.4 collective-permute-start.9
  46.7 0.1 add_convert_fusion.7
  46.7 1.2 %collective-permute-start.8 = (bf16[416,384]{1,0:T(8,128)(2,1)S(1)}, bf16[416,384]{1,0:T(8,128)(2,1)S(1)}, u32[]{:S(2)}, u32[]{:S(2)}) collective-permute-start(bf16[416,384]{1,0:T(8,128)(2,1)S(1)} %add_convert_fusion.7), channel_id=1, source_target_pairs={{0,4},{1,5},{4,8},{5,9},{8,12},{9,13},{12,14},{13,15},{14,10},{15,... | collective-permute-start | bytes 958472 | tf_op jit(solution)/shard_map/ppermute | solution.py:430
  47.9 2.4 %collective-permute-done.16 = bf16[416,384]{1,0:T(8,128)(2,1)S(1)} collective-permute-done((bf16[416,384]{1,0:T(8,128)(2,1)S(1)}, bf16[416,384]{1,0:T(8,128)(2,1)S(1)}, u32[]{:S(2)}, u32[]{:S(2)}) %collective-permute-start.16) | collective-permute-done | bytes 319520 | tf_op jit(solution)/shard_map/ppermute | solution.py:430
  50.4 0.1 add_convert_fusion
  50.4 0.4 collective-permute-start.17
  50.8 0.0 collective-permute-done.13
  50.8 0.1 add_convert_fusion.2
  50.9 1.2 %collective-permute-start.14 = (bf16[416,384]{1,0:T(8,128)(2,1)S(1)}, bf16[416,384]{1,0:T(8,128)(2,1)S(1)}, u32[]{:S(2)}, u32[]{:S(2)}) collective-permute-start(bf16[416,384]{1,0:T(8,128)(2,1)S(1)} %add_convert_fusion.2), channel_id=1, source_target_pairs={{0,4},{1,5},{4,8},{5,9},{8,12},{9,13},{12,14},{13,15},{14,10},{15,... | collective-permute-start | bytes 958472 | tf_op jit(solution)/shard_map/ppermute | solution.py:430
  52.1 5.1 %collective-permute-done.9.refs_1_ = bf16[416,384]{1,0:T(8,128)(2,1)S(1)} collective-permute-done((bf16[416,384]{1,0:T(8,128)(2,1)S(1)}, bf16[416,384]{1,0:T(8,128)(2,1)S(1)}, u32[]{:S(2)}, u32[]{:S(2)}) %collective-permute-start.9) | collective-permute-done | bytes 319520 | tf_op jit(solution)/shard_map/ppermute | solution.py:430
  57.2 2.8 %blocks3.1 = (f32[416,384]{1,0:T(8,128)S(1)}, f32[416,384]{1,0:T(8,128)S(1)}, f32[416,384]{1,0:T(8,128)S(1)}, f32[416,384]{1,0:T(8,128)S(1)}) custom-call(s32[16,20]{1,0:T(8,128)S(1)} %copy-done.1, bf16[3072,768]{1,0:T(8,128)(2,1)S(1)} %merge_second.1.turned_ref, bf16[768,1536]{1,0:T(8,128)(2,1)S(1)} %get-tuple-element.37.mine_ref, ...), custom_call_target="tpu_custom_call" | custom-call | flops 452984832 | tf_op jit(solution)/shard_map/blocks3/pallas_call | solution.py:234
  60.0 0.0 copy-start
  60.0 0.1 add_convert_fusion.4
  60.1 0.1 collective-permute-start.11
  60.2 0.1 add_convert_fusion.5
  60.2 1.5 %collective-permute-start.10 = (bf16[416,384]{1,0:T(8,128)(2,1)S(1)}, bf16[416,384]{1,0:T(8,128)(2,1)S(1)}, u32[]{:S(2)}, u32[]{:S(2)}) collective-permute-start(bf16[416,384]{1,0:T(8,128)(2,1)S(1)} %add_convert_fusion.5), channel_id=1, source_target_pairs={{0,4},{1,5},{4,8},{5,9},{8,12},{9,13},{12,14},{13,15},{14,10},{15,... | collective-permute-start | bytes 958472 | tf_op jit(solution)/shard_map/ppermute | solution.py:430
  61.7 2.3 %collective-permute-done.17.left0 = bf16[416,384]{1,0:T(8,128)(2,1)S(1)} collective-permute-done((bf16[416,384]{1,0:T(8,128)(2,1)S(1)}, bf16[416,384]{1,0:T(8,128)(2,1)S(1)}, u32[]{:S(2)}, u32[]{:S(2)}) %collective-permute-start.17) | collective-permute-done | bytes 319520 | tf_op jit(solution)/shard_map/ppermute | solution.py:430
  64.1 6.2 %collective-permute-done.11.left1 = bf16[416,384]{1,0:T(8,128)(2,1)S(1)} collective-permute-done((bf16[416,384]{1,0:T(8,128)(2,1)S(1)}, bf16[416,384]{1,0:T(8,128)(2,1)S(1)}, u32[]{:S(2)}, u32[]{:S(2)}) %collective-permute-start.11) | collective-permute-done | bytes 319520 | tf_op jit(solution)/shard_map/ppermute | solution.py:430
  70.2 0.0 collective-permute-done.10.right0
  70.2 1.0 %outgoing.1 = (bf16[384,384]{1,0:T(8,128)(2,1)S(1)}, bf16[320,384]{1,0:T(8,128)(2,1)S(1)}, f32[192,384]{1,0:T(8,128)S(1)}) custom-call(s32[16,5]{1,0:T(8,128)S(1)} %copy-done, f32[416,384]{1,0:T(8,128)S(1)} %get-tuple-element.44.own0, f32[416,384]{1,0:T(8,128)S(1)} %get-tuple-element.45.own1, bf16[416,384]{1,0:T(8,128)(2,1)S(1)} %collective-permute-done.10.right0, ...), custom_call_target="tpu_custom_call" | custom-call | tf_op jit(solution)/shard_map/outgoing/pallas_call | solution.py:459
  71.2 4.9 %collective-permute-start.19 = (bf16[384,384]{1,0:T(8,128)(2,1)S(1)}, bf16[384,384]{1,0:T(8,128)(2,1)S(1)}, u32[]{:S(2)}, u32[]{:S(2)}) collective-permute-start(bf16[384,384]{1,0:T(8,128)(2,1)S(1)} %get-tuple-element.56), channel_id=1, source_target_pairs={{0,2},{1,10},{2,4},{3,12},{4,6},{5,14},{6,0},{7,8},{8,5},{9,11},{1... | collective-permute-start | bytes 884744 | tf_op jit(solution)/shard_map/ppermute | solution.py:472
  76.1 0.0 collective-permute-start.18
  76.1 1.8 %own.1.result_ref = f32[384,1536]{1,0:T(8,128)} custom-call(s32[16,5]{1,0:T(8,128)S(1)} %copy-done, f32[416,384]{1,0:T(8,128)S(1)} %get-tuple-element.44.own0, f32[416,384]{1,0:T(8,128)S(1)} %get-tuple-element.45.own1, bf16[416,384]{1,0:T(8,128)(2,1)S(1)} %collective-permute-done.10.right0, bf16[416,384]{1,0:T(8,128)(2,1)S(1)} %collective-permute-done.11.left1, ...), custom_call_target="tpu_custom_call" | custom-call | tf_op jit(solution)/shard_map/own/pallas_call | solution.py:474
  78.0 4.5 %collective-permute-done.19.one = bf16[384,384]{1,0:T(8,128)(2,1)S(1)} collective-permute-done((bf16[384,384]{1,0:T(8,128)(2,1)S(1)}, bf16[384,384]{1,0:T(8,128)(2,1)S(1)}, u32[]{:S(2)}, u32[]{:S(2)}) %collective-permute-start.19) | collective-permute-done | bytes 294944 | tf_op jit(solution)/shard_map/ppermute | solution.py:472
  82.4 1.7 %one.1.result_ref = f32[384,1536]{1,0:T(8,128)} custom-call(s32[16,5]{1,0:T(8,128)S(1)} %copy-done, bf16[384,384]{1,0:T(8,128)(2,1)S(1)} %collective-permute-done.19.one, f32[384,1536]{1,0:T(8,128)} %own.1.result_ref), custom_call_target="tpu_custom_call", output_to_operand_aliasing={{}: (2, {})} | custom-call | tf_op jit(solution)/shard_map/one/pallas_call | solution.py:484
  84.1 4.6 %collective-permute-done.18.other = bf16[320,384]{1,0:T(8,128)(2,1)S(1)} collective-permute-done((bf16[320,384]{1,0:T(8,128)(2,1)S(1)}, bf16[320,384]{1,0:T(8,128)(2,1)S(1)}, u32[]{:S(2)}, u32[]{:S(2)}) %collective-permute-start.18) | collective-permute-done | bytes 245792 | tf_op jit(solution)/shard_map/ppermute | solution.py:473
  88.8 1.6 %other.1 = f32[384,1536]{1,0:T(8,128)} custom-call(s32[16,5]{1,0:T(8,128)S(1)} %copy-done, f32[192,384]{1,0:T(8,128)S(1)} %get-tuple-element.54.share, bf16[320,384]{1,0:T(8,128)(2,1)S(1)} %collective-permute-done.18.other, f32[384,1536]{1,0:T(8,128)} %one.1.result_ref), custom_call_target="tpu_custom_call", output_to_operand_aliasing={{}: (3, {})} | custom-call | tf_op jit(solution)/shard_map/other/pallas_call | solution.py:484
  (13 shorter events, 0.0 us)
Async XLA Ops:
  6.3 2.8 %collective-permute-start = (bf16[768,512]{1,0:T(8,128)(2,1)S(1)}, bf16[768,512]{1,0:T(8,128)(2,1)S(1)}, u32[]{:S(2)}, u32[]{:S(2)}) collective-permute-start(bf16[768,512]{1,0:T(8,128)(2,1)S(1)} %get-tuple-element.32.refs_0_), channel_id=1, source_target_pairs={{0,1},{1,0},{2,3},{3,2},{4,5},{5,4},{6,7},{7,6},{8,9},{9,8},{10,11... | collective-permute-start | bytes 2359304 | tf_op jit(solution)/shard_map/ppermute | solution.py:505
  8.6 4.8 %collective-permute-start.3 = (bf16[768,1024]{1,0:T(8,128)(2,1)S(1)}, bf16[768,1024]{1,0:T(8,128)(2,1)S(1)}, u32[]{:S(2)}, u32[]{:S(2)}) collective-permute-start(bf16[768,1024]{1,0:T(8,128)(2,1)S(1)} %pick.3.refs_1_), channel_id=1, source_target_pairs={{0,1},{1,0},{2,3},{3,2},{4,5},{5,4},{6,7},{7,6},{8,9},{9,8},{10,11... | collective-permute-start | bytes 4718600 | tf_op jit(solution)/shard_map/ppermute | solution.py:509
  11.3 4.6 %collective-permute-start.1 = (bf16[768,1024]{1,0:T(8,128)(2,1)S(1)}, bf16[768,1024]{1,0:T(8,128)(2,1)S(1)}, u32[]{:S(2)}, u32[]{:S(2)}) collective-permute-start(bf16[768,1024]{1,0:T(8,128)(2,1)S(1)} %pick.4.refs_0_), channel_id=1, source_target_pairs={{0,1},{1,0},{2,3},{3,2},{4,5},{5,4},{6,7},{7,6},{8,9},{9,8},{10,11... | collective-permute-start | bytes 4718600 | tf_op jit(solution)/shard_map/ppermute | solution.py:509
  12.9 3.0 %collective-permute-start.2 = (bf16[768,512]{1,0:T(8,128)(2,1)S(1)}, bf16[768,512]{1,0:T(8,128)(2,1)S(1)}, u32[]{:S(2)}, u32[]{:S(2)}) collective-permute-start(bf16[768,512]{1,0:T(8,128)(2,1)S(1)} %pick.5.refs_1_), channel_id=1, source_target_pairs={{0,1},{1,0},{2,3},{3,2},{4,5},{5,4},{6,7},{7,6},{8,9},{9,8},{10,11... | collective-permute-start | bytes 2359304 | tf_op jit(solution)/shard_map/ppermute | solution.py:509
  15.9 1.3 %copy-start.5 = (s32[16,10]{1,0:T(8,128)S(1)}, s32[16,10]{1,0:T(8,128)}, u32[]{:S(2)}) copy-start(s32[16,10]{1,0:T(8,128)} %constant.12.clone.table) | copy-start | bytes 1924
  17.2 4.3 %copy-start.4 = (s32[16,10]{1,0:T(8,128)S(1)}, s32[16,10]{1,0:T(8,128)}, u32[]{:S(2)}) copy-start(s32[16,10]{1,0:T(8,128)} %constant.13.clone.table) | copy-start | bytes 1924
  18.9 10.0 %collective-permute-start.4 = (bf16[416,384]{1,0:T(8,128)(2,1)S(1)}, bf16[416,384]{1,0:T(8,128)(2,1)S(1)}, u32[]{:S(2)}, u32[]{:S(2)}) collective-permute-start(bf16[416,384]{1,0:T(8,128)(2,1)S(1)} %get-tuple-element.38.refs_0_), channel_id=1, source_target_pairs={{0,4},{1,5},{4,8},{5,9},{8,12},{9,13},{12,14},{13,15},{14,10},{15,... | collective-permute-start | bytes 958472 | tf_op jit(solution)/shard_map/ppermute | solution.py:430
  21.4 8.4 %copy-start.3 = (s32[16,20]{1,0:T(8,128)S(1)}, s32[16,20]{1,0:T(8,128)}, u32[]{:S(2)}) copy-start(s32[16,20]{1,0:T(8,128)} %constant.14.clone.table) | copy-start | bytes 3844
  21.4 8.4 %collective-permute-start.5 = (bf16[416,384]{1,0:T(8,128)(2,1)S(1)}, bf16[416,384]{1,0:T(8,128)(2,1)S(1)}, u32[]{:S(2)}, u32[]{:S(2)}) collective-permute-start(bf16[416,384]{1,0:T(8,128)(2,1)S(1)} %get-tuple-element.39), channel_id=1, source_target_pairs={{0,2},{1,3},{4,0},{5,1},{8,4},{9,5},{12,8},{13,9},{14,12},{15,13},... | collective-permute-start | bytes 958472 | tf_op jit(solution)/shard_map/ppermute | solution.py:430
  23.1 13.5 %collective-permute-start.15 = (bf16[416,384]{1,0:T(8,128)(2,1)S(1)}, bf16[416,384]{1,0:T(8,128)(2,1)S(1)}, u32[]{:S(2)}, u32[]{:S(2)}) collective-permute-start(bf16[416,384]{1,0:T(8,128)(2,1)S(1)} %get-tuple-element.51), channel_id=1, source_target_pairs={{0,2},{1,3},{4,0},{5,1},{8,4},{9,5},{12,8},{13,9},{14,12},{15,13},... | collective-permute-start | bytes 958472 | tf_op jit(solution)/shard_map/ppermute | solution.py:430
  24.6 12.5 %collective-permute-start.12 = (bf16[416,384]{1,0:T(8,128)(2,1)S(1)}, bf16[416,384]{1,0:T(8,128)(2,1)S(1)}, u32[]{:S(2)}, u32[]{:S(2)}) collective-permute-start(bf16[416,384]{1,0:T(8,128)(2,1)S(1)} %get-tuple-element.48), channel_id=1, source_target_pairs={{0,4},{1,5},{4,8},{5,9},{8,12},{9,13},{12,14},{13,15},{14,10},{15,... | collective-permute-start | bytes 958472 | tf_op jit(solution)/shard_map/ppermute | solution.py:430
  32.5 11.0 %copy-start.2 = (s32[16,20]{1,0:T(8,128)S(1)}, s32[16,20]{1,0:T(8,128)}, u32[]{:S(2)}) copy-start(s32[16,20]{1,0:T(8,128)} %constant.15.clone.table) | copy-start | bytes 3844
  32.6 10.9 %collective-permute-start.7 = (bf16[416,384]{1,0:T(8,128)(2,1)S(1)}, bf16[416,384]{1,0:T(8,128)(2,1)S(1)}, u32[]{:S(2)}, u32[]{:S(2)}) collective-permute-start(bf16[416,384]{1,0:T(8,128)(2,1)S(1)} %add_convert_fusion.8), channel_id=1, source_target_pairs={{0,2},{1,3},{4,0},{5,1},{8,4},{9,5},{12,8},{13,9},{14,12},{15,13},... | collective-permute-start | bytes 958472 | tf_op jit(solution)/shard_map/ppermute | solution.py:430
  33.0 10.5 %collective-permute-start.6 = (bf16[416,384]{1,0:T(8,128)(2,1)S(1)}, bf16[416,384]{1,0:T(8,128)(2,1)S(1)}, u32[]{:S(2)}, u32[]{:S(2)}) collective-permute-start(bf16[416,384]{1,0:T(8,128)(2,1)S(1)} %add_convert_fusion.9), channel_id=1, source_target_pairs={{0,4},{1,5},{4,8},{5,9},{8,12},{9,13},{12,14},{13,15},{14,10},{15,... | collective-permute-start | bytes 958472 | tf_op jit(solution)/shard_map/ppermute | solution.py:430
  36.7 13.6 %collective-permute-start.16 = (bf16[416,384]{1,0:T(8,128)(2,1)S(1)}, bf16[416,384]{1,0:T(8,128)(2,1)S(1)}, u32[]{:S(2)}, u32[]{:S(2)}) collective-permute-start(bf16[416,384]{1,0:T(8,128)(2,1)S(1)} %add_convert_fusion.1), channel_id=1, source_target_pairs={{0,2},{1,3},{4,0},{5,1},{8,4},{9,5},{12,8},{13,9},{14,12},{15,13},... | collective-permute-start | bytes 958472 | tf_op jit(solution)/shard_map/ppermute | solution.py:430
  37.2 13.6 %collective-permute-start.13 = (bf16[416,384]{1,0:T(8,128)(2,1)S(1)}, bf16[416,384]{1,0:T(8,128)(2,1)S(1)}, u32[]{:S(2)}, u32[]{:S(2)}) collective-permute-start(bf16[416,384]{1,0:T(8,128)(2,1)S(1)} %add_convert_fusion.3), channel_id=1, source_target_pairs={{0,4},{1,5},{4,8},{5,9},{8,12},{9,13},{12,14},{13,15},{14,10},{15,... | collective-permute-start | bytes 958472 | tf_op jit(solution)/shard_map/ppermute | solution.py:430
  46.2 11.0 %copy-start.1 = (s32[16,20]{1,0:T(8,128)S(1)}, s32[16,20]{1,0:T(8,128)}, u32[]{:S(2)}) copy-start(s32[16,20]{1,0:T(8,128)} %constant.16.clone.table) | copy-start | bytes 3844
  46.3 10.9 %collective-permute-start.9 = (bf16[416,384]{1,0:T(8,128)(2,1)S(1)}, bf16[416,384]{1,0:T(8,128)(2,1)S(1)}, u32[]{:S(2)}, u32[]{:S(2)}) collective-permute-start(bf16[416,384]{1,0:T(8,128)(2,1)S(1)} %add_convert_fusion.6), channel_id=1, source_target_pairs={{0,2},{1,3},{4,0},{5,1},{8,4},{9,5},{12,8},{13,9},{14,12},{15,13},... | collective-permute-start | bytes 958472 | tf_op jit(solution)/shard_map/ppermute | solution.py:430
  46.7 10.5 %collective-permute-start.8 = (bf16[416,384]{1,0:T(8,128)(2,1)S(1)}, bf16[416,384]{1,0:T(8,128)(2,1)S(1)}, u32[]{:S(2)}, u32[]{:S(2)}) collective-permute-start(bf16[416,384]{1,0:T(8,128)(2,1)S(1)} %add_convert_fusion.7), channel_id=1, source_target_pairs={{0,4},{1,5},{4,8},{5,9},{8,12},{9,13},{12,14},{13,15},{14,10},{15,... | collective-permute-start | bytes 958472 | tf_op jit(solution)/shard_map/ppermute | solution.py:430
  50.4 13.6 %collective-permute-start.17 = (bf16[416,384]{1,0:T(8,128)(2,1)S(1)}, bf16[416,384]{1,0:T(8,128)(2,1)S(1)}, u32[]{:S(2)}, u32[]{:S(2)}) collective-permute-start(bf16[416,384]{1,0:T(8,128)(2,1)S(1)} %add_convert_fusion), channel_id=1, source_target_pairs={{0,2},{1,3},{4,0},{5,1},{8,4},{9,5},{12,8},{13,9},{14,12},{15,13},... | collective-permute-start | bytes 958472 | tf_op jit(solution)/shard_map/ppermute | solution.py:430
  50.9 13.2 %collective-permute-start.14 = (bf16[416,384]{1,0:T(8,128)(2,1)S(1)}, bf16[416,384]{1,0:T(8,128)(2,1)S(1)}, u32[]{:S(2)}, u32[]{:S(2)}) collective-permute-start(bf16[416,384]{1,0:T(8,128)(2,1)S(1)} %add_convert_fusion.2), channel_id=1, source_target_pairs={{0,4},{1,5},{4,8},{5,9},{8,12},{9,13},{12,14},{13,15},{14,10},{15,... | collective-permute-start | bytes 958472 | tf_op jit(solution)/shard_map/ppermute | solution.py:430
  60.0 10.2 %copy-start = (s32[16,5]{1,0:T(8,128)S(1)}, s32[16,5]{1,0:T(8,128)}, u32[]{:S(2)}) copy-start(s32[16,5]{1,0:T(8,128)} %constant.17.clone.place) | copy-start | bytes 964
  60.1 10.1 %collective-permute-start.11 = (bf16[416,384]{1,0:T(8,128)(2,1)S(1)}, bf16[416,384]{1,0:T(8,128)(2,1)S(1)}, u32[]{:S(2)}, u32[]{:S(2)}) collective-permute-start(bf16[416,384]{1,0:T(8,128)(2,1)S(1)} %add_convert_fusion.4), channel_id=1, source_target_pairs={{0,2},{1,3},{4,0},{5,1},{8,4},{9,5},{12,8},{13,9},{14,12},{15,13},... | collective-permute-start | bytes 958472 | tf_op jit(solution)/shard_map/ppermute | solution.py:430
  60.2 10.0 %collective-permute-start.10 = (bf16[416,384]{1,0:T(8,128)(2,1)S(1)}, bf16[416,384]{1,0:T(8,128)(2,1)S(1)}, u32[]{:S(2)}, u32[]{:S(2)}) collective-permute-start(bf16[416,384]{1,0:T(8,128)(2,1)S(1)} %add_convert_fusion.5), channel_id=1, source_target_pairs={{0,4},{1,5},{4,8},{5,9},{8,12},{9,13},{12,14},{13,15},{14,10},{15,... | collective-permute-start | bytes 958472 | tf_op jit(solution)/shard_map/ppermute | solution.py:430
  71.2 11.2 %collective-permute-start.19 = (bf16[384,384]{1,0:T(8,128)(2,1)S(1)}, bf16[384,384]{1,0:T(8,128)(2,1)S(1)}, u32[]{:S(2)}, u32[]{:S(2)}) collective-permute-start(bf16[384,384]{1,0:T(8,128)(2,1)S(1)} %get-tuple-element.56), channel_id=1, source_target_pairs={{0,2},{1,10},{2,4},{3,12},{4,6},{5,14},{6,0},{7,8},{8,5},{9,11},{1... | collective-permute-start | bytes 884744 | tf_op jit(solution)/shard_map/ppermute | solution.py:472
  76.1 12.6 %collective-permute-start.18 = (bf16[320,384]{1,0:T(8,128)(2,1)S(1)}, bf16[320,384]{1,0:T(8,128)(2,1)S(1)}, u32[]{:S(2)}, u32[]{:S(2)}) collective-permute-start(bf16[320,384]{1,0:T(8,128)(2,1)S(1)} %get-tuple-element.55), channel_id=1, source_target_pairs={{0,4},{1,8},{2,6},{3,10},{4,0},{5,12},{6,2},{7,14},{8,3},{9,13},{1... | collective-permute-start | bytes 737288 | tf_op jit(solution)/shard_map/ppermute | solution.py:473

commit v10 on v9

--- a/solution.py
+++ b/solution.py
@@ -57,40 +57,22 @@
             pick_ref[(2 * b + k) * BATCH : (2 * b + k + 1) * BATCH, :] = jnp.where(columns == at, 1.0, 0.0).astype(BF16)
 
 
-def pick_kernel(first, tiles, *refs):
-    if first:
-        ids_hbm, gates_hbm, rows_ref, out_ref, held, pick_ref, starts_ref, coef_ref = refs[:8]
-        in_sems, starts, ids_ref, gates_ref, small_sems = refs[8:]
-    else:
-        starts, pick_ref, coef_ref, held = refs[:4]
-        out_ref = refs[-1]
-    tokens = out_ref.shape[0]
-    count, _, tile = held.shape
+def start_loads(rows_ref, held, sems, side):
+    tile = held.shape[2]
+    loads = []
+    for j in range(held.shape[0]):
+        at = pl.ds(pl.multiple_of((side * held.shape[0] + j) * tile, 128), tile)
+        loads.append(pltpu.make_async_copy(rows_ref.at[:, at], held.at[j], sems.at[j]))
+        loads[-1].start()
+    return loads
+
+
+def pick_tiles(tiles, starts, pick_ref, coef_ref, held, out_ref, loads=None):
+    tokens, tile = out_ref.shape[0], held.shape[2]
     local = EXPERTS // 2
     member = lax.axis_index("expert")
-
-    loads = []
-    if first:
-        small = [
-            pltpu.make_async_copy(ids_hbm, ids_ref, small_sems.at[0]),
-            pltpu.make_async_copy(gates_hbm, gates_ref, small_sems.at[1]),
-        ]
-        for copy in small:
-            copy.start()
-        for j in range(count):
-            side = 1 - member if j < count // 2 else member
-            at = side * (count // 2 * tile) + j % (count // 2) * tile
-            at = pl.ds(pl.multiple_of(at, 128), tile)
-            loads.append(pltpu.make_async_copy(rows_ref.at[:, at], held.at[j], in_sems.at[j]))
-            loads[-1].start()
-        for copy in small:
-            copy.wait()
-        plan_tokens(ids_ref, gates_ref, pick_ref, starts_ref, coef_ref)
-        copy = pltpu.make_async_copy(starts_ref, starts, small_sems.at[2])
-        copy.start()
-        copy.wait()
     for n, j in enumerate(tiles):
-        if first:
+        if loads is not None:
             loads[j].wait()
         for b in range(tokens // BATCH):
             windows = []
@@ -105,31 +87,63 @@
             rows = slice(b * BATCH, (b + 1) * BATCH)
             total = coef_ref[rows, 0:1] * picked[:BATCH] + coef_ref[rows, 1:2] * picked[BATCH:]
             out_ref[rows, n * tile : (n + 1) * tile] = total.astype(BF16)
-    for j, load in enumerate(loads):
-        if j not in tiles:
-            load.wait()
-
-
-def pick_call(first, tiles, args, out_shape, in_specs, scratch, tile):
+
+
+def pick_first_kernel(ids_hbm, gates_hbm, rows_ref, out_ref, held, pick_ref, starts_ref, coef_ref, *scratch):
+    in_sems, starts, ids_ref, gates_ref, small_sems = scratch
+    small = [
+        pltpu.make_async_copy(ids_hbm, ids_ref, small_sems.at[0]),
+        pltpu.make_async_copy(gates_hbm, gates_ref, small_sems.at[1]),
+    ]
+    for copy in small:
+        copy.start()
+    loads = start_loads(rows_ref, held, in_sems, 1 - lax.axis_index("expert"))
+    for copy in small:
+        copy.wait()
+    plan_tokens(ids_ref, gates_ref, pick_ref, starts_ref, coef_ref)
+    copy = pltpu.make_async_copy(starts_ref, starts, small_sems.at[2])
+    copy.start()
+    copy.wait()
+    pick_tiles((0,), starts, pick_ref, coef_ref, held, out_ref, loads)
+    for load in loads[1:]:
+        load.wait()
+
+
+def pick_rest_kernel(starts, pick_ref, coef_ref, held, rows_ref, out_ref, next_held, in_sems):
+    loads = start_loads(rows_ref, next_held, in_sems, lax.axis_index("expert"))
+    pick_tiles(range(1, held.shape[0]), starts, pick_ref, coef_ref, held, out_ref)
+    for load in loads:
+        load.wait()
+
+
+def pick_mine_kernel(tiles, starts, pick_ref, coef_ref, held, *refs):
+    pick_tiles(tiles, starts, pick_ref, coef_ref, held, refs[-1])
+
+
+def pick_call(kernel, count, args, out_shape, in_specs, scratch, tile, name):
     tokens = out_shape[0].shape[0]
     vmem = pl.BlockSpec(memory_space=pltpu.VMEM)
     return pl.pallas_call(
-        functools.partial(pick_kernel, first, tiles),
+        kernel,
         out_shape=out_shape,
         in_specs=in_specs,
         out_specs=[vmem] * len(out_shape),
         scratch_shapes=scratch,
         cost_estimate=pl.CostEstimate(
-            flops=tokens * EXPERTS * WINDOW * len(tiles) * tile, bytes_accessed=0, transcendentals=0
+            flops=tokens * EXPERTS * WINDOW * count * tile, bytes_accessed=0, transcendentals=0
         ),
         compiler_params=pltpu.CompilerParams(vmem_limit_bytes=24 << 20),
-        name="pick_first" if first else "pick",
+        name=name,
     )(*args)
 
 
-def pick_rows(ids, gates, rows, tile):
+def in_hbm(x):
+    return pltpu.with_memory_space_constraint(x, pltpu.HBM)
+
+
+def pick_first(ids, gates, rows, tile):
     tokens, (depth, channels) = ids.shape[1], rows.shape
-    count = channels // tile
+    count = channels // 2 // tile
     out_shape = [
         jax.ShapeDtypeStruct((tokens, tile), BF16),
         jax.ShapeDtypeStruct((count, depth, tile), BF16),
@@ -144,17 +158,33 @@
         pltpu.VMEM((2, tokens), F32),
         pltpu.SemaphoreType.DMA((3,)),
     ]
-    args = [pltpu.with_memory_space_constraint(x, pltpu.HBM) for x in (ids, gates, rows)]
-    return pick_call(True, (0,), args, out_shape, [pl.BlockSpec(memory_space=pl.ANY)] * 3, scratch, tile)
-
-
-def pick_more(tiles, starts, pick, coef, held, after=()):
+    args = [in_hbm(x) for x in (ids, gates, rows)]
+    any_ = pl.BlockSpec(memory_space=pl.ANY)
+    return pick_call(pick_first_kernel, 1, args, out_shape, [any_] * 3, scratch, tile, "pick_first")
+
+
+def pick_rest(starts, pick, coef, held, rows):
+    tokens, (count, _, tile) = coef.shape[0], held.shape
+    smem, vmem, any_ = [pl.BlockSpec(memory_space=m) for m in (pltpu.SMEM, pltpu.VMEM, pl.ANY)]
+    out_shape = [
+        jax.ShapeDtypeStruct((tokens, (count - 1) * tile), BF16),
+        jax.ShapeDtypeStruct(held.shape, BF16),
+    ]
+    args = (starts, pick, coef, held, in_hbm(rows))
+    scratch = [pltpu.SemaphoreType.DMA((count,))]
+    return pick_call(
+        pick_rest_kernel, count - 1, args, out_shape, [smem] + [vmem] * 3 + [any_], scratch, tile, "pick_rest"
+    )
+
+
+def pick_mine(tiles, starts, pick, coef, held, after=()):
     tokens, tile = coef.shape[0], held.shape[2]
-    vmem = pl.BlockSpec(memory_space=pltpu.VMEM)
+    smem, vmem, any_ = [pl.BlockSpec(memory_space=m) for m in (pltpu.SMEM, pltpu.VMEM, pl.ANY)]
     out_shape = [jax.ShapeDtypeStruct((tokens, len(tiles) * tile), BF16)]
-    in_specs = [pl.BlockSpec(memory_space=pltpu.SMEM)] + [vmem] * 3
-    in_specs += [pl.BlockSpec(memory_space=pl.ANY)] * len(after)
-    return pick_call(False, tiles, (starts, pick, coef, held, *after), out_shape, in_specs, [], tile)[0]
+    in_specs = [smem] + [vmem] * 3 + [any_] * len(after)
+    kernel = functools.partial(pick_mine_kernel, tiles)
+    args = (starts, pick, coef, held, *after)
+    return pick_call(kernel, len(tiles), args, out_shape, in_specs, [], tile, "pick_mine")[0]
 
 
 def merge_kernel(first, tile, pieces, coef_ref, *refs):
@@ -433,6 +463,7 @@
     compute(ROUNDS[0][2:], "blocks0b", BF16, after=(blocks[0, 4],))
     moving = {key: blocks[key] for key in ROUNDS[0]}
     arrived = {}
+    before = ()
     for n in range(4):
         landed = {}
         for key in ROUNDS[n]:
@@ -440,7 +471,12 @@
                 landed[key] = hop(moving[key], key)
         if n < 3:
             early = [landed[key] for key in ROUNDS[n][:2]]
-            compute(ROUNDS[n + 1], f"blocks{n + 1}", F32, after=early)
+            if n == 0:
+                compute(ROUNDS[1], "blocks1", F32, after=early)
+            else:
+                compute(ROUNDS[n + 1][:2], f"blocks{n + 1}", F32, after=before)
+                compute(ROUNDS[n + 1][2:], f"blocks{n + 1}b", F32, after=early)
+            before = early
         moving = {}
         for (x, t), value in landed.items():
             rightwards = t <= (4 if x == 0 else 3)
@@ -501,12 +537,15 @@
     half = channels // 2
     swap = [(0, 1), (1, 0)]
 
-    picked, held, pick, starts, coef = pick_rows(expert_ids.T, gates.T, expert_out, half // 3)
-    picked, arrived = [picked], [lax.ppermute(picked, "expert", swap)]
-    for tiles in ((1, 2), (3, 4), (5,)):
-        after = arrived[:1] if len(picked) == 2 else ()
-        picked.append(pick_more(tiles, starts, pick, coef, held, after))
-        arrived.append(lax.ppermute(picked[-1], "expert", swap))
+    send = lambda x: lax.ppermute(x, "expert", swap)
+    first, held, pick, starts, coef = pick_first(expert_ids.T, gates.T, expert_out, half // 3)
+    picked, arrived = [first], [send(first)]
+    rest, held = pick_rest(starts, pick, coef, held, expert_out)
+    picked.append(rest)
+    arrived.append(send(rest))
+    for tiles in ((0, 1), (2,)):
+        picked.append(pick_mine(tiles, starts, pick, coef, held, arrived[:1] if tiles[0] == 0 else ()))
+        arrived.append(send(picked[-1]))
     rows, turned = merge(coef, picked[2:], arrived[:2], half)
     (turned,) = merge(coef, picked[:2], arrived[2:], half, turned)
 

time: 90.6 us -> 89.6 us (0.989)
  waiting for transfers between devices: 38.9 us -> 31.3 us
  starting transfers between devices: 18.3 us -> 23.5 us
  Pallas kernels: 32.1 us -> 33.5 us
    ppermute x14, waiting for transfers between devices: 28.5 us -> 22.4 us  [hop(): lax.ppermute(value, both, ring_perm(1 if key[1] <= (4 if key[0] == 0 else...]
    ppermute x14, starting transfers between devices: 12.1 us -> 16.1 us  [hop(): lax.ppermute(value, both, ring_perm(1 if key[1] <= (4 if key[0] == 0 else...]
    pallas_call x5 -> x7, Pallas kernels: 11.5 us -> 13 us  [moment_blocks(): pl.pallas_call(functools.partial(blocks_kernel, pieces, width), out_shape...]
    ppermute x1, waiting for transfers between devices: 4.64 us -> 3.24 us  [symmetric_moment(): other = lax.ppermute(other, both, perm_other)]
    ppermute x1, starting transfers between devices: 4.9 us -> 6.14 us  [symmetric_moment(): one = lax.ppermute(one, both, perm_one)]
  transfers between devices with their start and end apart: 20 -> 20, of which waited for: 11 -> 13; matrix products, arithmetic and copies ran while one was open for 1% -> 1% of each run, Pallas kernels for 22% -> 27%
where the time goes in v10:
time: 89.6 us; the launch traced here: 89.4 us
  Pallas kernels  33.5 us (37%)
  waiting for transfers between devices  31.3 us (35%)
  starting transfers between devices  23.5 us (26%)
    ppermute x14, waiting for transfers between devices, hop(): lax.ppermute(value, both, ring_perm(1 if key[1] <= (4 if key[0] == 0 else...  22.4 us
    ppermute x14, starting transfers between devices, hop(): lax.ppermute(value, both, ring_perm(1 if key[1] <= (4 if key[0] == 0 else...  16.1 us
    pallas_call x7, Pallas kernels, moment_blocks(): pl.pallas_call(functools.partial(blocks_kernel, pieces, width), out_shape...  13 us
    pallas_call x4, Pallas kernels, pick_call(): pl.pallas_call(kernel, out_shape=out_shape, in_specs=in_specs, out_specs=...  11.9 us
    ppermute x1, starting transfers between devices, symmetric_moment(): one = lax.ppermute(one, both, perm_one)  6.14 us
    ppermute x1, waiting for transfers between devices, symmetric_moment(): one = lax.ppermute(one, both, perm_one)  4.47 us
    ppermute x1, waiting for transfers between devices, symmetric_moment(): other = lax.ppermute(other, both, perm_other)  3.24 us
    pallas_call x2, Pallas kernels, symmetric_moment(): pl.pallas_call(kernel, out_shape=result, in_specs=[smem] + [vmem] * len(a...  3.22 us
  transfers between devices with their start and end apart: 20, of which 13 were waited for; matrix products, arithmetic and copies ran while one was open for 1% of the time, Pallas kernels for 27%

profile of v10, /device:TPU:1, one launch (start us, length us, event | category | flops | bytes accessed | tf_op | source)
XLA Modules:
  0.0 89.4 jit_solution(9933923361351895611)
XLA Ops:
  0.0 3.9 %pick_first.1 = (bf16[768,512]{1,0:T(8,128)(2,1)S(1)}, bf16[3,1536,512]{2,1,0:T(8,128)(2,1)S(1)}, bf16[1536,256]{1,0:T(8,128)(2,1)S(1)}, s32[16,128]{1,0:T(8,128)S(1)}, f32[768,128]{1,0:T(8,128)S(1)}) custom-call(s32[2,768]{1,0:T(2,128)} %bitcast.2, f32[2,768]{1,0:T(2,128)} %bitcast.3, bf16[1536,3072]{1,0:T(8,128)(2,1)} %rows_ref.3), custom_call_target="tpu_custom_call" | custom-call | flops 201326592 | tf_op jit(solution)/shard_map/pick_first/pallas_call | solution.py:126
  3.9 0.1 collective-permute-start
  4.1 4.4 %pick_rest.1 = (bf16[768,1024]{1,0:T(8,128)(2,1)S(1)}, bf16[3,1536,512]{2,1,0:T(8,128)(2,1)S(1)}) custom-call(s32[16,128]{1,0:T(8,128)S(1)} %get-tuple-element.35.starts, bf16[1536,256]{1,0:T(8,128)(2,1)S(1)} %get-tuple-element.36.pick_ref, f32[768,128]{1,0:T(8,128)S(1)} %get-tuple-element.33.coef_ref, bf16[3,1536,512]{2,1,0:T(8,128)(2,1)S(1)} %get-tuple-element.37.held, ...), custom_call_target="tpu_custom_call" | custom-call | flops 402653184 | tf_op jit(solution)/shard_map/pick_rest/pallas_call | solution.py:126
  8.5 0.5 collective-permute-start.3
  9.0 2.1 %pick_mine.2.refs_0_ = bf16[768,1024]{1,0:T(8,128)(2,1)S(1)} custom-call(s32[16,128]{1,0:T(8,128)S(1)} %get-tuple-element.35.starts, bf16[1536,256]{1,0:T(8,128)(2,1)S(1)} %get-tuple-element.36.pick_ref, f32[768,128]{1,0:T(8,128)S(1)} %get-tuple-element.33.coef_ref, bf16[3,1536,512]{2,1,0:T(8,128)(2,1)S(1)} %get-tuple-element.39.held, ...), custom_call_target="tpu_custom_call" | custom-call | flops 402653184 | tf_op jit(solution)/shard_map/pick_mine/pallas_call | solution.py:126
  11.1 0.1 collective-permute-start.1
  11.3 1.5 %pick_mine.3.refs_1_ = bf16[768,512]{1,0:T(8,128)(2,1)S(1)} custom-call(s32[16,128]{1,0:T(8,128)S(1)} %get-tuple-element.35.starts, bf16[1536,256]{1,0:T(8,128)(2,1)S(1)} %get-tuple-element.36.pick_ref, f32[768,128]{1,0:T(8,128)S(1)} %get-tuple-element.33.coef_ref, bf16[3,1536,512]{2,1,0:T(8,128)(2,1)S(1)} %get-tuple-element.39.held), custom_call_target="tpu_custom_call" | custom-call | flops 201326592 | tf_op jit(solution)/shard_map/pick_mine/pallas_call | solution.py:126
  12.7 0.5 collective-permute-start.2
  13.3 1.3 %merge_first.1 = (bf16[768,1536]{1,0:T(8,128)(2,1)S(1)}, bf16[3072,768]{1,0:T(8,128)(2,1)S(1)}) custom-call(f32[768,128]{1,0:T(8,128)S(1)} %get-tuple-element.33.coef_ref, bf16[768,1024]{1,0:T(8,128)(2,1)S(1)} %pick_mine.2.refs_0_, bf16[768,512]{1,0:T(8,128)(2,1)S(1)} %pick_mine.3.refs_1_, bf16[768,512]{1,0:T(8,128)(2,1)S(1)} %collective-permute-done.refs_0_.refs_2_, ...), custom_call_target="tpu_custom_call" | custom-call | flops 4718592 | tf_op jit(solution)/shard_map/merge_first/pallas_call | solution.py:216
  14.6 1.2 %collective-permute-done.2.refs_3_ = bf16[768,512]{1,0:T(8,128)(2,1)S(1)} collective-permute-done((bf16[768,512]{1,0:T(8,128)(2,1)S(1)}, bf16[768,512]{1,0:T(8,128)(2,1)S(1)}, u32[]{:S(2)}, u32[]{:S(2)}) %collective-permute-start.2) | collective-permute-done | bytes 786464 | tf_op jit(solution)/shard_map/ppermute | solution.py:540
  15.7 1.2 %merge_second.1.turned_ref = bf16[3072,768]{1,0:T(8,128)(2,1)S(1)} custom-call(f32[768,128]{1,0:T(8,128)S(1)} %get-tuple-element.33.coef_ref, bf16[768,512]{1,0:T(8,128)(2,1)S(1)} %get-tuple-element.34.refs_0_, bf16[768,1024]{1,0:T(8,128)(2,1)S(1)} %get-tuple-element.38.refs_1_, ...), custom_call_target="tpu_custom_call", output_to_operand_aliasing={{}: (5, {})} | custom-call | flops 4718592 | tf_op jit(solution)/shard_map/merge_second/pallas_call | solution.py:216
  17.0 0.0 copy-start.6
  17.0 1.7 %blocks0.1 = (bf16[416,384]{1,0:T(8,128)(2,1)S(1)}, bf16[416,384]{1,0:T(8,128)(2,1)S(1)}) custom-call(s32[16,10]{1,0:T(8,128)S(1)} %copy-done.7, bf16[3072,768]{1,0:T(8,128)(2,1)S(1)} %merge_second.1.turned_ref, bf16[768,1536]{1,0:T(8,128)(2,1)S(1)} %get-tuple-element.41.mine_ref), custom_call_target="tpu_custom_call" | custom-call | flops 226492416 | tf_op jit(solution)/shard_map/blocks0/pallas_call | solution.py:264
  18.7 2.4 %collective-permute-start.5 = (bf16[416,384]{1,0:T(8,128)(2,1)S(1)}, bf16[416,384]{1,0:T(8,128)(2,1)S(1)}, u32[]{:S(2)}, u32[]{:S(2)}) collective-permute-start(bf16[416,384]{1,0:T(8,128)(2,1)S(1)} %get-tuple-element.43), channel_id=1, source_target_pairs={{0,2},{1,3},{4,0},{5,1},{8,4},{9,5},{12,8},{13,9},{14,12},{15,13},... | collective-permute-start | bytes 958472 | tf_op jit(solution)/shard_map/ppermute | solution.py:460
  21.2 0.1 collective-permute-start.4
  21.3 1.7 %blocks0b.1 = (bf16[416,384]{1,0:T(8,128)(2,1)S(1)}, bf16[416,384]{1,0:T(8,128)(2,1)S(1)}) custom-call(s32[16,10]{1,0:T(8,128)S(1)} %copy-done.6, bf16[3072,768]{1,0:T(8,128)(2,1)S(1)} %merge_second.1.turned_ref, bf16[768,1536]{1,0:T(8,128)(2,1)S(1)} %get-tuple-element.41.mine_ref, bf16[416,384]{1,0:T(8,128)(2,1)S(1)} %get-tuple-element.42.refs_0_), custom_call_target="tpu_custom_call" | custom-call | flops 226492416 | tf_op jit(solution)/shard_map/blocks0b/pallas_call | solution.py:264
  23.0 1.4 %collective-permute-start.12 = (bf16[416,384]{1,0:T(8,128)(2,1)S(1)}, bf16[416,384]{1,0:T(8,128)(2,1)S(1)}, u32[]{:S(2)}, u32[]{:S(2)}) collective-permute-start(bf16[416,384]{1,0:T(8,128)(2,1)S(1)} %get-tuple-element.52), channel_id=1, source_target_pairs={{0,4},{1,5},{4,8},{5,9},{8,12},{9,13},{12,14},{13,15},{14,10},{15,... | collective-permute-start | bytes 958472 | tf_op jit(solution)/shard_map/ppermute | solution.py:460
  24.5 0.2 collective-permute-start.15
  24.6 4.1 %collective-permute-done.5.refs_1_ = bf16[416,384]{1,0:T(8,128)(2,1)S(1)} collective-permute-done((bf16[416,384]{1,0:T(8,128)(2,1)S(1)}, bf16[416,384]{1,0:T(8,128)(2,1)S(1)}, u32[]{:S(2)}, u32[]{:S(2)}) %collective-permute-start.5) | collective-permute-done | bytes 319520 | tf_op jit(solution)/shard_map/ppermute | solution.py:460
  28.8 0.8 collective-permute-done.4.refs_0_
  29.6 2.6 %blocks1.1 = (f32[416,384]{1,0:T(8,128)S(1)}, f32[416,384]{1,0:T(8,128)S(1)}, f32[416,384]{1,0:T(8,128)S(1)}, f32[416,384]{1,0:T(8,128)S(1)}) custom-call(s32[16,20]{1,0:T(8,128)S(1)} %copy-done.5, bf16[3072,768]{1,0:T(8,128)(2,1)S(1)} %merge_second.1.turned_ref, bf16[768,1536]{1,0:T(8,128)(2,1)S(1)} %get-tuple-element.41.mine_ref, ...), custom_call_target="tpu_custom_call" | custom-call | flops 452984832 | tf_op jit(solution)/shard_map/blocks1/pallas_call | solution.py:264
  32.2 0.0 copy-start.4
  32.2 0.1 add_convert_fusion.7
  32.3 1.4 %collective-permute-start.8 = (bf16[416,384]{1,0:T(8,128)(2,1)S(1)}, bf16[416,384]{1,0:T(8,128)(2,1)S(1)}, u32[]{:S(2)}, u32[]{:S(2)}) collective-permute-start(bf16[416,384]{1,0:T(8,128)(2,1)S(1)} %add_convert_fusion.7), channel_id=1, source_target_pairs={{0,2},{1,3},{4,0},{5,1},{8,4},{9,5},{12,8},{13,9},{14,12},{15,13},... | collective-permute-start | bytes 958472 | tf_op jit(solution)/shard_map/ppermute | solution.py:460
  33.7 0.1 add_convert_fusion.9
  33.7 0.2 collective-permute-start.6
  33.9 2.5 %collective-permute-done.12 = bf16[416,384]{1,0:T(8,128)(2,1)S(1)} collective-permute-done((bf16[416,384]{1,0:T(8,128)(2,1)S(1)}, bf16[416,384]{1,0:T(8,128)(2,1)S(1)}, u32[]{:S(2)}, u32[]{:S(2)}) %collective-permute-start.12) | collective-permute-done | bytes 319520 | tf_op jit(solution)/shard_map/ppermute | solution.py:460
  36.4 0.1 add_convert_fusion.3
  36.5 0.5 collective-permute-start.13
  37.0 0.1 add_convert_fusion.1
  37.1 1.1 %collective-permute-start.16 = (bf16[416,384]{1,0:T(8,128)(2,1)S(1)}, bf16[416,384]{1,0:T(8,128)(2,1)S(1)}, u32[]{:S(2)}, u32[]{:S(2)}) collective-permute-start(bf16[416,384]{1,0:T(8,128)(2,1)S(1)} %add_convert_fusion.1), channel_id=1, source_target_pairs={{0,2},{1,3},{4,0},{5,1},{8,4},{9,5},{12,8},{13,9},{14,12},{15,13},... | collective-permute-start | bytes 958472 | tf_op jit(solution)/shard_map/ppermute | solution.py:460
  38.1 1.7 %blocks2.1 = (f32[416,384]{1,0:T(8,128)S(1)}, f32[416,384]{1,0:T(8,128)S(1)}) custom-call(s32[16,10]{1,0:T(8,128)S(1)} %copy-done.4, bf16[3072,768]{1,0:T(8,128)(2,1)S(1)} %merge_second.1.turned_ref, bf16[768,1536]{1,0:T(8,128)(2,1)S(1)} %get-tuple-element.41.mine_ref, bf16[416,384]{1,0:T(8,128)(2,1)S(1)} %collective-permute-done.4.refs_0_, ...), custom_call_target="tpu_custom_call" | custom-call | flops 226492416 | tf_op jit(solution)/shard_map/blocks2/pallas_call | solution.py:264
  39.9 1.0 %collective-permute-done.8.refs_1_ = bf16[416,384]{1,0:T(8,128)(2,1)S(1)} collective-permute-done((bf16[416,384]{1,0:T(8,128)(2,1)S(1)}, bf16[416,384]{1,0:T(8,128)(2,1)S(1)}, u32[]{:S(2)}, u32[]{:S(2)}) %collective-permute-start.8) | collective-permute-done | bytes 319520 | tf_op jit(solution)/shard_map/ppermute | solution.py:460
  40.8 0.1 add_convert_fusion.6
  40.9 1.6 %collective-permute-start.9 = (bf16[416,384]{1,0:T(8,128)(2,1)S(1)}, bf16[416,384]{1,0:T(8,128)(2,1)S(1)}, u32[]{:S(2)}, u32[]{:S(2)}) collective-permute-start(bf16[416,384]{1,0:T(8,128)(2,1)S(1)} %add_convert_fusion.6), channel_id=1, source_target_pairs={{0,2},{1,3},{4,0},{5,1},{8,4},{9,5},{12,8},{13,9},{14,12},{15,13},... | collective-permute-start | bytes 958472 | tf_op jit(solution)/shard_map/ppermute | solution.py:460
  42.5 0.1 add_convert_fusion.8
  42.5 1.4 %collective-permute-start.7 = (bf16[416,384]{1,0:T(8,128)(2,1)S(1)}, bf16[416,384]{1,0:T(8,128)(2,1)S(1)}, u32[]{:S(2)}, u32[]{:S(2)}) collective-permute-start(bf16[416,384]{1,0:T(8,128)(2,1)S(1)} %add_convert_fusion.8), channel_id=1, source_target_pairs={{0,4},{1,5},{4,8},{5,9},{8,12},{9,13},{12,14},{13,15},{14,10},{15,... | collective-permute-start | bytes 958472 | tf_op jit(solution)/shard_map/ppermute | solution.py:460
  43.9 1.7 %blocks2b.1 = (f32[416,384]{1,0:T(8,128)S(1)}, f32[416,384]{1,0:T(8,128)S(1)}) custom-call(s32[16,10]{1,0:T(8,128)S(1)} %copy-done.3, bf16[3072,768]{1,0:T(8,128)(2,1)S(1)} %merge_second.1.turned_ref, bf16[768,1536]{1,0:T(8,128)(2,1)S(1)} %get-tuple-element.41.mine_ref, bf16[416,384]{1,0:T(8,128)(2,1)S(1)} %collective-permute-done.6.refs_0_, ...), custom_call_target="tpu_custom_call" | custom-call | flops 226492416 | tf_op jit(solution)/shard_map/blocks2b/pallas_call | solution.py:264
  45.6 0.0 copy-start.2
  45.6 2.0 %collective-permute-done.16 = bf16[416,384]{1,0:T(8,128)(2,1)S(1)} collective-permute-done((bf16[416,384]{1,0:T(8,128)(2,1)S(1)}, bf16[416,384]{1,0:T(8,128)(2,1)S(1)}, u32[]{:S(2)}, u32[]{:S(2)}) %collective-permute-start.16) | collective-permute-done | bytes 319520 | tf_op jit(solution)/shard_map/ppermute | solution.py:460
  47.7 0.1 add_convert_fusion
  47.8 1.6 %collective-permute-start.17 = (bf16[416,384]{1,0:T(8,128)(2,1)S(1)}, bf16[416,384]{1,0:T(8,128)(2,1)S(1)}, u32[]{:S(2)}, u32[]{:S(2)}) collective-permute-start(bf16[416,384]{1,0:T(8,128)(2,1)S(1)} %add_convert_fusion), channel_id=1, source_target_pairs={{0,2},{1,3},{4,0},{5,1},{8,4},{9,5},{12,8},{13,9},{14,12},{15,13},... | collective-permute-start | bytes 958472 | tf_op jit(solution)/shard_map/ppermute | solution.py:460
  49.3 0.1 add_convert_fusion.2
  49.4 1.4 %collective-permute-start.14 = (bf16[416,384]{1,0:T(8,128)(2,1)S(1)}, bf16[416,384]{1,0:T(8,128)(2,1)S(1)}, u32[]{:S(2)}, u32[]{:S(2)}) collective-permute-start(bf16[416,384]{1,0:T(8,128)(2,1)S(1)} %add_convert_fusion.2), channel_id=1, source_target_pairs={{0,4},{1,5},{4,8},{5,9},{8,12},{9,13},{12,14},{13,15},{14,10},{15,... | collective-permute-start | bytes 958472 | tf_op jit(solution)/shard_map/ppermute | solution.py:460
  50.7 1.7 %blocks3.1 = (f32[416,384]{1,0:T(8,128)S(1)}, f32[416,384]{1,0:T(8,128)S(1)}) custom-call(s32[16,10]{1,0:T(8,128)S(1)} %copy-done.2, bf16[3072,768]{1,0:T(8,128)(2,1)S(1)} %merge_second.1.turned_ref, bf16[768,1536]{1,0:T(8,128)(2,1)S(1)} %get-tuple-element.41.mine_ref, bf16[416,384]{1,0:T(8,128)(2,1)S(1)} %collective-permute-done.6.refs_0_, ...), custom_call_target="tpu_custom_call" | custom-call | flops 226492416 | tf_op jit(solution)/shard_map/blocks3/pallas_call | solution.py:264
  52.5 0.0 copy-start.1
  52.5 2.0 %collective-permute-done.9.refs_1_ = bf16[416,384]{1,0:T(8,128)(2,1)S(1)} collective-permute-done((bf16[416,384]{1,0:T(8,128)(2,1)S(1)}, bf16[416,384]{1,0:T(8,128)(2,1)S(1)}, u32[]{:S(2)}, u32[]{:S(2)}) %collective-permute-start.9) | collective-permute-done | bytes 319520 | tf_op jit(solution)/shard_map/ppermute | solution.py:460
  54.5 0.1 add_convert_fusion.4
  54.6 1.6 %collective-permute-start.11 = (bf16[416,384]{1,0:T(8,128)(2,1)S(1)}, bf16[416,384]{1,0:T(8,128)(2,1)S(1)}, u32[]{:S(2)}, u32[]{:S(2)}) collective-permute-start(bf16[416,384]{1,0:T(8,128)(2,1)S(1)} %add_convert_fusion.4), channel_id=1, source_target_pairs={{0,2},{1,3},{4,0},{5,1},{8,4},{9,5},{12,8},{13,9},{14,12},{15,13},... | collective-permute-start | bytes 958472 | tf_op jit(solution)/shard_map/ppermute | solution.py:460
  56.2 0.1 add_convert_fusion.5
  56.3 0.0 copy-start
  56.3 1.4 %collective-permute-start.10 = (bf16[416,384]{1,0:T(8,128)(2,1)S(1)}, bf16[416,384]{1,0:T(8,128)(2,1)S(1)}, u32[]{:S(2)}, u32[]{:S(2)}) collective-permute-start(bf16[416,384]{1,0:T(8,128)(2,1)S(1)} %add_convert_fusion.5), channel_id=1, source_target_pairs={{0,4},{1,5},{4,8},{5,9},{8,12},{9,13},{12,14},{13,15},{14,10},{15,... | collective-permute-start | bytes 958472 | tf_op jit(solution)/shard_map/ppermute | solution.py:460
  57.6 1.7 %blocks3b.1 = (f32[416,384]{1,0:T(8,128)S(1)}, f32[416,384]{1,0:T(8,128)S(1)}) custom-call(s32[16,10]{1,0:T(8,128)S(1)} %copy-done.1, bf16[3072,768]{1,0:T(8,128)(2,1)S(1)} %merge_second.1.turned_ref, bf16[768,1536]{1,0:T(8,128)(2,1)S(1)} %get-tuple-element.41.mine_ref, bf16[416,384]{1,0:T(8,128)(2,1)S(1)} %collective-permute-done.7.refs_0_, ...), custom_call_target="tpu_custom_call" | custom-call | flops 226492416 | tf_op jit(solution)/shard_map/blocks3b/pallas_call | solution.py:264
  59.4 2.0 %collective-permute-done.17.left0 = bf16[416,384]{1,0:T(8,128)(2,1)S(1)} collective-permute-done((bf16[416,384]{1,0:T(8,128)(2,1)S(1)}, bf16[416,384]{1,0:T(8,128)(2,1)S(1)}, u32[]{:S(2)}, u32[]{:S(2)}) %collective-permute-start.17) | collective-permute-done | bytes 319520 | tf_op jit(solution)/shard_map/ppermute | solution.py:460
  61.4 1.1 %collective-permute-done.14.right1 = bf16[416,384]{1,0:T(8,128)(2,1)S(1)} collective-permute-done((bf16[416,384]{1,0:T(8,128)(2,1)S(1)}, bf16[416,384]{1,0:T(8,128)(2,1)S(1)}, u32[]{:S(2)}, u32[]{:S(2)}) %collective-permute-start.14) | collective-permute-done | bytes 319520 | tf_op jit(solution)/shard_map/ppermute | solution.py:460
  62.5 5.7 %collective-permute-done.11.left1 = bf16[416,384]{1,0:T(8,128)(2,1)S(1)} collective-permute-done((bf16[416,384]{1,0:T(8,128)(2,1)S(1)}, bf16[416,384]{1,0:T(8,128)(2,1)S(1)}, u32[]{:S(2)}, u32[]{:S(2)}) %collective-permute-start.11) | collective-permute-done | bytes 319520 | tf_op jit(solution)/shard_map/ppermute | solution.py:460
  68.2 1.1 %collective-permute-done.10.right0 = bf16[416,384]{1,0:T(8,128)(2,1)S(1)} collective-permute-done((bf16[416,384]{1,0:T(8,128)(2,1)S(1)}, bf16[416,384]{1,0:T(8,128)(2,1)S(1)}, u32[]{:S(2)}, u32[]{:S(2)}) %collective-permute-start.10) | collective-permute-done | bytes 319520 | tf_op jit(solution)/shard_map/ppermute | solution.py:460
  69.3 1.0 %outgoing.1 = (bf16[384,384]{1,0:T(8,128)(2,1)S(1)}, bf16[320,384]{1,0:T(8,128)(2,1)S(1)}, f32[192,384]{1,0:T(8,128)S(1)}) custom-call(s32[16,5]{1,0:T(8,128)S(1)} %copy-done, f32[416,384]{1,0:T(8,128)S(1)} %get-tuple-element.48.own0, f32[416,384]{1,0:T(8,128)S(1)} %get-tuple-element.49.own1, bf16[416,384]{1,0:T(8,128)(2,1)S(1)} %collective-permute-done.10.right0, ...), custom_call_target="tpu_custom_call" | custom-call | tf_op jit(solution)/shard_map/outgoing/pallas_call | solution.py:495
  70.4 6.1 %collective-permute-start.19 = (bf16[384,384]{1,0:T(8,128)(2,1)S(1)}, bf16[384,384]{1,0:T(8,128)(2,1)S(1)}, u32[]{:S(2)}, u32[]{:S(2)}) collective-permute-start(bf16[384,384]{1,0:T(8,128)(2,1)S(1)} %get-tuple-element.60), channel_id=1, source_target_pairs={{0,2},{1,10},{2,4},{3,12},{4,6},{5,14},{6,0},{7,8},{8,5},{9,11},{1... | collective-permute-start | bytes 884744 | tf_op jit(solution)/shard_map/ppermute | solution.py:508
  76.5 1.8 %own.1.result_ref = f32[384,1536]{1,0:T(8,128)} custom-call(s32[16,5]{1,0:T(8,128)S(1)} %copy-done, f32[416,384]{1,0:T(8,128)S(1)} %get-tuple-element.48.own0, f32[416,384]{1,0:T(8,128)S(1)} %get-tuple-element.49.own1, bf16[416,384]{1,0:T(8,128)(2,1)S(1)} %collective-permute-done.10.right0, bf16[416,384]{1,0:T(8,128)(2,1)S(1)} %collective-permute-done.11.left1, ...), custom_call_target="tpu_custom_call" | custom-call | tf_op jit(solution)/shard_map/own/pallas_call | solution.py:510
  78.3 4.5 %collective-permute-done.19.one = bf16[384,384]{1,0:T(8,128)(2,1)S(1)} collective-permute-done((bf16[384,384]{1,0:T(8,128)(2,1)S(1)}, bf16[384,384]{1,0:T(8,128)(2,1)S(1)}, u32[]{:S(2)}, u32[]{:S(2)}) %collective-permute-start.19) | collective-permute-done | bytes 294944 | tf_op jit(solution)/shard_map/ppermute | solution.py:508
  82.8 1.7 %one.1.result_ref = f32[384,1536]{1,0:T(8,128)} custom-call(s32[16,5]{1,0:T(8,128)S(1)} %copy-done, bf16[384,384]{1,0:T(8,128)(2,1)S(1)} %collective-permute-done.19.one, f32[384,1536]{1,0:T(8,128)} %own.1.result_ref), custom_call_target="tpu_custom_call", output_to_operand_aliasing={{}: (2, {})} | custom-call | tf_op jit(solution)/shard_map/one/pallas_call | solution.py:520
  84.5 3.2 %collective-permute-done.18.other = bf16[320,384]{1,0:T(8,128)(2,1)S(1)} collective-permute-done((bf16[320,384]{1,0:T(8,128)(2,1)S(1)}, bf16[320,384]{1,0:T(8,128)(2,1)S(1)}, u32[]{:S(2)}, u32[]{:S(2)}) %collective-permute-start.18) | collective-permute-done | bytes 245792 | tf_op jit(solution)/shard_map/ppermute | solution.py:509
  87.7 1.6 %other.1 = f32[384,1536]{1,0:T(8,128)} custom-call(s32[16,5]{1,0:T(8,128)S(1)} %copy-done, f32[192,384]{1,0:T(8,128)S(1)} %get-tuple-element.58.share, bf16[320,384]{1,0:T(8,128)(2,1)S(1)} %collective-permute-done.18.other, f32[384,1536]{1,0:T(8,128)} %one.1.result_ref), custom_call_target="tpu_custom_call", output_to_operand_aliasing={{}: (3, {})} | custom-call | tf_op jit(solution)/shard_map/other/pallas_call | solution.py:520
  (19 shorter events, 0.0 us)
Async XLA Ops:
  3.9 5.0 %collective-permute-start = (bf16[768,512]{1,0:T(8,128)(2,1)S(1)}, bf16[768,512]{1,0:T(8,128)(2,1)S(1)}, u32[]{:S(2)}, u32[]{:S(2)}) collective-permute-start(bf16[768,512]{1,0:T(8,128)(2,1)S(1)} %get-tuple-element.34.refs_0_), channel_id=1, source_target_pairs={{0,1},{1,0},{2,3},{3,2},{4,5},{5,4},{6,7},{7,6},{8,9},{9,8},{10,11... | collective-permute-start | bytes 2359304 | tf_op jit(solution)/shard_map/ppermute | solution.py:540
  8.5 4.8 %collective-permute-start.3 = (bf16[768,1024]{1,0:T(8,128)(2,1)S(1)}, bf16[768,1024]{1,0:T(8,128)(2,1)S(1)}, u32[]{:S(2)}, u32[]{:S(2)}) collective-permute-start(bf16[768,1024]{1,0:T(8,128)(2,1)S(1)} %get-tuple-element.38.refs_1_), channel_id=1, source_target_pairs={{0,1},{1,0},{2,3},{3,2},{4,5},{5,4},{6,7},{7,6},{8,9},{9,8},{10,11... | collective-permute-start | bytes 4718600 | tf_op jit(solution)/shard_map/ppermute | solution.py:540
  11.1 4.6 %collective-permute-start.1 = (bf16[768,1024]{1,0:T(8,128)(2,1)S(1)}, bf16[768,1024]{1,0:T(8,128)(2,1)S(1)}, u32[]{:S(2)}, u32[]{:S(2)}) collective-permute-start(bf16[768,1024]{1,0:T(8,128)(2,1)S(1)} %pick_mine.2.refs_0_), channel_id=1, source_target_pairs={{0,1},{1,0},{2,3},{3,2},{4,5},{5,4},{6,7},{7,6},{8,9},{9,8},{10,11... | collective-permute-start | bytes 4718600 | tf_op jit(solution)/shard_map/ppermute | solution.py:540
  12.7 3.0 %collective-permute-start.2 = (bf16[768,512]{1,0:T(8,128)(2,1)S(1)}, bf16[768,512]{1,0:T(8,128)(2,1)S(1)}, u32[]{:S(2)}, u32[]{:S(2)}) collective-permute-start(bf16[768,512]{1,0:T(8,128)(2,1)S(1)} %pick_mine.3.refs_1_), channel_id=1, source_target_pairs={{0,1},{1,0},{2,3},{3,2},{4,5},{5,4},{6,7},{7,6},{8,9},{9,8},{10,11... | collective-permute-start | bytes 2359304 | tf_op jit(solution)/shard_map/ppermute | solution.py:540
  15.7 1.2 %copy-start.7 = (s32[16,10]{1,0:T(8,128)S(1)}, s32[16,10]{1,0:T(8,128)}, u32[]{:S(2)}) copy-start(s32[16,10]{1,0:T(8,128)} %constant.16.clone.table) | copy-start | bytes 1924
  17.0 4.3 %copy-start.6 = (s32[16,10]{1,0:T(8,128)S(1)}, s32[16,10]{1,0:T(8,128)}, u32[]{:S(2)}) copy-start(s32[16,10]{1,0:T(8,128)} %constant.17.clone.table) | copy-start | bytes 1924
  18.7 10.1 %collective-permute-start.5 = (bf16[416,384]{1,0:T(8,128)(2,1)S(1)}, bf16[416,384]{1,0:T(8,128)(2,1)S(1)}, u32[]{:S(2)}, u32[]{:S(2)}) collective-permute-start(bf16[416,384]{1,0:T(8,128)(2,1)S(1)} %get-tuple-element.43), channel_id=1, source_target_pairs={{0,2},{1,3},{4,0},{5,1},{8,4},{9,5},{12,8},{13,9},{14,12},{15,13},... | collective-permute-start | bytes 958472 | tf_op jit(solution)/shard_map/ppermute | solution.py:460
  21.2 8.4 %copy-start.5 = (s32[16,20]{1,0:T(8,128)S(1)}, s32[16,20]{1,0:T(8,128)}, u32[]{:S(2)}) copy-start(s32[16,20]{1,0:T(8,128)} %constant.18.clone.table) | copy-start | bytes 3844
  21.2 8.4 %collective-permute-start.4 = (bf16[416,384]{1,0:T(8,128)(2,1)S(1)}, bf16[416,384]{1,0:T(8,128)(2,1)S(1)}, u32[]{:S(2)}, u32[]{:S(2)}) collective-permute-start(bf16[416,384]{1,0:T(8,128)(2,1)S(1)} %get-tuple-element.42.refs_0_), channel_id=1, source_target_pairs={{0,4},{1,5},{4,8},{5,9},{8,12},{9,13},{12,14},{13,15},{14,10},{15,... | collective-permute-start | bytes 958472 | tf_op jit(solution)/shard_map/ppermute | solution.py:460
  23.0 13.4 %collective-permute-start.12 = (bf16[416,384]{1,0:T(8,128)(2,1)S(1)}, bf16[416,384]{1,0:T(8,128)(2,1)S(1)}, u32[]{:S(2)}, u32[]{:S(2)}) collective-permute-start(bf16[416,384]{1,0:T(8,128)(2,1)S(1)} %get-tuple-element.52), channel_id=1, source_target_pairs={{0,4},{1,5},{4,8},{5,9},{8,12},{9,13},{12,14},{13,15},{14,10},{15,... | collective-permute-start | bytes 958472 | tf_op jit(solution)/shard_map/ppermute | solution.py:460
  24.5 12.5 %collective-permute-start.15 = (bf16[416,384]{1,0:T(8,128)(2,1)S(1)}, bf16[416,384]{1,0:T(8,128)(2,1)S(1)}, u32[]{:S(2)}, u32[]{:S(2)}) collective-permute-start(bf16[416,384]{1,0:T(8,128)(2,1)S(1)} %get-tuple-element.55), channel_id=1, source_target_pairs={{0,2},{1,3},{4,0},{5,1},{8,4},{9,5},{12,8},{13,9},{14,12},{15,13},... | collective-permute-start | bytes 958472 | tf_op jit(solution)/shard_map/ppermute | solution.py:460
  32.2 5.9 %copy-start.4 = (s32[16,10]{1,0:T(8,128)S(1)}, s32[16,10]{1,0:T(8,128)}, u32[]{:S(2)}) copy-start(s32[16,10]{1,0:T(8,128)} %constant.19.clone.table) | copy-start | bytes 1924
  32.3 8.5 %collective-permute-start.8 = (bf16[416,384]{1,0:T(8,128)(2,1)S(1)}, bf16[416,384]{1,0:T(8,128)(2,1)S(1)}, u32[]{:S(2)}, u32[]{:S(2)}) collective-permute-start(bf16[416,384]{1,0:T(8,128)(2,1)S(1)} %add_convert_fusion.7), channel_id=1, source_target_pairs={{0,2},{1,3},{4,0},{5,1},{8,4},{9,5},{12,8},{13,9},{14,12},{15,13},... | collective-permute-start | bytes 958472 | tf_op jit(solution)/shard_map/ppermute | solution.py:460
  33.7 8.7 %collective-permute-start.6 = (bf16[416,384]{1,0:T(8,128)(2,1)S(1)}, bf16[416,384]{1,0:T(8,128)(2,1)S(1)}, u32[]{:S(2)}, u32[]{:S(2)}) collective-permute-start(bf16[416,384]{1,0:T(8,128)(2,1)S(1)} %add_convert_fusion.9), channel_id=1, source_target_pairs={{0,4},{1,5},{4,8},{5,9},{8,12},{9,13},{12,14},{13,15},{14,10},{15,... | collective-permute-start | bytes 958472 | tf_op jit(solution)/shard_map/ppermute | solution.py:460
  36.5 12.8 %collective-permute-start.13 = (bf16[416,384]{1,0:T(8,128)(2,1)S(1)}, bf16[416,384]{1,0:T(8,128)(2,1)S(1)}, u32[]{:S(2)}, u32[]{:S(2)}) collective-permute-start(bf16[416,384]{1,0:T(8,128)(2,1)S(1)} %add_convert_fusion.3), channel_id=1, source_target_pairs={{0,4},{1,5},{4,8},{5,9},{8,12},{9,13},{12,14},{13,15},{14,10},{15,... | collective-permute-start | bytes 958472 | tf_op jit(solution)/shard_map/ppermute | solution.py:460
  37.1 10.6 %collective-permute-start.16 = (bf16[416,384]{1,0:T(8,128)(2,1)S(1)}, bf16[416,384]{1,0:T(8,128)(2,1)S(1)}, u32[]{:S(2)}, u32[]{:S(2)}) collective-permute-start(bf16[416,384]{1,0:T(8,128)(2,1)S(1)} %add_convert_fusion.1), channel_id=1, source_target_pairs={{0,2},{1,3},{4,0},{5,1},{8,4},{9,5},{12,8},{13,9},{14,12},{15,13},... | collective-permute-start | bytes 958472 | tf_op jit(solution)/shard_map/ppermute | solution.py:460
  39.9 4.0 %copy-start.3 = (s32[16,10]{1,0:T(8,128)S(1)}, s32[16,10]{1,0:T(8,128)}, u32[]{:S(2)}) copy-start(s32[16,10]{1,0:T(8,128)} %constant.20.clone.table) | copy-start | bytes 1924
  40.9 13.6 %collective-permute-start.9 = (bf16[416,384]{1,0:T(8,128)(2,1)S(1)}, bf16[416,384]{1,0:T(8,128)(2,1)S(1)}, u32[]{:S(2)}, u32[]{:S(2)}) collective-permute-start(bf16[416,384]{1,0:T(8,128)(2,1)S(1)} %add_convert_fusion.6), channel_id=1, source_target_pairs={{0,2},{1,3},{4,0},{5,1},{8,4},{9,5},{12,8},{13,9},{14,12},{15,13},... | collective-permute-start | bytes 958472 | tf_op jit(solution)/shard_map/ppermute | solution.py:460
  42.5 13.6 %collective-permute-start.7 = (bf16[416,384]{1,0:T(8,128)(2,1)S(1)}, bf16[416,384]{1,0:T(8,128)(2,1)S(1)}, u32[]{:S(2)}, u32[]{:S(2)}) collective-permute-start(bf16[416,384]{1,0:T(8,128)(2,1)S(1)} %add_convert_fusion.8), channel_id=1, source_target_pairs={{0,4},{1,5},{4,8},{5,9},{8,12},{9,13},{12,14},{13,15},{14,10},{15,... | collective-permute-start | bytes 958472 | tf_op jit(solution)/shard_map/ppermute | solution.py:460
  45.6 5.1 %copy-start.2 = (s32[16,10]{1,0:T(8,128)S(1)}, s32[16,10]{1,0:T(8,128)}, u32[]{:S(2)}) copy-start(s32[16,10]{1,0:T(8,128)} %constant.21.clone.table) | copy-start | bytes 1924
  47.8 13.6 %collective-permute-start.17 = (bf16[416,384]{1,0:T(8,128)(2,1)S(1)}, bf16[416,384]{1,0:T(8,128)(2,1)S(1)}, u32[]{:S(2)}, u32[]{:S(2)}) collective-permute-start(bf16[416,384]{1,0:T(8,128)(2,1)S(1)} %add_convert_fusion), channel_id=1, source_target_pairs={{0,2},{1,3},{4,0},{5,1},{8,4},{9,5},{12,8},{13,9},{14,12},{15,13},... | collective-permute-start | bytes 958472 | tf_op jit(solution)/shard_map/ppermute | solution.py:460
  49.4 13.1 %collective-permute-start.14 = (bf16[416,384]{1,0:T(8,128)(2,1)S(1)}, bf16[416,384]{1,0:T(8,128)(2,1)S(1)}, u32[]{:S(2)}, u32[]{:S(2)}) collective-permute-start(bf16[416,384]{1,0:T(8,128)(2,1)S(1)} %add_convert_fusion.2), channel_id=1, source_target_pairs={{0,4},{1,5},{4,8},{5,9},{8,12},{9,13},{12,14},{13,15},{14,10},{15,... | collective-permute-start | bytes 958472 | tf_op jit(solution)/shard_map/ppermute | solution.py:460
  52.5 5.1 %copy-start.1 = (s32[16,10]{1,0:T(8,128)S(1)}, s32[16,10]{1,0:T(8,128)}, u32[]{:S(2)}) copy-start(s32[16,10]{1,0:T(8,128)} %constant.22.clone.table) | copy-start | bytes 1924
  54.6 13.6 %collective-permute-start.11 = (bf16[416,384]{1,0:T(8,128)(2,1)S(1)}, bf16[416,384]{1,0:T(8,128)(2,1)S(1)}, u32[]{:S(2)}, u32[]{:S(2)}) collective-permute-start(bf16[416,384]{1,0:T(8,128)(2,1)S(1)} %add_convert_fusion.4), channel_id=1, source_target_pairs={{0,2},{1,3},{4,0},{5,1},{8,4},{9,5},{12,8},{13,9},{14,12},{15,13},... | collective-permute-start | bytes 958472 | tf_op jit(solution)/shard_map/ppermute | solution.py:460
  56.3 13.1 %copy-start = (s32[16,5]{1,0:T(8,128)S(1)}, s32[16,5]{1,0:T(8,128)}, u32[]{:S(2)}) copy-start(s32[16,5]{1,0:T(8,128)} %constant.23.clone.place) | copy-start | bytes 964
  56.3 13.1 %collective-permute-start.10 = (bf16[416,384]{1,0:T(8,128)(2,1)S(1)}, bf16[416,384]{1,0:T(8,128)(2,1)S(1)}, u32[]{:S(2)}, u32[]{:S(2)}) collective-permute-start(bf16[416,384]{1,0:T(8,128)(2,1)S(1)} %add_convert_fusion.5), channel_id=1, source_target_pairs={{0,4},{1,5},{4,8},{5,9},{8,12},{9,13},{12,14},{13,15},{14,10},{15,... | collective-permute-start | bytes 958472 | tf_op jit(solution)/shard_map/ppermute | solution.py:460
  70.4 12.4 %collective-permute-start.19 = (bf16[384,384]{1,0:T(8,128)(2,1)S(1)}, bf16[384,384]{1,0:T(8,128)(2,1)S(1)}, u32[]{:S(2)}, u32[]{:S(2)}) collective-permute-start(bf16[384,384]{1,0:T(8,128)(2,1)S(1)} %get-tuple-element.60), channel_id=1, source_target_pairs={{0,2},{1,10},{2,4},{3,12},{4,6},{5,14},{6,0},{7,8},{8,5},{9,11},{1... | collective-permute-start | bytes 884744 | tf_op jit(solution)/shard_map/ppermute | solution.py:508
  76.5 11.2 %collective-permute-start.18 = (bf16[320,384]{1,0:T(8,128)(2,1)S(1)}, bf16[320,384]{1,0:T(8,128)(2,1)S(1)}, u32[]{:S(2)}, u32[]{:S(2)}) collective-permute-start(bf16[320,384]{1,0:T(8,128)(2,1)S(1)} %get-tuple-element.59), channel_id=1, source_target_pairs={{0,4},{1,8},{2,6},{3,10},{4,0},{5,12},{6,2},{7,14},{8,3},{9,13},{1... | collective-permute-start | bytes 737288 | tf_op jit(solution)/shard_map/ppermute | solution.py:509

commit v11 on v8

--- a/solution.py
+++ b/solution.py
@@ -142,37 +142,40 @@
     )(*args, in_hbm(rows))
 
 
-def merge_kernel(first, coef_ref, ours_ref, theirs_ref, *refs):
-    tokens, width = ours_ref.shape
-    tile = 384
+def merge_kernel(first, tile, pieces, coef_ref, *refs):
+    tokens = coef_ref.shape[0]
+    sides = []
+    for count in pieces:
+        sides.append([ref.at[:, j : j + tile] for ref in refs[:count] for j in range(0, ref.shape[1], tile)])
+        refs = refs[count:]
+    width = len(sides[0]) * tile
     ours = jnp.broadcast_to(coef_ref[:, 2:3], (tokens, tile))
     theirs = jnp.broadcast_to(coef_ref[:, 3:4], (tokens, tile))
-    for j in range(width // tile):
-        at = slice(j * tile, (j + 1) * tile)
-        total = (ours * ours_ref[:, at].astype(F32) + theirs * theirs_ref[:, at].astype(F32)).astype(BF16)
+    for j, (a, b) in enumerate(zip(*sides)):
+        total = (ours * a[...].astype(F32) + theirs * b[...].astype(F32)).astype(BF16)
         if first:
-            refs[0][:, at] = total
-            refs[-1][at, :] = total.T
+            refs[0][:, j * tile : (j + 1) * tile] = total
+            refs[-1][j * tile : (j + 1) * tile, :] = total.T
         else:
             refs[-1][width + j * tile : width + (j + 1) * tile, :] = total.T
 
 
-def merge(coef, ours, theirs, turned=None):
-    tokens, width = ours.shape
+def merge(coef, ours, theirs, width, turned=None, tile=256):
+    tokens = coef.shape[0]
     first = turned is None
     vmem = pl.BlockSpec(memory_space=pltpu.VMEM)
-    args = [coef, ours, theirs] + ([] if first else [turned])
+    args = [coef, *ours, *theirs] + ([] if first else [turned])
     out_shape = [jax.ShapeDtypeStruct((2 * width, tokens), BF16)]
     if first:
         out_shape.insert(0, jax.ShapeDtypeStruct((tokens, width), BF16))
     return pl.pallas_call(
-        functools.partial(merge_kernel, first),
+        functools.partial(merge_kernel, first, tile, (len(ours), len(theirs))),
         out_shape=out_shape,
         in_specs=[vmem] * len(args),
         out_specs=[vmem] * len(out_shape),
-        input_output_aliases={} if first else {3: 0},
+        input_output_aliases={} if first else {len(args) - 1: 0},
         compiler_params=pltpu.CompilerParams(vmem_limit_bytes=24 << 20),
-        cost_estimate=pl.CostEstimate(flops=4 * ours.size, bytes_accessed=6 * ours.size, transcendentals=0),
+        cost_estimate=pl.CostEstimate(flops=4 * tokens * width, bytes_accessed=0, transcendentals=0),
         name="merge_first" if first else "merge_second",
     )(*args)
 
@@ -219,7 +222,7 @@
         in_specs=[smem, vmem, vmem] + [any_] * len(after),
         out_specs=[vmem] * count,
         cost_estimate=pl.CostEstimate(
-            flops=2 * count * mine.shape[0] * width * piece[0],
+            flops=count * mine.shape[0] * width * width,
             bytes_accessed=0,
             transcendentals=0,
         ),
@@ -412,17 +415,20 @@
         return lax.ppermute(value, both, ring_perm(1 if key[1] <= (4 if key[0] == 0 else 3) else -1))
 
     compute(ROUNDS[0][:2], "blocks0", BF16)
-    compute(ROUNDS[0][2:], "blocks0b", BF16)
-    compute(ROUNDS[1], "blocks1", F32)
+    compute(ROUNDS[0][2:], "blocks0b", BF16, after=(blocks[0, 4],))
     moving = {key: blocks[key] for key in ROUNDS[0]}
     arrived = {}
+    before = ()
     for n in range(4):
         landed = {}
         for key in ROUNDS[n]:
             if key in moving:
                 landed[key] = hop(moving[key], key)
-        if n < 2:
-            compute(ROUNDS[n + 2], f"blocks{n + 2}", F32, after=(landed[ROUNDS[n][0]],))
+        if n < 3:
+            early = [landed[key] for key in ROUNDS[n][:2]]
+            compute(ROUNDS[n + 1][:2], f"blocks{n + 1}", F32, after=(blocks[ROUNDS[n][3]], *before))
+            compute(ROUNDS[n + 1][2:], f"blocks{n + 1}b", F32, after=early[:1])
+            before = early
         moving = {}
         for (x, t), value in landed.items():
             rightwards = t <= (4 if x == 0 else 3)
@@ -487,8 +493,8 @@
     from_peer = lax.ppermute(sent, "expert", swap)
     (kept,) = pick_half((starts, pick, coef), expert_out, tokens, half, False)
     from_peer_too = lax.ppermute(kept, "expert", swap)
-    rows, turned = merge(coef, kept, from_peer)
-    (turned,) = merge(coef, sent, from_peer_too, turned)
+    rows, turned = merge(coef, [kept], [from_peer], half)
+    (turned,) = merge(coef, [sent], [from_peer_too], half, turned)
 
     total_tokens = tokens * dp_size
     if dp_size == 8 and channels == 8 * 384:

time: 92.6 us -> 89.3 us (0.964)
  waiting for transfers between devices: 41.2 us -> 38.2 us
  Pallas kernels: 30 us -> 32.3 us
  starting transfers between devices: 19.4 us -> 17.5 us
    ppermute x14, waiting for transfers between devices: 31.4 us -> 27.2 us  [hop(): lax.ppermute(value, both, ring_perm(1 if key[1] <= (4 if key[0] == 0 else...]
    pallas_call x5 -> x8, Pallas kernels: 11.5 us -> 13.8 us  [moment_blocks(): pl.pallas_call(functools.partial(blocks_kernel, pieces, width), out_shape...]
    ppermute x1, waiting for transfers between devices: 2.36 us -> 3.57 us  [symmetric_moment(): other = lax.ppermute(other, both, perm_other)]
    ppermute x1, starting transfers between devices: 5.6 us -> 4.61 us  [symmetric_moment(): one = lax.ppermute(one, both, perm_one)]
  transfers between devices with their start and end apart: 18 -> 18, of which waited for: 11 -> 12; matrix products, arithmetic and copies ran while one was open for 1% -> 1% of each run, Pallas kernels for 21% -> 24%
where the time goes in v11:
time: 89.3 us; the launch traced here: 89.1 us
  waiting for transfers between devices  38.2 us (43%)
  Pallas kernels  32.3 us (36%)
  starting transfers between devices  17.5 us (20%)
    ppermute x14, waiting for transfers between devices, hop(): lax.ppermute(value, both, ring_perm(1 if key[1] <= (4 if key[0] == 0 else...  27.2 us
    pallas_call x8, Pallas kernels, moment_blocks(): pl.pallas_call(functools.partial(blocks_kernel, pieces, width), out_shape...  13.8 us
    ppermute x14, starting transfers between devices, hop(): lax.ppermute(value, both, ring_perm(1 if key[1] <= (4 if key[0] == 0 else...  12.3 us
    pallas_call x2, Pallas kernels, pick_half(): pl.pallas_call(functools.partial(pick_kernel, first), out_shape=out_shape...  10.1 us
    ppermute x1, starting transfers between devices, symmetric_moment(): one = lax.ppermute(one, both, perm_one)  4.61 us
    ppermute x1, waiting for transfers between devices, symmetric_moment(): one = lax.ppermute(one, both, perm_one)  4.49 us
    ppermute x1, waiting for transfers between devices, symmetric_moment(): other = lax.ppermute(other, both, perm_other)  3.57 us
    pallas_call x2, Pallas kernels, symmetric_moment(): pl.pallas_call(kernel, out_shape=result, in_specs=[smem] + [vmem] * len(a...  3.22 us
  transfers between devices with their start and end apart: 18, of which 12 were waited for; matrix products, arithmetic and copies ran while one was open for 1% of the time, Pallas kernels for 24%

profile of v11, /device:TPU:1, one launch (start us, length us, event | category | flops | bytes accessed | tf_op | source)
XLA Modules:
  0.0 89.1 jit_solution(1893808561413373219)
XLA Ops:
  0.0 5.5 %pick_first.1 = (bf16[768,1536]{1,0:T(8,128)(2,1)S(1)}, bf16[1536,256]{1,0:T(8,128)(2,1)S(1)}, s32[16,128]{1,0:T(8,128)S(1)}, f32[768,128]{1,0:T(8,128)S(1)}) custom-call(s32[2,768]{1,0:T(2,128)} %bitcast.2, f32[2,768]{1,0:T(2,128)} %bitcast.3, bf16[1536,3072]{1,0:T(8,128)(2,1)} %refs_3_.1), custom_call_target="tpu_custom_call" | custom-call | flops 1207959552 | bytes 7077888 | tf_op jit(solution)/shard_map/pick_first/pallas_call | solution.py:131
  5.6 0.1 collective-permute-start.1
  5.7 4.6 %pick_second.1.refs_0_ = bf16[768,1536]{1,0:T(8,128)(2,1)S(1)} custom-call(s32[16,128]{1,0:T(8,128)S(1)} %get-tuple-element.32.refs_0_, bf16[1536,256]{1,0:T(8,128)(2,1)S(1)} %get-tuple-element.33.refs_1_, f32[768,128]{1,0:T(8,128)S(1)} %get-tuple-element.30.refs_2_.coef_ref, bf16[1536,3072]{1,0:T(8,128)(2,1)} %refs_3_.1), custom_call_target="tpu_custom_call" | custom-call | flops 1207959552 | bytes 7077888 | tf_op jit(solution)/shard_map/pick_second/pallas_call | solution.py:131
  10.2 0.5 collective-permute-start
  10.8 0.0 collective-permute-done.1.refs_1_
  10.8 1.2 %merge_first.1 = (bf16[768,1536]{1,0:T(8,128)(2,1)S(1)}, bf16[3072,768]{1,0:T(8,128)(2,1)S(1)}) custom-call(f32[768,128]{1,0:T(8,128)S(1)} %get-tuple-element.30.refs_2_.coef_ref, bf16[768,1536]{1,0:T(8,128)(2,1)S(1)} %pick_second.1.refs_0_, bf16[768,1536]{1,0:T(8,128)(2,1)S(1)} %collective-permute-done.1.refs_1_), custom_call_target="tpu_custom_call" | custom-call | flops 4718592 | tf_op jit(solution)/shard_map/merge_first/pallas_call | solution.py:171
  12.0 2.9 %collective-permute-done.refs_1_ = bf16[768,1536]{1,0:T(8,128)(2,1)S(1)} collective-permute-done((bf16[768,1536]{1,0:T(8,128)(2,1)S(1)}, bf16[768,1536]{1,0:T(8,128)(2,1)S(1)}, u32[]{:S(2)}, u32[]{:S(2)}) %collective-permute-start) | collective-permute-done | bytes 2359328 | tf_op jit(solution)/shard_map/ppermute | solution.py:495
  14.9 1.1 %merge_second.1.turned_ref = bf16[3072,768]{1,0:T(8,128)(2,1)S(1)} custom-call(f32[768,128]{1,0:T(8,128)S(1)} %get-tuple-element.30.refs_2_.coef_ref, bf16[768,1536]{1,0:T(8,128)(2,1)S(1)} %get-tuple-element.31.refs_0_, bf16[768,1536]{1,0:T(8,128)(2,1)S(1)} %collective-permute-done.refs_1_, ...), custom_call_target="tpu_custom_call", output_to_operand_aliasing={{}: (3, {})} | custom-call | flops 4718592 | tf_op jit(solution)/shard_map/merge_second/pallas_call | solution.py:171
  16.1 0.0 copy-start.7
  16.1 1.7 %blocks0.1 = (bf16[416,384]{1,0:T(8,128)(2,1)S(1)}, bf16[416,384]{1,0:T(8,128)(2,1)S(1)}) custom-call(s32[16,10]{1,0:T(8,128)S(1)} %copy-done.8, bf16[3072,768]{1,0:T(8,128)(2,1)S(1)} %merge_second.1.turned_ref, bf16[768,1536]{1,0:T(8,128)(2,1)S(1)} %get-tuple-element.35.mine_ref), custom_call_target="tpu_custom_call" | custom-call | flops 226492416 | tf_op jit(solution)/shard_map/blocks0/pallas_call | solution.py:219
  17.8 2.7 %collective-permute-start.4 = (bf16[416,384]{1,0:T(8,128)(2,1)S(1)}, bf16[416,384]{1,0:T(8,128)(2,1)S(1)}, u32[]{:S(2)}, u32[]{:S(2)}) collective-permute-start(bf16[416,384]{1,0:T(8,128)(2,1)S(1)} %get-tuple-element.40), channel_id=1, source_target_pairs={{0,2},{1,3},{4,0},{5,1},{8,4},{9,5},{12,8},{13,9},{14,12},{15,13},... | collective-permute-start | bytes 958472 | tf_op jit(solution)/shard_map/ppermute | solution.py:415
  20.5 0.1 collective-permute-start.2
  20.6 1.7 %blocks0b.1 = (bf16[416,384]{1,0:T(8,128)(2,1)S(1)}, bf16[416,384]{1,0:T(8,128)(2,1)S(1)}) custom-call(s32[16,10]{1,0:T(8,128)S(1)} %copy-done.7, bf16[3072,768]{1,0:T(8,128)(2,1)S(1)} %merge_second.1.turned_ref, bf16[768,1536]{1,0:T(8,128)(2,1)S(1)} %get-tuple-element.35.mine_ref, bf16[416,384]{1,0:T(8,128)(2,1)S(1)} %get-tuple-element.36.refs_0_), custom_call_target="tpu_custom_call" | custom-call | flops 226492416 | tf_op jit(solution)/shard_map/blocks0b/pallas_call | solution.py:219
  22.3 1.4 %collective-permute-start.10 = (bf16[416,384]{1,0:T(8,128)(2,1)S(1)}, bf16[416,384]{1,0:T(8,128)(2,1)S(1)}, u32[]{:S(2)}, u32[]{:S(2)}) collective-permute-start(bf16[416,384]{1,0:T(8,128)(2,1)S(1)} %get-tuple-element.49), channel_id=1, source_target_pairs={{0,4},{1,5},{4,8},{5,9},{8,12},{9,13},{12,14},{13,15},{14,10},{15,... | collective-permute-start | bytes 958472 | tf_op jit(solution)/shard_map/ppermute | solution.py:415
  23.8 0.2 collective-permute-start.13
  24.0 1.7 %blocks1.1 = (f32[416,384]{1,0:T(8,128)S(1)}, f32[416,384]{1,0:T(8,128)S(1)}) custom-call(s32[16,10]{1,0:T(8,128)S(1)} %copy-done.6, bf16[3072,768]{1,0:T(8,128)(2,1)S(1)} %merge_second.1.turned_ref, bf16[768,1536]{1,0:T(8,128)(2,1)S(1)} %get-tuple-element.35.mine_ref, bf16[416,384]{1,0:T(8,128)(2,1)S(1)} %get-tuple-element.37.refs_0_), custom_call_target="tpu_custom_call" | custom-call | flops 226492416 | tf_op jit(solution)/shard_map/blocks1/pallas_call | solution.py:219
  25.7 0.0 copy-start.5
  25.7 2.6 %collective-permute-done.4.refs_2_ = bf16[416,384]{1,0:T(8,128)(2,1)S(1)} collective-permute-done((bf16[416,384]{1,0:T(8,128)(2,1)S(1)}, bf16[416,384]{1,0:T(8,128)(2,1)S(1)}, u32[]{:S(2)}, u32[]{:S(2)}) %collective-permute-start.4) | collective-permute-done | bytes 319520 | tf_op jit(solution)/shard_map/ppermute | solution.py:415
  28.3 0.1 add_convert_fusion.7
  28.4 1.2 %collective-permute-start.6 = (bf16[416,384]{1,0:T(8,128)(2,1)S(1)}, bf16[416,384]{1,0:T(8,128)(2,1)S(1)}, u32[]{:S(2)}, u32[]{:S(2)}) collective-permute-start(bf16[416,384]{1,0:T(8,128)(2,1)S(1)} %add_convert_fusion.7), channel_id=1, source_target_pairs={{0,2},{1,3},{4,0},{5,1},{8,4},{9,5},{12,8},{13,9},{14,12},{15,13},... | collective-permute-start | bytes 958472 | tf_op jit(solution)/shard_map/ppermute | solution.py:415
  29.6 0.0 collective-permute-done.2.refs_0_.refs_1_
  29.6 0.1 add_convert_fusion.9
  29.7 0.3 collective-permute-start.3
  30.0 1.7 %blocks1b.1 = (f32[416,384]{1,0:T(8,128)S(1)}, f32[416,384]{1,0:T(8,128)S(1)}) custom-call(s32[16,10]{1,0:T(8,128)S(1)} %copy-done.5, bf16[3072,768]{1,0:T(8,128)(2,1)S(1)} %merge_second.1.turned_ref, bf16[768,1536]{1,0:T(8,128)(2,1)S(1)} %get-tuple-element.35.mine_ref, bf16[416,384]{1,0:T(8,128)(2,1)S(1)} %collective-permute-done.2.refs_0_.refs_1_), custom_call_target="tpu_custom_call" | custom-call | flops 226492416 | tf_op jit(solution)/shard_map/blocks1b/pallas_call | solution.py:219
  31.7 0.0 copy-start.4
  31.7 3.4 %collective-permute-done.13 = bf16[416,384]{1,0:T(8,128)(2,1)S(1)} collective-permute-done((bf16[416,384]{1,0:T(8,128)(2,1)S(1)}, bf16[416,384]{1,0:T(8,128)(2,1)S(1)}, u32[]{:S(2)}, u32[]{:S(2)}) %collective-permute-start.13) | collective-permute-done | bytes 319520 | tf_op jit(solution)/shard_map/ppermute | solution.py:415
  35.1 0.1 add_convert_fusion.1
  35.2 1.2 %collective-permute-start.14 = (bf16[416,384]{1,0:T(8,128)(2,1)S(1)}, bf16[416,384]{1,0:T(8,128)(2,1)S(1)}, u32[]{:S(2)}, u32[]{:S(2)}) collective-permute-start(bf16[416,384]{1,0:T(8,128)(2,1)S(1)} %add_convert_fusion.1), channel_id=1, source_target_pairs={{0,2},{1,3},{4,0},{5,1},{8,4},{9,5},{12,8},{13,9},{14,12},{15,13},... | collective-permute-start | bytes 958472 | tf_op jit(solution)/shard_map/ppermute | solution.py:415
  36.4 0.1 add_convert_fusion.3
  36.5 0.3 collective-permute-start.11
  36.9 1.7 %blocks2.1 = (f32[416,384]{1,0:T(8,128)S(1)}, f32[416,384]{1,0:T(8,128)S(1)}) custom-call(s32[16,10]{1,0:T(8,128)S(1)} %copy-done.4, bf16[3072,768]{1,0:T(8,128)(2,1)S(1)} %merge_second.1.turned_ref, bf16[768,1536]{1,0:T(8,128)(2,1)S(1)} %get-tuple-element.35.mine_ref, f32[416,384]{1,0:T(8,128)S(1)} %get-tuple-element.39.refs_0_, ...), custom_call_target="tpu_custom_call" | custom-call | flops 226492416 | tf_op jit(solution)/shard_map/blocks2/pallas_call | solution.py:219
  38.6 0.0 copy-start.3
  38.6 3.4 %collective-permute-done.6.refs_2_ = bf16[416,384]{1,0:T(8,128)(2,1)S(1)} collective-permute-done((bf16[416,384]{1,0:T(8,128)(2,1)S(1)}, bf16[416,384]{1,0:T(8,128)(2,1)S(1)}, u32[]{:S(2)}, u32[]{:S(2)}) %collective-permute-start.6) | collective-permute-done | bytes 319520 | tf_op jit(solution)/shard_map/ppermute | solution.py:415
  42.0 0.1 add_convert_fusion.5
  42.1 1.2 %collective-permute-start.8 = (bf16[416,384]{1,0:T(8,128)(2,1)S(1)}, bf16[416,384]{1,0:T(8,128)(2,1)S(1)}, u32[]{:S(2)}, u32[]{:S(2)}) collective-permute-start(bf16[416,384]{1,0:T(8,128)(2,1)S(1)} %add_convert_fusion.5), channel_id=1, source_target_pairs={{0,2},{1,3},{4,0},{5,1},{8,4},{9,5},{12,8},{13,9},{14,12},{15,13},... | collective-permute-start | bytes 958472 | tf_op jit(solution)/shard_map/ppermute | solution.py:415
  43.3 0.1 add_convert_fusion.8
  43.4 0.3 collective-permute-start.5
  43.7 1.7 %blocks2b.1 = (f32[416,384]{1,0:T(8,128)S(1)}, f32[416,384]{1,0:T(8,128)S(1)}) custom-call(s32[16,10]{1,0:T(8,128)S(1)} %copy-done.3, bf16[3072,768]{1,0:T(8,128)(2,1)S(1)} %merge_second.1.turned_ref, bf16[768,1536]{1,0:T(8,128)(2,1)S(1)} %get-tuple-element.35.mine_ref, bf16[416,384]{1,0:T(8,128)(2,1)S(1)} %collective-permute-done.3.refs_0_.refs_1_), custom_call_target="tpu_custom_call" | custom-call | flops 226492416 | tf_op jit(solution)/shard_map/blocks2b/pallas_call | solution.py:219
  45.4 0.0 copy-start.2
  45.4 3.4 %collective-permute-done.14 = bf16[416,384]{1,0:T(8,128)(2,1)S(1)} collective-permute-done((bf16[416,384]{1,0:T(8,128)(2,1)S(1)}, bf16[416,384]{1,0:T(8,128)(2,1)S(1)}, u32[]{:S(2)}, u32[]{:S(2)}) %collective-permute-start.14) | collective-permute-done | bytes 319520 | tf_op jit(solution)/shard_map/ppermute | solution.py:415
  48.8 0.1 add_convert_fusion
  48.9 1.2 %collective-permute-start.15 = (bf16[416,384]{1,0:T(8,128)(2,1)S(1)}, bf16[416,384]{1,0:T(8,128)(2,1)S(1)}, u32[]{:S(2)}, u32[]{:S(2)}) collective-permute-start(bf16[416,384]{1,0:T(8,128)(2,1)S(1)} %add_convert_fusion), channel_id=1, source_target_pairs={{0,2},{1,3},{4,0},{5,1},{8,4},{9,5},{12,8},{13,9},{14,12},{15,13},... | collective-permute-start | bytes 958472 | tf_op jit(solution)/shard_map/ppermute | solution.py:415
  50.1 0.1 add_convert_fusion.2
  50.2 0.3 collective-permute-start.12
  50.5 1.7 %blocks3.1 = (f32[416,384]{1,0:T(8,128)S(1)}, f32[416,384]{1,0:T(8,128)S(1)}) custom-call(s32[16,10]{1,0:T(8,128)S(1)} %copy-done.2, bf16[3072,768]{1,0:T(8,128)(2,1)S(1)} %merge_second.1.turned_ref, bf16[768,1536]{1,0:T(8,128)(2,1)S(1)} %get-tuple-element.35.mine_ref, f32[416,384]{1,0:T(8,128)S(1)} %get-tuple-element.44.refs_0_, ...), custom_call_target="tpu_custom_call" | custom-call | flops 226492416 | tf_op jit(solution)/shard_map/blocks3/pallas_call | solution.py:219
  52.3 0.0 copy-start.1
  52.3 3.4 %collective-permute-done.8 = bf16[416,384]{1,0:T(8,128)(2,1)S(1)} collective-permute-done((bf16[416,384]{1,0:T(8,128)(2,1)S(1)}, bf16[416,384]{1,0:T(8,128)(2,1)S(1)}, u32[]{:S(2)}, u32[]{:S(2)}) %collective-permute-start.8) | collective-permute-done | bytes 319520 | tf_op jit(solution)/shard_map/ppermute | solution.py:415
  55.7 0.1 add_convert_fusion.4
  55.7 1.2 %collective-permute-start.9 = (bf16[416,384]{1,0:T(8,128)(2,1)S(1)}, bf16[416,384]{1,0:T(8,128)(2,1)S(1)}, u32[]{:S(2)}, u32[]{:S(2)}) collective-permute-start(bf16[416,384]{1,0:T(8,128)(2,1)S(1)} %add_convert_fusion.4), channel_id=1, source_target_pairs={{0,2},{1,3},{4,0},{5,1},{8,4},{9,5},{12,8},{13,9},{14,12},{15,13},... | collective-permute-start | bytes 958472 | tf_op jit(solution)/shard_map/ppermute | solution.py:415
  57.0 0.1 add_convert_fusion.6
  57.1 0.0 copy-start
  57.1 0.3 collective-permute-start.7
  57.4 1.7 %blocks3b.1 = (f32[416,384]{1,0:T(8,128)S(1)}, f32[416,384]{1,0:T(8,128)S(1)}) custom-call(s32[16,10]{1,0:T(8,128)S(1)} %copy-done.1, bf16[3072,768]{1,0:T(8,128)(2,1)S(1)} %merge_second.1.turned_ref, bf16[768,1536]{1,0:T(8,128)(2,1)S(1)} %get-tuple-element.35.mine_ref, bf16[416,384]{1,0:T(8,128)(2,1)S(1)} %collective-permute-done.5.refs_0_), custom_call_target="tpu_custom_call" | custom-call | flops 226492416 | tf_op jit(solution)/shard_map/blocks3b/pallas_call | solution.py:219
  59.2 3.4 %collective-permute-done.15.left0 = bf16[416,384]{1,0:T(8,128)(2,1)S(1)} collective-permute-done((bf16[416,384]{1,0:T(8,128)(2,1)S(1)}, bf16[416,384]{1,0:T(8,128)(2,1)S(1)}, u32[]{:S(2)}, u32[]{:S(2)}) %collective-permute-start.15) | collective-permute-done | bytes 319520 | tf_op jit(solution)/shard_map/ppermute | solution.py:415
  62.5 0.9 collective-permute-done.12.right1
  63.4 6.0 %collective-permute-done.9.left1 = bf16[416,384]{1,0:T(8,128)(2,1)S(1)} collective-permute-done((bf16[416,384]{1,0:T(8,128)(2,1)S(1)}, bf16[416,384]{1,0:T(8,128)(2,1)S(1)}, u32[]{:S(2)}, u32[]{:S(2)}) %collective-permute-start.9) | collective-permute-done | bytes 319520 | tf_op jit(solution)/shard_map/ppermute | solution.py:415
  69.4 0.9 collective-permute-done.7.right0
  70.2 1.0 %outgoing.1 = (bf16[384,384]{1,0:T(8,128)(2,1)S(1)}, bf16[320,384]{1,0:T(8,128)(2,1)S(1)}, f32[192,384]{1,0:T(8,128)S(1)}) custom-call(s32[16,5]{1,0:T(8,128)S(1)} %copy-done, f32[416,384]{1,0:T(8,128)S(1)} %get-tuple-element.42.own0, f32[416,384]{1,0:T(8,128)S(1)} %get-tuple-element.43.own1, bf16[416,384]{1,0:T(8,128)(2,1)S(1)} %collective-permute-done.7.right0, ...), custom_call_target="tpu_custom_call" | custom-call | tf_op jit(solution)/shard_map/outgoing/pallas_call | solution.py:447
  71.2 4.6 %collective-permute-start.17 = (bf16[384,384]{1,0:T(8,128)(2,1)S(1)}, bf16[384,384]{1,0:T(8,128)(2,1)S(1)}, u32[]{:S(2)}, u32[]{:S(2)}) collective-permute-start(bf16[384,384]{1,0:T(8,128)(2,1)S(1)} %get-tuple-element.54), channel_id=1, source_target_pairs={{0,2},{1,10},{2,4},{3,12},{4,6},{5,14},{6,0},{7,8},{8,5},{9,11},{1... | collective-permute-start | bytes 884744 | tf_op jit(solution)/shard_map/ppermute | solution.py:460
  75.8 1.8 %own.1.result_ref = f32[384,1536]{1,0:T(8,128)} custom-call(s32[16,5]{1,0:T(8,128)S(1)} %copy-done, f32[416,384]{1,0:T(8,128)S(1)} %get-tuple-element.42.own0, f32[416,384]{1,0:T(8,128)S(1)} %get-tuple-element.43.own1, bf16[416,384]{1,0:T(8,128)(2,1)S(1)} %collective-permute-done.7.right0, bf16[416,384]{1,0:T(8,128)(2,1)S(1)} %collective-permute-done.9.left1, ...), custom_call_target="tpu_custom_call" | custom-call | tf_op jit(solution)/shard_map/own/pallas_call | solution.py:462
  77.6 4.5 %collective-permute-done.17.one = bf16[384,384]{1,0:T(8,128)(2,1)S(1)} collective-permute-done((bf16[384,384]{1,0:T(8,128)(2,1)S(1)}, bf16[384,384]{1,0:T(8,128)(2,1)S(1)}, u32[]{:S(2)}, u32[]{:S(2)}) %collective-permute-start.17) | collective-permute-done | bytes 294944 | tf_op jit(solution)/shard_map/ppermute | solution.py:460
  82.1 1.7 %one.1.result_ref = f32[384,1536]{1,0:T(8,128)} custom-call(s32[16,5]{1,0:T(8,128)S(1)} %copy-done, bf16[384,384]{1,0:T(8,128)(2,1)S(1)} %collective-permute-done.17.one, f32[384,1536]{1,0:T(8,128)} %own.1.result_ref), custom_call_target="tpu_custom_call", output_to_operand_aliasing={{}: (2, {})} | custom-call | tf_op jit(solution)/shard_map/one/pallas_call | solution.py:472
  83.8 3.6 %collective-permute-done.16.other = bf16[320,384]{1,0:T(8,128)(2,1)S(1)} collective-permute-done((bf16[320,384]{1,0:T(8,128)(2,1)S(1)}, bf16[320,384]{1,0:T(8,128)(2,1)S(1)}, u32[]{:S(2)}, u32[]{:S(2)}) %collective-permute-start.16) | collective-permute-done | bytes 245792 | tf_op jit(solution)/shard_map/ppermute | solution.py:461
  87.4 1.6 %other.1 = f32[384,1536]{1,0:T(8,128)} custom-call(s32[16,5]{1,0:T(8,128)S(1)} %copy-done, f32[192,384]{1,0:T(8,128)S(1)} %get-tuple-element.52.share, bf16[320,384]{1,0:T(8,128)(2,1)S(1)} %collective-permute-done.16.other, f32[384,1536]{1,0:T(8,128)} %one.1.result_ref), custom_call_target="tpu_custom_call", output_to_operand_aliasing={{}: (3, {})} | custom-call | tf_op jit(solution)/shard_map/other/pallas_call | solution.py:472
  (16 shorter events, 0.0 us)
Async XLA Ops:
  5.6 5.2 %collective-permute-start.1 = (bf16[768,1536]{1,0:T(8,128)(2,1)S(1)}, bf16[768,1536]{1,0:T(8,128)(2,1)S(1)}, u32[]{:S(2)}, u32[]{:S(2)}) collective-permute-start(bf16[768,1536]{1,0:T(8,128)(2,1)S(1)} %get-tuple-element.31.refs_0_), channel_id=1, source_target_pairs={{0,1},{1,0},{2,3},{3,2},{4,5},{5,4},{6,7},{7,6},{8,9},{9,8},{10,11... | collective-permute-start | bytes 7077896 | tf_op jit(solution)/shard_map/ppermute | solution.py:493
  10.2 4.7 %collective-permute-start = (bf16[768,1536]{1,0:T(8,128)(2,1)S(1)}, bf16[768,1536]{1,0:T(8,128)(2,1)S(1)}, u32[]{:S(2)}, u32[]{:S(2)}) collective-permute-start(bf16[768,1536]{1,0:T(8,128)(2,1)S(1)} %pick_second.1.refs_0_), channel_id=1, source_target_pairs={{0,1},{1,0},{2,3},{3,2},{4,5},{5,4},{6,7},{7,6},{8,9},{9,8},{10,11... | collective-permute-start | bytes 7077896 | tf_op jit(solution)/shard_map/ppermute | solution.py:495
  14.9 1.1 %copy-start.8 = (s32[16,10]{1,0:T(8,128)S(1)}, s32[16,10]{1,0:T(8,128)}, u32[]{:S(2)}) copy-start(s32[16,10]{1,0:T(8,128)} %constant.18.clone.table) | copy-start | bytes 1924
  16.1 4.5 %copy-start.7 = (s32[16,10]{1,0:T(8,128)S(1)}, s32[16,10]{1,0:T(8,128)}, u32[]{:S(2)}) copy-start(s32[16,10]{1,0:T(8,128)} %constant.19.clone.table) | copy-start | bytes 1924
  17.8 10.5 %collective-permute-start.4 = (bf16[416,384]{1,0:T(8,128)(2,1)S(1)}, bf16[416,384]{1,0:T(8,128)(2,1)S(1)}, u32[]{:S(2)}, u32[]{:S(2)}) collective-permute-start(bf16[416,384]{1,0:T(8,128)(2,1)S(1)} %get-tuple-element.40), channel_id=1, source_target_pairs={{0,2},{1,3},{4,0},{5,1},{8,4},{9,5},{12,8},{13,9},{14,12},{15,13},... | collective-permute-start | bytes 958472 | tf_op jit(solution)/shard_map/ppermute | solution.py:415
  20.5 3.5 %copy-start.6 = (s32[16,10]{1,0:T(8,128)S(1)}, s32[16,10]{1,0:T(8,128)}, u32[]{:S(2)}) copy-start(s32[16,10]{1,0:T(8,128)} %constant.20.clone.table) | copy-start | bytes 1924
  20.5 9.1 %collective-permute-start.2 = (bf16[416,384]{1,0:T(8,128)(2,1)S(1)}, bf16[416,384]{1,0:T(8,128)(2,1)S(1)}, u32[]{:S(2)}, u32[]{:S(2)}) collective-permute-start(bf16[416,384]{1,0:T(8,128)(2,1)S(1)} %get-tuple-element.36.refs_0_), channel_id=1, source_target_pairs={{0,4},{1,5},{4,8},{5,9},{8,12},{9,13},{12,14},{13,15},{14,10},{15,... | collective-permute-start | bytes 958472 | tf_op jit(solution)/shard_map/ppermute | solution.py:415
  22.3 14.1 %collective-permute-start.10 = (bf16[416,384]{1,0:T(8,128)(2,1)S(1)}, bf16[416,384]{1,0:T(8,128)(2,1)S(1)}, u32[]{:S(2)}, u32[]{:S(2)}) collective-permute-start(bf16[416,384]{1,0:T(8,128)(2,1)S(1)} %get-tuple-element.49), channel_id=1, source_target_pairs={{0,4},{1,5},{4,8},{5,9},{8,12},{9,13},{12,14},{13,15},{14,10},{15,... | collective-permute-start | bytes 958472 | tf_op jit(solution)/shard_map/ppermute | solution.py:415
  23.8 11.3 %collective-permute-start.13 = (bf16[416,384]{1,0:T(8,128)(2,1)S(1)}, bf16[416,384]{1,0:T(8,128)(2,1)S(1)}, u32[]{:S(2)}, u32[]{:S(2)}) collective-permute-start(bf16[416,384]{1,0:T(8,128)(2,1)S(1)} %get-tuple-element.37.refs_0_), channel_id=1, source_target_pairs={{0,2},{1,3},{4,0},{5,1},{8,4},{9,5},{12,8},{13,9},{14,12},{15,13},... | collective-permute-start | bytes 958472 | tf_op jit(solution)/shard_map/ppermute | solution.py:415
  25.7 4.3 %copy-start.5 = (s32[16,10]{1,0:T(8,128)S(1)}, s32[16,10]{1,0:T(8,128)}, u32[]{:S(2)}) copy-start(s32[16,10]{1,0:T(8,128)} %constant.21.clone.table) | copy-start | bytes 1924
  28.4 13.6 %collective-permute-start.6 = (bf16[416,384]{1,0:T(8,128)(2,1)S(1)}, bf16[416,384]{1,0:T(8,128)(2,1)S(1)}, u32[]{:S(2)}, u32[]{:S(2)}) collective-permute-start(bf16[416,384]{1,0:T(8,128)(2,1)S(1)} %add_convert_fusion.7), channel_id=1, source_target_pairs={{0,2},{1,3},{4,0},{5,1},{8,4},{9,5},{12,8},{13,9},{14,12},{15,13},... | collective-permute-start | bytes 958472 | tf_op jit(solution)/shard_map/ppermute | solution.py:415
  29.7 13.6 %collective-permute-start.3 = (bf16[416,384]{1,0:T(8,128)(2,1)S(1)}, bf16[416,384]{1,0:T(8,128)(2,1)S(1)}, u32[]{:S(2)}, u32[]{:S(2)}) collective-permute-start(bf16[416,384]{1,0:T(8,128)(2,1)S(1)} %add_convert_fusion.9), channel_id=1, source_target_pairs={{0,4},{1,5},{4,8},{5,9},{8,12},{9,13},{12,14},{13,15},{14,10},{15,... | collective-permute-start | bytes 958472 | tf_op jit(solution)/shard_map/ppermute | solution.py:415
  31.7 5.1 %copy-start.4 = (s32[16,10]{1,0:T(8,128)S(1)}, s32[16,10]{1,0:T(8,128)}, u32[]{:S(2)}) copy-start(s32[16,10]{1,0:T(8,128)} %constant.22.clone.table) | copy-start | bytes 1924
  35.2 13.6 %collective-permute-start.14 = (bf16[416,384]{1,0:T(8,128)(2,1)S(1)}, bf16[416,384]{1,0:T(8,128)(2,1)S(1)}, u32[]{:S(2)}, u32[]{:S(2)}) collective-permute-start(bf16[416,384]{1,0:T(8,128)(2,1)S(1)} %add_convert_fusion.1), channel_id=1, source_target_pairs={{0,2},{1,3},{4,0},{5,1},{8,4},{9,5},{12,8},{13,9},{14,12},{15,13},... | collective-permute-start | bytes 958472 | tf_op jit(solution)/shard_map/ppermute | solution.py:415
  36.5 13.6 %collective-permute-start.11 = (bf16[416,384]{1,0:T(8,128)(2,1)S(1)}, bf16[416,384]{1,0:T(8,128)(2,1)S(1)}, u32[]{:S(2)}, u32[]{:S(2)}) collective-permute-start(bf16[416,384]{1,0:T(8,128)(2,1)S(1)} %add_convert_fusion.3), channel_id=1, source_target_pairs={{0,4},{1,5},{4,8},{5,9},{8,12},{9,13},{12,14},{13,15},{14,10},{15,... | collective-permute-start | bytes 958472 | tf_op jit(solution)/shard_map/ppermute | solution.py:415
  38.6 5.1 %copy-start.3 = (s32[16,10]{1,0:T(8,128)S(1)}, s32[16,10]{1,0:T(8,128)}, u32[]{:S(2)}) copy-start(s32[16,10]{1,0:T(8,128)} %constant.23.clone.table) | copy-start | bytes 1924
  42.1 13.6 %collective-permute-start.8 = (bf16[416,384]{1,0:T(8,128)(2,1)S(1)}, bf16[416,384]{1,0:T(8,128)(2,1)S(1)}, u32[]{:S(2)}, u32[]{:S(2)}) collective-permute-start(bf16[416,384]{1,0:T(8,128)(2,1)S(1)} %add_convert_fusion.5), channel_id=1, source_target_pairs={{0,2},{1,3},{4,0},{5,1},{8,4},{9,5},{12,8},{13,9},{14,12},{15,13},... | collective-permute-start | bytes 958472 | tf_op jit(solution)/shard_map/ppermute | solution.py:415
  43.4 13.6 %collective-permute-start.5 = (bf16[416,384]{1,0:T(8,128)(2,1)S(1)}, bf16[416,384]{1,0:T(8,128)(2,1)S(1)}, u32[]{:S(2)}, u32[]{:S(2)}) collective-permute-start(bf16[416,384]{1,0:T(8,128)(2,1)S(1)} %add_convert_fusion.8), channel_id=1, source_target_pairs={{0,4},{1,5},{4,8},{5,9},{8,12},{9,13},{12,14},{13,15},{14,10},{15,... | collective-permute-start | bytes 958472 | tf_op jit(solution)/shard_map/ppermute | solution.py:415
  45.4 5.1 %copy-start.2 = (s32[16,10]{1,0:T(8,128)S(1)}, s32[16,10]{1,0:T(8,128)}, u32[]{:S(2)}) copy-start(s32[16,10]{1,0:T(8,128)} %constant.24.clone.table) | copy-start | bytes 1924
  48.9 13.6 %collective-permute-start.15 = (bf16[416,384]{1,0:T(8,128)(2,1)S(1)}, bf16[416,384]{1,0:T(8,128)(2,1)S(1)}, u32[]{:S(2)}, u32[]{:S(2)}) collective-permute-start(bf16[416,384]{1,0:T(8,128)(2,1)S(1)} %add_convert_fusion), channel_id=1, source_target_pairs={{0,2},{1,3},{4,0},{5,1},{8,4},{9,5},{12,8},{13,9},{14,12},{15,13},... | collective-permute-start | bytes 958472 | tf_op jit(solution)/shard_map/ppermute | solution.py:415
  50.2 13.2 %collective-permute-start.12 = (bf16[416,384]{1,0:T(8,128)(2,1)S(1)}, bf16[416,384]{1,0:T(8,128)(2,1)S(1)}, u32[]{:S(2)}, u32[]{:S(2)}) collective-permute-start(bf16[416,384]{1,0:T(8,128)(2,1)S(1)} %add_convert_fusion.2), channel_id=1, source_target_pairs={{0,4},{1,5},{4,8},{5,9},{8,12},{9,13},{12,14},{13,15},{14,10},{15,... | collective-permute-start | bytes 958472 | tf_op jit(solution)/shard_map/ppermute | solution.py:415
  52.3 5.1 %copy-start.1 = (s32[16,10]{1,0:T(8,128)S(1)}, s32[16,10]{1,0:T(8,128)}, u32[]{:S(2)}) copy-start(s32[16,10]{1,0:T(8,128)} %constant.25.clone.table) | copy-start | bytes 1924
  55.7 13.6 %collective-permute-start.9 = (bf16[416,384]{1,0:T(8,128)(2,1)S(1)}, bf16[416,384]{1,0:T(8,128)(2,1)S(1)}, u32[]{:S(2)}, u32[]{:S(2)}) collective-permute-start(bf16[416,384]{1,0:T(8,128)(2,1)S(1)} %add_convert_fusion.4), channel_id=1, source_target_pairs={{0,2},{1,3},{4,0},{5,1},{8,4},{9,5},{12,8},{13,9},{14,12},{15,13},... | collective-permute-start | bytes 958472 | tf_op jit(solution)/shard_map/ppermute | solution.py:415
  57.1 13.2 %copy-start = (s32[16,5]{1,0:T(8,128)S(1)}, s32[16,5]{1,0:T(8,128)}, u32[]{:S(2)}) copy-start(s32[16,5]{1,0:T(8,128)} %constant.26.clone.place) | copy-start | bytes 964
  57.1 13.2 %collective-permute-start.7 = (bf16[416,384]{1,0:T(8,128)(2,1)S(1)}, bf16[416,384]{1,0:T(8,128)(2,1)S(1)}, u32[]{:S(2)}, u32[]{:S(2)}) collective-permute-start(bf16[416,384]{1,0:T(8,128)(2,1)S(1)} %add_convert_fusion.6), channel_id=1, source_target_pairs={{0,4},{1,5},{4,8},{5,9},{8,12},{9,13},{12,14},{13,15},{14,10},{15,... | collective-permute-start | bytes 958472 | tf_op jit(solution)/shard_map/ppermute | solution.py:415
  71.2 10.9 %collective-permute-start.17 = (bf16[384,384]{1,0:T(8,128)(2,1)S(1)}, bf16[384,384]{1,0:T(8,128)(2,1)S(1)}, u32[]{:S(2)}, u32[]{:S(2)}) collective-permute-start(bf16[384,384]{1,0:T(8,128)(2,1)S(1)} %get-tuple-element.54), channel_id=1, source_target_pairs={{0,2},{1,10},{2,4},{3,12},{4,6},{5,14},{6,0},{7,8},{8,5},{9,11},{1... | collective-permute-start | bytes 884744 | tf_op jit(solution)/shard_map/ppermute | solution.py:460
  75.8 11.5 %collective-permute-start.16 = (bf16[320,384]{1,0:T(8,128)(2,1)S(1)}, bf16[320,384]{1,0:T(8,128)(2,1)S(1)}, u32[]{:S(2)}, u32[]{:S(2)}) collective-permute-start(bf16[320,384]{1,0:T(8,128)(2,1)S(1)} %get-tuple-element.53), channel_id=1, source_target_pairs={{0,4},{1,8},{2,6},{3,10},{4,0},{5,12},{6,2},{7,14},{8,3},{9,13},{1... | collective-permute-start | bytes 737288 | tf_op jit(solution)/shard_map/ppermute | solution.py:461

commit v12 on v11

--- a/solution.py
+++ b/solution.py
@@ -16,7 +16,7 @@
 F32, BF16, I32 = jnp.float32, jnp.bfloat16, jnp.int32
 
 
-def plan_tokens(ids_ref, gates_ref, pick_ref, starts_ref, coef_ref):
+def plan_tokens(ids_ref, gates_ref, pick_ref, starts_ref, coef_ref, starts_copy):
     tokens = ids_ref.shape[1]
     local = EXPERTS // 2
     lanes = lax.broadcasted_iota(I32, (tokens, 128), 1)
@@ -29,6 +29,12 @@
         lax.broadcasted_iota(I32, (tokens, tokens), 1) < lax.broadcasted_iota(I32, (tokens, tokens), 0), 1.0, 0.0
     ).astype(BF16)
     before = jnp.dot(earlier, named, preferred_element_type=F32)
+    firsts = []
+    for b in range(tokens // BATCH):
+        start = before[b * BATCH : b * BATCH + 1, :].astype(I32)
+        firsts.append(jnp.minimum((start >> 4) << 4, CAP - WINDOW))
+        starts_ref[b : b + 1, :] = firsts[-1]
+    starts_copy.start()
 
     slots = [ids[k] - lax.axis_index("expert") * local for k in range(2)]
     here = [jnp.where((slots[k] >= 0) & (slots[k] < local), 1.0, 0.0) for k in range(2)]
@@ -47,10 +53,7 @@
     columns = lax.broadcasted_iota(I32, (BATCH, local * WINDOW), 1)
     for b in range(tokens // BATCH):
         rows = slice(b * BATCH, (b + 1) * BATCH)
-        start = before[b * BATCH : b * BATCH + 1, :].astype(I32)
-        start = jnp.minimum((start >> 4) << 4, CAP - WINDOW)
-        starts_ref[b : b + 1, :] = start
-        ahead = before[rows] - start.astype(F32)
+        ahead = before[rows] - firsts[b].astype(F32)
         for k in range(2):
             offset = jnp.sum(jnp.where(hits[k][rows], ahead, 0.0), axis=1, keepdims=True).astype(I32)
             at = jnp.where(here[k][rows] > 0.5, slots[k][rows] * WINDOW + offset, -1)
@@ -84,9 +87,8 @@
     if first:
         for copy in small:
             copy.wait()
-        plan_tokens(ids_ref, gates_ref, pick_ref, starts_ref, coef_ref)
         copy = pltpu.make_async_copy(starts_ref, starts, small_sems.at[2])
-        copy.start()
+        plan_tokens(ids_ref, gates_ref, pick_ref, starts_ref, coef_ref, copy)
         copy.wait()
     for j in range(tiles):
         loads[j].wait()
@@ -315,12 +317,14 @@
     return own[rows, :] + right[rows, :].astype(F32) + left[rows, :].astype(F32)
 
 
-def outgoing_kernel(scale, place, own0, own1, right0, left1, right1, left0, one, other, share):
-    width = one.shape[0]
-    third, half = width // 3, width // 2
-    tall = width + STRIP
+def outgoing_one_kernel(scale, own1, right1, left1, one):
+    one[...] = (total(own1, right1, left1, slice(0, one.shape[0])) * scale).astype(BF16)
+
+
+def outgoing_other_kernel(scale, place, own0, own1, right0, left1, right1, left0, after, other, share):
+    half, width = share.shape
+    third, tall = width // 3, width + STRIP
     kind = place[my_row(), 4]
-    one[...] = (total(own1, right1, left1, slice(0, width)) * scale).astype(BF16)
     tail = total(own1, right1, left1, slice(width, tall)) * scale
 
     @pl.when(kind == 0)
@@ -444,19 +448,26 @@
     params = pltpu.CompilerParams(vmem_limit_bytes=24 << 20)
     sums = (blocks[0, 0], blocks[1, 0], arrived[0, True], arrived[1, False], arrived[1, True], arrived[0, False])
     scale = 1.0 / total_tokens
-    one, other, share = pl.pallas_call(
-        functools.partial(outgoing_kernel, scale),
+    perm_one, perm_other = mirror_perms()
+    one = pl.pallas_call(
+        functools.partial(outgoing_one_kernel, scale),
+        out_shape=jax.ShapeDtypeStruct((width, width), BF16),
+        in_specs=[vmem] * 3,
+        out_specs=vmem,
+        compiler_params=params,
+        name="outgoing_one",
+    )(sums[1], sums[4], sums[3])
+    other, share = pl.pallas_call(
+        functools.partial(outgoing_other_kernel, scale),
         out_shape=[
-            jax.ShapeDtypeStruct((width, width), BF16),
             jax.ShapeDtypeStruct((width - 2 * STRIP, width), BF16),
             jax.ShapeDtypeStruct((width // 2, width), F32),
         ],
-        in_specs=[smem] + [vmem] * 6,
-        out_specs=[vmem] * 3,
+        in_specs=[smem] + [vmem] * 6 + [any_],
+        out_specs=[vmem] * 2,
         compiler_params=params,
-        name="outgoing",
-    )(place, *sums)
-    perm_one, perm_other = mirror_perms()
+        name="outgoing_other",
+    )(place, *sums, one)
     one = lax.ppermute(one, both, perm_one)
     other = lax.ppermute(other, both, perm_other)
     partial_result = pl.pallas_call(

time: 89.3 us -> 88.4 us (0.990)
    ppermute x1, waiting for transfers between devices: 3.57 us -> 4.77 us  [symmetric_moment(): other = lax.ppermute(other, both, perm_other)]
  transfers between devices with their start and end apart: 18 -> 18, of which waited for: 12 -> 10; matrix products, arithmetic and copies ran while one was open for 1% -> 1% of each run, Pallas kernels for 24% -> 25%
where the time goes in v12:
time: 88.4 us; the launch traced here: 88.2 us
  waiting for transfers between devices  37.6 us (43%)
  Pallas kernels  32.3 us (37%)
  starting transfers between devices  17.1 us (19%)
    ppermute x14, waiting for transfers between devices, hop(): lax.ppermute(value, both, ring_perm(1 if key[1] <= (4 if key[0] == 0 else...  26.3 us
    pallas_call x8, Pallas kernels, moment_blocks(): pl.pallas_call(functools.partial(blocks_kernel, pieces, width), out_shape...  13.8 us
    ppermute x14, starting transfers between devices, hop(): lax.ppermute(value, both, ring_perm(1 if key[1] <= (4 if key[0] == 0 else...  12.3 us
    pallas_call x2, Pallas kernels, pick_half(): pl.pallas_call(functools.partial(pick_kernel, first), out_shape=out_shape...  10.1 us
    ppermute x1, waiting for transfers between devices, symmetric_moment(): other = lax.ppermute(other, both, perm_other)  4.77 us
    ppermute x1, starting transfers between devices, symmetric_moment(): one = lax.ppermute(one, both, perm_one)  4.17 us
    ppermute x1, waiting for transfers between devices, symmetric_moment(): one = lax.ppermute(one, both, perm_one)  3.63 us
    pallas_call x2, Pallas kernels, symmetric_moment(): pl.pallas_call(kernel, out_shape=result, in_specs=[smem] + [vmem] * len(a...  3.22 us
  transfers between devices with their start and end apart: 18, of which 10 were waited for; matrix products, arithmetic and copies ran while one was open for 1% of the time, Pallas kernels for 25%

profile of v12, /device:TPU:1, one launch (start us, length us, event | category | flops | bytes accessed | tf_op | source)
XLA Modules:
  0.0 88.2 jit_solution(14090113228081503382)
XLA Ops:
  0.0 5.5 %pick_first.1 = (bf16[768,1536]{1,0:T(8,128)(2,1)S(1)}, bf16[1536,256]{1,0:T(8,128)(2,1)S(1)}, s32[16,128]{1,0:T(8,128)S(1)}, f32[768,128]{1,0:T(8,128)S(1)}) custom-call(s32[2,768]{1,0:T(2,128)} %bitcast.2, f32[2,768]{1,0:T(2,128)} %bitcast.3, bf16[1536,3072]{1,0:T(8,128)(2,1)} %refs_3_.1), custom_call_target="tpu_custom_call" | custom-call | flops 1207959552 | bytes 7077888 | tf_op jit(solution)/shard_map/pick_first/pallas_call | solution.py:133
  5.6 0.1 collective-permute-start.1
  5.7 4.6 %pick_second.1.refs_0_ = bf16[768,1536]{1,0:T(8,128)(2,1)S(1)} custom-call(s32[16,128]{1,0:T(8,128)S(1)} %get-tuple-element.31.refs_0_, bf16[1536,256]{1,0:T(8,128)(2,1)S(1)} %get-tuple-element.32.refs_1_, f32[768,128]{1,0:T(8,128)S(1)} %get-tuple-element.29.refs_2_.coef_ref, bf16[1536,3072]{1,0:T(8,128)(2,1)} %refs_3_.1), custom_call_target="tpu_custom_call" | custom-call | flops 1207959552 | bytes 7077888 | tf_op jit(solution)/shard_map/pick_second/pallas_call | solution.py:133
  10.2 0.5 collective-permute-start
  10.8 0.0 collective-permute-done.1.refs_1_
  10.8 1.2 %merge_first.1 = (bf16[768,1536]{1,0:T(8,128)(2,1)S(1)}, bf16[3072,768]{1,0:T(8,128)(2,1)S(1)}) custom-call(f32[768,128]{1,0:T(8,128)S(1)} %get-tuple-element.29.refs_2_.coef_ref, bf16[768,1536]{1,0:T(8,128)(2,1)S(1)} %pick_second.1.refs_0_, bf16[768,1536]{1,0:T(8,128)(2,1)S(1)} %collective-permute-done.1.refs_1_), custom_call_target="tpu_custom_call" | custom-call | flops 4718592 | tf_op jit(solution)/shard_map/merge_first/pallas_call | solution.py:173
  12.0 2.9 %collective-permute-done.refs_1_ = bf16[768,1536]{1,0:T(8,128)(2,1)S(1)} collective-permute-done((bf16[768,1536]{1,0:T(8,128)(2,1)S(1)}, bf16[768,1536]{1,0:T(8,128)(2,1)S(1)}, u32[]{:S(2)}, u32[]{:S(2)}) %collective-permute-start) | collective-permute-done | bytes 2359328 | tf_op jit(solution)/shard_map/ppermute | solution.py:506
  14.9 1.1 %merge_second.1.turned_ref = bf16[3072,768]{1,0:T(8,128)(2,1)S(1)} custom-call(f32[768,128]{1,0:T(8,128)S(1)} %get-tuple-element.29.refs_2_.coef_ref, bf16[768,1536]{1,0:T(8,128)(2,1)S(1)} %get-tuple-element.30.refs_0_, bf16[768,1536]{1,0:T(8,128)(2,1)S(1)} %collective-permute-done.refs_1_, ...), custom_call_target="tpu_custom_call", output_to_operand_aliasing={{}: (3, {})} | custom-call | flops 4718592 | tf_op jit(solution)/shard_map/merge_second/pallas_call | solution.py:173
  16.1 0.0 copy-start.7
  16.1 1.7 %blocks0.1 = (bf16[416,384]{1,0:T(8,128)(2,1)S(1)}, bf16[416,384]{1,0:T(8,128)(2,1)S(1)}) custom-call(s32[16,10]{1,0:T(8,128)S(1)} %copy-done.8, bf16[3072,768]{1,0:T(8,128)(2,1)S(1)} %merge_second.1.turned_ref, bf16[768,1536]{1,0:T(8,128)(2,1)S(1)} %get-tuple-element.34.mine_ref), custom_call_target="tpu_custom_call" | custom-call | flops 226492416 | tf_op jit(solution)/shard_map/blocks0/pallas_call | solution.py:221
  17.8 2.7 %collective-permute-start.4 = (bf16[416,384]{1,0:T(8,128)(2,1)S(1)}, bf16[416,384]{1,0:T(8,128)(2,1)S(1)}, u32[]{:S(2)}, u32[]{:S(2)}) collective-permute-start(bf16[416,384]{1,0:T(8,128)(2,1)S(1)} %get-tuple-element.39), channel_id=1, source_target_pairs={{0,2},{1,3},{4,0},{5,1},{8,4},{9,5},{12,8},{13,9},{14,12},{15,13},... | collective-permute-start | bytes 958472 | tf_op jit(solution)/shard_map/ppermute | solution.py:419
  20.5 0.1 collective-permute-start.2
  20.6 1.7 %blocks0b.1 = (bf16[416,384]{1,0:T(8,128)(2,1)S(1)}, bf16[416,384]{1,0:T(8,128)(2,1)S(1)}) custom-call(s32[16,10]{1,0:T(8,128)S(1)} %copy-done.7, bf16[3072,768]{1,0:T(8,128)(2,1)S(1)} %merge_second.1.turned_ref, bf16[768,1536]{1,0:T(8,128)(2,1)S(1)} %get-tuple-element.34.mine_ref, bf16[416,384]{1,0:T(8,128)(2,1)S(1)} %get-tuple-element.35.refs_0_), custom_call_target="tpu_custom_call" | custom-call | flops 226492416 | tf_op jit(solution)/shard_map/blocks0b/pallas_call | solution.py:221
  22.3 1.4 %collective-permute-start.10 = (bf16[416,384]{1,0:T(8,128)(2,1)S(1)}, bf16[416,384]{1,0:T(8,128)(2,1)S(1)}, u32[]{:S(2)}, u32[]{:S(2)}) collective-permute-start(bf16[416,384]{1,0:T(8,128)(2,1)S(1)} %get-tuple-element.48), channel_id=1, source_target_pairs={{0,4},{1,5},{4,8},{5,9},{8,12},{9,13},{12,14},{13,15},{14,10},{15,... | collective-permute-start | bytes 958472 | tf_op jit(solution)/shard_map/ppermute | solution.py:419
  23.8 0.2 collective-permute-start.13
  24.0 1.7 %blocks1.1 = (f32[416,384]{1,0:T(8,128)S(1)}, f32[416,384]{1,0:T(8,128)S(1)}) custom-call(s32[16,10]{1,0:T(8,128)S(1)} %copy-done.6, bf16[3072,768]{1,0:T(8,128)(2,1)S(1)} %merge_second.1.turned_ref, bf16[768,1536]{1,0:T(8,128)(2,1)S(1)} %get-tuple-element.34.mine_ref, bf16[416,384]{1,0:T(8,128)(2,1)S(1)} %get-tuple-element.36.refs_0_), custom_call_target="tpu_custom_call" | custom-call | flops 226492416 | tf_op jit(solution)/shard_map/blocks1/pallas_call | solution.py:221
  25.7 0.0 copy-start.5
  25.7 2.6 %collective-permute-done.4.refs_2_ = bf16[416,384]{1,0:T(8,128)(2,1)S(1)} collective-permute-done((bf16[416,384]{1,0:T(8,128)(2,1)S(1)}, bf16[416,384]{1,0:T(8,128)(2,1)S(1)}, u32[]{:S(2)}, u32[]{:S(2)}) %collective-permute-start.4) | collective-permute-done | bytes 319520 | tf_op jit(solution)/shard_map/ppermute | solution.py:419
  28.3 0.1 add_convert_fusion.7
  28.4 1.2 %collective-permute-start.6 = (bf16[416,384]{1,0:T(8,128)(2,1)S(1)}, bf16[416,384]{1,0:T(8,128)(2,1)S(1)}, u32[]{:S(2)}, u32[]{:S(2)}) collective-permute-start(bf16[416,384]{1,0:T(8,128)(2,1)S(1)} %add_convert_fusion.7), channel_id=1, source_target_pairs={{0,2},{1,3},{4,0},{5,1},{8,4},{9,5},{12,8},{13,9},{14,12},{15,13},... | collective-permute-start | bytes 958472 | tf_op jit(solution)/shard_map/ppermute | solution.py:419
  29.6 0.0 collective-permute-done.2.refs_0_.refs_1_
  29.6 0.1 add_convert_fusion.9
  29.7 0.3 collective-permute-start.3
  30.0 1.7 %blocks1b.1 = (f32[416,384]{1,0:T(8,128)S(1)}, f32[416,384]{1,0:T(8,128)S(1)}) custom-call(s32[16,10]{1,0:T(8,128)S(1)} %copy-done.5, bf16[3072,768]{1,0:T(8,128)(2,1)S(1)} %merge_second.1.turned_ref, bf16[768,1536]{1,0:T(8,128)(2,1)S(1)} %get-tuple-element.34.mine_ref, bf16[416,384]{1,0:T(8,128)(2,1)S(1)} %collective-permute-done.2.refs_0_.refs_1_), custom_call_target="tpu_custom_call" | custom-call | flops 226492416 | tf_op jit(solution)/shard_map/blocks1b/pallas_call | solution.py:221
  31.7 0.0 copy-start.4
  31.7 3.4 %collective-permute-done.13 = bf16[416,384]{1,0:T(8,128)(2,1)S(1)} collective-permute-done((bf16[416,384]{1,0:T(8,128)(2,1)S(1)}, bf16[416,384]{1,0:T(8,128)(2,1)S(1)}, u32[]{:S(2)}, u32[]{:S(2)}) %collective-permute-start.13) | collective-permute-done | bytes 319520 | tf_op jit(solution)/shard_map/ppermute | solution.py:419
  35.1 0.1 add_convert_fusion.1
  35.2 1.2 %collective-permute-start.14 = (bf16[416,384]{1,0:T(8,128)(2,1)S(1)}, bf16[416,384]{1,0:T(8,128)(2,1)S(1)}, u32[]{:S(2)}, u32[]{:S(2)}) collective-permute-start(bf16[416,384]{1,0:T(8,128)(2,1)S(1)} %add_convert_fusion.1), channel_id=1, source_target_pairs={{0,2},{1,3},{4,0},{5,1},{8,4},{9,5},{12,8},{13,9},{14,12},{15,13},... | collective-permute-start | bytes 958472 | tf_op jit(solution)/shard_map/ppermute | solution.py:419
  36.4 0.1 add_convert_fusion.3
  36.5 0.3 collective-permute-start.11
  36.9 1.7 %blocks2.1 = (f32[416,384]{1,0:T(8,128)S(1)}, f32[416,384]{1,0:T(8,128)S(1)}) custom-call(s32[16,10]{1,0:T(8,128)S(1)} %copy-done.4, bf16[3072,768]{1,0:T(8,128)(2,1)S(1)} %merge_second.1.turned_ref, bf16[768,1536]{1,0:T(8,128)(2,1)S(1)} %get-tuple-element.34.mine_ref, f32[416,384]{1,0:T(8,128)S(1)} %get-tuple-element.38.refs_0_, ...), custom_call_target="tpu_custom_call" | custom-call | flops 226492416 | tf_op jit(solution)/shard_map/blocks2/pallas_call | solution.py:221
  38.6 0.0 copy-start.3
  38.6 3.4 %collective-permute-done.6.refs_2_ = bf16[416,384]{1,0:T(8,128)(2,1)S(1)} collective-permute-done((bf16[416,384]{1,0:T(8,128)(2,1)S(1)}, bf16[416,384]{1,0:T(8,128)(2,1)S(1)}, u32[]{:S(2)}, u32[]{:S(2)}) %collective-permute-start.6) | collective-permute-done | bytes 319520 | tf_op jit(solution)/shard_map/ppermute | solution.py:419
  42.0 0.1 add_convert_fusion.5
  42.1 1.2 %collective-permute-start.8 = (bf16[416,384]{1,0:T(8,128)(2,1)S(1)}, bf16[416,384]{1,0:T(8,128)(2,1)S(1)}, u32[]{:S(2)}, u32[]{:S(2)}) collective-permute-start(bf16[416,384]{1,0:T(8,128)(2,1)S(1)} %add_convert_fusion.5), channel_id=1, source_target_pairs={{0,2},{1,3},{4,0},{5,1},{8,4},{9,5},{12,8},{13,9},{14,12},{15,13},... | collective-permute-start | bytes 958472 | tf_op jit(solution)/shard_map/ppermute | solution.py:419
  43.3 0.1 add_convert_fusion.8
  43.4 0.3 collective-permute-start.5
  43.7 1.7 %blocks2b.1 = (f32[416,384]{1,0:T(8,128)S(1)}, f32[416,384]{1,0:T(8,128)S(1)}) custom-call(s32[16,10]{1,0:T(8,128)S(1)} %copy-done.3, bf16[3072,768]{1,0:T(8,128)(2,1)S(1)} %merge_second.1.turned_ref, bf16[768,1536]{1,0:T(8,128)(2,1)S(1)} %get-tuple-element.34.mine_ref, bf16[416,384]{1,0:T(8,128)(2,1)S(1)} %collective-permute-done.3.refs_0_.refs_1_), custom_call_target="tpu_custom_call" | custom-call | flops 226492416 | tf_op jit(solution)/shard_map/blocks2b/pallas_call | solution.py:221
  45.4 0.0 copy-start.2
  45.4 3.4 %collective-permute-done.14 = bf16[416,384]{1,0:T(8,128)(2,1)S(1)} collective-permute-done((bf16[416,384]{1,0:T(8,128)(2,1)S(1)}, bf16[416,384]{1,0:T(8,128)(2,1)S(1)}, u32[]{:S(2)}, u32[]{:S(2)}) %collective-permute-start.14) | collective-permute-done | bytes 319520 | tf_op jit(solution)/shard_map/ppermute | solution.py:419
  48.8 0.1 add_convert_fusion
  48.9 1.2 %collective-permute-start.15 = (bf16[416,384]{1,0:T(8,128)(2,1)S(1)}, bf16[416,384]{1,0:T(8,128)(2,1)S(1)}, u32[]{:S(2)}, u32[]{:S(2)}) collective-permute-start(bf16[416,384]{1,0:T(8,128)(2,1)S(1)} %add_convert_fusion), channel_id=1, source_target_pairs={{0,2},{1,3},{4,0},{5,1},{8,4},{9,5},{12,8},{13,9},{14,12},{15,13},... | collective-permute-start | bytes 958472 | tf_op jit(solution)/shard_map/ppermute | solution.py:419
  50.1 0.1 add_convert_fusion.2
  50.2 0.3 collective-permute-start.12
  50.6 1.7 %blocks3.1 = (f32[416,384]{1,0:T(8,128)S(1)}, f32[416,384]{1,0:T(8,128)S(1)}) custom-call(s32[16,10]{1,0:T(8,128)S(1)} %copy-done.2, bf16[3072,768]{1,0:T(8,128)(2,1)S(1)} %merge_second.1.turned_ref, bf16[768,1536]{1,0:T(8,128)(2,1)S(1)} %get-tuple-element.34.mine_ref, f32[416,384]{1,0:T(8,128)S(1)} %get-tuple-element.43.refs_0_, ...), custom_call_target="tpu_custom_call" | custom-call | flops 226492416 | tf_op jit(solution)/shard_map/blocks3/pallas_call | solution.py:221
  52.3 0.0 copy-start.1
  52.3 3.4 %collective-permute-done.8 = bf16[416,384]{1,0:T(8,128)(2,1)S(1)} collective-permute-done((bf16[416,384]{1,0:T(8,128)(2,1)S(1)}, bf16[416,384]{1,0:T(8,128)(2,1)S(1)}, u32[]{:S(2)}, u32[]{:S(2)}) %collective-permute-start.8) | collective-permute-done | bytes 319520 | tf_op jit(solution)/shard_map/ppermute | solution.py:419
  55.7 0.1 add_convert_fusion.4
  55.7 1.2 %collective-permute-start.9 = (bf16[416,384]{1,0:T(8,128)(2,1)S(1)}, bf16[416,384]{1,0:T(8,128)(2,1)S(1)}, u32[]{:S(2)}, u32[]{:S(2)}) collective-permute-start(bf16[416,384]{1,0:T(8,128)(2,1)S(1)} %add_convert_fusion.4), channel_id=1, source_target_pairs={{0,2},{1,3},{4,0},{5,1},{8,4},{9,5},{12,8},{13,9},{14,12},{15,13},... | collective-permute-start | bytes 958472 | tf_op jit(solution)/shard_map/ppermute | solution.py:419
  57.0 0.1 add_convert_fusion.6
  57.0 0.0 copy-start
  57.1 0.3 collective-permute-start.7
  57.4 1.7 %blocks3b.1 = (f32[416,384]{1,0:T(8,128)S(1)}, f32[416,384]{1,0:T(8,128)S(1)}) custom-call(s32[16,10]{1,0:T(8,128)S(1)} %copy-done.1, bf16[3072,768]{1,0:T(8,128)(2,1)S(1)} %merge_second.1.turned_ref, bf16[768,1536]{1,0:T(8,128)(2,1)S(1)} %get-tuple-element.34.mine_ref, bf16[416,384]{1,0:T(8,128)(2,1)S(1)} %collective-permute-done.5.refs_0_), custom_call_target="tpu_custom_call" | custom-call | flops 226492416 | tf_op jit(solution)/shard_map/blocks3b/pallas_call | solution.py:221
  59.2 4.2 %collective-permute-done.12.right1 = bf16[416,384]{1,0:T(8,128)(2,1)S(1)} collective-permute-done((bf16[416,384]{1,0:T(8,128)(2,1)S(1)}, bf16[416,384]{1,0:T(8,128)(2,1)S(1)}, u32[]{:S(2)}, u32[]{:S(2)}) %collective-permute-start.12) | collective-permute-done | bytes 319520 | tf_op jit(solution)/shard_map/ppermute | solution.py:419
  63.4 6.0 %collective-permute-done.9.left1 = bf16[416,384]{1,0:T(8,128)(2,1)S(1)} collective-permute-done((bf16[416,384]{1,0:T(8,128)(2,1)S(1)}, bf16[416,384]{1,0:T(8,128)(2,1)S(1)}, u32[]{:S(2)}, u32[]{:S(2)}) %collective-permute-start.9) | collective-permute-done | bytes 319520 | tf_op jit(solution)/shard_map/ppermute | solution.py:419
  69.4 0.1 outgoing_one.1.after
  69.5 4.2 %collective-permute-start.17 = (bf16[384,384]{1,0:T(8,128)(2,1)S(1)}, bf16[384,384]{1,0:T(8,128)(2,1)S(1)}, u32[]{:S(2)}, u32[]{:S(2)}) collective-permute-start(bf16[384,384]{1,0:T(8,128)(2,1)S(1)} %outgoing_one.1.after), channel_id=1, source_target_pairs={{0,2},{1,10},{2,4},{3,12},{4,6},{5,14},{6,0},{7,8},{8,5},{9,11},{1... | collective-permute-start | bytes 884744 | tf_op jit(solution)/shard_map/ppermute | solution.py:471
  73.7 0.9 outgoing_other.1
  74.5 0.1 collective-permute-start.16
  74.6 1.8 %own.1.result_ref = f32[384,1536]{1,0:T(8,128)} custom-call(s32[16,5]{1,0:T(8,128)S(1)} %copy-done, f32[416,384]{1,0:T(8,128)S(1)} %get-tuple-element.41.own0, f32[416,384]{1,0:T(8,128)S(1)} %get-tuple-element.42.own1, bf16[416,384]{1,0:T(8,128)(2,1)S(1)} %collective-permute-done.7.right0, bf16[416,384]{1,0:T(8,128)(2,1)S(1)} %collective-permute-done.9.left1, ...), custom_call_target="tpu_custom_call" | custom-call | tf_op jit(solution)/shard_map/own/pallas_call | solution.py:473
  76.4 3.6 %collective-permute-done.17.one = bf16[384,384]{1,0:T(8,128)(2,1)S(1)} collective-permute-done((bf16[384,384]{1,0:T(8,128)(2,1)S(1)}, bf16[384,384]{1,0:T(8,128)(2,1)S(1)}, u32[]{:S(2)}, u32[]{:S(2)}) %collective-permute-start.17) | collective-permute-done | bytes 294944 | tf_op jit(solution)/shard_map/ppermute | solution.py:471
  80.1 1.7 %one.1.result_ref = f32[384,1536]{1,0:T(8,128)} custom-call(s32[16,5]{1,0:T(8,128)S(1)} %copy-done, bf16[384,384]{1,0:T(8,128)(2,1)S(1)} %collective-permute-done.17.one, f32[384,1536]{1,0:T(8,128)} %own.1.result_ref), custom_call_target="tpu_custom_call", output_to_operand_aliasing={{}: (2, {})} | custom-call | tf_op jit(solution)/shard_map/one/pallas_call | solution.py:483
  81.7 4.8 %collective-permute-done.16.other = bf16[320,384]{1,0:T(8,128)(2,1)S(1)} collective-permute-done((bf16[320,384]{1,0:T(8,128)(2,1)S(1)}, bf16[320,384]{1,0:T(8,128)(2,1)S(1)}, u32[]{:S(2)}, u32[]{:S(2)}) %collective-permute-start.16) | collective-permute-done | bytes 245792 | tf_op jit(solution)/shard_map/ppermute | solution.py:472
  86.5 1.6 %other.1 = f32[384,1536]{1,0:T(8,128)} custom-call(s32[16,5]{1,0:T(8,128)S(1)} %copy-done, f32[192,384]{1,0:T(8,128)S(1)} %get-tuple-element.51.share, bf16[320,384]{1,0:T(8,128)(2,1)S(1)} %collective-permute-done.16.other, f32[384,1536]{1,0:T(8,128)} %one.1.result_ref), custom_call_target="tpu_custom_call", output_to_operand_aliasing={{}: (3, {})} | custom-call | tf_op jit(solution)/shard_map/other/pallas_call | solution.py:483
  (17 shorter events, 0.0 us)
Async XLA Ops:
  5.6 5.2 %collective-permute-start.1 = (bf16[768,1536]{1,0:T(8,128)(2,1)S(1)}, bf16[768,1536]{1,0:T(8,128)(2,1)S(1)}, u32[]{:S(2)}, u32[]{:S(2)}) collective-permute-start(bf16[768,1536]{1,0:T(8,128)(2,1)S(1)} %get-tuple-element.30.refs_0_), channel_id=1, source_target_pairs={{0,1},{1,0},{2,3},{3,2},{4,5},{5,4},{6,7},{7,6},{8,9},{9,8},{10,11... | collective-permute-start | bytes 7077896 | tf_op jit(solution)/shard_map/ppermute | solution.py:504
  10.2 4.7 %collective-permute-start = (bf16[768,1536]{1,0:T(8,128)(2,1)S(1)}, bf16[768,1536]{1,0:T(8,128)(2,1)S(1)}, u32[]{:S(2)}, u32[]{:S(2)}) collective-permute-start(bf16[768,1536]{1,0:T(8,128)(2,1)S(1)} %pick_second.1.refs_0_), channel_id=1, source_target_pairs={{0,1},{1,0},{2,3},{3,2},{4,5},{5,4},{6,7},{7,6},{8,9},{9,8},{10,11... | collective-permute-start | bytes 7077896 | tf_op jit(solution)/shard_map/ppermute | solution.py:506
  14.9 1.1 %copy-start.8 = (s32[16,10]{1,0:T(8,128)S(1)}, s32[16,10]{1,0:T(8,128)}, u32[]{:S(2)}) copy-start(s32[16,10]{1,0:T(8,128)} %constant.18.clone.table) | copy-start | bytes 1924
  16.1 4.5 %copy-start.7 = (s32[16,10]{1,0:T(8,128)S(1)}, s32[16,10]{1,0:T(8,128)}, u32[]{:S(2)}) copy-start(s32[16,10]{1,0:T(8,128)} %constant.19.clone.table) | copy-start | bytes 1924
  17.8 10.5 %collective-permute-start.4 = (bf16[416,384]{1,0:T(8,128)(2,1)S(1)}, bf16[416,384]{1,0:T(8,128)(2,1)S(1)}, u32[]{:S(2)}, u32[]{:S(2)}) collective-permute-start(bf16[416,384]{1,0:T(8,128)(2,1)S(1)} %get-tuple-element.39), channel_id=1, source_target_pairs={{0,2},{1,3},{4,0},{5,1},{8,4},{9,5},{12,8},{13,9},{14,12},{15,13},... | collective-permute-start | bytes 958472 | tf_op jit(solution)/shard_map/ppermute | solution.py:419
  20.5 3.5 %copy-start.6 = (s32[16,10]{1,0:T(8,128)S(1)}, s32[16,10]{1,0:T(8,128)}, u32[]{:S(2)}) copy-start(s32[16,10]{1,0:T(8,128)} %constant.20.clone.table) | copy-start | bytes 1924
  20.5 9.1 %collective-permute-start.2 = (bf16[416,384]{1,0:T(8,128)(2,1)S(1)}, bf16[416,384]{1,0:T(8,128)(2,1)S(1)}, u32[]{:S(2)}, u32[]{:S(2)}) collective-permute-start(bf16[416,384]{1,0:T(8,128)(2,1)S(1)} %get-tuple-element.35.refs_0_), channel_id=1, source_target_pairs={{0,4},{1,5},{4,8},{5,9},{8,12},{9,13},{12,14},{13,15},{14,10},{15,... | collective-permute-start | bytes 958472 | tf_op jit(solution)/shard_map/ppermute | solution.py:419
  22.3 14.1 %collective-permute-start.10 = (bf16[416,384]{1,0:T(8,128)(2,1)S(1)}, bf16[416,384]{1,0:T(8,128)(2,1)S(1)}, u32[]{:S(2)}, u32[]{:S(2)}) collective-permute-start(bf16[416,384]{1,0:T(8,128)(2,1)S(1)} %get-tuple-element.48), channel_id=1, source_target_pairs={{0,4},{1,5},{4,8},{5,9},{8,12},{9,13},{12,14},{13,15},{14,10},{15,... | collective-permute-start | bytes 958472 | tf_op jit(solution)/shard_map/ppermute | solution.py:419
  23.8 11.3 %collective-permute-start.13 = (bf16[416,384]{1,0:T(8,128)(2,1)S(1)}, bf16[416,384]{1,0:T(8,128)(2,1)S(1)}, u32[]{:S(2)}, u32[]{:S(2)}) collective-permute-start(bf16[416,384]{1,0:T(8,128)(2,1)S(1)} %get-tuple-element.36.refs_0_), channel_id=1, source_target_pairs={{0,2},{1,3},{4,0},{5,1},{8,4},{9,5},{12,8},{13,9},{14,12},{15,13},... | collective-permute-start | bytes 958472 | tf_op jit(solution)/shard_map/ppermute | solution.py:419
  25.7 4.3 %copy-start.5 = (s32[16,10]{1,0:T(8,128)S(1)}, s32[16,10]{1,0:T(8,128)}, u32[]{:S(2)}) copy-start(s32[16,10]{1,0:T(8,128)} %constant.21.clone.table) | copy-start | bytes 1924
  28.4 13.6 %collective-permute-start.6 = (bf16[416,384]{1,0:T(8,128)(2,1)S(1)}, bf16[416,384]{1,0:T(8,128)(2,1)S(1)}, u32[]{:S(2)}, u32[]{:S(2)}) collective-permute-start(bf16[416,384]{1,0:T(8,128)(2,1)S(1)} %add_convert_fusion.7), channel_id=1, source_target_pairs={{0,2},{1,3},{4,0},{5,1},{8,4},{9,5},{12,8},{13,9},{14,12},{15,13},... | collective-permute-start | bytes 958472 | tf_op jit(solution)/shard_map/ppermute | solution.py:419
  29.7 13.6 %collective-permute-start.3 = (bf16[416,384]{1,0:T(8,128)(2,1)S(1)}, bf16[416,384]{1,0:T(8,128)(2,1)S(1)}, u32[]{:S(2)}, u32[]{:S(2)}) collective-permute-start(bf16[416,384]{1,0:T(8,128)(2,1)S(1)} %add_convert_fusion.9), channel_id=1, source_target_pairs={{0,4},{1,5},{4,8},{5,9},{8,12},{9,13},{12,14},{13,15},{14,10},{15,... | collective-permute-start | bytes 958472 | tf_op jit(solution)/shard_map/ppermute | solution.py:419
  31.7 5.1 %copy-start.4 = (s32[16,10]{1,0:T(8,128)S(1)}, s32[16,10]{1,0:T(8,128)}, u32[]{:S(2)}) copy-start(s32[16,10]{1,0:T(8,128)} %constant.22.clone.table) | copy-start | bytes 1924
  35.2 13.6 %collective-permute-start.14 = (bf16[416,384]{1,0:T(8,128)(2,1)S(1)}, bf16[416,384]{1,0:T(8,128)(2,1)S(1)}, u32[]{:S(2)}, u32[]{:S(2)}) collective-permute-start(bf16[416,384]{1,0:T(8,128)(2,1)S(1)} %add_convert_fusion.1), channel_id=1, source_target_pairs={{0,2},{1,3},{4,0},{5,1},{8,4},{9,5},{12,8},{13,9},{14,12},{15,13},... | collective-permute-start | bytes 958472 | tf_op jit(solution)/shard_map/ppermute | solution.py:419
  36.5 13.6 %collective-permute-start.11 = (bf16[416,384]{1,0:T(8,128)(2,1)S(1)}, bf16[416,384]{1,0:T(8,128)(2,1)S(1)}, u32[]{:S(2)}, u32[]{:S(2)}) collective-permute-start(bf16[416,384]{1,0:T(8,128)(2,1)S(1)} %add_convert_fusion.3), channel_id=1, source_target_pairs={{0,4},{1,5},{4,8},{5,9},{8,12},{9,13},{12,14},{13,15},{14,10},{15,... | collective-permute-start | bytes 958472 | tf_op jit(solution)/shard_map/ppermute | solution.py:419
  38.6 5.1 %copy-start.3 = (s32[16,10]{1,0:T(8,128)S(1)}, s32[16,10]{1,0:T(8,128)}, u32[]{:S(2)}) copy-start(s32[16,10]{1,0:T(8,128)} %constant.23.clone.table) | copy-start | bytes 1924
  42.1 13.6 %collective-permute-start.8 = (bf16[416,384]{1,0:T(8,128)(2,1)S(1)}, bf16[416,384]{1,0:T(8,128)(2,1)S(1)}, u32[]{:S(2)}, u32[]{:S(2)}) collective-permute-start(bf16[416,384]{1,0:T(8,128)(2,1)S(1)} %add_convert_fusion.5), channel_id=1, source_target_pairs={{0,2},{1,3},{4,0},{5,1},{8,4},{9,5},{12,8},{13,9},{14,12},{15,13},... | collective-permute-start | bytes 958472 | tf_op jit(solution)/shard_map/ppermute | solution.py:419
  43.4 13.6 %collective-permute-start.5 = (bf16[416,384]{1,0:T(8,128)(2,1)S(1)}, bf16[416,384]{1,0:T(8,128)(2,1)S(1)}, u32[]{:S(2)}, u32[]{:S(2)}) collective-permute-start(bf16[416,384]{1,0:T(8,128)(2,1)S(1)} %add_convert_fusion.8), channel_id=1, source_target_pairs={{0,4},{1,5},{4,8},{5,9},{8,12},{9,13},{12,14},{13,15},{14,10},{15,... | collective-permute-start | bytes 958472 | tf_op jit(solution)/shard_map/ppermute | solution.py:419
  45.4 5.1 %copy-start.2 = (s32[16,10]{1,0:T(8,128)S(1)}, s32[16,10]{1,0:T(8,128)}, u32[]{:S(2)}) copy-start(s32[16,10]{1,0:T(8,128)} %constant.24.clone.table) | copy-start | bytes 1924
  48.9 24.8 %collective-permute-start.15 = (bf16[416,384]{1,0:T(8,128)(2,1)S(1)}, bf16[416,384]{1,0:T(8,128)(2,1)S(1)}, u32[]{:S(2)}, u32[]{:S(2)}) collective-permute-start(bf16[416,384]{1,0:T(8,128)(2,1)S(1)} %add_convert_fusion), channel_id=1, source_target_pairs={{0,2},{1,3},{4,0},{5,1},{8,4},{9,5},{12,8},{13,9},{14,12},{15,13},... | collective-permute-start | bytes 958472 | tf_op jit(solution)/shard_map/ppermute | solution.py:419
  50.2 13.2 %collective-permute-start.12 = (bf16[416,384]{1,0:T(8,128)(2,1)S(1)}, bf16[416,384]{1,0:T(8,128)(2,1)S(1)}, u32[]{:S(2)}, u32[]{:S(2)}) collective-permute-start(bf16[416,384]{1,0:T(8,128)(2,1)S(1)} %add_convert_fusion.2), channel_id=1, source_target_pairs={{0,4},{1,5},{4,8},{5,9},{8,12},{9,13},{12,14},{13,15},{14,10},{15,... | collective-permute-start | bytes 958472 | tf_op jit(solution)/shard_map/ppermute | solution.py:419
  52.3 5.1 %copy-start.1 = (s32[16,10]{1,0:T(8,128)S(1)}, s32[16,10]{1,0:T(8,128)}, u32[]{:S(2)}) copy-start(s32[16,10]{1,0:T(8,128)} %constant.25.clone.table) | copy-start | bytes 1924
  55.7 13.6 %collective-permute-start.9 = (bf16[416,384]{1,0:T(8,128)(2,1)S(1)}, bf16[416,384]{1,0:T(8,128)(2,1)S(1)}, u32[]{:S(2)}, u32[]{:S(2)}) collective-permute-start(bf16[416,384]{1,0:T(8,128)(2,1)S(1)} %add_convert_fusion.4), channel_id=1, source_target_pairs={{0,2},{1,3},{4,0},{5,1},{8,4},{9,5},{12,8},{13,9},{14,12},{15,13},... | collective-permute-start | bytes 958472 | tf_op jit(solution)/shard_map/ppermute | solution.py:419
  57.0 16.6 %copy-start = (s32[16,5]{1,0:T(8,128)S(1)}, s32[16,5]{1,0:T(8,128)}, u32[]{:S(2)}) copy-start(s32[16,5]{1,0:T(8,128)} %constant.26.clone.place) | copy-start | bytes 964
  57.1 16.6 %collective-permute-start.7 = (bf16[416,384]{1,0:T(8,128)(2,1)S(1)}, bf16[416,384]{1,0:T(8,128)(2,1)S(1)}, u32[]{:S(2)}, u32[]{:S(2)}) collective-permute-start(bf16[416,384]{1,0:T(8,128)(2,1)S(1)} %add_convert_fusion.6), channel_id=1, source_target_pairs={{0,4},{1,5},{4,8},{5,9},{8,12},{9,13},{12,14},{13,15},{14,10},{15,... | collective-permute-start | bytes 958472 | tf_op jit(solution)/shard_map/ppermute | solution.py:419
  69.5 10.6 %collective-permute-start.17 = (bf16[384,384]{1,0:T(8,128)(2,1)S(1)}, bf16[384,384]{1,0:T(8,128)(2,1)S(1)}, u32[]{:S(2)}, u32[]{:S(2)}) collective-permute-start(bf16[384,384]{1,0:T(8,128)(2,1)S(1)} %outgoing_one.1.after), channel_id=1, source_target_pairs={{0,2},{1,10},{2,4},{3,12},{4,6},{5,14},{6,0},{7,8},{8,5},{9,11},{1... | collective-permute-start | bytes 884744 | tf_op jit(solution)/shard_map/ppermute | solution.py:471
  74.5 11.9 %collective-permute-start.16 = (bf16[320,384]{1,0:T(8,128)(2,1)S(1)}, bf16[320,384]{1,0:T(8,128)(2,1)S(1)}, u32[]{:S(2)}, u32[]{:S(2)}) collective-permute-start(bf16[320,384]{1,0:T(8,128)(2,1)S(1)} %get-tuple-element.52), channel_id=1, source_target_pairs={{0,4},{1,8},{2,6},{3,10},{4,0},{5,12},{6,2},{7,14},{8,3},{9,13},{1... | collective-permute-start | bytes 737288 | tf_op jit(solution)/shard_map/ppermute | solution.py:472

commit v13 on v12

--- a/solution.py
+++ b/solution.py
@@ -16,19 +16,21 @@
 F32, BF16, I32 = jnp.float32, jnp.bfloat16, jnp.int32
 
 
-def plan_tokens(ids_ref, gates_ref, pick_ref, starts_ref, coef_ref, starts_copy):
+def plan_tokens(ids_ref, gates_ref, pick_ref, starts_ref, coef_ref, earlier_ref, inputs, starts_copy):
     tokens = ids_ref.shape[1]
     local = EXPERTS // 2
+    earlier_ref[...] = jnp.where(
+        lax.broadcasted_iota(I32, (tokens, tokens), 1) < lax.broadcasted_iota(I32, (tokens, tokens), 0), 1.0, 0.0
+    ).astype(BF16)
+    for copy in inputs:
+        copy.wait()
     lanes = lax.broadcasted_iota(I32, (tokens, 128), 1)
     rows = jnp.concatenate([ids_ref[...].astype(F32), gates_ref[...], jnp.zeros((4, tokens), F32)], axis=0).T
     ids = [rows[:, k : k + 1].astype(I32) for k in range(2)]
     gates = [rows[:, k : k + 1] for k in (2, 3)]
     hits = [ids[k] == lanes for k in range(2)]
     named = jnp.where(hits[0] | hits[1], 1.0, 0.0).astype(BF16)
-    earlier = jnp.where(
-        lax.broadcasted_iota(I32, (tokens, tokens), 1) < lax.broadcasted_iota(I32, (tokens, tokens), 0), 1.0, 0.0
-    ).astype(BF16)
-    before = jnp.dot(earlier, named, preferred_element_type=F32)
+    before = jnp.dot(earlier_ref[...], named, preferred_element_type=F32)
     firsts = []
     for b in range(tokens // BATCH):
         start = before[b * BATCH : b * BATCH + 1, :].astype(I32)
@@ -63,9 +65,9 @@
 def pick_kernel(first, *refs):
     if first:
         ids_hbm, gates_hbm, rows_ref, out_ref, pick_ref, starts_ref, coef_ref = refs[:7]
-        held, in_sems, starts, ids_ref, gates_ref, small_sems = refs[7:]
+        held, in_sems, starts, small_sems, ids_ref, gates_ref, earlier_ref = refs[7:]
     else:
-        starts, pick_ref, coef_ref, rows_ref, out_ref, held, in_sems = refs
+        starts_ref, pick_ref, coef_ref, rows_ref, out_ref, held, in_sems, starts, small_sems = refs
     tokens, width = out_ref.shape
     tiles, _, tile = held.shape
     local = EXPERTS // 2
@@ -84,12 +86,12 @@
         at = pl.ds(pl.multiple_of(base + j * tile, 128), tile)
         loads.append(pltpu.make_async_copy(rows_ref.at[:, at], held.at[j], in_sems.at[j]))
         loads[-1].start()
+    copy = pltpu.make_async_copy(starts_ref, starts, small_sems.at[2])
     if first:
-        for copy in small:
-            copy.wait()
-        copy = pltpu.make_async_copy(starts_ref, starts, small_sems.at[2])
-        plan_tokens(ids_ref, gates_ref, pick_ref, starts_ref, coef_ref, copy)
-        copy.wait()
+        plan_tokens(ids_ref, gates_ref, pick_ref, starts_ref, coef_ref, earlier_ref, small, copy)
+    else:
+        copy.start()
+    copy.wait()
     for j in range(tiles):
         loads[j].wait()
         for b in range(tokens // BATCH):
@@ -113,7 +115,12 @@
     any_, vmem = pl.BlockSpec(memory_space=pl.ANY), pl.BlockSpec(memory_space=pltpu.VMEM)
     in_hbm = lambda x: pltpu.with_memory_space_constraint(x, pltpu.HBM)
     out_shape = [jax.ShapeDtypeStruct((tokens, width), BF16)]
-    scratch = [pltpu.VMEM((tiles, rows.shape[0], tile), BF16), pltpu.SemaphoreType.DMA((tiles,))]
+    scratch = [
+        pltpu.VMEM((tiles, rows.shape[0], tile), BF16),
+        pltpu.SemaphoreType.DMA((tiles,)),
+        pltpu.SMEM((tokens // BATCH, 128), I32),
+        pltpu.SemaphoreType.DMA((3,)),
+    ]
     if first:
         out_shape += [
             jax.ShapeDtypeStruct((2 * tokens, depth), BF16),
@@ -123,13 +130,12 @@
         args = [in_hbm(x) for x in args]
         in_specs = [any_] * 3
         scratch += [
-            pltpu.SMEM((tokens // BATCH, 128), I32),
             pltpu.VMEM((2, tokens), I32),
             pltpu.VMEM((2, tokens), F32),
-            pltpu.SemaphoreType.DMA((3,)),
+            pltpu.VMEM((tokens, tokens), BF16),
         ]
     else:
-        in_specs = [pl.BlockSpec(memory_space=pltpu.SMEM), vmem, vmem, any_]
+        in_specs = [vmem, vmem, vmem, any_]
     return pl.pallas_call(
         functools.partial(pick_kernel, first),
         out_shape=out_shape,

time: 88.4 us -> 87.8 us (level)
  no operation moved by 1% of the time
where the time goes in v13:
time: 87.8 us; the launch traced here: 87.6 us
  waiting for transfers between devices  37.7 us (43%)
  Pallas kernels  31.6 us (36%)
  starting transfers between devices  17.1 us (19%)
    ppermute x14, waiting for transfers between devices, hop(): lax.ppermute(value, both, ring_perm(1 if key[1] <= (4 if key[0] == 0 else...  26.3 us
    pallas_call x8, Pallas kernels, moment_blocks(): pl.pallas_call(functools.partial(blocks_kernel, pieces, width), out_shape...  13.8 us
    ppermute x14, starting transfers between devices, hop(): lax.ppermute(value, both, ring_perm(1 if key[1] <= (4 if key[0] == 0 else...  12.3 us
    pallas_call x2, Pallas kernels, pick_half(): pl.pallas_call(functools.partial(pick_kernel, first), out_shape=out_shape...  9.46 us
    ppermute x1, waiting for transfers between devices, symmetric_moment(): other = lax.ppermute(other, both, perm_other)  4.77 us
    ppermute x1, starting transfers between devices, symmetric_moment(): one = lax.ppermute(one, both, perm_one)  4.15 us
    ppermute x1, waiting for transfers between devices, symmetric_moment(): one = lax.ppermute(one, both, perm_one)  3.63 us
    pallas_call x2, Pallas kernels, symmetric_moment(): pl.pallas_call(kernel, out_shape=result, in_specs=[smem] + [vmem] * len(a...  3.22 us
  transfers between devices with their start and end apart: 18, of which 10 were waited for; matrix products, arithmetic and copies ran while one was open for 1% of the time, Pallas kernels for 25%

profile of v13, /device:TPU:1, one launch (start us, length us, event | category | flops | bytes accessed | tf_op | source)
XLA Modules:
  0.0 87.6 jit_solution(17054099878356455293)
XLA Ops:
  0.0 5.6 %pick_first.1 = (bf16[768,1536]{1,0:T(8,128)(2,1)S(1)}, bf16[1536,256]{1,0:T(8,128)(2,1)S(1)}, s32[16,128]{1,0:T(8,128)S(1)}, f32[768,128]{1,0:T(8,128)S(1)}) custom-call(s32[2,768]{1,0:T(2,128)} %bitcast.2, f32[2,768]{1,0:T(2,128)} %bitcast.3, bf16[1536,3072]{1,0:T(8,128)(2,1)} %refs_3_.1), custom_call_target="tpu_custom_call" | custom-call | flops 1207959552 | bytes 7077888 | tf_op jit(solution)/shard_map/pick_first/pallas_call | solution.py:139
  5.6 0.1 collective-permute-start.1
  5.7 3.9 %pick_second.1.refs_0_ = bf16[768,1536]{1,0:T(8,128)(2,1)S(1)} custom-call(s32[16,128]{1,0:T(8,128)S(1)} %get-tuple-element.31.refs_0_, bf16[1536,256]{1,0:T(8,128)(2,1)S(1)} %get-tuple-element.32.refs_1_, f32[768,128]{1,0:T(8,128)S(1)} %get-tuple-element.29.refs_2_.coef_ref, bf16[1536,3072]{1,0:T(8,128)(2,1)} %refs_3_.1), custom_call_target="tpu_custom_call" | custom-call | flops 1207959552 | bytes 7077888 | tf_op jit(solution)/shard_map/pick_second/pallas_call | solution.py:139
  9.6 0.5 collective-permute-start
  10.1 0.0 collective-permute-done.1.refs_1_
  10.2 1.2 %merge_first.1 = (bf16[768,1536]{1,0:T(8,128)(2,1)S(1)}, bf16[3072,768]{1,0:T(8,128)(2,1)S(1)}) custom-call(f32[768,128]{1,0:T(8,128)S(1)} %get-tuple-element.29.refs_2_.coef_ref, bf16[768,1536]{1,0:T(8,128)(2,1)S(1)} %pick_second.1.refs_0_, bf16[768,1536]{1,0:T(8,128)(2,1)S(1)} %collective-permute-done.1.refs_1_), custom_call_target="tpu_custom_call" | custom-call | flops 4718592 | tf_op jit(solution)/shard_map/merge_first/pallas_call | solution.py:179
  11.4 2.9 %collective-permute-done.refs_1_ = bf16[768,1536]{1,0:T(8,128)(2,1)S(1)} collective-permute-done((bf16[768,1536]{1,0:T(8,128)(2,1)S(1)}, bf16[768,1536]{1,0:T(8,128)(2,1)S(1)}, u32[]{:S(2)}, u32[]{:S(2)}) %collective-permute-start) | collective-permute-done | bytes 2359328 | tf_op jit(solution)/shard_map/ppermute | solution.py:512
  14.3 1.1 %merge_second.1.turned_ref = bf16[3072,768]{1,0:T(8,128)(2,1)S(1)} custom-call(f32[768,128]{1,0:T(8,128)S(1)} %get-tuple-element.29.refs_2_.coef_ref, bf16[768,1536]{1,0:T(8,128)(2,1)S(1)} %get-tuple-element.30.refs_0_, bf16[768,1536]{1,0:T(8,128)(2,1)S(1)} %collective-permute-done.refs_1_, ...), custom_call_target="tpu_custom_call", output_to_operand_aliasing={{}: (3, {})} | custom-call | flops 4718592 | tf_op jit(solution)/shard_map/merge_second/pallas_call | solution.py:179
  15.4 0.0 copy-start.7
  15.5 1.7 %blocks0.1 = (bf16[416,384]{1,0:T(8,128)(2,1)S(1)}, bf16[416,384]{1,0:T(8,128)(2,1)S(1)}) custom-call(s32[16,10]{1,0:T(8,128)S(1)} %copy-done.8, bf16[3072,768]{1,0:T(8,128)(2,1)S(1)} %merge_second.1.turned_ref, bf16[768,1536]{1,0:T(8,128)(2,1)S(1)} %get-tuple-element.34.mine_ref), custom_call_target="tpu_custom_call" | custom-call | flops 226492416 | tf_op jit(solution)/shard_map/blocks0/pallas_call | solution.py:227
  17.2 2.7 %collective-permute-start.4 = (bf16[416,384]{1,0:T(8,128)(2,1)S(1)}, bf16[416,384]{1,0:T(8,128)(2,1)S(1)}, u32[]{:S(2)}, u32[]{:S(2)}) collective-permute-start(bf16[416,384]{1,0:T(8,128)(2,1)S(1)} %get-tuple-element.39), channel_id=1, source_target_pairs={{0,2},{1,3},{4,0},{5,1},{8,4},{9,5},{12,8},{13,9},{14,12},{15,13},... | collective-permute-start | bytes 958472 | tf_op jit(solution)/shard_map/ppermute | solution.py:425
  19.8 0.1 collective-permute-start.2
  20.0 1.7 %blocks0b.1 = (bf16[416,384]{1,0:T(8,128)(2,1)S(1)}, bf16[416,384]{1,0:T(8,128)(2,1)S(1)}) custom-call(s32[16,10]{1,0:T(8,128)S(1)} %copy-done.7, bf16[3072,768]{1,0:T(8,128)(2,1)S(1)} %merge_second.1.turned_ref, bf16[768,1536]{1,0:T(8,128)(2,1)S(1)} %get-tuple-element.34.mine_ref, bf16[416,384]{1,0:T(8,128)(2,1)S(1)} %get-tuple-element.35.refs_0_), custom_call_target="tpu_custom_call" | custom-call | flops 226492416 | tf_op jit(solution)/shard_map/blocks0b/pallas_call | solution.py:227
  21.7 1.4 %collective-permute-start.10 = (bf16[416,384]{1,0:T(8,128)(2,1)S(1)}, bf16[416,384]{1,0:T(8,128)(2,1)S(1)}, u32[]{:S(2)}, u32[]{:S(2)}) collective-permute-start(bf16[416,384]{1,0:T(8,128)(2,1)S(1)} %get-tuple-element.48), channel_id=1, source_target_pairs={{0,4},{1,5},{4,8},{5,9},{8,12},{9,13},{12,14},{13,15},{14,10},{15,... | collective-permute-start | bytes 958472 | tf_op jit(solution)/shard_map/ppermute | solution.py:425
  23.2 0.2 collective-permute-start.13
  23.3 1.7 %blocks1.1 = (f32[416,384]{1,0:T(8,128)S(1)}, f32[416,384]{1,0:T(8,128)S(1)}) custom-call(s32[16,10]{1,0:T(8,128)S(1)} %copy-done.6, bf16[3072,768]{1,0:T(8,128)(2,1)S(1)} %merge_second.1.turned_ref, bf16[768,1536]{1,0:T(8,128)(2,1)S(1)} %get-tuple-element.34.mine_ref, bf16[416,384]{1,0:T(8,128)(2,1)S(1)} %get-tuple-element.36.refs_0_), custom_call_target="tpu_custom_call" | custom-call | flops 226492416 | tf_op jit(solution)/shard_map/blocks1/pallas_call | solution.py:227
  25.1 0.0 copy-start.5
  25.1 2.6 %collective-permute-done.4.refs_2_ = bf16[416,384]{1,0:T(8,128)(2,1)S(1)} collective-permute-done((bf16[416,384]{1,0:T(8,128)(2,1)S(1)}, bf16[416,384]{1,0:T(8,128)(2,1)S(1)}, u32[]{:S(2)}, u32[]{:S(2)}) %collective-permute-start.4) | collective-permute-done | bytes 319520 | tf_op jit(solution)/shard_map/ppermute | solution.py:425
  27.7 0.1 add_convert_fusion.7
  27.7 1.2 %collective-permute-start.6 = (bf16[416,384]{1,0:T(8,128)(2,1)S(1)}, bf16[416,384]{1,0:T(8,128)(2,1)S(1)}, u32[]{:S(2)}, u32[]{:S(2)}) collective-permute-start(bf16[416,384]{1,0:T(8,128)(2,1)S(1)} %add_convert_fusion.7), channel_id=1, source_target_pairs={{0,2},{1,3},{4,0},{5,1},{8,4},{9,5},{12,8},{13,9},{14,12},{15,13},... | collective-permute-start | bytes 958472 | tf_op jit(solution)/shard_map/ppermute | solution.py:425
  29.0 0.1 add_convert_fusion.9
  29.0 0.4 collective-permute-start.3
  29.4 1.7 %blocks1b.1 = (f32[416,384]{1,0:T(8,128)S(1)}, f32[416,384]{1,0:T(8,128)S(1)}) custom-call(s32[16,10]{1,0:T(8,128)S(1)} %copy-done.5, bf16[3072,768]{1,0:T(8,128)(2,1)S(1)} %merge_second.1.turned_ref, bf16[768,1536]{1,0:T(8,128)(2,1)S(1)} %get-tuple-element.34.mine_ref, bf16[416,384]{1,0:T(8,128)(2,1)S(1)} %collective-permute-done.2.refs_0_.refs_1_), custom_call_target="tpu_custom_call" | custom-call | flops 226492416 | tf_op jit(solution)/shard_map/blocks1b/pallas_call | solution.py:227
  31.1 0.0 copy-start.4
  31.1 3.4 %collective-permute-done.13 = bf16[416,384]{1,0:T(8,128)(2,1)S(1)} collective-permute-done((bf16[416,384]{1,0:T(8,128)(2,1)S(1)}, bf16[416,384]{1,0:T(8,128)(2,1)S(1)}, u32[]{:S(2)}, u32[]{:S(2)}) %collective-permute-start.13) | collective-permute-done | bytes 319520 | tf_op jit(solution)/shard_map/ppermute | solution.py:425
  34.5 0.1 add_convert_fusion.1
  34.6 1.2 %collective-permute-start.14 = (bf16[416,384]{1,0:T(8,128)(2,1)S(1)}, bf16[416,384]{1,0:T(8,128)(2,1)S(1)}, u32[]{:S(2)}, u32[]{:S(2)}) collective-permute-start(bf16[416,384]{1,0:T(8,128)(2,1)S(1)} %add_convert_fusion.1), channel_id=1, source_target_pairs={{0,2},{1,3},{4,0},{5,1},{8,4},{9,5},{12,8},{13,9},{14,12},{15,13},... | collective-permute-start | bytes 958472 | tf_op jit(solution)/shard_map/ppermute | solution.py:425
  35.8 0.0 collective-permute-done.10
  35.8 0.1 add_convert_fusion.3
  35.9 0.4 collective-permute-start.11
  36.2 1.7 %blocks2.1 = (f32[416,384]{1,0:T(8,128)S(1)}, f32[416,384]{1,0:T(8,128)S(1)}) custom-call(s32[16,10]{1,0:T(8,128)S(1)} %copy-done.4, bf16[3072,768]{1,0:T(8,128)(2,1)S(1)} %merge_second.1.turned_ref, bf16[768,1536]{1,0:T(8,128)(2,1)S(1)} %get-tuple-element.34.mine_ref, f32[416,384]{1,0:T(8,128)S(1)} %get-tuple-element.38.refs_0_, ...), custom_call_target="tpu_custom_call" | custom-call | flops 226492416 | tf_op jit(solution)/shard_map/blocks2/pallas_call | solution.py:227
  38.0 0.0 copy-start.3
  38.0 3.4 %collective-permute-done.6.refs_2_ = bf16[416,384]{1,0:T(8,128)(2,1)S(1)} collective-permute-done((bf16[416,384]{1,0:T(8,128)(2,1)S(1)}, bf16[416,384]{1,0:T(8,128)(2,1)S(1)}, u32[]{:S(2)}, u32[]{:S(2)}) %collective-permute-start.6) | collective-permute-done | bytes 319520 | tf_op jit(solution)/shard_map/ppermute | solution.py:425
  41.4 0.1 add_convert_fusion.5
  41.4 1.2 %collective-permute-start.8 = (bf16[416,384]{1,0:T(8,128)(2,1)S(1)}, bf16[416,384]{1,0:T(8,128)(2,1)S(1)}, u32[]{:S(2)}, u32[]{:S(2)}) collective-permute-start(bf16[416,384]{1,0:T(8,128)(2,1)S(1)} %add_convert_fusion.5), channel_id=1, source_target_pairs={{0,2},{1,3},{4,0},{5,1},{8,4},{9,5},{12,8},{13,9},{14,12},{15,13},... | collective-permute-start | bytes 958472 | tf_op jit(solution)/shard_map/ppermute | solution.py:425
  42.7 0.1 add_convert_fusion.8
  42.7 0.4 collective-permute-start.5
  43.1 1.7 %blocks2b.1 = (f32[416,384]{1,0:T(8,128)S(1)}, f32[416,384]{1,0:T(8,128)S(1)}) custom-call(s32[16,10]{1,0:T(8,128)S(1)} %copy-done.3, bf16[3072,768]{1,0:T(8,128)(2,1)S(1)} %merge_second.1.turned_ref, bf16[768,1536]{1,0:T(8,128)(2,1)S(1)} %get-tuple-element.34.mine_ref, bf16[416,384]{1,0:T(8,128)(2,1)S(1)} %collective-permute-done.3.refs_0_.refs_1_), custom_call_target="tpu_custom_call" | custom-call | flops 226492416 | tf_op jit(solution)/shard_map/blocks2b/pallas_call | solution.py:227
  44.8 0.0 copy-start.2
  44.8 3.4 %collective-permute-done.14 = bf16[416,384]{1,0:T(8,128)(2,1)S(1)} collective-permute-done((bf16[416,384]{1,0:T(8,128)(2,1)S(1)}, bf16[416,384]{1,0:T(8,128)(2,1)S(1)}, u32[]{:S(2)}, u32[]{:S(2)}) %collective-permute-start.14) | collective-permute-done | bytes 319520 | tf_op jit(solution)/shard_map/ppermute | solution.py:425
  48.2 0.1 add_convert_fusion
  48.3 1.2 %collective-permute-start.15 = (bf16[416,384]{1,0:T(8,128)(2,1)S(1)}, bf16[416,384]{1,0:T(8,128)(2,1)S(1)}, u32[]{:S(2)}, u32[]{:S(2)}) collective-permute-start(bf16[416,384]{1,0:T(8,128)(2,1)S(1)} %add_convert_fusion), channel_id=1, source_target_pairs={{0,2},{1,3},{4,0},{5,1},{8,4},{9,5},{12,8},{13,9},{14,12},{15,13},... | collective-permute-start | bytes 958472 | tf_op jit(solution)/shard_map/ppermute | solution.py:425
  49.5 0.1 add_convert_fusion.2
  49.6 0.4 collective-permute-start.12
  49.9 1.7 %blocks3.1 = (f32[416,384]{1,0:T(8,128)S(1)}, f32[416,384]{1,0:T(8,128)S(1)}) custom-call(s32[16,10]{1,0:T(8,128)S(1)} %copy-done.2, bf16[3072,768]{1,0:T(8,128)(2,1)S(1)} %merge_second.1.turned_ref, bf16[768,1536]{1,0:T(8,128)(2,1)S(1)} %get-tuple-element.34.mine_ref, f32[416,384]{1,0:T(8,128)S(1)} %get-tuple-element.43.refs_0_, ...), custom_call_target="tpu_custom_call" | custom-call | flops 226492416 | tf_op jit(solution)/shard_map/blocks3/pallas_call | solution.py:227
  51.7 0.0 copy-start.1
  51.7 3.4 %collective-permute-done.8 = bf16[416,384]{1,0:T(8,128)(2,1)S(1)} collective-permute-done((bf16[416,384]{1,0:T(8,128)(2,1)S(1)}, bf16[416,384]{1,0:T(8,128)(2,1)S(1)}, u32[]{:S(2)}, u32[]{:S(2)}) %collective-permute-start.8) | collective-permute-done | bytes 319520 | tf_op jit(solution)/shard_map/ppermute | solution.py:425
  55.1 0.1 add_convert_fusion.4
  55.1 1.2 %collective-permute-start.9 = (bf16[416,384]{1,0:T(8,128)(2,1)S(1)}, bf16[416,384]{1,0:T(8,128)(2,1)S(1)}, u32[]{:S(2)}, u32[]{:S(2)}) collective-permute-start(bf16[416,384]{1,0:T(8,128)(2,1)S(1)} %add_convert_fusion.4), channel_id=1, source_target_pairs={{0,2},{1,3},{4,0},{5,1},{8,4},{9,5},{12,8},{13,9},{14,12},{15,13},... | collective-permute-start | bytes 958472 | tf_op jit(solution)/shard_map/ppermute | solution.py:425
  56.3 0.1 add_convert_fusion.6
  56.4 0.0 copy-start
  56.4 0.4 collective-permute-start.7
  56.8 1.7 %blocks3b.1 = (f32[416,384]{1,0:T(8,128)S(1)}, f32[416,384]{1,0:T(8,128)S(1)}) custom-call(s32[16,10]{1,0:T(8,128)S(1)} %copy-done.1, bf16[3072,768]{1,0:T(8,128)(2,1)S(1)} %merge_second.1.turned_ref, bf16[768,1536]{1,0:T(8,128)(2,1)S(1)} %get-tuple-element.34.mine_ref, bf16[416,384]{1,0:T(8,128)(2,1)S(1)} %collective-permute-done.5.refs_0_), custom_call_target="tpu_custom_call" | custom-call | flops 226492416 | tf_op jit(solution)/shard_map/blocks3b/pallas_call | solution.py:227
  58.5 4.2 %collective-permute-done.12.right1 = bf16[416,384]{1,0:T(8,128)(2,1)S(1)} collective-permute-done((bf16[416,384]{1,0:T(8,128)(2,1)S(1)}, bf16[416,384]{1,0:T(8,128)(2,1)S(1)}, u32[]{:S(2)}, u32[]{:S(2)}) %collective-permute-start.12) | collective-permute-done | bytes 319520 | tf_op jit(solution)/shard_map/ppermute | solution.py:425
  62.8 6.0 %collective-permute-done.9.left1 = bf16[416,384]{1,0:T(8,128)(2,1)S(1)} collective-permute-done((bf16[416,384]{1,0:T(8,128)(2,1)S(1)}, bf16[416,384]{1,0:T(8,128)(2,1)S(1)}, u32[]{:S(2)}, u32[]{:S(2)}) %collective-permute-start.9) | collective-permute-done | bytes 319520 | tf_op jit(solution)/shard_map/ppermute | solution.py:425
  68.7 0.1 outgoing_one.1.after
  68.9 4.1 %collective-permute-start.17 = (bf16[384,384]{1,0:T(8,128)(2,1)S(1)}, bf16[384,384]{1,0:T(8,128)(2,1)S(1)}, u32[]{:S(2)}, u32[]{:S(2)}) collective-permute-start(bf16[384,384]{1,0:T(8,128)(2,1)S(1)} %outgoing_one.1.after), channel_id=1, source_target_pairs={{0,2},{1,10},{2,4},{3,12},{4,6},{5,14},{6,0},{7,8},{8,5},{9,11},{1... | collective-permute-start | bytes 884744 | tf_op jit(solution)/shard_map/ppermute | solution.py:477
  73.0 0.9 %outgoing_other.1 = (bf16[320,384]{1,0:T(8,128)(2,1)S(1)}, f32[192,384]{1,0:T(8,128)S(1)}) custom-call(s32[16,5]{1,0:T(8,128)S(1)} %copy-done, f32[416,384]{1,0:T(8,128)S(1)} %get-tuple-element.41.own0, f32[416,384]{1,0:T(8,128)S(1)} %get-tuple-element.42.own1, bf16[416,384]{1,0:T(8,128)(2,1)S(1)} %collective-permute-done.7.right0, ...), custom_call_target="tpu_custom_call" | custom-call | tf_op jit(solution)/shard_map/outgoing_other/pallas_call | solution.py:466
  73.9 0.1 collective-permute-start.16
  74.0 1.8 %own.1.result_ref = f32[384,1536]{1,0:T(8,128)} custom-call(s32[16,5]{1,0:T(8,128)S(1)} %copy-done, f32[416,384]{1,0:T(8,128)S(1)} %get-tuple-element.41.own0, f32[416,384]{1,0:T(8,128)S(1)} %get-tuple-element.42.own1, bf16[416,384]{1,0:T(8,128)(2,1)S(1)} %collective-permute-done.7.right0, bf16[416,384]{1,0:T(8,128)(2,1)S(1)} %collective-permute-done.9.left1, ...), custom_call_target="tpu_custom_call" | custom-call | tf_op jit(solution)/shard_map/own/pallas_call | solution.py:479
  75.8 3.6 %collective-permute-done.17.one = bf16[384,384]{1,0:T(8,128)(2,1)S(1)} collective-permute-done((bf16[384,384]{1,0:T(8,128)(2,1)S(1)}, bf16[384,384]{1,0:T(8,128)(2,1)S(1)}, u32[]{:S(2)}, u32[]{:S(2)}) %collective-permute-start.17) | collective-permute-done | bytes 294944 | tf_op jit(solution)/shard_map/ppermute | solution.py:477
  79.4 1.7 %one.1.result_ref = f32[384,1536]{1,0:T(8,128)} custom-call(s32[16,5]{1,0:T(8,128)S(1)} %copy-done, bf16[384,384]{1,0:T(8,128)(2,1)S(1)} %collective-permute-done.17.one, f32[384,1536]{1,0:T(8,128)} %own.1.result_ref), custom_call_target="tpu_custom_call", output_to_operand_aliasing={{}: (2, {})} | custom-call | tf_op jit(solution)/shard_map/one/pallas_call | solution.py:489
  81.1 4.8 %collective-permute-done.16.other = bf16[320,384]{1,0:T(8,128)(2,1)S(1)} collective-permute-done((bf16[320,384]{1,0:T(8,128)(2,1)S(1)}, bf16[320,384]{1,0:T(8,128)(2,1)S(1)}, u32[]{:S(2)}, u32[]{:S(2)}) %collective-permute-start.16) | collective-permute-done | bytes 245792 | tf_op jit(solution)/shard_map/ppermute | solution.py:478
  85.8 1.6 %other.1 = f32[384,1536]{1,0:T(8,128)} custom-call(s32[16,5]{1,0:T(8,128)S(1)} %copy-done, f32[192,384]{1,0:T(8,128)S(1)} %get-tuple-element.51.share, bf16[320,384]{1,0:T(8,128)(2,1)S(1)} %collective-permute-done.16.other, f32[384,1536]{1,0:T(8,128)} %one.1.result_ref), custom_call_target="tpu_custom_call", output_to_operand_aliasing={{}: (3, {})} | custom-call | tf_op jit(solution)/shard_map/other/pallas_call | solution.py:489
  (17 shorter events, 0.0 us)
Async XLA Ops:
  5.6 4.6 %collective-permute-start.1 = (bf16[768,1536]{1,0:T(8,128)(2,1)S(1)}, bf16[768,1536]{1,0:T(8,128)(2,1)S(1)}, u32[]{:S(2)}, u32[]{:S(2)}) collective-permute-start(bf16[768,1536]{1,0:T(8,128)(2,1)S(1)} %get-tuple-element.30.refs_0_), channel_id=1, source_target_pairs={{0,1},{1,0},{2,3},{3,2},{4,5},{5,4},{6,7},{7,6},{8,9},{9,8},{10,11... | collective-permute-start | bytes 7077896 | tf_op jit(solution)/shard_map/ppermute | solution.py:510
  9.6 4.7 %collective-permute-start = (bf16[768,1536]{1,0:T(8,128)(2,1)S(1)}, bf16[768,1536]{1,0:T(8,128)(2,1)S(1)}, u32[]{:S(2)}, u32[]{:S(2)}) collective-permute-start(bf16[768,1536]{1,0:T(8,128)(2,1)S(1)} %pick_second.1.refs_0_), channel_id=1, source_target_pairs={{0,1},{1,0},{2,3},{3,2},{4,5},{5,4},{6,7},{7,6},{8,9},{9,8},{10,11... | collective-permute-start | bytes 7077896 | tf_op jit(solution)/shard_map/ppermute | solution.py:512
  14.3 1.1 %copy-start.8 = (s32[16,10]{1,0:T(8,128)S(1)}, s32[16,10]{1,0:T(8,128)}, u32[]{:S(2)}) copy-start(s32[16,10]{1,0:T(8,128)} %constant.18.clone.table) | copy-start | bytes 1924
  15.4 4.5 %copy-start.7 = (s32[16,10]{1,0:T(8,128)S(1)}, s32[16,10]{1,0:T(8,128)}, u32[]{:S(2)}) copy-start(s32[16,10]{1,0:T(8,128)} %constant.19.clone.table) | copy-start | bytes 1924
  17.2 10.5 %collective-permute-start.4 = (bf16[416,384]{1,0:T(8,128)(2,1)S(1)}, bf16[416,384]{1,0:T(8,128)(2,1)S(1)}, u32[]{:S(2)}, u32[]{:S(2)}) collective-permute-start(bf16[416,384]{1,0:T(8,128)(2,1)S(1)} %get-tuple-element.39), channel_id=1, source_target_pairs={{0,2},{1,3},{4,0},{5,1},{8,4},{9,5},{12,8},{13,9},{14,12},{15,13},... | collective-permute-start | bytes 958472 | tf_op jit(solution)/shard_map/ppermute | solution.py:425
  19.8 3.5 %copy-start.6 = (s32[16,10]{1,0:T(8,128)S(1)}, s32[16,10]{1,0:T(8,128)}, u32[]{:S(2)}) copy-start(s32[16,10]{1,0:T(8,128)} %constant.20.clone.table) | copy-start | bytes 1924
  19.8 9.1 %collective-permute-start.2 = (bf16[416,384]{1,0:T(8,128)(2,1)S(1)}, bf16[416,384]{1,0:T(8,128)(2,1)S(1)}, u32[]{:S(2)}, u32[]{:S(2)}) collective-permute-start(bf16[416,384]{1,0:T(8,128)(2,1)S(1)} %get-tuple-element.35.refs_0_), channel_id=1, source_target_pairs={{0,4},{1,5},{4,8},{5,9},{8,12},{9,13},{12,14},{13,15},{14,10},{15,... | collective-permute-start | bytes 958472 | tf_op jit(solution)/shard_map/ppermute | solution.py:425
  21.7 14.1 %collective-permute-start.10 = (bf16[416,384]{1,0:T(8,128)(2,1)S(1)}, bf16[416,384]{1,0:T(8,128)(2,1)S(1)}, u32[]{:S(2)}, u32[]{:S(2)}) collective-permute-start(bf16[416,384]{1,0:T(8,128)(2,1)S(1)} %get-tuple-element.48), channel_id=1, source_target_pairs={{0,4},{1,5},{4,8},{5,9},{8,12},{9,13},{12,14},{13,15},{14,10},{15,... | collective-permute-start | bytes 958472 | tf_op jit(solution)/shard_map/ppermute | solution.py:425
  23.2 11.4 %collective-permute-start.13 = (bf16[416,384]{1,0:T(8,128)(2,1)S(1)}, bf16[416,384]{1,0:T(8,128)(2,1)S(1)}, u32[]{:S(2)}, u32[]{:S(2)}) collective-permute-start(bf16[416,384]{1,0:T(8,128)(2,1)S(1)} %get-tuple-element.36.refs_0_), channel_id=1, source_target_pairs={{0,2},{1,3},{4,0},{5,1},{8,4},{9,5},{12,8},{13,9},{14,12},{15,13},... | collective-permute-start | bytes 958472 | tf_op jit(solution)/shard_map/ppermute | solution.py:425
  25.1 4.3 %copy-start.5 = (s32[16,10]{1,0:T(8,128)S(1)}, s32[16,10]{1,0:T(8,128)}, u32[]{:S(2)}) copy-start(s32[16,10]{1,0:T(8,128)} %constant.21.clone.table) | copy-start | bytes 1924
  27.7 13.6 %collective-permute-start.6 = (bf16[416,384]{1,0:T(8,128)(2,1)S(1)}, bf16[416,384]{1,0:T(8,128)(2,1)S(1)}, u32[]{:S(2)}, u32[]{:S(2)}) collective-permute-start(bf16[416,384]{1,0:T(8,128)(2,1)S(1)} %add_convert_fusion.7), channel_id=1, source_target_pairs={{0,2},{1,3},{4,0},{5,1},{8,4},{9,5},{12,8},{13,9},{14,12},{15,13},... | collective-permute-start | bytes 958472 | tf_op jit(solution)/shard_map/ppermute | solution.py:425
  29.0 13.6 %collective-permute-start.3 = (bf16[416,384]{1,0:T(8,128)(2,1)S(1)}, bf16[416,384]{1,0:T(8,128)(2,1)S(1)}, u32[]{:S(2)}, u32[]{:S(2)}) collective-permute-start(bf16[416,384]{1,0:T(8,128)(2,1)S(1)} %add_convert_fusion.9), channel_id=1, source_target_pairs={{0,4},{1,5},{4,8},{5,9},{8,12},{9,13},{12,14},{13,15},{14,10},{15,... | collective-permute-start | bytes 958472 | tf_op jit(solution)/shard_map/ppermute | solution.py:425
  31.1 5.1 %copy-start.4 = (s32[16,10]{1,0:T(8,128)S(1)}, s32[16,10]{1,0:T(8,128)}, u32[]{:S(2)}) copy-start(s32[16,10]{1,0:T(8,128)} %constant.22.clone.table) | copy-start | bytes 1924
  34.6 13.6 %collective-permute-start.14 = (bf16[416,384]{1,0:T(8,128)(2,1)S(1)}, bf16[416,384]{1,0:T(8,128)(2,1)S(1)}, u32[]{:S(2)}, u32[]{:S(2)}) collective-permute-start(bf16[416,384]{1,0:T(8,128)(2,1)S(1)} %add_convert_fusion.1), channel_id=1, source_target_pairs={{0,2},{1,3},{4,0},{5,1},{8,4},{9,5},{12,8},{13,9},{14,12},{15,13},... | collective-permute-start | bytes 958472 | tf_op jit(solution)/shard_map/ppermute | solution.py:425
  35.9 13.6 %collective-permute-start.11 = (bf16[416,384]{1,0:T(8,128)(2,1)S(1)}, bf16[416,384]{1,0:T(8,128)(2,1)S(1)}, u32[]{:S(2)}, u32[]{:S(2)}) collective-permute-start(bf16[416,384]{1,0:T(8,128)(2,1)S(1)} %add_convert_fusion.3), channel_id=1, source_target_pairs={{0,4},{1,5},{4,8},{5,9},{8,12},{9,13},{12,14},{13,15},{14,10},{15,... | collective-permute-start | bytes 958472 | tf_op jit(solution)/shard_map/ppermute | solution.py:425
  38.0 5.1 %copy-start.3 = (s32[16,10]{1,0:T(8,128)S(1)}, s32[16,10]{1,0:T(8,128)}, u32[]{:S(2)}) copy-start(s32[16,10]{1,0:T(8,128)} %constant.23.clone.table) | copy-start | bytes 1924
  41.4 13.6 %collective-permute-start.8 = (bf16[416,384]{1,0:T(8,128)(2,1)S(1)}, bf16[416,384]{1,0:T(8,128)(2,1)S(1)}, u32[]{:S(2)}, u32[]{:S(2)}) collective-permute-start(bf16[416,384]{1,0:T(8,128)(2,1)S(1)} %add_convert_fusion.5), channel_id=1, source_target_pairs={{0,2},{1,3},{4,0},{5,1},{8,4},{9,5},{12,8},{13,9},{14,12},{15,13},... | collective-permute-start | bytes 958472 | tf_op jit(solution)/shard_map/ppermute | solution.py:425
  42.7 13.6 %collective-permute-start.5 = (bf16[416,384]{1,0:T(8,128)(2,1)S(1)}, bf16[416,384]{1,0:T(8,128)(2,1)S(1)}, u32[]{:S(2)}, u32[]{:S(2)}) collective-permute-start(bf16[416,384]{1,0:T(8,128)(2,1)S(1)} %add_convert_fusion.8), channel_id=1, source_target_pairs={{0,4},{1,5},{4,8},{5,9},{8,12},{9,13},{12,14},{13,15},{14,10},{15,... | collective-permute-start | bytes 958472 | tf_op jit(solution)/shard_map/ppermute | solution.py:425
  44.8 5.1 %copy-start.2 = (s32[16,10]{1,0:T(8,128)S(1)}, s32[16,10]{1,0:T(8,128)}, u32[]{:S(2)}) copy-start(s32[16,10]{1,0:T(8,128)} %constant.24.clone.table) | copy-start | bytes 1924
  48.3 24.7 %collective-permute-start.15 = (bf16[416,384]{1,0:T(8,128)(2,1)S(1)}, bf16[416,384]{1,0:T(8,128)(2,1)S(1)}, u32[]{:S(2)}, u32[]{:S(2)}) collective-permute-start(bf16[416,384]{1,0:T(8,128)(2,1)S(1)} %add_convert_fusion), channel_id=1, source_target_pairs={{0,2},{1,3},{4,0},{5,1},{8,4},{9,5},{12,8},{13,9},{14,12},{15,13},... | collective-permute-start | bytes 958472 | tf_op jit(solution)/shard_map/ppermute | solution.py:425
  49.6 13.2 %collective-permute-start.12 = (bf16[416,384]{1,0:T(8,128)(2,1)S(1)}, bf16[416,384]{1,0:T(8,128)(2,1)S(1)}, u32[]{:S(2)}, u32[]{:S(2)}) collective-permute-start(bf16[416,384]{1,0:T(8,128)(2,1)S(1)} %add_convert_fusion.2), channel_id=1, source_target_pairs={{0,4},{1,5},{4,8},{5,9},{8,12},{9,13},{12,14},{13,15},{14,10},{15,... | collective-permute-start | bytes 958472 | tf_op jit(solution)/shard_map/ppermute | solution.py:425
  51.7 5.1 %copy-start.1 = (s32[16,10]{1,0:T(8,128)S(1)}, s32[16,10]{1,0:T(8,128)}, u32[]{:S(2)}) copy-start(s32[16,10]{1,0:T(8,128)} %constant.25.clone.table) | copy-start | bytes 1924
  55.1 13.6 %collective-permute-start.9 = (bf16[416,384]{1,0:T(8,128)(2,1)S(1)}, bf16[416,384]{1,0:T(8,128)(2,1)S(1)}, u32[]{:S(2)}, u32[]{:S(2)}) collective-permute-start(bf16[416,384]{1,0:T(8,128)(2,1)S(1)} %add_convert_fusion.4), channel_id=1, source_target_pairs={{0,2},{1,3},{4,0},{5,1},{8,4},{9,5},{12,8},{13,9},{14,12},{15,13},... | collective-permute-start | bytes 958472 | tf_op jit(solution)/shard_map/ppermute | solution.py:425
  56.4 16.6 %copy-start = (s32[16,5]{1,0:T(8,128)S(1)}, s32[16,5]{1,0:T(8,128)}, u32[]{:S(2)}) copy-start(s32[16,5]{1,0:T(8,128)} %constant.26.clone.place) | copy-start | bytes 964
  56.4 16.6 %collective-permute-start.7 = (bf16[416,384]{1,0:T(8,128)(2,1)S(1)}, bf16[416,384]{1,0:T(8,128)(2,1)S(1)}, u32[]{:S(2)}, u32[]{:S(2)}) collective-permute-start(bf16[416,384]{1,0:T(8,128)(2,1)S(1)} %add_convert_fusion.6), channel_id=1, source_target_pairs={{0,4},{1,5},{4,8},{5,9},{8,12},{9,13},{12,14},{13,15},{14,10},{15,... | collective-permute-start | bytes 958472 | tf_op jit(solution)/shard_map/ppermute | solution.py:425
  68.9 10.5 %collective-permute-start.17 = (bf16[384,384]{1,0:T(8,128)(2,1)S(1)}, bf16[384,384]{1,0:T(8,128)(2,1)S(1)}, u32[]{:S(2)}, u32[]{:S(2)}) collective-permute-start(bf16[384,384]{1,0:T(8,128)(2,1)S(1)} %outgoing_one.1.after), channel_id=1, source_target_pairs={{0,2},{1,10},{2,4},{3,12},{4,6},{5,14},{6,0},{7,8},{8,5},{9,11},{1... | collective-permute-start | bytes 884744 | tf_op jit(solution)/shard_map/ppermute | solution.py:477
  73.9 11.9 %collective-permute-start.16 = (bf16[320,384]{1,0:T(8,128)(2,1)S(1)}, bf16[320,384]{1,0:T(8,128)(2,1)S(1)}, u32[]{:S(2)}, u32[]{:S(2)}) collective-permute-start(bf16[320,384]{1,0:T(8,128)(2,1)S(1)} %get-tuple-element.52), channel_id=1, source_target_pairs={{0,4},{1,8},{2,6},{3,10},{4,0},{5,12},{6,2},{7,14},{8,3},{9,13},{1... | collective-permute-start | bytes 737288 | tf_op jit(solution)/shard_map/ppermute | solution.py:478

commit v14 on v13

--- a/solution.py
+++ b/solution.py
@@ -24,21 +24,8 @@
     ).astype(BF16)
     for copy in inputs:
         copy.wait()
-    lanes = lax.broadcasted_iota(I32, (tokens, 128), 1)
-    rows = jnp.concatenate([ids_ref[...].astype(F32), gates_ref[...], jnp.zeros((4, tokens), F32)], axis=0).T
-    ids = [rows[:, k : k + 1].astype(I32) for k in range(2)]
-    gates = [rows[:, k : k + 1] for k in (2, 3)]
-    hits = [ids[k] == lanes for k in range(2)]
-    named = jnp.where(hits[0] | hits[1], 1.0, 0.0).astype(BF16)
-    before = jnp.dot(earlier_ref[...], named, preferred_element_type=F32)
-    firsts = []
-    for b in range(tokens // BATCH):
-        start = before[b * BATCH : b * BATCH + 1, :].astype(I32)
-        firsts.append(jnp.minimum((start >> 4) << 4, CAP - WINDOW))
-        starts_ref[b : b + 1, :] = firsts[-1]
-    starts_copy.start()
-
-    slots = [ids[k] - lax.axis_index("expert") * local for k in range(2)]
+    slots = [ids_ref[k : k + 1, :] - lax.axis_index("expert") * local for k in range(2)]
+    gates = [gates_ref[k : k + 1, :] for k in range(2)]
     here = [jnp.where((slots[k] >= 0) & (slots[k] < local), 1.0, 0.0) for k in range(2)]
     both = here[0] * here[1]
     neither = (1.0 - here[0]) * (1.0 - here[1])
@@ -48,18 +35,28 @@
     theirs = (1.0 - here[0]) * gates[0] + (1.0 - here[1]) * gates[1]
     ours = jnp.where(mixed > 0.5, ours, both)
     theirs = jnp.where(mixed > 0.5, theirs, neither)
-    coef_ref[...] = jnp.where(
-        lanes == 0, weights[0], jnp.where(lanes == 1, weights[1], jnp.where(lanes == 2, ours, theirs))
-    )
-
-    columns = lax.broadcasted_iota(I32, (BATCH, local * WINDOW), 1)
+    bases = [jnp.where(here[k] > 0.5, (slots[k] * WINDOW).astype(F32), -4.0 * CAP) for k in range(2)]
+    columns = jnp.concatenate([*weights, ours, theirs, ids_ref[...].astype(F32), *bases], axis=0).T
+    coef_ref[...] = columns
+    lanes = lax.broadcasted_iota(I32, (tokens, 128), 1)
+    hits = [columns[:, 4 + k : 5 + k].astype(I32) == lanes for k in range(2)]
+    named = jnp.where(hits[0] | hits[1], 1.0, 0.0).astype(BF16)
+    before = jnp.dot(earlier_ref[...], named, preferred_element_type=F32)
+    firsts = []
+    for b in range(tokens // BATCH):
+        start = before[b * BATCH : b * BATCH + 1, :].astype(I32)
+        firsts.append(jnp.minimum((start >> 4) << 4, CAP - WINDOW))
+        starts_ref[b : b + 1, :] = firsts[-1]
+    starts_copy.start()
+
+    places = lax.broadcasted_iota(I32, (BATCH, local * WINDOW), 1)
     for b in range(tokens // BATCH):
         rows = slice(b * BATCH, (b + 1) * BATCH)
         ahead = before[rows] - firsts[b].astype(F32)
         for k in range(2):
-            offset = jnp.sum(jnp.where(hits[k][rows], ahead, 0.0), axis=1, keepdims=True).astype(I32)
-            at = jnp.where(here[k][rows] > 0.5, slots[k][rows] * WINDOW + offset, -1)
-            pick_ref[(2 * b + k) * BATCH : (2 * b + k + 1) * BATCH, :] = jnp.where(columns == at, 1.0, 0.0).astype(BF16)
+            offset = jnp.sum(jnp.where(hits[k][rows], ahead, 0.0), axis=1, keepdims=True)
+            at = (columns[rows, 6 + k : 7 + k] + offset).astype(I32)
+            pick_ref[(2 * b + k) * BATCH : (2 * b + k + 1) * BATCH, :] = jnp.where(places == at, 1.0, 0.0).astype(BF16)
 
 
 def pick_kernel(first, *refs):
@@ -125,7 +122,7 @@
         out_shape += [
             jax.ShapeDtypeStruct((2 * tokens, depth), BF16),
             jax.ShapeDtypeStruct((tokens // BATCH, 128), I32),
-            jax.ShapeDtypeStruct((tokens, 128), F32),
+            jax.ShapeDtypeStruct((tokens, 8), F32),
         ]
         args = [in_hbm(x) for x in args]
         in_specs = [any_] * 3

time: 87.8 us -> 87.4 us (level)
  no operation moved by 1% of the time
where the time goes in v14:
time: 87.4 us; the launch traced here: 87.2 us
  waiting for transfers between devices  37.6 us (43%)
  Pallas kernels  31.4 us (36%)
  starting transfers between devices  17 us (19%)
    ppermute x14, waiting for transfers between devices, hop(): lax.ppermute(value, both, ring_perm(1 if key[1] <= (4 if key[0] == 0 else...  26.3 us
    pallas_call x8, Pallas kernels, moment_blocks(): pl.pallas_call(functools.partial(blocks_kernel, pieces, width), out_shape...  14 us
    ppermute x14, starting transfers between devices, hop(): lax.ppermute(value, both, ring_perm(1 if key[1] <= (4 if key[0] == 0 else...  12.2 us
    pallas_call x2, Pallas kernels, pick_half(): pl.pallas_call(functools.partial(pick_kernel, first), out_shape=out_shape...  9.1 us
    ppermute x1, waiting for transfers between devices, symmetric_moment(): other = lax.ppermute(other, both, perm_other)  4.74 us
    ppermute x1, starting transfers between devices, symmetric_moment(): one = lax.ppermute(one, both, perm_one)  4.15 us
    ppermute x1, waiting for transfers between devices, symmetric_moment(): one = lax.ppermute(one, both, perm_one)  3.66 us
    pallas_call x2, Pallas kernels, symmetric_moment(): pl.pallas_call(kernel, out_shape=result, in_specs=[smem] + [vmem] * len(a...  3.22 us
  transfers between devices with their start and end apart: 18, of which 10 were waited for; matrix products, arithmetic and copies ran while one was open for 1% of the time, Pallas kernels for 25%

profile of v14, /device:TPU:1, one launch (start us, length us, event | category | flops | bytes accessed | tf_op | source)
XLA Modules:
  0.0 87.2 jit_solution(7715170037844865581)
XLA Ops:
  0.0 5.2 %pick_first.1 = (bf16[768,1536]{1,0:T(8,128)(2,1)S(1)}, bf16[1536,256]{1,0:T(8,128)(2,1)S(1)}, s32[16,128]{1,0:T(8,128)S(1)}, f32[768,8]{1,0:T(8,128)S(1)}) custom-call(s32[2,768]{1,0:T(2,128)} %bitcast.2, f32[2,768]{1,0:T(2,128)} %bitcast.3, bf16[1536,3072]{1,0:T(8,128)(2,1)} %refs_3_.1), custom_call_target="tpu_custom_call" | custom-call | flops 1207959552 | bytes 7077888 | tf_op jit(solution)/shard_map/pick_first/pallas_call | solution.py:136
  5.2 0.1 collective-permute-start.1
  5.3 3.9 %pick_second.1.refs_0_ = bf16[768,1536]{1,0:T(8,128)(2,1)S(1)} custom-call(s32[16,128]{1,0:T(8,128)S(1)} %get-tuple-element.31.refs_0_, bf16[1536,256]{1,0:T(8,128)(2,1)S(1)} %get-tuple-element.32.refs_1_, f32[768,8]{1,0:T(8,128)S(1)} %get-tuple-element.29.refs_2_.coef_ref, bf16[1536,3072]{1,0:T(8,128)(2,1)} %refs_3_.1), custom_call_target="tpu_custom_call" | custom-call | flops 1207959552 | bytes 7077888 | tf_op jit(solution)/shard_map/pick_second/pallas_call | solution.py:136
  9.2 0.5 collective-permute-start
  9.8 0.0 collective-permute-done.1.refs_1_
  9.8 1.2 %merge_first.1 = (bf16[768,1536]{1,0:T(8,128)(2,1)S(1)}, bf16[3072,768]{1,0:T(8,128)(2,1)S(1)}) custom-call(f32[768,8]{1,0:T(8,128)S(1)} %get-tuple-element.29.refs_2_.coef_ref, bf16[768,1536]{1,0:T(8,128)(2,1)S(1)} %pick_second.1.refs_0_, bf16[768,1536]{1,0:T(8,128)(2,1)S(1)} %collective-permute-done.1.refs_1_), custom_call_target="tpu_custom_call" | custom-call | flops 4718592 | tf_op jit(solution)/shard_map/merge_first/pallas_call | solution.py:176
  11.0 2.9 %collective-permute-done.refs_1_ = bf16[768,1536]{1,0:T(8,128)(2,1)S(1)} collective-permute-done((bf16[768,1536]{1,0:T(8,128)(2,1)S(1)}, bf16[768,1536]{1,0:T(8,128)(2,1)S(1)}, u32[]{:S(2)}, u32[]{:S(2)}) %collective-permute-start) | collective-permute-done | bytes 2359328 | tf_op jit(solution)/shard_map/ppermute | solution.py:509
  13.9 1.1 %merge_second.1.turned_ref = bf16[3072,768]{1,0:T(8,128)(2,1)S(1)} custom-call(f32[768,8]{1,0:T(8,128)S(1)} %get-tuple-element.29.refs_2_.coef_ref, bf16[768,1536]{1,0:T(8,128)(2,1)S(1)} %get-tuple-element.30.refs_0_, bf16[768,1536]{1,0:T(8,128)(2,1)S(1)} %collective-permute-done.refs_1_, ...), custom_call_target="tpu_custom_call", output_to_operand_aliasing={{}: (3, {})} | custom-call | flops 4718592 | tf_op jit(solution)/shard_map/merge_second/pallas_call | solution.py:176
  15.1 0.0 copy-start.7
  15.1 1.7 %blocks0.1 = (bf16[416,384]{1,0:T(8,128)(2,1)S(1)}, bf16[416,384]{1,0:T(8,128)(2,1)S(1)}) custom-call(s32[16,10]{1,0:T(8,128)S(1)} %copy-done.8, bf16[3072,768]{1,0:T(8,128)(2,1)S(1)} %merge_second.1.turned_ref, bf16[768,1536]{1,0:T(8,128)(2,1)S(1)} %get-tuple-element.34.mine_ref), custom_call_target="tpu_custom_call" | custom-call | flops 226492416 | tf_op jit(solution)/shard_map/blocks0/pallas_call | solution.py:224
  16.8 2.7 %collective-permute-start.4 = (bf16[416,384]{1,0:T(8,128)(2,1)S(1)}, bf16[416,384]{1,0:T(8,128)(2,1)S(1)}, u32[]{:S(2)}, u32[]{:S(2)}) collective-permute-start(bf16[416,384]{1,0:T(8,128)(2,1)S(1)} %get-tuple-element.39), channel_id=1, source_target_pairs={{0,2},{1,3},{4,0},{5,1},{8,4},{9,5},{12,8},{13,9},{14,12},{15,13},... | collective-permute-start | bytes 958472 | tf_op jit(solution)/shard_map/ppermute | solution.py:422
  19.5 0.1 collective-permute-start.2
  19.6 1.7 %blocks0b.1 = (bf16[416,384]{1,0:T(8,128)(2,1)S(1)}, bf16[416,384]{1,0:T(8,128)(2,1)S(1)}) custom-call(s32[16,10]{1,0:T(8,128)S(1)} %copy-done.7, bf16[3072,768]{1,0:T(8,128)(2,1)S(1)} %merge_second.1.turned_ref, bf16[768,1536]{1,0:T(8,128)(2,1)S(1)} %get-tuple-element.34.mine_ref, bf16[416,384]{1,0:T(8,128)(2,1)S(1)} %get-tuple-element.35.refs_0_), custom_call_target="tpu_custom_call" | custom-call | flops 226492416 | tf_op jit(solution)/shard_map/blocks0b/pallas_call | solution.py:224
  21.3 1.4 %collective-permute-start.10 = (bf16[416,384]{1,0:T(8,128)(2,1)S(1)}, bf16[416,384]{1,0:T(8,128)(2,1)S(1)}, u32[]{:S(2)}, u32[]{:S(2)}) collective-permute-start(bf16[416,384]{1,0:T(8,128)(2,1)S(1)} %get-tuple-element.48), channel_id=1, source_target_pairs={{0,4},{1,5},{4,8},{5,9},{8,12},{9,13},{12,14},{13,15},{14,10},{15,... | collective-permute-start | bytes 958472 | tf_op jit(solution)/shard_map/ppermute | solution.py:422
  22.8 0.1 collective-permute-start.13
  22.9 1.9 %blocks1.1 = (f32[416,384]{1,0:T(8,128)S(1)}, f32[416,384]{1,0:T(8,128)S(1)}) custom-call(s32[16,10]{1,0:T(8,128)S(1)} %copy-done.6, bf16[3072,768]{1,0:T(8,128)(2,1)S(1)} %merge_second.1.turned_ref, bf16[768,1536]{1,0:T(8,128)(2,1)S(1)} %get-tuple-element.34.mine_ref, bf16[416,384]{1,0:T(8,128)(2,1)S(1)} %get-tuple-element.36.refs_0_), custom_call_target="tpu_custom_call" | custom-call | flops 226492416 | tf_op jit(solution)/shard_map/blocks1/pallas_call | solution.py:224
  24.8 0.0 copy-start.5
  24.8 2.5 %collective-permute-done.4.refs_2_ = bf16[416,384]{1,0:T(8,128)(2,1)S(1)} collective-permute-done((bf16[416,384]{1,0:T(8,128)(2,1)S(1)}, bf16[416,384]{1,0:T(8,128)(2,1)S(1)}, u32[]{:S(2)}, u32[]{:S(2)}) %collective-permute-start.4) | collective-permute-done | bytes 319520 | tf_op jit(solution)/shard_map/ppermute | solution.py:422
  27.3 0.1 add_convert_fusion.7
  27.4 1.2 %collective-permute-start.6 = (bf16[416,384]{1,0:T(8,128)(2,1)S(1)}, bf16[416,384]{1,0:T(8,128)(2,1)S(1)}, u32[]{:S(2)}, u32[]{:S(2)}) collective-permute-start(bf16[416,384]{1,0:T(8,128)(2,1)S(1)} %add_convert_fusion.7), channel_id=1, source_target_pairs={{0,2},{1,3},{4,0},{5,1},{8,4},{9,5},{12,8},{13,9},{14,12},{15,13},... | collective-permute-start | bytes 958472 | tf_op jit(solution)/shard_map/ppermute | solution.py:422
  28.6 0.0 collective-permute-done.2.refs_0_.refs_1_
  28.6 0.1 add_convert_fusion.9
  28.7 0.3 collective-permute-start.3
  29.0 1.7 %blocks1b.1 = (f32[416,384]{1,0:T(8,128)S(1)}, f32[416,384]{1,0:T(8,128)S(1)}) custom-call(s32[16,10]{1,0:T(8,128)S(1)} %copy-done.5, bf16[3072,768]{1,0:T(8,128)(2,1)S(1)} %merge_second.1.turned_ref, bf16[768,1536]{1,0:T(8,128)(2,1)S(1)} %get-tuple-element.34.mine_ref, bf16[416,384]{1,0:T(8,128)(2,1)S(1)} %collective-permute-done.2.refs_0_.refs_1_), custom_call_target="tpu_custom_call" | custom-call | flops 226492416 | tf_op jit(solution)/shard_map/blocks1b/pallas_call | solution.py:224
  30.7 0.0 copy-start.4
  30.8 3.4 %collective-permute-done.13 = bf16[416,384]{1,0:T(8,128)(2,1)S(1)} collective-permute-done((bf16[416,384]{1,0:T(8,128)(2,1)S(1)}, bf16[416,384]{1,0:T(8,128)(2,1)S(1)}, u32[]{:S(2)}, u32[]{:S(2)}) %collective-permute-start.13) | collective-permute-done | bytes 319520 | tf_op jit(solution)/shard_map/ppermute | solution.py:422
  34.1 0.1 add_convert_fusion.1
  34.2 1.2 %collective-permute-start.14 = (bf16[416,384]{1,0:T(8,128)(2,1)S(1)}, bf16[416,384]{1,0:T(8,128)(2,1)S(1)}, u32[]{:S(2)}, u32[]{:S(2)}) collective-permute-start(bf16[416,384]{1,0:T(8,128)(2,1)S(1)} %add_convert_fusion.1), channel_id=1, source_target_pairs={{0,2},{1,3},{4,0},{5,1},{8,4},{9,5},{12,8},{13,9},{14,12},{15,13},... | collective-permute-start | bytes 958472 | tf_op jit(solution)/shard_map/ppermute | solution.py:422
  35.5 0.1 add_convert_fusion.3
  35.5 0.3 collective-permute-start.11
  35.9 1.7 %blocks2.1 = (f32[416,384]{1,0:T(8,128)S(1)}, f32[416,384]{1,0:T(8,128)S(1)}) custom-call(s32[16,10]{1,0:T(8,128)S(1)} %copy-done.4, bf16[3072,768]{1,0:T(8,128)(2,1)S(1)} %merge_second.1.turned_ref, bf16[768,1536]{1,0:T(8,128)(2,1)S(1)} %get-tuple-element.34.mine_ref, f32[416,384]{1,0:T(8,128)S(1)} %get-tuple-element.38.refs_0_, ...), custom_call_target="tpu_custom_call" | custom-call | flops 226492416 | tf_op jit(solution)/shard_map/blocks2/pallas_call | solution.py:224
  37.6 0.0 copy-start.3
  37.6 3.4 %collective-permute-done.6.refs_2_ = bf16[416,384]{1,0:T(8,128)(2,1)S(1)} collective-permute-done((bf16[416,384]{1,0:T(8,128)(2,1)S(1)}, bf16[416,384]{1,0:T(8,128)(2,1)S(1)}, u32[]{:S(2)}, u32[]{:S(2)}) %collective-permute-start.6) | collective-permute-done | bytes 319520 | tf_op jit(solution)/shard_map/ppermute | solution.py:422
  41.0 0.1 add_convert_fusion.5
  41.1 1.2 %collective-permute-start.8 = (bf16[416,384]{1,0:T(8,128)(2,1)S(1)}, bf16[416,384]{1,0:T(8,128)(2,1)S(1)}, u32[]{:S(2)}, u32[]{:S(2)}) collective-permute-start(bf16[416,384]{1,0:T(8,128)(2,1)S(1)} %add_convert_fusion.5), channel_id=1, source_target_pairs={{0,2},{1,3},{4,0},{5,1},{8,4},{9,5},{12,8},{13,9},{14,12},{15,13},... | collective-permute-start | bytes 958472 | tf_op jit(solution)/shard_map/ppermute | solution.py:422
  42.3 0.1 add_convert_fusion.8
  42.4 0.3 collective-permute-start.5
  42.7 1.7 %blocks2b.1 = (f32[416,384]{1,0:T(8,128)S(1)}, f32[416,384]{1,0:T(8,128)S(1)}) custom-call(s32[16,10]{1,0:T(8,128)S(1)} %copy-done.3, bf16[3072,768]{1,0:T(8,128)(2,1)S(1)} %merge_second.1.turned_ref, bf16[768,1536]{1,0:T(8,128)(2,1)S(1)} %get-tuple-element.34.mine_ref, bf16[416,384]{1,0:T(8,128)(2,1)S(1)} %collective-permute-done.3.refs_0_.refs_1_), custom_call_target="tpu_custom_call" | custom-call | flops 226492416 | tf_op jit(solution)/shard_map/blocks2b/pallas_call | solution.py:224
  44.4 0.0 copy-start.2
  44.5 3.4 %collective-permute-done.14 = bf16[416,384]{1,0:T(8,128)(2,1)S(1)} collective-permute-done((bf16[416,384]{1,0:T(8,128)(2,1)S(1)}, bf16[416,384]{1,0:T(8,128)(2,1)S(1)}, u32[]{:S(2)}, u32[]{:S(2)}) %collective-permute-start.14) | collective-permute-done | bytes 319520 | tf_op jit(solution)/shard_map/ppermute | solution.py:422
  47.8 0.1 add_convert_fusion
  47.9 1.2 %collective-permute-start.15 = (bf16[416,384]{1,0:T(8,128)(2,1)S(1)}, bf16[416,384]{1,0:T(8,128)(2,1)S(1)}, u32[]{:S(2)}, u32[]{:S(2)}) collective-permute-start(bf16[416,384]{1,0:T(8,128)(2,1)S(1)} %add_convert_fusion), channel_id=1, source_target_pairs={{0,2},{1,3},{4,0},{5,1},{8,4},{9,5},{12,8},{13,9},{14,12},{15,13},... | collective-permute-start | bytes 958472 | tf_op jit(solution)/shard_map/ppermute | solution.py:422
  49.1 0.1 add_convert_fusion.2
  49.2 0.3 collective-permute-start.12
  49.6 1.7 %blocks3.1 = (f32[416,384]{1,0:T(8,128)S(1)}, f32[416,384]{1,0:T(8,128)S(1)}) custom-call(s32[16,10]{1,0:T(8,128)S(1)} %copy-done.2, bf16[3072,768]{1,0:T(8,128)(2,1)S(1)} %merge_second.1.turned_ref, bf16[768,1536]{1,0:T(8,128)(2,1)S(1)} %get-tuple-element.34.mine_ref, f32[416,384]{1,0:T(8,128)S(1)} %get-tuple-element.43.refs_0_, ...), custom_call_target="tpu_custom_call" | custom-call | flops 226492416 | tf_op jit(solution)/shard_map/blocks3/pallas_call | solution.py:224
  51.3 0.0 copy-start.1
  51.3 3.4 %collective-permute-done.8 = bf16[416,384]{1,0:T(8,128)(2,1)S(1)} collective-permute-done((bf16[416,384]{1,0:T(8,128)(2,1)S(1)}, bf16[416,384]{1,0:T(8,128)(2,1)S(1)}, u32[]{:S(2)}, u32[]{:S(2)}) %collective-permute-start.8) | collective-permute-done | bytes 319520 | tf_op jit(solution)/shard_map/ppermute | solution.py:422
  54.7 0.1 add_convert_fusion.4
  54.8 1.2 %collective-permute-start.9 = (bf16[416,384]{1,0:T(8,128)(2,1)S(1)}, bf16[416,384]{1,0:T(8,128)(2,1)S(1)}, u32[]{:S(2)}, u32[]{:S(2)}) collective-permute-start(bf16[416,384]{1,0:T(8,128)(2,1)S(1)} %add_convert_fusion.4), channel_id=1, source_target_pairs={{0,2},{1,3},{4,0},{5,1},{8,4},{9,5},{12,8},{13,9},{14,12},{15,13},... | collective-permute-start | bytes 958472 | tf_op jit(solution)/shard_map/ppermute | solution.py:422
  56.0 0.1 add_convert_fusion.6
  56.1 0.0 copy-start
  56.1 0.3 collective-permute-start.7
  56.4 1.7 %blocks3b.1 = (f32[416,384]{1,0:T(8,128)S(1)}, f32[416,384]{1,0:T(8,128)S(1)}) custom-call(s32[16,10]{1,0:T(8,128)S(1)} %copy-done.1, bf16[3072,768]{1,0:T(8,128)(2,1)S(1)} %merge_second.1.turned_ref, bf16[768,1536]{1,0:T(8,128)(2,1)S(1)} %get-tuple-element.34.mine_ref, bf16[416,384]{1,0:T(8,128)(2,1)S(1)} %collective-permute-done.5.refs_0_), custom_call_target="tpu_custom_call" | custom-call | flops 226492416 | tf_op jit(solution)/shard_map/blocks3b/pallas_call | solution.py:224
  58.2 4.2 %collective-permute-done.12.right1 = bf16[416,384]{1,0:T(8,128)(2,1)S(1)} collective-permute-done((bf16[416,384]{1,0:T(8,128)(2,1)S(1)}, bf16[416,384]{1,0:T(8,128)(2,1)S(1)}, u32[]{:S(2)}, u32[]{:S(2)}) %collective-permute-start.12) | collective-permute-done | bytes 319520 | tf_op jit(solution)/shard_map/ppermute | solution.py:422
  62.4 6.0 %collective-permute-done.9.left1 = bf16[416,384]{1,0:T(8,128)(2,1)S(1)} collective-permute-done((bf16[416,384]{1,0:T(8,128)(2,1)S(1)}, bf16[416,384]{1,0:T(8,128)(2,1)S(1)}, u32[]{:S(2)}, u32[]{:S(2)}) %collective-permute-start.9) | collective-permute-done | bytes 319520 | tf_op jit(solution)/shard_map/ppermute | solution.py:422
  68.4 0.1 outgoing_one.1.after
  68.5 4.1 %collective-permute-start.17 = (bf16[384,384]{1,0:T(8,128)(2,1)S(1)}, bf16[384,384]{1,0:T(8,128)(2,1)S(1)}, u32[]{:S(2)}, u32[]{:S(2)}) collective-permute-start(bf16[384,384]{1,0:T(8,128)(2,1)S(1)} %outgoing_one.1.after), channel_id=1, source_target_pairs={{0,2},{1,10},{2,4},{3,12},{4,6},{5,14},{6,0},{7,8},{8,5},{9,11},{1... | collective-permute-start | bytes 884744 | tf_op jit(solution)/shard_map/ppermute | solution.py:474
  72.7 0.9 %outgoing_other.1 = (bf16[320,384]{1,0:T(8,128)(2,1)S(1)}, f32[192,384]{1,0:T(8,128)S(1)}) custom-call(s32[16,5]{1,0:T(8,128)S(1)} %copy-done, f32[416,384]{1,0:T(8,128)S(1)} %get-tuple-element.41.own0, f32[416,384]{1,0:T(8,128)S(1)} %get-tuple-element.42.own1, bf16[416,384]{1,0:T(8,128)(2,1)S(1)} %collective-permute-done.7.right0, ...), custom_call_target="tpu_custom_call" | custom-call | tf_op jit(solution)/shard_map/outgoing_other/pallas_call | solution.py:463
  73.5 0.1 collective-permute-start.16
  73.6 1.8 %own.1.result_ref = f32[384,1536]{1,0:T(8,128)} custom-call(s32[16,5]{1,0:T(8,128)S(1)} %copy-done, f32[416,384]{1,0:T(8,128)S(1)} %get-tuple-element.41.own0, f32[416,384]{1,0:T(8,128)S(1)} %get-tuple-element.42.own1, bf16[416,384]{1,0:T(8,128)(2,1)S(1)} %collective-permute-done.7.right0, bf16[416,384]{1,0:T(8,128)(2,1)S(1)} %collective-permute-done.9.left1, ...), custom_call_target="tpu_custom_call" | custom-call | tf_op jit(solution)/shard_map/own/pallas_call | solution.py:476
  75.4 3.7 %collective-permute-done.17.one = bf16[384,384]{1,0:T(8,128)(2,1)S(1)} collective-permute-done((bf16[384,384]{1,0:T(8,128)(2,1)S(1)}, bf16[384,384]{1,0:T(8,128)(2,1)S(1)}, u32[]{:S(2)}, u32[]{:S(2)}) %collective-permute-start.17) | collective-permute-done | bytes 294944 | tf_op jit(solution)/shard_map/ppermute | solution.py:474
  79.1 1.7 %one.1.result_ref = f32[384,1536]{1,0:T(8,128)} custom-call(s32[16,5]{1,0:T(8,128)S(1)} %copy-done, bf16[384,384]{1,0:T(8,128)(2,1)S(1)} %collective-permute-done.17.one, f32[384,1536]{1,0:T(8,128)} %own.1.result_ref), custom_call_target="tpu_custom_call", output_to_operand_aliasing={{}: (2, {})} | custom-call | tf_op jit(solution)/shard_map/one/pallas_call | solution.py:486
  80.7 4.7 %collective-permute-done.16.other = bf16[320,384]{1,0:T(8,128)(2,1)S(1)} collective-permute-done((bf16[320,384]{1,0:T(8,128)(2,1)S(1)}, bf16[320,384]{1,0:T(8,128)(2,1)S(1)}, u32[]{:S(2)}, u32[]{:S(2)}) %collective-permute-start.16) | collective-permute-done | bytes 245792 | tf_op jit(solution)/shard_map/ppermute | solution.py:475
  85.5 1.6 %other.1 = f32[384,1536]{1,0:T(8,128)} custom-call(s32[16,5]{1,0:T(8,128)S(1)} %copy-done, f32[192,384]{1,0:T(8,128)S(1)} %get-tuple-element.51.share, bf16[320,384]{1,0:T(8,128)(2,1)S(1)} %collective-permute-done.16.other, f32[384,1536]{1,0:T(8,128)} %one.1.result_ref), custom_call_target="tpu_custom_call", output_to_operand_aliasing={{}: (3, {})} | custom-call | tf_op jit(solution)/shard_map/other/pallas_call | solution.py:486
  (17 shorter events, 0.0 us)
Async XLA Ops:
  5.2 4.6 %collective-permute-start.1 = (bf16[768,1536]{1,0:T(8,128)(2,1)S(1)}, bf16[768,1536]{1,0:T(8,128)(2,1)S(1)}, u32[]{:S(2)}, u32[]{:S(2)}) collective-permute-start(bf16[768,1536]{1,0:T(8,128)(2,1)S(1)} %get-tuple-element.30.refs_0_), channel_id=1, source_target_pairs={{0,1},{1,0},{2,3},{3,2},{4,5},{5,4},{6,7},{7,6},{8,9},{9,8},{10,11... | collective-permute-start | bytes 7077896 | tf_op jit(solution)/shard_map/ppermute | solution.py:507
  9.2 4.7 %collective-permute-start = (bf16[768,1536]{1,0:T(8,128)(2,1)S(1)}, bf16[768,1536]{1,0:T(8,128)(2,1)S(1)}, u32[]{:S(2)}, u32[]{:S(2)}) collective-permute-start(bf16[768,1536]{1,0:T(8,128)(2,1)S(1)} %pick_second.1.refs_0_), channel_id=1, source_target_pairs={{0,1},{1,0},{2,3},{3,2},{4,5},{5,4},{6,7},{7,6},{8,9},{9,8},{10,11... | collective-permute-start | bytes 7077896 | tf_op jit(solution)/shard_map/ppermute | solution.py:509
  13.9 1.1 %copy-start.8 = (s32[16,10]{1,0:T(8,128)S(1)}, s32[16,10]{1,0:T(8,128)}, u32[]{:S(2)}) copy-start(s32[16,10]{1,0:T(8,128)} %constant.18.clone.table) | copy-start | bytes 1924
  15.1 4.5 %copy-start.7 = (s32[16,10]{1,0:T(8,128)S(1)}, s32[16,10]{1,0:T(8,128)}, u32[]{:S(2)}) copy-start(s32[16,10]{1,0:T(8,128)} %constant.19.clone.table) | copy-start | bytes 1924
  16.8 10.5 %collective-permute-start.4 = (bf16[416,384]{1,0:T(8,128)(2,1)S(1)}, bf16[416,384]{1,0:T(8,128)(2,1)S(1)}, u32[]{:S(2)}, u32[]{:S(2)}) collective-permute-start(bf16[416,384]{1,0:T(8,128)(2,1)S(1)} %get-tuple-element.39), channel_id=1, source_target_pairs={{0,2},{1,3},{4,0},{5,1},{8,4},{9,5},{12,8},{13,9},{14,12},{15,13},... | collective-permute-start | bytes 958472 | tf_op jit(solution)/shard_map/ppermute | solution.py:422
  19.5 3.4 %copy-start.6 = (s32[16,10]{1,0:T(8,128)S(1)}, s32[16,10]{1,0:T(8,128)}, u32[]{:S(2)}) copy-start(s32[16,10]{1,0:T(8,128)} %constant.20.clone.table) | copy-start | bytes 1924
  19.5 9.1 %collective-permute-start.2 = (bf16[416,384]{1,0:T(8,128)(2,1)S(1)}, bf16[416,384]{1,0:T(8,128)(2,1)S(1)}, u32[]{:S(2)}, u32[]{:S(2)}) collective-permute-start(bf16[416,384]{1,0:T(8,128)(2,1)S(1)} %get-tuple-element.35.refs_0_), channel_id=1, source_target_pairs={{0,4},{1,5},{4,8},{5,9},{8,12},{9,13},{12,14},{13,15},{14,10},{15,... | collective-permute-start | bytes 958472 | tf_op jit(solution)/shard_map/ppermute | solution.py:422
  21.3 14.1 %collective-permute-start.10 = (bf16[416,384]{1,0:T(8,128)(2,1)S(1)}, bf16[416,384]{1,0:T(8,128)(2,1)S(1)}, u32[]{:S(2)}, u32[]{:S(2)}) collective-permute-start(bf16[416,384]{1,0:T(8,128)(2,1)S(1)} %get-tuple-element.48), channel_id=1, source_target_pairs={{0,4},{1,5},{4,8},{5,9},{8,12},{9,13},{12,14},{13,15},{14,10},{15,... | collective-permute-start | bytes 958472 | tf_op jit(solution)/shard_map/ppermute | solution.py:422
  22.8 11.4 %collective-permute-start.13 = (bf16[416,384]{1,0:T(8,128)(2,1)S(1)}, bf16[416,384]{1,0:T(8,128)(2,1)S(1)}, u32[]{:S(2)}, u32[]{:S(2)}) collective-permute-start(bf16[416,384]{1,0:T(8,128)(2,1)S(1)} %get-tuple-element.36.refs_0_), channel_id=1, source_target_pairs={{0,2},{1,3},{4,0},{5,1},{8,4},{9,5},{12,8},{13,9},{14,12},{15,13},... | collective-permute-start | bytes 958472 | tf_op jit(solution)/shard_map/ppermute | solution.py:422
  24.8 4.2 %copy-start.5 = (s32[16,10]{1,0:T(8,128)S(1)}, s32[16,10]{1,0:T(8,128)}, u32[]{:S(2)}) copy-start(s32[16,10]{1,0:T(8,128)} %constant.21.clone.table) | copy-start | bytes 1924
  27.4 13.6 %collective-permute-start.6 = (bf16[416,384]{1,0:T(8,128)(2,1)S(1)}, bf16[416,384]{1,0:T(8,128)(2,1)S(1)}, u32[]{:S(2)}, u32[]{:S(2)}) collective-permute-start(bf16[416,384]{1,0:T(8,128)(2,1)S(1)} %add_convert_fusion.7), channel_id=1, source_target_pairs={{0,2},{1,3},{4,0},{5,1},{8,4},{9,5},{12,8},{13,9},{14,12},{15,13},... | collective-permute-start | bytes 958472 | tf_op jit(solution)/shard_map/ppermute | solution.py:422
  28.7 13.6 %collective-permute-start.3 = (bf16[416,384]{1,0:T(8,128)(2,1)S(1)}, bf16[416,384]{1,0:T(8,128)(2,1)S(1)}, u32[]{:S(2)}, u32[]{:S(2)}) collective-permute-start(bf16[416,384]{1,0:T(8,128)(2,1)S(1)} %add_convert_fusion.9), channel_id=1, source_target_pairs={{0,4},{1,5},{4,8},{5,9},{8,12},{9,13},{12,14},{13,15},{14,10},{15,... | collective-permute-start | bytes 958472 | tf_op jit(solution)/shard_map/ppermute | solution.py:422
  30.7 5.1 %copy-start.4 = (s32[16,10]{1,0:T(8,128)S(1)}, s32[16,10]{1,0:T(8,128)}, u32[]{:S(2)}) copy-start(s32[16,10]{1,0:T(8,128)} %constant.22.clone.table) | copy-start | bytes 1924
  34.2 13.6 %collective-permute-start.14 = (bf16[416,384]{1,0:T(8,128)(2,1)S(1)}, bf16[416,384]{1,0:T(8,128)(2,1)S(1)}, u32[]{:S(2)}, u32[]{:S(2)}) collective-permute-start(bf16[416,384]{1,0:T(8,128)(2,1)S(1)} %add_convert_fusion.1), channel_id=1, source_target_pairs={{0,2},{1,3},{4,0},{5,1},{8,4},{9,5},{12,8},{13,9},{14,12},{15,13},... | collective-permute-start | bytes 958472 | tf_op jit(solution)/shard_map/ppermute | solution.py:422
  35.5 13.6 %collective-permute-start.11 = (bf16[416,384]{1,0:T(8,128)(2,1)S(1)}, bf16[416,384]{1,0:T(8,128)(2,1)S(1)}, u32[]{:S(2)}, u32[]{:S(2)}) collective-permute-start(bf16[416,384]{1,0:T(8,128)(2,1)S(1)} %add_convert_fusion.3), channel_id=1, source_target_pairs={{0,4},{1,5},{4,8},{5,9},{8,12},{9,13},{12,14},{13,15},{14,10},{15,... | collective-permute-start | bytes 958472 | tf_op jit(solution)/shard_map/ppermute | solution.py:422
  37.6 5.1 %copy-start.3 = (s32[16,10]{1,0:T(8,128)S(1)}, s32[16,10]{1,0:T(8,128)}, u32[]{:S(2)}) copy-start(s32[16,10]{1,0:T(8,128)} %constant.23.clone.table) | copy-start | bytes 1924
  41.1 13.6 %collective-permute-start.8 = (bf16[416,384]{1,0:T(8,128)(2,1)S(1)}, bf16[416,384]{1,0:T(8,128)(2,1)S(1)}, u32[]{:S(2)}, u32[]{:S(2)}) collective-permute-start(bf16[416,384]{1,0:T(8,128)(2,1)S(1)} %add_convert_fusion.5), channel_id=1, source_target_pairs={{0,2},{1,3},{4,0},{5,1},{8,4},{9,5},{12,8},{13,9},{14,12},{15,13},... | collective-permute-start | bytes 958472 | tf_op jit(solution)/shard_map/ppermute | solution.py:422
  42.4 13.6 %collective-permute-start.5 = (bf16[416,384]{1,0:T(8,128)(2,1)S(1)}, bf16[416,384]{1,0:T(8,128)(2,1)S(1)}, u32[]{:S(2)}, u32[]{:S(2)}) collective-permute-start(bf16[416,384]{1,0:T(8,128)(2,1)S(1)} %add_convert_fusion.8), channel_id=1, source_target_pairs={{0,4},{1,5},{4,8},{5,9},{8,12},{9,13},{12,14},{13,15},{14,10},{15,... | collective-permute-start | bytes 958472 | tf_op jit(solution)/shard_map/ppermute | solution.py:422
  44.4 5.1 %copy-start.2 = (s32[16,10]{1,0:T(8,128)S(1)}, s32[16,10]{1,0:T(8,128)}, u32[]{:S(2)}) copy-start(s32[16,10]{1,0:T(8,128)} %constant.24.clone.table) | copy-start | bytes 1924
  47.9 24.7 %collective-permute-start.15 = (bf16[416,384]{1,0:T(8,128)(2,1)S(1)}, bf16[416,384]{1,0:T(8,128)(2,1)S(1)}, u32[]{:S(2)}, u32[]{:S(2)}) collective-permute-start(bf16[416,384]{1,0:T(8,128)(2,1)S(1)} %add_convert_fusion), channel_id=1, source_target_pairs={{0,2},{1,3},{4,0},{5,1},{8,4},{9,5},{12,8},{13,9},{14,12},{15,13},... | collective-permute-start | bytes 958472 | tf_op jit(solution)/shard_map/ppermute | solution.py:422
  49.2 13.2 %collective-permute-start.12 = (bf16[416,384]{1,0:T(8,128)(2,1)S(1)}, bf16[416,384]{1,0:T(8,128)(2,1)S(1)}, u32[]{:S(2)}, u32[]{:S(2)}) collective-permute-start(bf16[416,384]{1,0:T(8,128)(2,1)S(1)} %add_convert_fusion.2), channel_id=1, source_target_pairs={{0,4},{1,5},{4,8},{5,9},{8,12},{9,13},{12,14},{13,15},{14,10},{15,... | collective-permute-start | bytes 958472 | tf_op jit(solution)/shard_map/ppermute | solution.py:422
  51.3 5.1 %copy-start.1 = (s32[16,10]{1,0:T(8,128)S(1)}, s32[16,10]{1,0:T(8,128)}, u32[]{:S(2)}) copy-start(s32[16,10]{1,0:T(8,128)} %constant.25.clone.table) | copy-start | bytes 1924
  54.8 13.6 %collective-permute-start.9 = (bf16[416,384]{1,0:T(8,128)(2,1)S(1)}, bf16[416,384]{1,0:T(8,128)(2,1)S(1)}, u32[]{:S(2)}, u32[]{:S(2)}) collective-permute-start(bf16[416,384]{1,0:T(8,128)(2,1)S(1)} %add_convert_fusion.4), channel_id=1, source_target_pairs={{0,2},{1,3},{4,0},{5,1},{8,4},{9,5},{12,8},{13,9},{14,12},{15,13},... | collective-permute-start | bytes 958472 | tf_op jit(solution)/shard_map/ppermute | solution.py:422
  56.1 16.6 %copy-start = (s32[16,5]{1,0:T(8,128)S(1)}, s32[16,5]{1,0:T(8,128)}, u32[]{:S(2)}) copy-start(s32[16,5]{1,0:T(8,128)} %constant.26.clone.place) | copy-start | bytes 964
  56.1 16.6 %collective-permute-start.7 = (bf16[416,384]{1,0:T(8,128)(2,1)S(1)}, bf16[416,384]{1,0:T(8,128)(2,1)S(1)}, u32[]{:S(2)}, u32[]{:S(2)}) collective-permute-start(bf16[416,384]{1,0:T(8,128)(2,1)S(1)} %add_convert_fusion.6), channel_id=1, source_target_pairs={{0,4},{1,5},{4,8},{5,9},{8,12},{9,13},{12,14},{13,15},{14,10},{15,... | collective-permute-start | bytes 958472 | tf_op jit(solution)/shard_map/ppermute | solution.py:422
  68.5 10.6 %collective-permute-start.17 = (bf16[384,384]{1,0:T(8,128)(2,1)S(1)}, bf16[384,384]{1,0:T(8,128)(2,1)S(1)}, u32[]{:S(2)}, u32[]{:S(2)}) collective-permute-start(bf16[384,384]{1,0:T(8,128)(2,1)S(1)} %outgoing_one.1.after), channel_id=1, source_target_pairs={{0,2},{1,10},{2,4},{3,12},{4,6},{5,14},{6,0},{7,8},{8,5},{9,11},{1... | collective-permute-start | bytes 884744 | tf_op jit(solution)/shard_map/ppermute | solution.py:474
  73.5 11.9 %collective-permute-start.16 = (bf16[320,384]{1,0:T(8,128)(2,1)S(1)}, bf16[320,384]{1,0:T(8,128)(2,1)S(1)}, u32[]{:S(2)}, u32[]{:S(2)}) collective-permute-start(bf16[320,384]{1,0:T(8,128)(2,1)S(1)} %get-tuple-element.52), channel_id=1, source_target_pairs={{0,4},{1,8},{2,6},{3,10},{4,0},{5,12},{6,2},{7,14},{8,3},{9,13},{1... | collective-permute-start | bytes 737288 | tf_op jit(solution)/shard_map/ppermute | solution.py:475

commit v15 on v14

--- a/solution.py
+++ b/solution.py
@@ -380,7 +380,7 @@
 
 def one_kernel(place, one, result_ref, out_ref, made, sem):
     made[...] = one[...].astype(F32).T
-    copy = put(place, 2, made, out_ref, sem)
+    copy = put(place, 2, made, out_ref, sem.at[0])
     copy.start()
     copy.wait()
 
@@ -392,20 +392,35 @@
     @pl.when(kind == 0)
     def _():
         made[: 2 * STRIP, :] = share[: 2 * STRIP, :]
-        made[2 * STRIP :, :] = other[...].astype(F32)
+        made[2 * STRIP : half, :] = other[: half - 2 * STRIP, :].astype(F32)
 
     @pl.when(kind == 1)
     def _():
         made[:half, :] = share[...]
+
+    @pl.when(kind == 2)
+    def _():
+        made[...] = jnp.concatenate([other[:half, :].astype(F32), share[...]], axis=0).T
+
+    width = made.shape[0]
+    at = pl.ds(pl.multiple_of(place[my_row(), 3] * width, 128), width)
+    copies = [
+        pltpu.make_async_copy(made.at[rows], out_ref.at[rows, at], sem.at[n])
+        for n, rows in enumerate((slice(0, half), slice(half, width)))
+    ]
+    copies[0].start()
+
+    @pl.when(kind == 0)
+    def _():
+        made[half:, :] = other[half - 2 * STRIP :, :].astype(F32)
+
+    @pl.when(kind == 1)
+    def _():
         made[half:, :] = other[:half, :].astype(F32)
 
-    @pl.when(kind == 2)
-    def _():
-        made[...] = jnp.concatenate([other[:half, :].astype(F32), share[...]], axis=0).T
-
-    copy = put(place, 3, made, out_ref, sem)
-    copy.start()
-    copy.wait()
+    copies[1].start()
+    for copy in copies:
+        copy.wait()
 
 
 def symmetric_moment(mine, turned, total_tokens):
@@ -488,7 +503,7 @@
             out_shape=result,
             in_specs=[smem] + [vmem] * len(args) + [any_],
             out_specs=any_,
-            scratch_shapes=[pltpu.VMEM((width, width), F32), pltpu.SemaphoreType.DMA],
+            scratch_shapes=[pltpu.VMEM((width, width), F32), pltpu.SemaphoreType.DMA((2,))],
             input_output_aliases={len(args) + 1: 0},
             compiler_params=params,
             name=name,

time: 87.4 us -> 87.4 us (level)
  no operation moved by 1% of the time
where the time goes in v15:
time: 87.4 us; the launch traced here: 87.2 us
  waiting for transfers between devices  37.6 us (43%)
  Pallas kernels  31.4 us (36%)
  starting transfers between devices  17 us (19%)
    ppermute x14, waiting for transfers between devices, hop(): lax.ppermute(value, both, ring_perm(1 if key[1] <= (4 if key[0] == 0 else...  26.3 us
    pallas_call x8, Pallas kernels, moment_blocks(): pl.pallas_call(functools.partial(blocks_kernel, pieces, width), out_shape...  14 us
    ppermute x14, starting transfers between devices, hop(): lax.ppermute(value, both, ring_perm(1 if key[1] <= (4 if key[0] == 0 else...  12.2 us
    pallas_call x2, Pallas kernels, pick_half(): pl.pallas_call(functools.partial(pick_kernel, first), out_shape=out_shape...  9.1 us
    ppermute x1, waiting for transfers between devices, symmetric_moment(): other = lax.ppermute(other, both, perm_other)  4.73 us
    ppermute x1, starting transfers between devices, symmetric_moment(): one = lax.ppermute(one, both, perm_one)  4.15 us
    ppermute x1, waiting for transfers between devices, symmetric_moment(): one = lax.ppermute(one, both, perm_one)  3.66 us
    pallas_call x2, Pallas kernels, symmetric_moment(): pl.pallas_call(kernel, out_shape=result, in_specs=[smem] + [vmem] * len(a...  3.21 us
  transfers between devices with their start and end apart: 18, of which 10 were waited for; matrix products, arithmetic and copies ran while one was open for 1% of the time, Pallas kernels for 25%

profile of v15, /device:TPU:1, one launch (start us, length us, event | category | flops | bytes accessed | tf_op | source)
XLA Modules:
  0.0 87.2 jit_solution(276927909632805698)
XLA Ops:
  0.0 5.2 %pick_first.1 = (bf16[768,1536]{1,0:T(8,128)(2,1)S(1)}, bf16[1536,256]{1,0:T(8,128)(2,1)S(1)}, s32[16,128]{1,0:T(8,128)S(1)}, f32[768,8]{1,0:T(8,128)S(1)}) custom-call(s32[2,768]{1,0:T(2,128)} %bitcast.2, f32[2,768]{1,0:T(2,128)} %bitcast.3, bf16[1536,3072]{1,0:T(8,128)(2,1)} %refs_3_.1), custom_call_target="tpu_custom_call" | custom-call | flops 1207959552 | bytes 7077888 | tf_op jit(solution)/shard_map/pick_first/pallas_call | solution.py:136
  5.2 0.1 collective-permute-start.1
  5.3 3.9 %pick_second.1.refs_0_ = bf16[768,1536]{1,0:T(8,128)(2,1)S(1)} custom-call(s32[16,128]{1,0:T(8,128)S(1)} %get-tuple-element.31.refs_0_, bf16[1536,256]{1,0:T(8,128)(2,1)S(1)} %get-tuple-element.32.refs_1_, f32[768,8]{1,0:T(8,128)S(1)} %get-tuple-element.29.refs_2_.coef_ref, bf16[1536,3072]{1,0:T(8,128)(2,1)} %refs_3_.1), custom_call_target="tpu_custom_call" | custom-call | flops 1207959552 | bytes 7077888 | tf_op jit(solution)/shard_map/pick_second/pallas_call | solution.py:136
  9.2 0.5 collective-permute-start
  9.8 0.0 collective-permute-done.1.refs_1_
  9.8 1.2 %merge_first.1 = (bf16[768,1536]{1,0:T(8,128)(2,1)S(1)}, bf16[3072,768]{1,0:T(8,128)(2,1)S(1)}) custom-call(f32[768,8]{1,0:T(8,128)S(1)} %get-tuple-element.29.refs_2_.coef_ref, bf16[768,1536]{1,0:T(8,128)(2,1)S(1)} %pick_second.1.refs_0_, bf16[768,1536]{1,0:T(8,128)(2,1)S(1)} %collective-permute-done.1.refs_1_), custom_call_target="tpu_custom_call" | custom-call | flops 4718592 | tf_op jit(solution)/shard_map/merge_first/pallas_call | solution.py:176
  11.0 2.9 %collective-permute-done.refs_1_ = bf16[768,1536]{1,0:T(8,128)(2,1)S(1)} collective-permute-done((bf16[768,1536]{1,0:T(8,128)(2,1)S(1)}, bf16[768,1536]{1,0:T(8,128)(2,1)S(1)}, u32[]{:S(2)}, u32[]{:S(2)}) %collective-permute-start) | collective-permute-done | bytes 2359328 | tf_op jit(solution)/shard_map/ppermute | solution.py:524
  13.9 1.1 %merge_second.1.turned_ref = bf16[3072,768]{1,0:T(8,128)(2,1)S(1)} custom-call(f32[768,8]{1,0:T(8,128)S(1)} %get-tuple-element.29.refs_2_.coef_ref, bf16[768,1536]{1,0:T(8,128)(2,1)S(1)} %get-tuple-element.30.refs_0_, bf16[768,1536]{1,0:T(8,128)(2,1)S(1)} %collective-permute-done.refs_1_, ...), custom_call_target="tpu_custom_call", output_to_operand_aliasing={{}: (3, {})} | custom-call | flops 4718592 | tf_op jit(solution)/shard_map/merge_second/pallas_call | solution.py:176
  15.1 0.0 copy-start.7
  15.1 1.7 %blocks0.1 = (bf16[416,384]{1,0:T(8,128)(2,1)S(1)}, bf16[416,384]{1,0:T(8,128)(2,1)S(1)}) custom-call(s32[16,10]{1,0:T(8,128)S(1)} %copy-done.8, bf16[3072,768]{1,0:T(8,128)(2,1)S(1)} %merge_second.1.turned_ref, bf16[768,1536]{1,0:T(8,128)(2,1)S(1)} %get-tuple-element.34.mine_ref), custom_call_target="tpu_custom_call" | custom-call | flops 226492416 | tf_op jit(solution)/shard_map/blocks0/pallas_call | solution.py:224
  16.8 2.7 %collective-permute-start.4 = (bf16[416,384]{1,0:T(8,128)(2,1)S(1)}, bf16[416,384]{1,0:T(8,128)(2,1)S(1)}, u32[]{:S(2)}, u32[]{:S(2)}) collective-permute-start(bf16[416,384]{1,0:T(8,128)(2,1)S(1)} %get-tuple-element.39), channel_id=1, source_target_pairs={{0,2},{1,3},{4,0},{5,1},{8,4},{9,5},{12,8},{13,9},{14,12},{15,13},... | collective-permute-start | bytes 958472 | tf_op jit(solution)/shard_map/ppermute | solution.py:437
  19.5 0.1 collective-permute-start.2
  19.6 1.7 %blocks0b.1 = (bf16[416,384]{1,0:T(8,128)(2,1)S(1)}, bf16[416,384]{1,0:T(8,128)(2,1)S(1)}) custom-call(s32[16,10]{1,0:T(8,128)S(1)} %copy-done.7, bf16[3072,768]{1,0:T(8,128)(2,1)S(1)} %merge_second.1.turned_ref, bf16[768,1536]{1,0:T(8,128)(2,1)S(1)} %get-tuple-element.34.mine_ref, bf16[416,384]{1,0:T(8,128)(2,1)S(1)} %get-tuple-element.35.refs_0_), custom_call_target="tpu_custom_call" | custom-call | flops 226492416 | tf_op jit(solution)/shard_map/blocks0b/pallas_call | solution.py:224
  21.3 1.4 %collective-permute-start.10 = (bf16[416,384]{1,0:T(8,128)(2,1)S(1)}, bf16[416,384]{1,0:T(8,128)(2,1)S(1)}, u32[]{:S(2)}, u32[]{:S(2)}) collective-permute-start(bf16[416,384]{1,0:T(8,128)(2,1)S(1)} %get-tuple-element.48), channel_id=1, source_target_pairs={{0,4},{1,5},{4,8},{5,9},{8,12},{9,13},{12,14},{13,15},{14,10},{15,... | collective-permute-start | bytes 958472 | tf_op jit(solution)/shard_map/ppermute | solution.py:437
  22.8 0.1 collective-permute-start.13
  22.9 1.9 %blocks1.1 = (f32[416,384]{1,0:T(8,128)S(1)}, f32[416,384]{1,0:T(8,128)S(1)}) custom-call(s32[16,10]{1,0:T(8,128)S(1)} %copy-done.6, bf16[3072,768]{1,0:T(8,128)(2,1)S(1)} %merge_second.1.turned_ref, bf16[768,1536]{1,0:T(8,128)(2,1)S(1)} %get-tuple-element.34.mine_ref, bf16[416,384]{1,0:T(8,128)(2,1)S(1)} %get-tuple-element.36.refs_0_), custom_call_target="tpu_custom_call" | custom-call | flops 226492416 | tf_op jit(solution)/shard_map/blocks1/pallas_call | solution.py:224
  24.8 0.0 copy-start.5
  24.8 2.5 %collective-permute-done.4.refs_2_ = bf16[416,384]{1,0:T(8,128)(2,1)S(1)} collective-permute-done((bf16[416,384]{1,0:T(8,128)(2,1)S(1)}, bf16[416,384]{1,0:T(8,128)(2,1)S(1)}, u32[]{:S(2)}, u32[]{:S(2)}) %collective-permute-start.4) | collective-permute-done | bytes 319520 | tf_op jit(solution)/shard_map/ppermute | solution.py:437
  27.3 0.1 add_convert_fusion.7
  27.4 1.2 %collective-permute-start.6 = (bf16[416,384]{1,0:T(8,128)(2,1)S(1)}, bf16[416,384]{1,0:T(8,128)(2,1)S(1)}, u32[]{:S(2)}, u32[]{:S(2)}) collective-permute-start(bf16[416,384]{1,0:T(8,128)(2,1)S(1)} %add_convert_fusion.7), channel_id=1, source_target_pairs={{0,2},{1,3},{4,0},{5,1},{8,4},{9,5},{12,8},{13,9},{14,12},{15,13},... | collective-permute-start | bytes 958472 | tf_op jit(solution)/shard_map/ppermute | solution.py:437
  28.6 0.0 collective-permute-done.2.refs_0_.refs_1_
  28.6 0.1 add_convert_fusion.9
  28.7 0.3 collective-permute-start.3
  29.0 1.7 %blocks1b.1 = (f32[416,384]{1,0:T(8,128)S(1)}, f32[416,384]{1,0:T(8,128)S(1)}) custom-call(s32[16,10]{1,0:T(8,128)S(1)} %copy-done.5, bf16[3072,768]{1,0:T(8,128)(2,1)S(1)} %merge_second.1.turned_ref, bf16[768,1536]{1,0:T(8,128)(2,1)S(1)} %get-tuple-element.34.mine_ref, bf16[416,384]{1,0:T(8,128)(2,1)S(1)} %collective-permute-done.2.refs_0_.refs_1_), custom_call_target="tpu_custom_call" | custom-call | flops 226492416 | tf_op jit(solution)/shard_map/blocks1b/pallas_call | solution.py:224
  30.7 0.0 copy-start.4
  30.8 3.4 %collective-permute-done.13 = bf16[416,384]{1,0:T(8,128)(2,1)S(1)} collective-permute-done((bf16[416,384]{1,0:T(8,128)(2,1)S(1)}, bf16[416,384]{1,0:T(8,128)(2,1)S(1)}, u32[]{:S(2)}, u32[]{:S(2)}) %collective-permute-start.13) | collective-permute-done | bytes 319520 | tf_op jit(solution)/shard_map/ppermute | solution.py:437
  34.1 0.1 add_convert_fusion.1
  34.2 1.2 %collective-permute-start.14 = (bf16[416,384]{1,0:T(8,128)(2,1)S(1)}, bf16[416,384]{1,0:T(8,128)(2,1)S(1)}, u32[]{:S(2)}, u32[]{:S(2)}) collective-permute-start(bf16[416,384]{1,0:T(8,128)(2,1)S(1)} %add_convert_fusion.1), channel_id=1, source_target_pairs={{0,2},{1,3},{4,0},{5,1},{8,4},{9,5},{12,8},{13,9},{14,12},{15,13},... | collective-permute-start | bytes 958472 | tf_op jit(solution)/shard_map/ppermute | solution.py:437
  35.5 0.1 add_convert_fusion.3
  35.5 0.3 collective-permute-start.11
  35.9 1.7 %blocks2.1 = (f32[416,384]{1,0:T(8,128)S(1)}, f32[416,384]{1,0:T(8,128)S(1)}) custom-call(s32[16,10]{1,0:T(8,128)S(1)} %copy-done.4, bf16[3072,768]{1,0:T(8,128)(2,1)S(1)} %merge_second.1.turned_ref, bf16[768,1536]{1,0:T(8,128)(2,1)S(1)} %get-tuple-element.34.mine_ref, f32[416,384]{1,0:T(8,128)S(1)} %get-tuple-element.38.refs_0_, ...), custom_call_target="tpu_custom_call" | custom-call | flops 226492416 | tf_op jit(solution)/shard_map/blocks2/pallas_call | solution.py:224
  37.6 0.0 copy-start.3
  37.6 3.4 %collective-permute-done.6.refs_2_ = bf16[416,384]{1,0:T(8,128)(2,1)S(1)} collective-permute-done((bf16[416,384]{1,0:T(8,128)(2,1)S(1)}, bf16[416,384]{1,0:T(8,128)(2,1)S(1)}, u32[]{:S(2)}, u32[]{:S(2)}) %collective-permute-start.6) | collective-permute-done | bytes 319520 | tf_op jit(solution)/shard_map/ppermute | solution.py:437
  41.0 0.1 add_convert_fusion.5
  41.1 1.2 %collective-permute-start.8 = (bf16[416,384]{1,0:T(8,128)(2,1)S(1)}, bf16[416,384]{1,0:T(8,128)(2,1)S(1)}, u32[]{:S(2)}, u32[]{:S(2)}) collective-permute-start(bf16[416,384]{1,0:T(8,128)(2,1)S(1)} %add_convert_fusion.5), channel_id=1, source_target_pairs={{0,2},{1,3},{4,0},{5,1},{8,4},{9,5},{12,8},{13,9},{14,12},{15,13},... | collective-permute-start | bytes 958472 | tf_op jit(solution)/shard_map/ppermute | solution.py:437
  42.3 0.1 add_convert_fusion.8
  42.4 0.3 collective-permute-start.5
  42.7 1.7 %blocks2b.1 = (f32[416,384]{1,0:T(8,128)S(1)}, f32[416,384]{1,0:T(8,128)S(1)}) custom-call(s32[16,10]{1,0:T(8,128)S(1)} %copy-done.3, bf16[3072,768]{1,0:T(8,128)(2,1)S(1)} %merge_second.1.turned_ref, bf16[768,1536]{1,0:T(8,128)(2,1)S(1)} %get-tuple-element.34.mine_ref, bf16[416,384]{1,0:T(8,128)(2,1)S(1)} %collective-permute-done.3.refs_0_.refs_1_), custom_call_target="tpu_custom_call" | custom-call | flops 226492416 | tf_op jit(solution)/shard_map/blocks2b/pallas_call | solution.py:224
  44.4 0.0 copy-start.2
  44.5 3.4 %collective-permute-done.14 = bf16[416,384]{1,0:T(8,128)(2,1)S(1)} collective-permute-done((bf16[416,384]{1,0:T(8,128)(2,1)S(1)}, bf16[416,384]{1,0:T(8,128)(2,1)S(1)}, u32[]{:S(2)}, u32[]{:S(2)}) %collective-permute-start.14) | collective-permute-done | bytes 319520 | tf_op jit(solution)/shard_map/ppermute | solution.py:437
  47.8 0.1 add_convert_fusion
  47.9 1.2 %collective-permute-start.15 = (bf16[416,384]{1,0:T(8,128)(2,1)S(1)}, bf16[416,384]{1,0:T(8,128)(2,1)S(1)}, u32[]{:S(2)}, u32[]{:S(2)}) collective-permute-start(bf16[416,384]{1,0:T(8,128)(2,1)S(1)} %add_convert_fusion), channel_id=1, source_target_pairs={{0,2},{1,3},{4,0},{5,1},{8,4},{9,5},{12,8},{13,9},{14,12},{15,13},... | collective-permute-start | bytes 958472 | tf_op jit(solution)/shard_map/ppermute | solution.py:437
  49.1 0.1 add_convert_fusion.2
  49.2 0.3 collective-permute-start.12
  49.6 1.7 %blocks3.1 = (f32[416,384]{1,0:T(8,128)S(1)}, f32[416,384]{1,0:T(8,128)S(1)}) custom-call(s32[16,10]{1,0:T(8,128)S(1)} %copy-done.2, bf16[3072,768]{1,0:T(8,128)(2,1)S(1)} %merge_second.1.turned_ref, bf16[768,1536]{1,0:T(8,128)(2,1)S(1)} %get-tuple-element.34.mine_ref, f32[416,384]{1,0:T(8,128)S(1)} %get-tuple-element.43.refs_0_, ...), custom_call_target="tpu_custom_call" | custom-call | flops 226492416 | tf_op jit(solution)/shard_map/blocks3/pallas_call | solution.py:224
  51.3 0.0 copy-start.1
  51.3 3.4 %collective-permute-done.8 = bf16[416,384]{1,0:T(8,128)(2,1)S(1)} collective-permute-done((bf16[416,384]{1,0:T(8,128)(2,1)S(1)}, bf16[416,384]{1,0:T(8,128)(2,1)S(1)}, u32[]{:S(2)}, u32[]{:S(2)}) %collective-permute-start.8) | collective-permute-done | bytes 319520 | tf_op jit(solution)/shard_map/ppermute | solution.py:437
  54.7 0.1 add_convert_fusion.4
  54.8 1.2 %collective-permute-start.9 = (bf16[416,384]{1,0:T(8,128)(2,1)S(1)}, bf16[416,384]{1,0:T(8,128)(2,1)S(1)}, u32[]{:S(2)}, u32[]{:S(2)}) collective-permute-start(bf16[416,384]{1,0:T(8,128)(2,1)S(1)} %add_convert_fusion.4), channel_id=1, source_target_pairs={{0,2},{1,3},{4,0},{5,1},{8,4},{9,5},{12,8},{13,9},{14,12},{15,13},... | collective-permute-start | bytes 958472 | tf_op jit(solution)/shard_map/ppermute | solution.py:437
  56.0 0.1 add_convert_fusion.6
  56.1 0.0 copy-start
  56.1 0.3 collective-permute-start.7
  56.4 1.7 %blocks3b.1 = (f32[416,384]{1,0:T(8,128)S(1)}, f32[416,384]{1,0:T(8,128)S(1)}) custom-call(s32[16,10]{1,0:T(8,128)S(1)} %copy-done.1, bf16[3072,768]{1,0:T(8,128)(2,1)S(1)} %merge_second.1.turned_ref, bf16[768,1536]{1,0:T(8,128)(2,1)S(1)} %get-tuple-element.34.mine_ref, bf16[416,384]{1,0:T(8,128)(2,1)S(1)} %collective-permute-done.5.refs_0_), custom_call_target="tpu_custom_call" | custom-call | flops 226492416 | tf_op jit(solution)/shard_map/blocks3b/pallas_call | solution.py:224
  58.2 4.2 %collective-permute-done.12.right1 = bf16[416,384]{1,0:T(8,128)(2,1)S(1)} collective-permute-done((bf16[416,384]{1,0:T(8,128)(2,1)S(1)}, bf16[416,384]{1,0:T(8,128)(2,1)S(1)}, u32[]{:S(2)}, u32[]{:S(2)}) %collective-permute-start.12) | collective-permute-done | bytes 319520 | tf_op jit(solution)/shard_map/ppermute | solution.py:437
  62.4 6.0 %collective-permute-done.9.left1 = bf16[416,384]{1,0:T(8,128)(2,1)S(1)} collective-permute-done((bf16[416,384]{1,0:T(8,128)(2,1)S(1)}, bf16[416,384]{1,0:T(8,128)(2,1)S(1)}, u32[]{:S(2)}, u32[]{:S(2)}) %collective-permute-start.9) | collective-permute-done | bytes 319520 | tf_op jit(solution)/shard_map/ppermute | solution.py:437
  68.4 0.1 outgoing_one.1.after
  68.5 4.1 %collective-permute-start.17 = (bf16[384,384]{1,0:T(8,128)(2,1)S(1)}, bf16[384,384]{1,0:T(8,128)(2,1)S(1)}, u32[]{:S(2)}, u32[]{:S(2)}) collective-permute-start(bf16[384,384]{1,0:T(8,128)(2,1)S(1)} %outgoing_one.1.after), channel_id=1, source_target_pairs={{0,2},{1,10},{2,4},{3,12},{4,6},{5,14},{6,0},{7,8},{8,5},{9,11},{1... | collective-permute-start | bytes 884744 | tf_op jit(solution)/shard_map/ppermute | solution.py:489
  72.7 0.9 %outgoing_other.1 = (bf16[320,384]{1,0:T(8,128)(2,1)S(1)}, f32[192,384]{1,0:T(8,128)S(1)}) custom-call(s32[16,5]{1,0:T(8,128)S(1)} %copy-done, f32[416,384]{1,0:T(8,128)S(1)} %get-tuple-element.41.own0, f32[416,384]{1,0:T(8,128)S(1)} %get-tuple-element.42.own1, bf16[416,384]{1,0:T(8,128)(2,1)S(1)} %collective-permute-done.7.right0, ...), custom_call_target="tpu_custom_call" | custom-call | tf_op jit(solution)/shard_map/outgoing_other/pallas_call | solution.py:478
  73.5 0.1 collective-permute-start.16
  73.6 1.8 %own.1.result_ref = f32[384,1536]{1,0:T(8,128)} custom-call(s32[16,5]{1,0:T(8,128)S(1)} %copy-done, f32[416,384]{1,0:T(8,128)S(1)} %get-tuple-element.41.own0, f32[416,384]{1,0:T(8,128)S(1)} %get-tuple-element.42.own1, bf16[416,384]{1,0:T(8,128)(2,1)S(1)} %collective-permute-done.7.right0, bf16[416,384]{1,0:T(8,128)(2,1)S(1)} %collective-permute-done.9.left1, ...), custom_call_target="tpu_custom_call" | custom-call | tf_op jit(solution)/shard_map/own/pallas_call | solution.py:491
  75.4 3.7 %collective-permute-done.17.one = bf16[384,384]{1,0:T(8,128)(2,1)S(1)} collective-permute-done((bf16[384,384]{1,0:T(8,128)(2,1)S(1)}, bf16[384,384]{1,0:T(8,128)(2,1)S(1)}, u32[]{:S(2)}, u32[]{:S(2)}) %collective-permute-start.17) | collective-permute-done | bytes 294944 | tf_op jit(solution)/shard_map/ppermute | solution.py:489
  79.1 1.7 %one.1.result_ref = f32[384,1536]{1,0:T(8,128)} custom-call(s32[16,5]{1,0:T(8,128)S(1)} %copy-done, bf16[384,384]{1,0:T(8,128)(2,1)S(1)} %collective-permute-done.17.one, f32[384,1536]{1,0:T(8,128)} %own.1.result_ref), custom_call_target="tpu_custom_call", output_to_operand_aliasing={{}: (2, {})} | custom-call | tf_op jit(solution)/shard_map/one/pallas_call | solution.py:501
  80.7 4.7 %collective-permute-done.16.other = bf16[320,384]{1,0:T(8,128)(2,1)S(1)} collective-permute-done((bf16[320,384]{1,0:T(8,128)(2,1)S(1)}, bf16[320,384]{1,0:T(8,128)(2,1)S(1)}, u32[]{:S(2)}, u32[]{:S(2)}) %collective-permute-start.16) | collective-permute-done | bytes 245792 | tf_op jit(solution)/shard_map/ppermute | solution.py:490
  85.5 1.5 %other.1 = f32[384,1536]{1,0:T(8,128)} custom-call(s32[16,5]{1,0:T(8,128)S(1)} %copy-done, f32[192,384]{1,0:T(8,128)S(1)} %get-tuple-element.51.share, bf16[320,384]{1,0:T(8,128)(2,1)S(1)} %collective-permute-done.16.other, f32[384,1536]{1,0:T(8,128)} %one.1.result_ref), custom_call_target="tpu_custom_call", output_to_operand_aliasing={{}: (3, {})} | custom-call | tf_op jit(solution)/shard_map/other/pallas_call | solution.py:501
  (17 shorter events, 0.0 us)
Async XLA Ops:
  5.2 4.6 %collective-permute-start.1 = (bf16[768,1536]{1,0:T(8,128)(2,1)S(1)}, bf16[768,1536]{1,0:T(8,128)(2,1)S(1)}, u32[]{:S(2)}, u32[]{:S(2)}) collective-permute-start(bf16[768,1536]{1,0:T(8,128)(2,1)S(1)} %get-tuple-element.30.refs_0_), channel_id=1, source_target_pairs={{0,1},{1,0},{2,3},{3,2},{4,5},{5,4},{6,7},{7,6},{8,9},{9,8},{10,11... | collective-permute-start | bytes 7077896 | tf_op jit(solution)/shard_map/ppermute | solution.py:522
  9.2 4.7 %collective-permute-start = (bf16[768,1536]{1,0:T(8,128)(2,1)S(1)}, bf16[768,1536]{1,0:T(8,128)(2,1)S(1)}, u32[]{:S(2)}, u32[]{:S(2)}) collective-permute-start(bf16[768,1536]{1,0:T(8,128)(2,1)S(1)} %pick_second.1.refs_0_), channel_id=1, source_target_pairs={{0,1},{1,0},{2,3},{3,2},{4,5},{5,4},{6,7},{7,6},{8,9},{9,8},{10,11... | collective-permute-start | bytes 7077896 | tf_op jit(solution)/shard_map/ppermute | solution.py:524
  13.9 1.1 %copy-start.8 = (s32[16,10]{1,0:T(8,128)S(1)}, s32[16,10]{1,0:T(8,128)}, u32[]{:S(2)}) copy-start(s32[16,10]{1,0:T(8,128)} %constant.18.clone.table) | copy-start | bytes 1924
  15.1 4.5 %copy-start.7 = (s32[16,10]{1,0:T(8,128)S(1)}, s32[16,10]{1,0:T(8,128)}, u32[]{:S(2)}) copy-start(s32[16,10]{1,0:T(8,128)} %constant.19.clone.table) | copy-start | bytes 1924
  16.8 10.5 %collective-permute-start.4 = (bf16[416,384]{1,0:T(8,128)(2,1)S(1)}, bf16[416,384]{1,0:T(8,128)(2,1)S(1)}, u32[]{:S(2)}, u32[]{:S(2)}) collective-permute-start(bf16[416,384]{1,0:T(8,128)(2,1)S(1)} %get-tuple-element.39), channel_id=1, source_target_pairs={{0,2},{1,3},{4,0},{5,1},{8,4},{9,5},{12,8},{13,9},{14,12},{15,13},... | collective-permute-start | bytes 958472 | tf_op jit(solution)/shard_map/ppermute | solution.py:437
  19.5 3.4 %copy-start.6 = (s32[16,10]{1,0:T(8,128)S(1)}, s32[16,10]{1,0:T(8,128)}, u32[]{:S(2)}) copy-start(s32[16,10]{1,0:T(8,128)} %constant.20.clone.table) | copy-start | bytes 1924
  19.5 9.1 %collective-permute-start.2 = (bf16[416,384]{1,0:T(8,128)(2,1)S(1)}, bf16[416,384]{1,0:T(8,128)(2,1)S(1)}, u32[]{:S(2)}, u32[]{:S(2)}) collective-permute-start(bf16[416,384]{1,0:T(8,128)(2,1)S(1)} %get-tuple-element.35.refs_0_), channel_id=1, source_target_pairs={{0,4},{1,5},{4,8},{5,9},{8,12},{9,13},{12,14},{13,15},{14,10},{15,... | collective-permute-start | bytes 958472 | tf_op jit(solution)/shard_map/ppermute | solution.py:437
  21.3 14.1 %collective-permute-start.10 = (bf16[416,384]{1,0:T(8,128)(2,1)S(1)}, bf16[416,384]{1,0:T(8,128)(2,1)S(1)}, u32[]{:S(2)}, u32[]{:S(2)}) collective-permute-start(bf16[416,384]{1,0:T(8,128)(2,1)S(1)} %get-tuple-element.48), channel_id=1, source_target_pairs={{0,4},{1,5},{4,8},{5,9},{8,12},{9,13},{12,14},{13,15},{14,10},{15,... | collective-permute-start | bytes 958472 | tf_op jit(solution)/shard_map/ppermute | solution.py:437
  22.8 11.4 %collective-permute-start.13 = (bf16[416,384]{1,0:T(8,128)(2,1)S(1)}, bf16[416,384]{1,0:T(8,128)(2,1)S(1)}, u32[]{:S(2)}, u32[]{:S(2)}) collective-permute-start(bf16[416,384]{1,0:T(8,128)(2,1)S(1)} %get-tuple-element.36.refs_0_), channel_id=1, source_target_pairs={{0,2},{1,3},{4,0},{5,1},{8,4},{9,5},{12,8},{13,9},{14,12},{15,13},... | collective-permute-start | bytes 958472 | tf_op jit(solution)/shard_map/ppermute | solution.py:437
  24.8 4.2 %copy-start.5 = (s32[16,10]{1,0:T(8,128)S(1)}, s32[16,10]{1,0:T(8,128)}, u32[]{:S(2)}) copy-start(s32[16,10]{1,0:T(8,128)} %constant.21.clone.table) | copy-start | bytes 1924
  27.4 13.6 %collective-permute-start.6 = (bf16[416,384]{1,0:T(8,128)(2,1)S(1)}, bf16[416,384]{1,0:T(8,128)(2,1)S(1)}, u32[]{:S(2)}, u32[]{:S(2)}) collective-permute-start(bf16[416,384]{1,0:T(8,128)(2,1)S(1)} %add_convert_fusion.7), channel_id=1, source_target_pairs={{0,2},{1,3},{4,0},{5,1},{8,4},{9,5},{12,8},{13,9},{14,12},{15,13},... | collective-permute-start | bytes 958472 | tf_op jit(solution)/shard_map/ppermute | solution.py:437
  28.7 13.6 %collective-permute-start.3 = (bf16[416,384]{1,0:T(8,128)(2,1)S(1)}, bf16[416,384]{1,0:T(8,128)(2,1)S(1)}, u32[]{:S(2)}, u32[]{:S(2)}) collective-permute-start(bf16[416,384]{1,0:T(8,128)(2,1)S(1)} %add_convert_fusion.9), channel_id=1, source_target_pairs={{0,4},{1,5},{4,8},{5,9},{8,12},{9,13},{12,14},{13,15},{14,10},{15,... | collective-permute-start | bytes 958472 | tf_op jit(solution)/shard_map/ppermute | solution.py:437
  30.7 5.1 %copy-start.4 = (s32[16,10]{1,0:T(8,128)S(1)}, s32[16,10]{1,0:T(8,128)}, u32[]{:S(2)}) copy-start(s32[16,10]{1,0:T(8,128)} %constant.22.clone.table) | copy-start | bytes 1924
  34.2 13.6 %collective-permute-start.14 = (bf16[416,384]{1,0:T(8,128)(2,1)S(1)}, bf16[416,384]{1,0:T(8,128)(2,1)S(1)}, u32[]{:S(2)}, u32[]{:S(2)}) collective-permute-start(bf16[416,384]{1,0:T(8,128)(2,1)S(1)} %add_convert_fusion.1), channel_id=1, source_target_pairs={{0,2},{1,3},{4,0},{5,1},{8,4},{9,5},{12,8},{13,9},{14,12},{15,13},... | collective-permute-start | bytes 958472 | tf_op jit(solution)/shard_map/ppermute | solution.py:437
  35.5 13.6 %collective-permute-start.11 = (bf16[416,384]{1,0:T(8,128)(2,1)S(1)}, bf16[416,384]{1,0:T(8,128)(2,1)S(1)}, u32[]{:S(2)}, u32[]{:S(2)}) collective-permute-start(bf16[416,384]{1,0:T(8,128)(2,1)S(1)} %add_convert_fusion.3), channel_id=1, source_target_pairs={{0,4},{1,5},{4,8},{5,9},{8,12},{9,13},{12,14},{13,15},{14,10},{15,... | collective-permute-start | bytes 958472 | tf_op jit(solution)/shard_map/ppermute | solution.py:437
  37.6 5.1 %copy-start.3 = (s32[16,10]{1,0:T(8,128)S(1)}, s32[16,10]{1,0:T(8,128)}, u32[]{:S(2)}) copy-start(s32[16,10]{1,0:T(8,128)} %constant.23.clone.table) | copy-start | bytes 1924
  41.1 13.6 %collective-permute-start.8 = (bf16[416,384]{1,0:T(8,128)(2,1)S(1)}, bf16[416,384]{1,0:T(8,128)(2,1)S(1)}, u32[]{:S(2)}, u32[]{:S(2)}) collective-permute-start(bf16[416,384]{1,0:T(8,128)(2,1)S(1)} %add_convert_fusion.5), channel_id=1, source_target_pairs={{0,2},{1,3},{4,0},{5,1},{8,4},{9,5},{12,8},{13,9},{14,12},{15,13},... | collective-permute-start | bytes 958472 | tf_op jit(solution)/shard_map/ppermute | solution.py:437
  42.4 13.6 %collective-permute-start.5 = (bf16[416,384]{1,0:T(8,128)(2,1)S(1)}, bf16[416,384]{1,0:T(8,128)(2,1)S(1)}, u32[]{:S(2)}, u32[]{:S(2)}) collective-permute-start(bf16[416,384]{1,0:T(8,128)(2,1)S(1)} %add_convert_fusion.8), channel_id=1, source_target_pairs={{0,4},{1,5},{4,8},{5,9},{8,12},{9,13},{12,14},{13,15},{14,10},{15,... | collective-permute-start | bytes 958472 | tf_op jit(solution)/shard_map/ppermute | solution.py:437
  44.4 5.1 %copy-start.2 = (s32[16,10]{1,0:T(8,128)S(1)}, s32[16,10]{1,0:T(8,128)}, u32[]{:S(2)}) copy-start(s32[16,10]{1,0:T(8,128)} %constant.24.clone.table) | copy-start | bytes 1924
  47.9 24.7 %collective-permute-start.15 = (bf16[416,384]{1,0:T(8,128)(2,1)S(1)}, bf16[416,384]{1,0:T(8,128)(2,1)S(1)}, u32[]{:S(2)}, u32[]{:S(2)}) collective-permute-start(bf16[416,384]{1,0:T(8,128)(2,1)S(1)} %add_convert_fusion), channel_id=1, source_target_pairs={{0,2},{1,3},{4,0},{5,1},{8,4},{9,5},{12,8},{13,9},{14,12},{15,13},... | collective-permute-start | bytes 958472 | tf_op jit(solution)/shard_map/ppermute | solution.py:437
  49.2 13.2 %collective-permute-start.12 = (bf16[416,384]{1,0:T(8,128)(2,1)S(1)}, bf16[416,384]{1,0:T(8,128)(2,1)S(1)}, u32[]{:S(2)}, u32[]{:S(2)}) collective-permute-start(bf16[416,384]{1,0:T(8,128)(2,1)S(1)} %add_convert_fusion.2), channel_id=1, source_target_pairs={{0,4},{1,5},{4,8},{5,9},{8,12},{9,13},{12,14},{13,15},{14,10},{15,... | collective-permute-start | bytes 958472 | tf_op jit(solution)/shard_map/ppermute | solution.py:437
  51.3 5.1 %copy-start.1 = (s32[16,10]{1,0:T(8,128)S(1)}, s32[16,10]{1,0:T(8,128)}, u32[]{:S(2)}) copy-start(s32[16,10]{1,0:T(8,128)} %constant.25.clone.table) | copy-start | bytes 1924
  54.8 13.6 %collective-permute-start.9 = (bf16[416,384]{1,0:T(8,128)(2,1)S(1)}, bf16[416,384]{1,0:T(8,128)(2,1)S(1)}, u32[]{:S(2)}, u32[]{:S(2)}) collective-permute-start(bf16[416,384]{1,0:T(8,128)(2,1)S(1)} %add_convert_fusion.4), channel_id=1, source_target_pairs={{0,2},{1,3},{4,0},{5,1},{8,4},{9,5},{12,8},{13,9},{14,12},{15,13},... | collective-permute-start | bytes 958472 | tf_op jit(solution)/shard_map/ppermute | solution.py:437
  56.1 16.6 %copy-start = (s32[16,5]{1,0:T(8,128)S(1)}, s32[16,5]{1,0:T(8,128)}, u32[]{:S(2)}) copy-start(s32[16,5]{1,0:T(8,128)} %constant.26.clone.place) | copy-start | bytes 964
  56.1 16.6 %collective-permute-start.7 = (bf16[416,384]{1,0:T(8,128)(2,1)S(1)}, bf16[416,384]{1,0:T(8,128)(2,1)S(1)}, u32[]{:S(2)}, u32[]{:S(2)}) collective-permute-start(bf16[416,384]{1,0:T(8,128)(2,1)S(1)} %add_convert_fusion.6), channel_id=1, source_target_pairs={{0,4},{1,5},{4,8},{5,9},{8,12},{9,13},{12,14},{13,15},{14,10},{15,... | collective-permute-start | bytes 958472 | tf_op jit(solution)/shard_map/ppermute | solution.py:437
  68.5 10.6 %collective-permute-start.17 = (bf16[384,384]{1,0:T(8,128)(2,1)S(1)}, bf16[384,384]{1,0:T(8,128)(2,1)S(1)}, u32[]{:S(2)}, u32[]{:S(2)}) collective-permute-start(bf16[384,384]{1,0:T(8,128)(2,1)S(1)} %outgoing_one.1.after), channel_id=1, source_target_pairs={{0,2},{1,10},{2,4},{3,12},{4,6},{5,14},{6,0},{7,8},{8,5},{9,11},{1... | collective-permute-start | bytes 884744 | tf_op jit(solution)/shard_map/ppermute | solution.py:489
  73.5 11.9 %collective-permute-start.16 = (bf16[320,384]{1,0:T(8,128)(2,1)S(1)}, bf16[320,384]{1,0:T(8,128)(2,1)S(1)}, u32[]{:S(2)}, u32[]{:S(2)}) collective-permute-start(bf16[320,384]{1,0:T(8,128)(2,1)S(1)} %get-tuple-element.52), channel_id=1, source_target_pairs={{0,4},{1,8},{2,6},{3,10},{4,0},{5,12},{6,2},{7,14},{8,3},{9,13},{1... | collective-permute-start | bytes 737288 | tf_op jit(solution)/shard_map/ppermute | solution.py:490
